TPU v7x, 32 devices: a whole 2x2x4 slice. The times are simulated.
32 devices in a mesh: ep: 16 (over z, x, core), tp: 2 (over y).
Axes of the slice: x: 2, y: 2, z: 4, core: 2. Of those that a mesh axis runs over, the one named last changes fastest.
Arguments:
- tokens: bfloat16 [32768, 1024], P('ep'), may hold values from -6 to 6
- out_grad: bfloat16 [32768, 1024], P(('ep', 'tp')), may hold values from -12 to 12
- lengths: int32 [16], P('ep'), may hold values from 256 to 2048, as said below
- expert_ids: int32 [32768], P('ep'), may hold values from 0 to 15, as said below
- w_query: bfloat16 [1024, 1024], P(None, 'tp'), may hold values from -0.1875 to 0.1875
- w_key: bfloat16 [1024, 1024], P(None, 'tp'), may hold values from -0.1875 to 0.1875
- w_value: bfloat16 [1024, 1024], P(None, 'tp'), may hold values from -0.1875 to 0.1875
- w_output: bfloat16 [1024, 1024], P(None, 'tp'), may hold values from -1.5 to 1.5
- w_hidden: bfloat16 [1024, 4096], P(None, 'tp'), may hold values from -0.1875 to 0.1875
- w_return: bfloat16 [1024, 4096], P(None, 'tp'), may hold values from -0.09375 to 0.09375
- router: bfloat16 [1024, 16], replicated, may hold values from -0.125 to 0.125
- mix_weight: bfloat16 [1024, 2], replicated, may hold values from -0.125 to 0.125
- gain_attn: bfloat16 [1024], replicated, may hold values from 0.5 to 1.5
- bias_attn: bfloat16 [1024], replicated, may hold values from -1.25 to 1.25
- gain_ffn: bfloat16 [1024], replicated, may hold values from 0.5 to 1.5
- bias_ffn: bfloat16 [1024], replicated, may hold values from -1.25 to 1.25
- expert_in: bfloat16 [16, 1024, 4096], P('ep', None, 'tp'), may hold values from -0.1875 to 0.1875
- expert_out: bfloat16 [16, 1024, 4096], P('ep', None, 'tp'), may hold values from -0.09375 to 0.09375
Outputs:
- block_out: bfloat16 [32768, 1024], P(('ep', 'tp'))
- token_grad: float32 [32768, 1024], P(('ep', 'tp'))
- grad_query: float32 [1024, 1024], P('ep', 'tp')
- grad_key: float32 [1024, 1024], P('ep', 'tp')
- grad_value: float32 [1024, 1024], P('ep', 'tp')
- grad_output: float32 [1024, 1024], P('ep', 'tp')
- grad_hidden: float32 [1024, 4096], P('ep', 'tp')
- grad_return: float32 [1024, 4096], P('ep', 'tp')
- grad_router: float32 [1024, 16], replicated
- grad_mix: float32 [1024, 2], replicated
- grad_gain_attn: float32 [1024], replicated
- grad_bias_attn: float32 [1024], replicated
- grad_gain_ffn: float32 [1024], replicated
- grad_bias_ffn: float32 [1024], replicated
- grad_expert_in: float32 [16, 1024, 4096], P('ep', None, 'tp')
- grad_expert_out: float32 [16, 1024, 4096], P('ep', None, 'tp')
Inputs may be any that keep to these rules, and one draw needn't show every extreme that they name: `lengths`: entry i belongs to the sequence at rows i * 2048 to i * 2048 + 2047; positions at and past its length are padding. `expert_ids`: among the live rows of one index of ep (its 2048 rows) no expert is named more than 128 times; values on padding rows are never used.
All inputs are finite; a program needn't handle non-finite values.
Results may differ from a plain program's by a relative error of at most 0.018.
Values may be sent and summed in bfloat16 or wider, within the bound.
A program may use at most 320 MiB of HBM per device.

v0:
```python
from functools import partial

import jax
import jax.numpy as jnp
from jax import lax
from jax.sharding import PartitionSpec as P

HEAD_DIM = 64


EPS = 1e-05
NEG = -1e30


def layer_norm(values, gain, bias):
    middle = jnp.mean(values, axis=-1, keepdims=True)
    centred = values - middle
    spread = jnp.mean(centred * centred, axis=-1, keepdims=True)
    return centred * lax.rsqrt(spread + EPS) * gain + bias


def gelu_tanh(values):
    return jax.nn.gelu(values, approximate=True)


def matmul(left, right):
    return jnp.dot(left, right, preferred_element_type=jnp.float32)


def matmul_nt(left, right):
    return lax.dot_general(
        left, right, (((1,), (1,)), ((), ())), preferred_element_type=jnp.float32
    )


def matmul_tn(left, right):
    return lax.dot_general(
        left, right, (((0,), (0,)), ((), ())), preferred_element_type=jnp.float32
    )


def gate_and_mix(logits, mix_logits, one_hot):
    chances = jax.nn.softmax(logits, axis=-1)
    return (jnp.sum(chances * one_hot, axis=-1), jax.nn.softmax(mix_logits, axis=-1))


def block_scores(query_block, key_all, first_row, score_scale):
    scores = (
        jnp.einsum("qhd,khd->hqk", query_block, key_all, preferred_element_type=jnp.float32)
        * score_scale
    )
    query_pos = first_row + jnp.arange(query_block.shape[0])
    key_pos = jnp.arange(key_all.shape[0])
    allowed = key_pos[None, :] <= query_pos[:, None]
    return jnp.where(allowed[None], scores, NEG)


def attention_forward(queries, key_all, values, score_scale):
    seq_len, head_count, head_width = queries.shape
    block_rows = min(512, seq_len)
    count_blocks = seq_len // block_rows
    blocks = queries.reshape(count_blocks, block_rows, head_count, head_width)
    firsts = jnp.arange(count_blocks) * block_rows

    def one_block(inputs):
        query_block, first_row = inputs
        scores = block_scores(query_block, key_all, first_row, score_scale)
        row_max = jnp.max(scores, axis=-1, keepdims=True)
        weights = jnp.exp(scores - row_max)
        totals = jnp.sum(weights, axis=-1, keepdims=True)
        weights_low = (weights / totals).astype(jnp.bfloat16)
        output = jnp.einsum("hqk,khd->qhd", weights_low, values, preferred_element_type=jnp.float32)
        return (output.astype(jnp.bfloat16), (row_max + jnp.log(totals))[..., 0])

    outputs, log_sums = lax.map(one_block, (blocks, firsts))
    return (outputs.reshape(seq_len, head_count, head_width), log_sums)


def attention_backward(queries, key_all, values, heads_grad, log_sums, score_scale):
    seq_len, head_count, head_width = queries.shape
    block_rows = min(512, seq_len)
    count_blocks = seq_len // block_rows
    query_blocks = queries.reshape(count_blocks, block_rows, head_count, head_width)
    grad_blocks = heads_grad.reshape(count_blocks, block_rows, head_count, head_width)
    firsts = jnp.arange(count_blocks) * block_rows

    def one_block(running, inputs):
        key_grad, value_grad = running
        query_block, grad_block, log_sum, first_row = inputs
        scores = block_scores(query_block, key_all, first_row, score_scale)
        chances = jnp.exp(scores - log_sum[..., None])
        prob_grad = jnp.einsum(
            "qhd,khd->hqk", grad_block, values, preferred_element_type=jnp.float32
        )
        centre = jnp.sum(chances * prob_grad, axis=-1, keepdims=True)
        score_grad = (chances * (prob_grad - centre)).astype(jnp.bfloat16)
        query_grad = (
            jnp.einsum("hqk,khd->qhd", score_grad, key_all, preferred_element_type=jnp.float32)
            * score_scale
        )
        key_grad = (
            key_grad
            + jnp.einsum(
                "hqk,qhd->khd", score_grad, query_block, preferred_element_type=jnp.float32
            )
            * score_scale
        )
        value_grad = value_grad + jnp.einsum(
            "hqk,qhd->khd",
            chances.astype(jnp.bfloat16),
            grad_block,
            preferred_element_type=jnp.float32,
        )
        return ((key_grad, value_grad), query_grad)

    zero_grads = jnp.zeros((seq_len, head_count, head_width), jnp.float32)
    (key_grad, value_grad), query_grads = lax.scan(
        one_block, (zero_grads, zero_grads), (query_blocks, grad_blocks, log_sums, firsts)
    )
    return (query_grads.reshape(seq_len, head_count, head_width), key_grad, value_grad)


def on_device(
    tokens,
    out_grad,
    lengths,
    expert_ids,
    w_query,
    w_key,
    w_value,
    w_output,
    w_hidden,
    w_return,
    router,
    mix_weight,
    gain_attn,
    bias_attn,
    gain_ffn,
    bias_ffn,
    expert_in,
    expert_out,
):
    shard_rows = out_grad.shape[0]
    all_rows = tokens.shape[0]
    model_width = tokens.shape[1]
    expert_count = router.shape[1]
    local_experts = expert_in.shape[0]
    capacity = all_rows // expert_count
    seq_count = lengths.shape[0]
    seq_len = all_rows // seq_count
    head_width = HEAD_DIM
    local_width = w_query.shape[1]
    local_heads = local_width // head_width
    score_scale = head_width ** (-0.5)
    first_row = lax.axis_index("tp") * shard_rows

    def shard_of(values):
        return lax.dynamic_slice_in_dim(values, first_row, shard_rows, 0)

    positions = jnp.arange(all_rows)
    seq_index = positions // seq_len
    row_limit = jnp.sum(
        jnp.where(seq_index[:, None] == jnp.arange(seq_count)[None, :], lengths[None, :], 0), axis=1
    )
    live_all = (positions % seq_len < row_limit).astype(jnp.float32)[:, None]
    live = shard_of(live_all)
    attn_gain = gain_attn.astype(jnp.float32)
    attn_bias = bias_attn.astype(jnp.float32)
    ffn_gain = gain_ffn.astype(jnp.float32)
    ffn_bias = bias_ffn.astype(jnp.float32)
    tokens_wide = tokens.astype(jnp.float32)
    attn_in = layer_norm(tokens_wide, attn_gain, attn_bias).astype(jnp.bfloat16)
    qkv_weight = jnp.concatenate([w_query, w_key, w_value], axis=1)
    projected = matmul(attn_in, qkv_weight).astype(jnp.bfloat16)
    head_shape = (seq_count, seq_len, local_heads, head_width)
    queries = projected[:, :local_width].reshape(head_shape)
    key_all = projected[:, local_width : 2 * local_width].reshape(head_shape)
    values = projected[:, 2 * local_width :].reshape(head_shape)
    heads_low, log_sums = jax.vmap(attention_forward, in_axes=(0, 0, 0, None))(
        queries, key_all, values, score_scale
    )
    attn_out = heads_low.reshape(all_rows, local_width)
    attn_sum = lax.psum(matmul_nt(attn_out, w_output), "tp")
    resid = tokens_wide + attn_sum
    ffn_in = layer_norm(resid, ffn_gain, ffn_bias).astype(jnp.bfloat16)
    logits = matmul(ffn_in, router)
    mix_logits = matmul(ffn_in, mix_weight)
    one_hot = (expert_ids[:, None] == jnp.arange(expert_count)[None, :]).astype(jnp.float32)
    gate_all, mix_all = gate_and_mix(logits, mix_logits, one_hot)
    hidden_pre = matmul(ffn_in, w_hidden)
    hidden_low = gelu_tanh(hidden_pre).astype(jnp.bfloat16)
    dense_part = matmul_nt(hidden_low, w_return)
    routed = one_hot * live_all
    slots = jnp.sum((jnp.cumsum(routed, axis=0) - routed) * one_hot, axis=1).astype(jnp.int32)
    slot_count = expert_count * capacity
    target = jnp.where(live_all[:, 0] > 0, expert_ids * capacity + slots, slot_count)
    packed = jnp.zeros((slot_count, model_width), jnp.bfloat16).at[target].set(ffn_in, mode="drop")
    packed = packed.reshape(expert_count, capacity, model_width)
    mine = (live_all[:, 0] > 0) & (slots >= 0) & (slots < capacity)
    take_index = jnp.where(mine, expert_ids * capacity + slots, 0)
    mine_col = mine.astype(jnp.float32)[:, None]
    sent_rows = lax.all_to_all(packed, "ep", split_axis=0, concat_axis=0, tiled=True)
    source_count = sent_rows.shape[0]
    group_shape = (-1, local_experts, capacity, model_width)
    rows_grouped = sent_rows.reshape(group_shape)
    pre_grouped = jnp.einsum(
        "sekd,edf->sekf", rows_grouped, expert_in, preferred_element_type=jnp.float32
    )
    act_grouped = gelu_tanh(pre_grouped).astype(jnp.bfloat16)
    result = jnp.einsum(
        "sekf,edf->sekd", act_grouped, expert_out, preferred_element_type=jnp.float32
    )
    result = result.reshape(source_count, capacity, model_width)
    returned = lax.all_to_all(
        result.astype(jnp.bfloat16), "ep", split_axis=0, concat_axis=0, tiled=True
    ).astype(result.dtype)
    moe_part = returned.reshape(expert_count * capacity, model_width)[take_index] * mine_col
    stacked = jnp.stack([dense_part, moe_part], axis=1)
    summed = lax.psum_scatter(
        stacked.astype(jnp.bfloat16), "tp", scatter_dimension=0, tiled=True
    ).astype(jnp.float32)
    resid_shard = shard_of(resid)
    gate_shard = shard_of(gate_all)
    mix_shard = shard_of(mix_all)
    dense_sum = summed[:, 0]
    moe_sum = summed[:, 1]
    total_out = (
        resid_shard
        + mix_shard[:, 0:1] * dense_sum
        + mix_shard[:, 1:2] * gate_shard[:, None] * moe_sum
    )
    block_out = (live * total_out).astype(jnp.bfloat16)
    live_grad = live * out_grad.astype(jnp.float32)
    dense_grad = (live_grad * mix_shard[:, 0:1]).astype(jnp.bfloat16)
    moe_grad = (live_grad * mix_shard[:, 1:2] * gate_shard[:, None]).astype(jnp.bfloat16)
    outgoing = jnp.stack([dense_grad, moe_grad], axis=1)
    incoming = lax.all_gather(outgoing, "tp", axis=0, tiled=True)
    dense_all = incoming[:, 0]
    moe_all = incoming[:, 1]
    hidden_grad = matmul(dense_all, w_return)
    grad_return = matmul_tn(dense_all, hidden_low)
    gelu_pull = jax.vjp(gelu_tanh, hidden_pre)[1]
    pre_grad = gelu_pull(hidden_grad)[0].astype(jnp.bfloat16)
    grad_hidden = matmul_tn(ffn_in, pre_grad)
    input_part = matmul_nt(pre_grad, w_hidden)
    grad_packed = (
        jnp.zeros((slot_count, model_width), jnp.bfloat16).at[target].set(moe_all, mode="drop")
    )
    grad_packed = grad_packed.reshape(expert_count, capacity, model_width)
    grad_sent = lax.all_to_all(grad_packed, "ep", split_axis=0, concat_axis=0, tiled=True)
    grad_grouped = grad_sent.reshape(group_shape)
    act_grad = jnp.einsum(
        "sekd,edf->sekf", grad_grouped, expert_out, preferred_element_type=jnp.float32
    )
    grad_expert_out = jnp.einsum(
        "sekd,sekf->edf", grad_grouped, act_grouped, preferred_element_type=jnp.float32
    )
    expert_pull = jax.vjp(gelu_tanh, pre_grouped)[1]
    expert_pre_grad = expert_pull(act_grad)[0].astype(jnp.bfloat16)
    grad_expert_in = jnp.einsum(
        "sekd,sekf->edf", rows_grouped, expert_pre_grad, preferred_element_type=jnp.float32
    )
    row_grad = jnp.einsum(
        "sekf,edf->sekd", expert_pre_grad, expert_in, preferred_element_type=jnp.float32
    )
    row_grad = row_grad.reshape(source_count, capacity, model_width)
    back_grad = lax.all_to_all(
        row_grad.astype(jnp.bfloat16), "ep", split_axis=0, concat_axis=0, tiled=True
    ).astype(row_grad.dtype)
    input_part = (
        input_part + back_grad.reshape(expert_count * capacity, model_width)[take_index] * mine_col
    )
    input_grad = lax.psum_scatter(
        input_part.astype(jnp.bfloat16), "tp", scatter_dimension=0, tiled=True
    ).astype(jnp.float32)
    first_dot = jnp.sum(live_grad * dense_sum, axis=1)
    second_dot = jnp.sum(live_grad * moe_sum, axis=1)
    mix_grad = jnp.stack([first_dot, gate_shard * second_dot], axis=1)
    gate_grad = mix_shard[:, 1] * second_dot
    ffn_shard = shard_of(ffn_in)
    gate_pull = jax.vjp(
        partial(gate_and_mix, one_hot=shard_of(one_hot)), shard_of(logits), shard_of(mix_logits)
    )[1]
    logit_grad, mix_logit_grad = gate_pull((gate_grad, mix_grad))
    logit_low = logit_grad.astype(jnp.bfloat16)
    mix_low = mix_logit_grad.astype(jnp.bfloat16)
    grad_router = matmul_tn(ffn_shard, logit_low)
    grad_mix = matmul_tn(ffn_shard, mix_low)
    ffn_in_grad = input_grad + matmul_nt(logit_low, router) + matmul_nt(mix_low, mix_weight)
    norm_pull_two = jax.vjp(layer_norm, resid_shard, ffn_gain, ffn_bias)[1]
    resid_part, grad_gain_ffn, grad_bias_ffn = norm_pull_two(ffn_in_grad)
    resid_grad = live_grad + resid_part
    attn_grad_all = lax.all_gather(resid_grad.astype(jnp.bfloat16), "tp", axis=0, tiled=True)
    grad_output = matmul_tn(attn_grad_all, attn_out)
    heads_grad = matmul(attn_grad_all, w_output).astype(jnp.bfloat16).reshape(head_shape)
    query_grad, key_grad, value_grad = jax.vmap(attention_backward, in_axes=(0, 0, 0, 0, 0, None))(
        queries, key_all, values, heads_grad, log_sums, score_scale
    )
    qkv_grad = jnp.concatenate(
        [
            query_grad.reshape(all_rows, local_width),
            key_grad.reshape(all_rows, local_width),
            value_grad.reshape(all_rows, local_width),
        ],
        axis=1,
    ).astype(jnp.bfloat16)
    grad_weights = matmul_tn(attn_in, qkv_grad)
    grad_query = grad_weights[:, :local_width]
    grad_key = grad_weights[:, local_width : 2 * local_width]
    grad_value = grad_weights[:, 2 * local_width :]
    attn_in_grad = lax.psum_scatter(
        matmul_nt(qkv_grad, qkv_weight).astype(jnp.bfloat16), "tp", scatter_dimension=0, tiled=True
    ).astype(jnp.float32)
    norm_pull_one = jax.vjp(layer_norm, shard_of(tokens_wide), attn_gain, attn_bias)[1]
    token_part, grad_gain_attn, grad_bias_attn = norm_pull_one(attn_in_grad)
    token_grad = resid_grad + token_part
    grad_query, grad_key, grad_value, grad_output, grad_hidden, grad_return = (
        lax.psum_scatter(
            grad_query.astype(jnp.bfloat16), "ep", scatter_dimension=0, tiled=True
        ).astype(jnp.float32),
        lax.psum_scatter(
            grad_key.astype(jnp.bfloat16), "ep", scatter_dimension=0, tiled=True
        ).astype(jnp.float32),
        lax.psum_scatter(
            grad_value.astype(jnp.bfloat16), "ep", scatter_dimension=0, tiled=True
        ).astype(jnp.float32),
        lax.psum_scatter(
            grad_output.astype(jnp.bfloat16), "ep", scatter_dimension=0, tiled=True
        ).astype(jnp.float32),
        lax.psum_scatter(
            grad_hidden.astype(jnp.bfloat16), "ep", scatter_dimension=0, tiled=True
        ).astype(jnp.float32),
        lax.psum_scatter(
            grad_return.astype(jnp.bfloat16), "ep", scatter_dimension=0, tiled=True
        ).astype(jnp.float32),
    )
    grad_router, grad_mix, grad_gain_attn, grad_bias_attn, grad_gain_ffn, grad_bias_ffn = lax.psum(
        (grad_router, grad_mix, grad_gain_attn, grad_bias_attn, grad_gain_ffn, grad_bias_ffn),
        ("ep", "tp"),
    )
    return (
        block_out,
        token_grad,
        grad_query,
        grad_key,
        grad_value,
        grad_output,
        grad_hidden,
        grad_return,
        grad_router,
        grad_mix,
        grad_gain_attn,
        grad_bias_attn,
        grad_gain_ffn,
        grad_bias_ffn,
        grad_expert_in,
        grad_expert_out,
    )


def solution(mesh):
    in_specs = (
        P("ep", None),
        P(("ep", "tp"), None),
        P("ep"),
        P("ep"),
        P(None, "tp"),
        P(None, "tp"),
        P(None, "tp"),
        P(None, "tp"),
        P(None, "tp"),
        P(None, "tp"),
        P(),
        P(),
        P(),
        P(),
        P(),
        P(),
        P("ep", None, "tp"),
        P("ep", None, "tp"),
    )
    out_specs = (
        P(("ep", "tp"), None),
        P(("ep", "tp"), None),
        P("ep", "tp"),
        P("ep", "tp"),
        P("ep", "tp"),
        P("ep", "tp"),
        P("ep", "tp"),
        P("ep", "tp"),
        P(),
        P(),
        P(),
        P(),
        P(),
        P(),
        P("ep", None, "tp"),
        P("ep", None, "tp"),
    )
    return jax.shard_map(
        on_device, mesh=mesh, in_specs=in_specs, out_specs=out_specs, check_vma=False
    )
```

profile of v0, /device:TPU:0, one launch (start us, length us, event | category | flops | bytes accessed | tf_op | source)
XLA Modules:
  0.0 2242.3 jit_solution(8227098331032995823)
XLA Ops:
  29.4 193.0 %while.27 = (s32[]{:T(128)}, bf16[4,1,512,8,64]{2,4,3,1,0:T(8,128)(2,1)}, f32[4,1,8,512]{3,2,1,0:T(8,128)}, s32[4]{0:T(128)S(1)}, bf16[4,1,512,8,64]{2,4,3,1,0:T...) while((s32[]{:T(128)}, ...), condition=%wide.region_5.6_spmd, body=%wide.region_2.5_spmd.sunk | while | flops 2249454080 | bytes 110235768 | solution.py:75
  31.5 15.1 fusion.213
  46.6 15.0 fusion.214
  61.5 15.6 fusion.215
  79.6 15.1 fusion.213
  94.7 15.0 fusion.214
  109.7 15.6 fusion.215
  127.8 15.1 fusion.213
  142.9 15.0 fusion.214
  157.8 15.6 fusion.215
  175.9 15.1 fusion.213
  191.0 15.0 fusion.214
  206.0 15.6 fusion.215
  239.3 195.1 %all-reduce.4.cloned.1.call-done = f32[2048,1024]{1,0:T(8,128)} async-done(((f32[2048,1024]{1,0:T(8,128)}), f32[2048,1024]{1,0:T(8,128)}) %all-reduce.4.cloned.1.call-update) | async-done | bytes 8388624 | tf_op jit(solution)/shard_map/psum | solution.py:183
  449.3 15.1 scatter_custom_fusion
  464.4 98.1 %all_to_all.20 = bf16[16,128,1024]{2,1,0:T(8,128)(2,1)S(1)} all-to-all(bf16[16,128,1024]{2,1,0:T(8,128)(2,1)} %bitcast.317), channel_id=1, replica_groups=mesh['ep'=16,'tp'=2] {'ep'}, dimensions={0} | all-to-all | bytes 8388608 | tf_op jit(solution)/shard_map/all_to_all | solution.py:202
  564.5 11.4 fusion.91
  575.9 14.9 fusion.94
  596.3 15.4 fusion.169
  611.7 15.0 convert_bitcast_fusion
  626.7 47.1 %all-to-all-done.1 = bf16[16,128,1024]{2,1,0:T(8,128)(2,1)} async-done(((bf16[16,128,1024]{2,1,0:T(8,128)(2,1)}), bf16[16,128,1024]{2,1,0:T(8,128)(2,1)}, u32[]{:S(2)}, u32[]{:S(2)}) %all-to-all-start.1) | async-done | bytes 4194336 | tf_op jit(solution)/shard_map/all_to_all | solution.py:214
  680.5 15.2 gather_fusion
  710.6 109.1 %reduce-scatter.10.cloned.1.call-done = bf16[1024,2,1024]{2,0,1:T(8,128)(2,1)} async-done(((bf16[2048,2,1024]{2,0,1:T(8,128)(2,1)}), bf16[1024,2,1024]{2,0,1:T(8,128)(2,1)}) %reduce-scatter.10.cloned.1.call-update) | async-done | bytes 4194320 | tf_op jit(solution)/shard_map/reduce_scatter | solution.py:219
  830.8 104.2 %all-gather.3.cloned.1.call-done = bf16[2048,2,1024]{2,0,1:T(8,128)(2,1)} async-done(((bf16[1024,2,1024]{2,0,1:T(8,128)(2,1)}), bf16[2048,2,1024]{2,0,1:T(8,128)(2,1)}) %all-gather.3.cloned.1.call-update) | async-done | bytes 8388624 | tf_op jit(solution)/shard_map/all_gather | solution.py:237
  935.0 13.1 scatter_custom_fusion.1
  948.1 98.5 %all_to_all.21 = bf16[16,128,1024]{2,1,0:T(8,128)(2,1)S(1)} all-to-all(bf16[16,128,1024]{2,1,0:T(8,128)(2,1)} %bitcast.316), channel_id=1, replica_groups=mesh['ep'=16,'tp'=2] {'ep'}, dimensions={0} | all-to-all | bytes 8388608 | tf_op jit(solution)/shard_map/all_to_all | solution.py:250
  1046.6 24.3 %fusion.63 = bf16[16,1,128,2048]{3,2,0,1:T(8,128)(2,1)} fusion(f32[16,128,2048]{2,1,0:T(8,128)} %fusion.91, bf16[16,128,1024]{2,1,0:T(8,128)(2,1)S(1)} %all_to_all.21, bf16[1,1024,2048]{2,1,0:T(8,128)(2,1)S(1)} %copy-done.88), kind=kOutput, calls=%fused_computation.71 | convolution fusion | flops 8673820672 | bytes 33554432 | tf_op jit(solution)/shard_map/sekd,edf->sekf/dot_general | solution.py:252
  1071.0 13.9 fusion.99
  1090.4 23.7 %fusion.56 = bf16[2048,2048]{1,0:T(8,128)(2,1)} fusion(f32[2048,2048]{1,0:T(8,128)} %fusion.169, bf16[1024,2048]{1,0:T(8,128)(2,1)} %param.31, bf16[2048,2,1024]{2,0,1:T(8,128)(2,1)} %all-gather.3.cloned.1.call-done), kind=kOutput, calls=%fused_computation.64 | convolution fusion | flops 8673820672 | bytes 33554432 | tf_op jit(solution)/shard_map/dot_general | solution.py:27
  1114.1 53.7 %all-to-all-done.3 = bf16[16,128,1024]{2,1,0:T(8,128)(2,1)} async-done(((bf16[16,128,1024]{2,1,0:T(8,128)(2,1)}), bf16[16,128,1024]{2,1,0:T(8,128)(2,1)}, u32[]{:S(2)}, u32[]{:S(2)}) %all-to-all-start.3) | async-done | bytes 4194336 | tf_op jit(solution)/shard_map/all_to_all | solution.py:267
  1174.5 15.1 gather_fusion.1
  1189.6 15.8 add_convert_fusion
  1215.8 58.1 %reduce-scatter.12.cloned.1.call-done = bf16[1024,1024]{1,0:T(8,128)(2,1)} async-done(((bf16[2048,1024]{1,0:T(8,128)(2,1)}), bf16[1024,1024]{1,0:T(8,128)(2,1)}) %reduce-scatter.12.cloned.1.call-update) | async-done | bytes 2097168 | tf_op jit(solution)/shard_map/reduce_scatter | solution.py:273
  1291.2 15.6 convolution_convert_fusion.3
  1306.9 14.0 convolution_convert_fusion.4
  1321.1 27.0 %all-gather.5.cloned.1.call-done = bf16[2048,1024]{1,0:T(8,128)(2,1)} async-done(((bf16[1024,1024]{1,0:T(8,128)(2,1)}), bf16[2048,1024]{1,0:T(8,128)(2,1)}) %all-gather.5.cloned.1.call-update) | async-done | bytes 4194320 | tf_op jit(solution)/shard_map/all_gather | solution.py:293
  1362.0 439.7 %while.28 = (s32[]{:T(128)}, f32[1,2048,8,64]{1,3,2,0:T(8,128)}, f32[1,2048,8,64]{1,3,2,0:T(8,128)}, bf16[4,1,512,8,64]{2,4,3,1,0:T(8,128)(2,1)}, bf16[4,1,512,8...) while((s32[]{:T(128)}, f32[1,2048,8,64]{1,3,2,0:T(8,128)}, ...), condition=%wide.region_35.36_spmd.clone, body=%wide.region_33.35_spmd.clone.sunk | while | flops 5450756608 | bytes 347164864 | solution.py:117
  1364.8 18.1 fusion.224
  1382.9 26.3 %multiply_reduce_fusion.12 = (f32[8,512]{1,0:T(8,128)S(1)}, f32[8,512,2048]{2,1,0:T(8,128)}) fusion(f32[8,512,2048]{2,1,0:T(8,128)} %fusion.224, f32[8,512]{1,0:T(8,128)S(1)} %dynamic-slice_bitcast_fusion.2, bf16[1,2048,8,64]{1,3,2,0:T(8,128)(2,1)} %get-tuple-element.430, bf16[4,1,512,8,64]{2,4,3,1,0:T(8,128)(2,1)} %get-tuple-element.428, ...), kind=kOutput, calls=%fused_computation.25.clone.1 | convolution fusion | flops 1115680768 | bytes 70811648 | tf_op jit(solution)/shard_map/vmap()/while/body/eval_jaxpr/qhd,khd->hqk/dot_general | solution.py:49
  1409.2 27.9 %multiply_convert_fusion.14 = bf16[8,512,2048]{2,1,0:T(8,128)(2,1)} fusion(f32[8,512,2048]{2,1,0:T(8,128)} %get-tuple-element.374, f32[8,512,2048]{2,1,0:T(8,128)} %fusion.224, f32[8,512]{1,0:T(8,128)S(1)} %get-tuple-element.375), kind=kLoop, calls=%fused_computation.24.clone.1 | loop fusion | flops 25165824 | bytes 83902464 | tf_op jit(solution)/shard_map/vmap()/while/body/eval_jaxpr/convert_element_type | solution.py:96
  1437.1 17.3 bitcast_add_fusion.5
  1454.4 10.7 fusion.225
  1475.2 17.6 fusion.224
  1492.8 26.3 %multiply_reduce_fusion.12 = (f32[8,512]{1,0:T(8,128)S(1)}, f32[8,512,2048]{2,1,0:T(8,128)}) fusion(f32[8,512,2048]{2,1,0:T(8,128)} %fusion.224, f32[8,512]{1,0:T(8,128)S(1)} %dynamic-slice_bitcast_fusion.2, bf16[1,2048,8,64]{1,3,2,0:T(8,128)(2,1)} %get-tuple-element.430, bf16[4,1,512,8,64]{2,4,3,1,0:T(8,128)(2,1)} %get-tuple-element.428, ...), kind=kOutput, calls=%fused_computation.25.clone.1 | convolution fusion | flops 1115680768 | bytes 70811648 | tf_op jit(solution)/shard_map/vmap()/while/body/eval_jaxpr/qhd,khd->hqk/dot_general | solution.py:49
  1519.2 27.4 %multiply_convert_fusion.14 = bf16[8,512,2048]{2,1,0:T(8,128)(2,1)} fusion(f32[8,512,2048]{2,1,0:T(8,128)} %get-tuple-element.374, f32[8,512,2048]{2,1,0:T(8,128)} %fusion.224, f32[8,512]{1,0:T(8,128)S(1)} %get-tuple-element.375), kind=kLoop, calls=%fused_computation.24.clone.1 | loop fusion | flops 25165824 | bytes 83902464 | tf_op jit(solution)/shard_map/vmap()/while/body/eval_jaxpr/convert_element_type | solution.py:96
  1546.6 17.0 bitcast_add_fusion.5
  1585.0 17.4 fusion.224
  1602.4 26.3 %multiply_reduce_fusion.12 = (f32[8,512]{1,0:T(8,128)S(1)}, f32[8,512,2048]{2,1,0:T(8,128)}) fusion(f32[8,512,2048]{2,1,0:T(8,128)} %fusion.224, f32[8,512]{1,0:T(8,128)S(1)} %dynamic-slice_bitcast_fusion.2, bf16[1,2048,8,64]{1,3,2,0:T(8,128)(2,1)} %get-tuple-element.430, bf16[4,1,512,8,64]{2,4,3,1,0:T(8,128)(2,1)} %get-tuple-element.428, ...), kind=kOutput, calls=%fused_computation.25.clone.1 | convolution fusion | flops 1115680768 | bytes 70811648 | tf_op jit(solution)/shard_map/vmap()/while/body/eval_jaxpr/qhd,khd->hqk/dot_general | solution.py:49
  1628.7 27.4 %multiply_convert_fusion.14 = bf16[8,512,2048]{2,1,0:T(8,128)(2,1)} fusion(f32[8,512,2048]{2,1,0:T(8,128)} %get-tuple-element.374, f32[8,512,2048]{2,1,0:T(8,128)} %fusion.224, f32[8,512]{1,0:T(8,128)S(1)} %get-tuple-element.375), kind=kLoop, calls=%fused_computation.24.clone.1 | loop fusion | flops 25165824 | bytes 83902464 | tf_op jit(solution)/shard_map/vmap()/while/body/eval_jaxpr/convert_element_type | solution.py:96
  1656.1 17.0 bitcast_add_fusion.5
  1694.5 17.4 fusion.224
  1711.9 26.3 %multiply_reduce_fusion.12 = (f32[8,512]{1,0:T(8,128)S(1)}, f32[8,512,2048]{2,1,0:T(8,128)}) fusion(f32[8,512,2048]{2,1,0:T(8,128)} %fusion.224, f32[8,512]{1,0:T(8,128)S(1)} %dynamic-slice_bitcast_fusion.2, bf16[1,2048,8,64]{1,3,2,0:T(8,128)(2,1)} %get-tuple-element.430, bf16[4,1,512,8,64]{2,4,3,1,0:T(8,128)(2,1)} %get-tuple-element.428, ...), kind=kOutput, calls=%fused_computation.25.clone.1 | convolution fusion | flops 1115680768 | bytes 70811648 | tf_op jit(solution)/shard_map/vmap()/while/body/eval_jaxpr/qhd,khd->hqk/dot_general | solution.py:49
  1738.1 27.4 %multiply_convert_fusion.14 = bf16[8,512,2048]{2,1,0:T(8,128)(2,1)} fusion(f32[8,512,2048]{2,1,0:T(8,128)} %get-tuple-element.374, f32[8,512,2048]{2,1,0:T(8,128)} %fusion.224, f32[8,512]{1,0:T(8,128)S(1)} %get-tuple-element.375), kind=kLoop, calls=%fused_computation.24.clone.1 | loop fusion | flops 25165824 | bytes 83902464 | tf_op jit(solution)/shard_map/vmap()/while/body/eval_jaxpr/convert_element_type | solution.py:96
  1765.5 17.0 bitcast_add_fusion.5
  1815.5 11.1 convolution_convert_fusion.1
  1829.8 11.0 convolution_convert_fusion.2
  1854.8 16.4 fusion.79
  1871.1 13.6 fusion.82
  1886.3 47.2 %reduce-scatter.16.cloned.1.call-done = bf16[64,512]{1,0:T(8,128)(2,1)} async-done(((bf16[1024,512]{1,0:T(8,128)(2,1)}), bf16[64,512]{1,0:T(8,128)(2,1)}) %reduce-scatter.16.cloned.1.call-update) | async-done | bytes 65552 | tf_op jit(solution)/shard_map/reduce_scatter | solution.py:318
  1935.0 58.4 %reduce-scatter.18.cloned.1.call-done = bf16[64,512]{1,0:T(8,128)(2,1)} async-done(((bf16[1024,512]{1,0:T(8,128)(2,1)}), bf16[64,512]{1,0:T(8,128)(2,1)}) %reduce-scatter.18.cloned.1.call-update) | async-done | bytes 65552 | tf_op jit(solution)/shard_map/reduce_scatter | solution.py:321
  1994.9 58.9 %reduce-scatter.20.cloned.1.call-done = bf16[64,512]{1,0:T(8,128)(2,1)} async-done(((bf16[1024,512]{1,0:T(8,128)(2,1)}), bf16[64,512]{1,0:T(8,128)(2,1)}) %reduce-scatter.20.cloned.1.call-update) | async-done | bytes 65552 | tf_op jit(solution)/shard_map/reduce_scatter | solution.py:324
  2055.3 54.0 %reduce-scatter.14.cloned.1.call-done = bf16[1024,1024]{1,0:T(8,128)(2,1)} async-done(((bf16[2048,1024]{1,0:T(8,128)(2,1)}), bf16[1024,1024]{1,0:T(8,128)(2,1)}) %reduce-scatter.14.cloned.1.call-update) | async-done | bytes 2097168 | tf_op jit(solution)/shard_map/reduce_scatter | solution.py:311
  2123.4 39.9 %all-reduce = (f32[1024,2]{0,1:T(2,128)}, f32[1024]{0:T(1024)}, f32[1024]{0:T(1024)}, f32[1024]{0:T(1024)}, f32[1024]{0:T(1024)}) all-reduce(f32[1024,2]{0,1:T(2,128)S(1)} %fusion.112, f32[1024]{0:T(1024)S(1)} %get-tuple-element.182, f32[1024]{0:T(1024)S(1)} %get-tuple-element.189, ...), channel_id=1, replica_groups=mesh['ep'=16,'tp'=2] {'ep','tp'}, use_global_device_ids=true, to_apply=%region_48.49 | all-reduce | flops 6144 | bytes 49152 | tf_op jit(solution)/shard_map/psum | solution.py:337
  2163.3 70.7 %all-reduce.6.cloned.1.call-done = f32[1024,16]{0,1:T(8,128)} async-done(((f32[1024,16]{0,1:T(8,128)}), f32[1024,16]{0,1:T(8,128)}) %all-reduce.6.cloned.1.call-update) | async-done | bytes 65552 | tf_op jit(solution)/shard_map/psum | solution.py:337
  (368 shorter events, 282.7 us)
Async XLA Ops:
  7.2 220.4 %copy-start = (bf16[1024,512]{1,0:T(8,128)(2,1)S(1)}, bf16[1024,512]{1,0:T(8,128)(2,1)}, u32[]{:S(2)}) copy-start(bf16[1024,512]{1,0:T(8,128)(2,1)} %param.29) | copy-start | bytes 3145732
  7.2 427.2 %all-reduce.4.cloned.1.call-start = ((), (), s32[]{:S(2)}) async-start(), calls=%async_computation.13 | async-start | bytes 16777216 | tf_op jit(solution)/shard_map/psum | solution.py:183
  7.3 4.7 copy-start.9
  8.1 5.6 copy-start.50
  9.1 4.7 copy-start.83
  13.4 8.0 copy-start.80
  13.7 7.7 copy-start.30
  234.2 215.1 %copy-start.42 = (f32[1024]{0:T(1024)}, f32[1024]{0:T(1024)S(1)}, u32[]{:S(2)}) copy-start(f32[1024]{0:T(1024)S(1)} %convert_element_type.175) | copy-start | bytes 12292
  449.3 15.1 copy-start.82
  464.4 100.1 %copy-start.89 = (bf16[1,1024,2048]{2,1,0:T(8,128)(2,1)S(1)}, bf16[1,1024,2048]{2,1,0:T(8,128)(2,1)}, u32[]{:S(2)}) copy-start(bf16[1,1024,2048]{2,1,0:T(8,128)(2,1)} %param.38) | copy-start | bytes 12582916
  564.5 11.4 copy-start.87
  590.8 83.1 %all-to-all-start.1 = ((bf16[16,128,1024]{2,1,0:T(8,128)(2,1)}), bf16[16,128,1024]{2,1,0:T(8,128)(2,1)}, u32[]{:S(2)}, u32[]{:S(2)}) async-start(bf16[16,128,1024]{2,1,0:T(8,128)(2,1)} %fusion.94), calls=%async_computation.1 | async-start | bytes 8388608 | tf_op jit(solution)/shard_map/all_to_all | solution.py:214
  596.2 223.5 %reduce-scatter.10.cloned.1.call-start = ((), (), s32[]{:S(2)}) async-start(), calls=%async_computation.14 | async-start | bytes 12582912 | tf_op jit(solution)/shard_map/reduce_scatter | solution.py:219
  596.2 99.4 %copy-start.72 = (f32[2048]{0:T(1024)}, f32[2048]{0:T(1024)S(1)}, u32[]{:S(2)}) copy-start(f32[2048]{0:T(1024)S(1)} %fusion.145) | copy-start | bytes 24580
  596.3 15.5 copy-start.90
  705.9 229.0 %all-gather.3.cloned.1.call-start = ((), (), s32[]{:S(2)}) async-start(), calls=%async_computation.15 | async-start | bytes 12582912 | tf_op jit(solution)/shard_map/all_gather | solution.py:237
  706.6 120.8 %copy-start.33 = (f32[1024]{0:T(1024)}, f32[1024]{0:T(1024)S(1)}, u32[]{:S(2)}) copy-start(f32[1024]{0:T(1024)S(1)} %dynamic-slice.3) | copy-start | bytes 12292
  710.6 112.3 %copy-start.12 = (bf16[1024,1024]{1,0:T(8,128)(2,1)S(1)}, bf16[1024,1024]{1,0:T(8,128)(2,1)}, u32[]{:S(2)}) copy-start(bf16[1024,1024]{1,0:T(8,128)(2,1)} %param.23) | copy-start | bytes 6291460
  948.1 98.6 %copy-start.88 = (bf16[1,1024,2048]{2,1,0:T(8,128)(2,1)S(1)}, bf16[1,1024,2048]{2,1,0:T(8,128)(2,1)}, u32[]{:S(2)}) copy-start(bf16[1,1024,2048]{2,1,0:T(8,128)(2,1)} %param.39) | copy-start | bytes 12582916
  1046.6 24.3 %copy-start.21 = (bf16[16,128,1024]{2,1,0:T(8,128)(2,1)}, bf16[16,128,1024]{2,1,0:T(8,128)(2,1)S(1)}, u32[]{:S(2)}) copy-start(bf16[16,128,1024]{2,1,0:T(8,128)(2,1)S(1)} %all_to_all.21) | copy-start | bytes 12582916
  1084.8 83.0 %all-to-all-start.3 = ((bf16[16,128,1024]{2,1,0:T(8,128)(2,1)}), bf16[16,128,1024]{2,1,0:T(8,128)(2,1)}, u32[]{:S(2)}, u32[]{:S(2)}) async-start(bf16[16,128,1024]{2,1,0:T(8,128)(2,1)} %fusion.99), calls=%async_computation.4 | async-start | bytes 8388608 | tf_op jit(solution)/shard_map/all_to_all | solution.py:267
  1090.2 183.8 %reduce-scatter.12.cloned.1.call-start = ((), (), s32[]{:S(2)}) async-start(), calls=%async_computation.16 | async-start | bytes 6291456 | tf_op jit(solution)/shard_map/reduce_scatter | solution.py:273
  1174.5 15.1 copy-start.73
  1205.5 142.6 %all-gather.5.cloned.1.call-start = ((), (), s32[]{:S(2)}) async-start(), calls=%async_computation.17 | async-start | bytes 6291456 | tf_op jit(solution)/shard_map/all_gather | solution.py:293
  1206.2 5.9 copy-start.31
  1206.4 67.6 %copy-start.44 = (f32[1024]{0:T(1024)}, f32[1024]{0:T(1024)S(1)}, u32[]{:S(2)}) copy-start(f32[1024]{0:T(1024)S(1)} %dynamic-slice_reduce_fusion.3) | copy-start | bytes 12292
  1206.4 5.7 copy-start.40
  1206.4 5.5 copy-start.65
  1206.4 5.5 copy-start.67
  1206.4 5.5 copy-start.52
  1206.4 5.5 copy-start.54
  1206.4 6.6 copy-start.37
  1209.0 65.0 %copy-start.56 = (f32[1024]{0:T(1024)}, f32[1024]{0:T(1024)S(1)}, u32[]{:S(2)}) copy-start(f32[1024]{0:T(1024)S(1)} %fusion.156) | copy-start | bytes 12292
  1209.0 64.9 %copy-start.43 = (f32[1024]{0:T(1024)S(1)}, f32[1024]{0:T(1024)}, u32[]{:S(2)}) copy-start(f32[1024]{0:T(1024)} %copy-done.42) | copy-start | bytes 12292
  1209.0 64.9 %copy-start.79 = (bf16[1024,2]{0,1:T(2,128)(2,1)S(1)}, bf16[1024,2]{0,1:T(2,128)(2,1)}, u32[]{:S(2)}) copy-start(bf16[1024,2]{0,1:T(2,128)(2,1)} %param.33) | copy-start | bytes 12292
  1212.0 68.0 %copy-start.68 = (f32[1024]{0:T(1024)}, f32[1024]{0:T(1024)S(1)}, u32[]{:S(2)}) copy-start(f32[1024]{0:T(1024)S(1)} %neg.19) | copy-start | bytes 12292
  1215.8 64.1 %copy-start.34 = (f32[1024]{0:T(1024)S(1)}, f32[1024]{0:T(1024)}, u32[]{:S(2)}) copy-start(f32[1024]{0:T(1024)} %copy-done.33) | copy-start | bytes 12292
  1215.8 64.1 %copy-start.63 = (f32[1024,1]{0,1:T(1,128)S(1)}, f32[1024,1]{0,1:T(1,128)}, u32[]{:S(2)}) copy-start(f32[1024,1]{0,1:T(1,128)} %copy-done.62) | copy-start | bytes 12292
  1215.8 64.1 %copy-start.75 = (f32[1024,1]{0,1:T(1,128)S(1)}, f32[1024,1]{0,1:T(1,128)}, u32[]{:S(2)}) copy-start(f32[1024,1]{0,1:T(1,128)} %get-tuple-element.255) | copy-start | bytes 12292
  1280.0 9.1 copy-start.13
  1291.2 560.0 %reduce-scatter.26.cloned.1.call-start = ((), (), s32[]{:S(2)}) async-start(), calls=%async_computation.24 | async-start | bytes 4456448 | tf_op jit(solution)/shard_map/reduce_scatter | solution.py:333
  1306.9 546.1 %reduce-scatter.24.cloned.1.call-start = ((), (), s32[]{:S(2)}) async-start(), calls=%async_computation.23 | async-start | bytes 4456448 | tf_op jit(solution)/shard_map/reduce_scatter | solution.py:330
  1321.0 563.7 %reduce-scatter.22.cloned.1.call-start = ((), (), s32[]{:S(2)}) async-start(), calls=%async_computation.22 | async-start | bytes 1114112 | tf_op jit(solution)/shard_map/reduce_scatter | solution.py:327
  1356.2 5.7 copy-start.93
  1454.4 11.9 copy-start.1
  1563.5 11.3 copy-start.1
  1673.0 11.3 copy-start.1
  1782.5 11.3 copy-start.1
  1801.7 5.4 copy-start.4
  1807.4 4.6 copy-start.91
  1815.4 118.1 %reduce-scatter.16.cloned.1.call-start = ((), (), s32[]{:S(2)}) async-start(), calls=%async_computation.19 | async-start | bytes 1114112 | tf_op jit(solution)/shard_map/reduce_scatter | solution.py:318
  1828.5 165.0 %reduce-scatter.18.cloned.1.call-start = ((), (), s32[]{:S(2)}) async-start(), calls=%async_computation.20 | async-start | bytes 1114112 | tf_op jit(solution)/shard_map/reduce_scatter | solution.py:321
  1829.0 224.8 %reduce-scatter.20.cloned.1.call-start = ((), (), s32[]{:S(2)}) async-start(), calls=%async_computation.21 | async-start | bytes 1114112 | tf_op jit(solution)/shard_map/reduce_scatter | solution.py:324
  1829.8 279.6 %reduce-scatter.14.cloned.1.call-start = ((), (), s32[]{:S(2)}) async-start(), calls=%async_computation.18 | async-start | bytes 6291456 | tf_op jit(solution)/shard_map/reduce_scatter | solution.py:311
  1840.8 393.3 %all-reduce.6.cloned.1.call-start = ((), (), s32[]{:S(2)}) async-start(), calls=%async_computation.25 | async-start | bytes 131072 | tf_op jit(solution)/shard_map/psum | solution.py:337
  1840.9 6.9 copy-start.29
  1840.9 6.9 copy-start.45
  1840.9 6.9 copy-start.53
  1840.9 6.9 copy-start.55
  1840.9 6.9 copy-start.57
  1840.9 6.9 copy-start.69
  1854.8 16.4 copy-start.20
  2118.2 5.2 copy-start.76
  2118.2 5.2 copy-start.77
  (48 other events, 113.1 us)
Sparse Core Ops, SparseCore 0:
  233.6 200.7 all-reduce.3
  706.1 113.5 reduce-scatter.9
  830.9 104.0 all-gather.2
  1205.6 68.3 reduce-scatter.11
  1291.3 56.7 all-gather.4
  1351.8 72.3 reduce-scatter.25
  1428.6 71.8 reduce-scatter.23
  1815.5 57.4 reduce-scatter.21
  1877.1 56.3 reduce-scatter.15
  1937.0 56.4 reduce-scatter.17
  1997.5 56.3 reduce-scatter.19
  2056.0 53.3 reduce-scatter.13
  2116.5 117.5 all-reduce.5
where the time goes:
time: 2250 us; the launch traced here: 2240 us
  waiting for transfers between devices  885 us (39%)
  matrix products  689 us (31%)
  other arithmetic  295 us (13%)
  blocking collectives  237 us (11%)
  local copies, waits for them, and re-layouts  107 us (5%)
    psum x1, waiting for transfers between devices, on_device(): attn_sum = lax.psum(matmul_nt(attn_out, w_output), 'tp')  195 us
    dot_general x8, matrix products, block_scores(): jnp.einsum('qhd,khd->hqk', query_block, key_all, preferred_element_type=j...  166 us
    convert_element_type x4, other arithmetic, one_block(): score_grad = (chances * (prob_grad - centre)).astype(jnp.bfloat16)  110 us
    reduce_scatter x1, waiting for transfers between devices, on_device(): lax.psum_scatter(stacked.astype(jnp.bfloat16), 'tp', scatter_dimension=0,...  109 us
    all_gather x1, waiting for transfers between devices, on_device(): incoming = lax.all_gather(outgoing, 'tp', axis=0, tiled=True)  104 us
    all_to_all x1, blocking collectives, on_device(): lax.all_to_all(grad_packed, 'ep', split_axis=0, concat_axis=0, tiled=True)  98.5 us
    all_to_all x1, blocking collectives, on_device(): lax.all_to_all(packed, 'ep', split_axis=0, concat_axis=0, tiled=True)  98.1 us
    psum x1, waiting for transfers between devices, on_device(): lax.psum((grad_router, grad_mix, grad_gain_attn, grad_bias_attn, grad_gai...  70.7 us
  transfers between devices with their start and end apart: 15, of which 12 were waited for; matrix products, arithmetic and copies ran while one was open for 29% of the time, Pallas kernels for 0%

commit v1 on v0

v1 whole, which is shorter than its diff:
```python
import functools
from functools import partial

import jax
import jax.numpy as jnp
from jax import lax
from jax.experimental import pallas as pl
from jax.experimental.pallas import tpu as pltpu
from jax.sharding import PartitionSpec as P

HEAD_DIM = 64
PAIR = 2 * HEAD_DIM


EPS = 1e-05
NEG = -1e30
F32 = jnp.float32
BF16 = jnp.bfloat16
NT = (((1,), (1,)), ((), ()))


def layer_norm(values, gain, bias):
    middle = jnp.mean(values, axis=-1, keepdims=True)
    centred = values - middle
    spread = jnp.mean(centred * centred, axis=-1, keepdims=True)
    return centred * lax.rsqrt(spread + EPS) * gain + bias


def gelu_tanh(values):
    return jax.nn.gelu(values, approximate=True)


def matmul(left, right):
    return jnp.dot(left, right, preferred_element_type=jnp.float32)


def matmul_nt(left, right):
    return lax.dot_general(left, right, NT, preferred_element_type=jnp.float32)


def matmul_tn(left, right):
    return lax.dot_general(
        left, right, (((0,), (0,)), ((), ())), preferred_element_type=jnp.float32
    )


def gate_and_mix(logits, mix_logits, one_hot):
    chances = jax.nn.softmax(logits, axis=-1)
    return (jnp.sum(chances * one_hot, axis=-1), jax.nn.softmax(mix_logits, axis=-1))


def attention_forward_kernel(q_ref, k_ref, v_ref, o_ref, lse_ref, vt_ref, *, bq, bk, scale):
    qi = pl.program_id(2)

    @pl.when(qi == 0)
    def _():
        vt_ref[...] = v_ref[...].T

    lane = lax.broadcasted_iota(jnp.int32, (bq, PAIR), 1)
    q = q_ref[...] * jnp.asarray(scale, BF16)
    zero = jnp.zeros_like(q)
    halves = [jnp.where(lane < HEAD_DIM, q, zero), jnp.where(lane < HEAD_DIM, zero, q)]

    def step(j, carry, masked):
        off = pl.multiple_of(j * bk, bk)
        k = k_ref[pl.ds(off, bk), :]
        vt = vt_ref[:, pl.ds(off, bk)]
        scores = [lax.dot_general(k, half, NT, preferred_element_type=F32) for half in halves]
        if masked:
            key_pos = off + lax.broadcasted_iota(jnp.int32, (bk, bq), 0)
            query_pos = qi * bq + lax.broadcasted_iota(jnp.int32, (bk, bq), 1)
            allowed = key_pos <= query_pos
            scores = [jnp.where(allowed, s, NEG) for s in scores]
        new = []
        for h in range(2):
            m, l, acc = carry[h]
            m_new = jnp.maximum(m, jnp.max(scores[h], axis=0, keepdims=True))
            alpha = jnp.exp(m - m_new)
            p = jnp.exp(scores[h] - m_new)
            l = l * alpha + jnp.sum(p, axis=0, keepdims=True)
            part = jnp.dot(
                vt[h * HEAD_DIM : (h + 1) * HEAD_DIM], p.astype(BF16), preferred_element_type=F32
            )
            new.append((m_new, l, acc * alpha + part))
        return tuple(new)

    init = tuple(
        (jnp.full((1, bq), NEG, F32), jnp.zeros((1, bq), F32), jnp.zeros((HEAD_DIM, bq), F32))
        for _ in range(2)
    )
    full = qi * (bq // bk)
    carry = lax.fori_loop(0, full, lambda j, c: step(j, c, False), init)
    for d in range(bq // bk):
        carry = step(full + d, carry, True)
    outs = []
    for h in range(2):
        m, l, acc = carry[h]
        outs.append(acc / l)
        lse_ref[0, h : h + 1, :] = m + jnp.log(l)
    o_ref[...] = jnp.concatenate(outs, axis=0).T.astype(BF16)


def attention_forward(proj, seqs, heads, bq=512, bk=512):
    rows = proj.shape[0]
    length = rows // seqs
    pairs = heads // 2
    nq = length // bq
    flops = 2 * rows * length * heads * HEAD_DIM
    return pl.pallas_call(
        partial(attention_forward_kernel, bq=bq, bk=bk, scale=HEAD_DIM**-0.5),
        grid=(seqs, pairs, nq),
        in_specs=[
            pl.BlockSpec((bq, PAIR), lambda s, p, i: (s * nq + i, p)),
            pl.BlockSpec((length, PAIR), lambda s, p, i: (s, pairs + p)),
            pl.BlockSpec((length, PAIR), lambda s, p, i: (s, 2 * pairs + p)),
        ],
        out_specs=[
            pl.BlockSpec((bq, PAIR), lambda s, p, i: (s * nq + i, p)),
            pl.BlockSpec((1, 2, bq), lambda s, p, i: (p, 0, s * nq + i)),
        ],
        out_shape=[
            jax.ShapeDtypeStruct((rows, heads * HEAD_DIM), BF16),
            jax.ShapeDtypeStruct((pairs, 2, rows), F32),
        ],
        scratch_shapes=[pltpu.VMEM((PAIR, length), BF16)],
        cost_estimate=pl.CostEstimate(
            flops=flops * 4, bytes_accessed=8 * rows * heads * HEAD_DIM, transcendentals=0
        ),
        name="attention_forward",
    )(proj, proj, proj)


def attention_backward_kernel(
    q_ref,
    k_ref,
    v_ref,
    o_ref,
    do_ref,
    lse_ref,
    dq_ref,
    dk_ref,
    dv_ref,
    dqt_ref,
    qs_ref,
    dos_ref,
    kt_ref,
    dl_ref,
    *,
    bq,
    bk,
    scale,
    length,
):
    lane = lax.broadcasted_iota(jnp.int32, (length, PAIR), 1)
    first = lane < HEAD_DIM
    q = q_ref[...] * jnp.asarray(scale, BF16)
    do = do_ref[...]
    zero = jnp.zeros_like(q)
    qs_ref[0] = jnp.where(first, q, zero)
    qs_ref[1] = jnp.where(first, zero, q)
    dos_ref[0] = jnp.where(first, do, zero)
    dos_ref[1] = jnp.where(first, zero, do)
    kt_ref[...] = (k_ref[...] * jnp.asarray(scale, BF16)).T
    prod = (do.astype(F32) * o_ref[...].astype(F32)).T
    dl_ref[0:1, :] = jnp.sum(prod[:HEAD_DIM], axis=0, keepdims=True)
    dl_ref[1:2, :] = jnp.sum(prod[HEAD_DIM:], axis=0, keepdims=True)
    dqt_ref[...] = jnp.zeros_like(dqt_ref)
    nq = length // bq
    nk = length // bk

    def key_block(j, _):
        koff = pl.multiple_of(j * bk, bk)
        k = k_ref[pl.ds(koff, bk), :]
        v = v_ref[pl.ds(koff, bk), :]
        kt = kt_ref[:, pl.ds(koff, bk)]

        def step(i, carry, masked):
            dk, dv = carry
            qoff = pl.multiple_of(i * bq, bq)
            if masked:
                key_pos = koff + lax.broadcasted_iota(jnp.int32, (bk, bq), 0)
                query_pos = qoff + lax.broadcasted_iota(jnp.int32, (bk, bq), 1)
                allowed = key_pos <= query_pos
            qh = [qs_ref[h, pl.ds(qoff, bq), :] for h in range(2)]
            dh = [dos_ref[h, pl.ds(qoff, bq), :] for h in range(2)]
            scores = [lax.dot_general(k, x, NT, preferred_element_type=F32) for x in qh]
            pulls = [lax.dot_general(v, x, NT, preferred_element_type=F32) for x in dh]
            dqs = []
            for h in range(2):
                p = jnp.exp(scores[h] - lse_ref[0, h : h + 1, pl.ds(qoff, bq)])
                if masked:
                    p = jnp.where(allowed, p, 0.0)
                ds = (p * (pulls[h] - dl_ref[h : h + 1, pl.ds(qoff, bq)])).astype(BF16)
                dv = dv + jnp.dot(p.astype(BF16), dh[h], preferred_element_type=F32)
                dk = dk + jnp.dot(ds, qh[h], preferred_element_type=F32)
                dqs.append(
                    jnp.dot(
                        kt[h * HEAD_DIM : (h + 1) * HEAD_DIM], ds, preferred_element_type=F32
                    )
                )
            dqt_ref[:, pl.ds(qoff, bq)] += jnp.concatenate(dqs, axis=0)
            return dk, dv

        carry = (jnp.zeros((bk, PAIR), F32), jnp.zeros((bk, PAIR), F32))
        i0 = j * (bk // bq)
        for d in range(bk // bq):
            carry = step(i0 + d, carry, True)
        dk, dv = lax.fori_loop(i0 + bk // bq, nq, lambda i, c: step(i, c, False), carry)
        dk_ref[pl.ds(koff, bk), :] = dk.astype(BF16)
        dv_ref[pl.ds(koff, bk), :] = dv.astype(BF16)
        return 0

    lax.fori_loop(0, nk, key_block, 0)
    dq_ref[...] = dqt_ref[...].T.astype(BF16)


def attention_backward(proj, out, out_grad, lse, seqs, heads, bq=512, bk=512):
    rows = proj.shape[0]
    length = rows // seqs
    pairs = heads // 2

    def block(off):
        return pl.BlockSpec((length, PAIR), lambda s, p: (s, off + p))

    grad = jax.ShapeDtypeStruct((rows, heads * HEAD_DIM), BF16)
    flops = 5 * rows * length * heads * HEAD_DIM
    return pl.pallas_call(
        partial(attention_backward_kernel, bq=bq, bk=bk, scale=HEAD_DIM**-0.5, length=length),
        grid=(seqs, pairs),
        in_specs=[
            block(0),
            block(pairs),
            block(2 * pairs),
            block(0),
            block(0),
            pl.BlockSpec((1, 2, length), lambda s, p: (p, 0, s)),
        ],
        out_specs=[block(0)] * 3,
        out_shape=[grad] * 3,
        scratch_shapes=[
            pltpu.VMEM((PAIR, length), F32),
            pltpu.VMEM((2, length, PAIR), BF16),
            pltpu.VMEM((2, length, PAIR), BF16),
            pltpu.VMEM((PAIR, length), BF16),
            pltpu.VMEM((2, length), F32),
        ],
        cost_estimate=pl.CostEstimate(
            flops=flops * 4, bytes_accessed=16 * rows * heads * HEAD_DIM, transcendentals=0
        ),
        compiler_params=pltpu.CompilerParams(vmem_limit_bytes=40 * 1024 * 1024),
        name="attention_backward",
    )(proj, proj, proj, out, out_grad, lse)


def on_device(
    tp,
    tokens,
    out_grad,
    lengths,
    expert_ids,
    w_query,
    w_key,
    w_value,
    w_output,
    w_hidden,
    w_return,
    router,
    mix_weight,
    gain_attn,
    bias_attn,
    gain_ffn,
    bias_ffn,
    expert_in,
    expert_out,
):
    shard_rows = out_grad.shape[0]
    all_rows = tokens.shape[0]
    model_width = tokens.shape[1]
    expert_count = router.shape[1]
    capacity = all_rows // expert_count
    seq_count = lengths.shape[0]
    seq_len = all_rows // seq_count
    local_width = w_query.shape[1]
    local_heads = local_width // HEAD_DIM
    tp_index = lax.axis_index("tp")
    first_row = tp_index * shard_rows
    swap = [(0, 1), (1, 0)]

    def shard_of(values):
        return lax.dynamic_slice_in_dim(values, first_row, shard_rows, 0)

    def gather_rows(values):
        if tp != 2:
            return lax.all_gather(values, "tp", axis=0, tiled=True)
        other = lax.ppermute(values, "tp", swap)
        low = jnp.where(tp_index == 0, values, other)
        high = jnp.where(tp_index == 0, other, values)
        return jnp.concatenate([low, high], axis=0)

    def scatter_rows(partial_sums):
        if tp != 2:
            return lax.psum_scatter(
                partial_sums.astype(BF16), "tp", scatter_dimension=0, tiled=True
            ).astype(F32)
        theirs = lax.dynamic_slice_in_dim(partial_sums, shard_rows - first_row, shard_rows, 0)
        return shard_of(partial_sums) + lax.ppermute(theirs.astype(BF16), "tp", swap).astype(F32)

    def exchange(values):
        return lax.all_to_all(values, "ep", split_axis=0, concat_axis=0, tiled=True)

    positions = jnp.arange(all_rows)
    seq_index = positions // seq_len
    row_limit = jnp.sum(
        jnp.where(seq_index[:, None] == jnp.arange(seq_count)[None, :], lengths[None, :], 0), axis=1
    )
    live_all = (positions % seq_len < row_limit).astype(jnp.float32)[:, None]
    live = shard_of(live_all)
    one_hot = (expert_ids[:, None] == jnp.arange(expert_count)[None, :]).astype(jnp.float32)
    routed = one_hot * live_all
    slots = jnp.sum((jnp.cumsum(routed, axis=0) - routed) * one_hot, axis=1).astype(jnp.int32)
    slot_count = expert_count * capacity
    target = jnp.where(live_all[:, 0] > 0, expert_ids * capacity + slots, slot_count)
    mine = (live_all[:, 0] > 0) & (slots >= 0) & (slots < capacity)
    take_index = jnp.where(mine, expert_ids * capacity + slots, 0)
    mine_col = mine.astype(jnp.float32)[:, None]

    def pack(rows):
        packed = jnp.zeros((slot_count, model_width), BF16).at[target].set(rows, mode="drop")
        return packed.reshape(expert_count, capacity, model_width)

    grad_all = gather_rows(out_grad)
    grad_rows = exchange(pack(grad_all)).reshape(slot_count, model_width)

    attn_gain = gain_attn.astype(jnp.float32)
    attn_bias = bias_attn.astype(jnp.float32)
    ffn_gain = gain_ffn.astype(jnp.float32)
    ffn_bias = bias_ffn.astype(jnp.float32)
    tokens_wide = tokens.astype(jnp.float32)
    attn_in = layer_norm(tokens_wide, attn_gain, attn_bias).astype(BF16)
    qkv_weight = jnp.concatenate([w_query, w_key, w_value], axis=1)
    projected = matmul(attn_in, qkv_weight).astype(BF16)
    attn_out, log_sums = attention_forward(projected, seq_count, local_heads)
    if tp == 2:
        w_other = lax.ppermute(w_output, "tp", swap)
        heads_other = lax.ppermute(attn_out, "tp", swap)
        attn_sum = matmul_nt(attn_out, w_output) + matmul_nt(heads_other, w_other)
    else:
        w_all = lax.all_gather(w_output, "tp", axis=1, tiled=True)
        attn_sum = matmul_nt(lax.all_gather(attn_out, "tp", axis=1, tiled=True), w_all)
    resid = tokens_wide + attn_sum
    ffn_in = layer_norm(resid, ffn_gain, ffn_bias).astype(BF16)
    sent_rows = exchange(pack(ffn_in)).reshape(slot_count, model_width)

    logits = matmul(ffn_in, router)
    mix_logits = matmul(ffn_in, mix_weight)
    gate_all, mix_all = gate_and_mix(logits, mix_logits, one_hot)

    live_grad_all = live_all * grad_all.astype(jnp.float32)
    dense_grad = (live_grad_all * mix_all[:, 0:1]).astype(BF16)
    hidden_pre = matmul(ffn_in, w_hidden)
    hidden_low, gelu_pull = jax.vjp(gelu_tanh, hidden_pre)
    hidden_low = hidden_low.astype(BF16)
    dense_part = matmul_nt(hidden_low, w_return)
    hidden_grad = matmul(dense_grad, w_return)
    grad_return = matmul_tn(dense_grad, hidden_low)
    pre_grad = gelu_pull(hidden_grad)[0].astype(BF16)
    grad_hidden = matmul_tn(ffn_in, pre_grad)
    input_part = matmul_nt(pre_grad, w_hidden)
    first_dot = jnp.sum(live_grad_all * dense_part, axis=1)

    my_expert = lax.axis_index("ep")
    here = (jnp.arange(expert_count) == my_expert).astype(F32)[None, :]
    gate_here, mix_here = gate_and_mix(
        matmul(sent_rows, router), matmul(sent_rows, mix_weight), here
    )
    moe_grad = (grad_rows.astype(F32) * mix_here[:, 1:2] * gate_here[:, None]).astype(BF16)
    w_in = expert_in[0]
    w_out = expert_out[0]
    expert_pre = matmul(sent_rows, w_in)
    expert_act, expert_pull = jax.vjp(gelu_tanh, expert_pre)
    expert_act = expert_act.astype(BF16)
    result = matmul_nt(expert_act, w_out)
    dot_here = jnp.sum(grad_rows.astype(F32) * result, axis=1)
    act_grad = matmul(moe_grad, w_out)
    expert_pre_grad = expert_pull(act_grad)[0].astype(BF16)
    row_grad = matmul_nt(expert_pre_grad, w_in)
    grad_expert_out = matmul_tn(moe_grad, expert_act)[None]
    grad_expert_in = matmul_tn(sent_rows, expert_pre_grad)[None]

    blocks = (expert_count, capacity, model_width)
    back_grad = exchange(row_grad.astype(BF16).reshape(blocks)).reshape(slot_count, model_width)
    returned = exchange(result.astype(BF16).reshape(blocks)).reshape(slot_count, model_width)
    dots = exchange(dot_here.reshape(expert_count, capacity))
    slot_hot = (slots[:, None] == jnp.arange(capacity)[None, :]).astype(F32) * mine_col
    second_dot = jnp.sum(jnp.dot(one_hot, dots, precision=lax.Precision.HIGHEST) * slot_hot, axis=1)

    both_dots = lax.psum(jnp.stack([first_dot, second_dot]), "tp")
    gate_shard = shard_of(gate_all)
    mix_shard = shard_of(mix_all)
    first_shard = lax.dynamic_slice_in_dim(both_dots[0], first_row, shard_rows)
    second_shard = lax.dynamic_slice_in_dim(both_dots[1], first_row, shard_rows)
    mix_grad = jnp.stack([first_shard, gate_shard * second_shard], axis=1)
    gate_grad = mix_shard[:, 1] * second_shard
    gate_pull = jax.vjp(
        partial(gate_and_mix, one_hot=shard_of(one_hot)), shard_of(logits), shard_of(mix_logits)
    )[1]
    logit_grad, mix_logit_grad = gate_pull((gate_grad, mix_grad))
    logit_low = logit_grad.astype(BF16)
    mix_low = mix_logit_grad.astype(BF16)
    ffn_shard = shard_of(ffn_in)
    grad_router = matmul_tn(ffn_shard, logit_low)
    grad_mix = matmul_tn(ffn_shard, mix_low)
    input_part = input_part + back_grad[take_index].astype(F32) * mine_col
    input_grad = scatter_rows(input_part)
    ffn_in_grad = input_grad + matmul_nt(logit_low, router) + matmul_nt(mix_low, mix_weight)
    resid_shard = shard_of(resid)
    norm_pull_two = jax.vjp(layer_norm, resid_shard, ffn_gain, ffn_bias)[1]
    resid_part, grad_gain_ffn, grad_bias_ffn = norm_pull_two(ffn_in_grad)
    live_grad = live * out_grad.astype(jnp.float32)
    resid_grad = live_grad + resid_part

    attn_grad_all = gather_rows(resid_grad.astype(BF16))
    grad_output = matmul_tn(attn_grad_all, attn_out)
    heads_grad = matmul(attn_grad_all, w_output).astype(BF16)
    qkv_grad = attention_backward(
        projected, attn_out, heads_grad, log_sums, seq_count, local_heads
    )
    qkv_grad = jnp.concatenate(qkv_grad, axis=1)
    grad_weights = matmul_tn(attn_in, qkv_grad)
    attn_in_part = matmul_nt(qkv_grad, qkv_weight)
    norm_all = layer_norm(tokens_wide, 1.0, 0.0)
    grad_gain_attn = jnp.sum(attn_in_part * norm_all, axis=0)
    grad_bias_attn = jnp.sum(attn_in_part, axis=0)
    attn_in_grad = scatter_rows(attn_in_part)
    norm_pull_one = jax.vjp(layer_norm, shard_of(tokens_wide), attn_gain, attn_bias)[1]
    token_part = norm_pull_one(attn_in_grad)[0]
    token_grad = resid_grad + token_part

    moe_part = returned[take_index].astype(F32) * mine_col
    weighted = mix_all[:, 0:1] * dense_part + mix_all[:, 1:2] * gate_all[:, None] * moe_part
    block_out = (live * (resid_shard + scatter_rows(weighted))).astype(BF16)

    def over_sequences(values):
        return lax.psum_scatter(
            values.astype(BF16), "ep", scatter_dimension=0, tiled=True
        ).astype(F32)

    grad_hidden = over_sequences(grad_hidden)
    grad_return = over_sequences(grad_return)
    square = over_sequences(jnp.concatenate([grad_weights, grad_output], axis=1))
    grad_query, grad_key, grad_value, grad_output = jnp.split(square, 4, axis=1)
    grad_router, grad_mix, grad_gain_ffn, grad_bias_ffn = lax.psum(
        (grad_router, grad_mix, grad_gain_ffn, grad_bias_ffn), ("ep", "tp")
    )
    grad_gain_attn, grad_bias_attn = lax.psum((grad_gain_attn, grad_bias_attn), ("ep", "tp"))
    return (
        block_out,
        token_grad,
        grad_query,
        grad_key,
        grad_value,
        grad_output,
        grad_hidden,
        grad_return,
        grad_router,
        grad_mix,
        grad_gain_attn,
        grad_bias_attn,
        grad_gain_ffn,
        grad_bias_ffn,
        grad_expert_in,
        grad_expert_out,
    )


def solution(mesh):
    in_specs = (
        P("ep", None),
        P(("ep", "tp"), None),
        P("ep"),
        P("ep"),
        P(None, "tp"),
        P(None, "tp"),
        P(None, "tp"),
        P(None, "tp"),
        P(None, "tp"),
        P(None, "tp"),
        P(),
        P(),
        P(),
        P(),
        P(),
        P(),
        P("ep", None, "tp"),
        P("ep", None, "tp"),
    )
    out_specs = (
        P(("ep", "tp"), None),
        P(("ep", "tp"), None),
        P("ep", "tp"),
        P("ep", "tp"),
        P("ep", "tp"),
        P("ep", "tp"),
        P("ep", "tp"),
        P("ep", "tp"),
        P(),
        P(),
        P(),
        P(),
        P(),
        P(),
        P("ep", None, "tp"),
        P("ep", None, "tp"),
    )
    return jax.shard_map(
        partial(on_device, mesh.shape["tp"]),
        mesh=mesh,
        in_specs=in_specs,
        out_specs=out_specs,
        check_vma=False,
    )
```

time: 2250 us -> 1140 us (0.51)
  waiting for transfers between devices: 885 us -> 281 us
  matrix products: 689 us -> 262 us
  other arithmetic: 295 us -> 67.1 us
  Pallas kernels: 0 us -> 114 us
  blocking collectives: 237 us -> 149 us
  starting transfers between devices: 12 us -> 97.9 us
  local copies, waits for them, and re-layouts: 107 us -> 146 us
    dot_general x40 -> x10, matrix products: 587 us -> 87.2 us  [the longest x9 86.5 us: matmul_nt(): return lax.dot_general(left, right, NT, preferred_element_type=jnp.float32)]
    reduce_scatter x9 -> x3, waiting for transfers between devices: 386 us -> 0.02 us  [over_sequences(): lax.psum_scatter(values.astype(BF16), 'ep', scatter_dimension=0, tiled=True)]
    psum x2 -> x1, waiting for transfers between devices: 266 us -> 33.6 us  [on_device(): lax.psum((grad_router, grad_mix, grad_gain_ffn, grad_bias_ffn), ('ep', 't...]
    all_to_all x2 -> x0, blocking collectives: 197 us -> none  [the longest x1 98.5 us: on_device(): lax.all_to_all(grad_packed, 'ep', split_axis=0, concat_axis=0, tiled=True)]
    ppermute x0 -> x7, waiting for transfers between devices: none -> 143 us  [the longest x2 85.4 us: gather_rows(): other = lax.ppermute(values, 'tp', swap)]
    all_gather x2 -> x0, waiting for transfers between devices: 131 us -> none  [the longest x1 104 us: on_device(): incoming = lax.all_gather(outgoing, 'tp', axis=0, tiled=True)]
    convert_element_type x13 -> x7, other arithmetic: 126 us -> 11.6 us  [the longest x2 3.56 us: over_sequences(): return lax.psum_scatter(values.astype(BF16), 'ep', scatter_dimension=0, t...]
    pallas_call x0 -> x2, Pallas kernels: none -> 114 us  [the longest x1 67.9 us: attention_backward(): pl.pallas_call(partial(attention_backward_kernel, bq=bq, bk=bk, scale=HEA...]
  transfers between devices with their start and end apart: 15 -> 16, of which waited for: 12 -> 9; matrix products, arithmetic and copies ran while one was open for 29% -> 32% of each run, Pallas kernels for 0% -> 0%
where the time goes in v1:
time: 1140 us; the launch traced here: 1130 us
  waiting for transfers between devices  281 us (25%)
  matrix products  262 us (23%)
  blocking collectives  149 us (13%)
  local copies, waits for them, and re-layouts  146 us (13%)
  Pallas kernels  114 us (10%)
  starting transfers between devices  97.9 us (9%)
  other arithmetic  67.1 us (6%)
  between operations  17.3 us (2%)
    all_to_all x5, waiting for transfers between devices, exchange(): return lax.all_to_all(values, 'ep', split_axis=0, concat_axis=0, tiled=True)  104 us
    dot_general x10, matrix products, matmul(): return jnp.dot(left, right, preferred_element_type=jnp.float32)  101 us
    all_to_all x5, starting transfers between devices, exchange(): return lax.all_to_all(values, 'ep', split_axis=0, concat_axis=0, tiled=True)  90.1 us
    dot_general x9, matrix products, matmul_nt(): return lax.dot_general(left, right, NT, preferred_element_type=jnp.float32)  86.5 us
    ppermute x2, waiting for transfers between devices, gather_rows(): other = lax.ppermute(values, 'tp', swap)  85.4 us
    psum x1, blocking collectives, on_device(): lax.psum((grad_router, grad_mix, grad_gain_ffn, grad_bias_ffn), ('ep', 't...  78.9 us
    dot_general x8, matrix products, matmul_tn(): lax.dot_general(left, right, (((0,), (0,)), ((), ())), preferred_element_...  74.1 us
    psum x1, blocking collectives, on_device(): both_dots = lax.psum(jnp.stack([first_dot, second_dot]), 'tp')  69.9 us
  transfers between devices with their start and end apart: 16, of which 9 were waited for; matrix products, arithmetic and copies ran while one was open for 32% of the time, Pallas kernels for 0%

profile of v1, /device:TPU:0, one launch (start us, length us, event | category | flops | bytes accessed | tf_op | source)
XLA Modules:
  0.0 1133.8 jit_solution(7920780237983096368)
XLA Ops:
  10.7 6.4 copy.50
  17.1 3.0 convert_reduce_fusion
  22.4 9.4 convolution_convert_fusion.q_ref.k_ref.v_ref
  31.8 45.7 %attention_forward.1 = (bf16[2048,512]{1,0:T(8,128)(2,1)}, f32[4,2,2048]{2,1,0:T(2,128)}) custom-call(bf16[2048,1536]{1,0:T(8,128)(2,1)} %convolution_convert_fusion.q_ref.k_ref.v_ref, bf16[2048,1536]{1,0:T(8,128)(2,1)} %convolution_convert_fusion.q_ref.k_ref.v_ref, bf16[2048,1536]{1,0:T(8,128)(2,1)} %convolution_convert_fusion.q_ref.k_ref.v_ref), custom_call_target="tpu_custom_call" | custom-call | flops 17179869184 | bytes 8388608 | tf_op jit(solution)/shard_map/attention_forward/pallas_call | solution.py:109
  77.4 3.0 collective-permute-start
  81.2 4.9 reduce-window.6
  86.6 4.4 fusion.95
  91.0 57.7 %collective-permute-done.1 = bf16[1024,512]{1,0:T(8,128)(2,1)S(1)} collective-permute-done((bf16[1024,512]{1,0:T(8,128)(2,1)}, bf16[1024,512]{1,0:T(8,128)(2,1)S(1)}, u32[]{:S(2)}, u32[]{:S(2)}) %collective-permute-start.1) | collective-permute-done | bytes 1048608 | tf_op jit(solution)/shard_map/ppermute | solution.py:344
  157.4 6.4 copy.51
  168.0 13.0 %scatter_custom_fusion = bf16[2048,1024]{1,0:T(8,128)(2,1)} fusion(s32[2048]{0:T(1024)S(1)} %get-tuple-element.95, bf16[2048,1024]{1,0:T(8,128)(2,1)} %copy.51, bf16[]{:T(256)} %constant.105.clone.1), kind=kCustom, calls=%fused_computation.88 | custom fusion | bytes 4194816 | tf_op jit(solution)/shard_map/scatter | solution.py:328
  181.1 17.7 %all-to-all-start = ((bf16[16,128,1024]{2,1,0:T(8,128)(2,1)}), bf16[16,128,1024]{2,1,0:T(8,128)(2,1)}, u32[]{:S(2)}, u32[]{:S(2)}) async-start(bf16[16,128,1024]{2,1,0:T(8,128)(2,1)} %bitcast.116), calls=%async_computation | async-start | bytes 8388608 | tf_op jit(solution)/shard_map/all_to_all | solution.py:309
  198.7 2.9 copy.53
  203.2 46.6 %collective-permute-done.3 = bf16[1024,1024]{0,1:T(8,128)(2,1)} collective-permute-done((bf16[1024,1024]{0,1:T(8,128)(2,1)S(1)}, bf16[1024,1024]{0,1:T(8,128)(2,1)}, u32[]{:S(2)}, u32[]{:S(2)}) %collective-permute-start.3) | collective-permute-done | bytes 2097184 | tf_op jit(solution)/shard_map/ppermute | solution.py:295
  256.2 6.4 copy.57
  262.6 13.1 %scatter_custom_fusion.1 = bf16[2048,1024]{1,0:T(8,128)(2,1)} fusion(s32[2048]{0:T(1024)S(1)} %get-tuple-element.95, bf16[2048,1024]{1,0:T(8,128)(2,1)} %copy.57, bf16[]{:T(256)} %constant.105.clone.1), kind=kCustom, calls=%fused_computation.86 | custom fusion | bytes 4194816 | tf_op jit(solution)/shard_map/scatter | solution.py:328
  276.4 19.8 %all-to-all-start.2 = ((bf16[16,128,1024]{2,1,0:T(8,128)(2,1)}), bf16[16,128,1024]{2,1,0:T(8,128)(2,1)}, u32[]{:S(2)}, u32[]{:S(2)}) async-start(bf16[16,128,1024]{2,1,0:T(8,128)(2,1)} %bitcast.115), calls=%async_computation.2 | async-start | bytes 8388608 | tf_op jit(solution)/shard_map/all_to_all | solution.py:309
  296.8 3.0 fusion.91
  300.5 14.5 %fusion.96 = f32[2048,2048]{1,0:T(8,128)} fusion(bf16[2048,1024]{0,1:T(8,128)(2,1)S(1)} %copy-done.8, bf16[1024,2048]{1,0:T(8,128)(2,1)} %param.26), kind=kOutput, calls=%fused_computation.214 | convolution fusion | flops 8589934592 | bytes 25165824 | tf_op jit(solution)/shard_map/dot_general | solution.py:34
  315.0 3.4 fusion.92
  318.5 3.5 fusion.93
  322.2 13.9 %fusion.27 = f32[2048,2048]{1,0:T(8,128)} fusion(bf16[2048,1024]{1,0:T(8,128)(2,1)} %bitcast.7, bf16[1,1024,2048]{2,1,0:T(8,128)(2,1)S(1)} %copy-done.71), kind=kOutput, calls=%fused_computation.58 | convolution fusion | flops 8589934592 | bytes 25165824 | tf_op jit(solution)/shard_map/dot_general | solution.py:34
  336.1 37.8 %all-to-all-done.2 = bf16[16,128,1024]{2,1,0:T(8,128)(2,1)} async-done(((bf16[16,128,1024]{2,1,0:T(8,128)(2,1)}), bf16[16,128,1024]{2,1,0:T(8,128)(2,1)}, u32[]{:S(2)}, u32[]{:S(2)}) %all-to-all-start.2) | async-done | bytes 4194336 | tf_op jit(solution)/shard_map/all_to_all | solution.py:309
  373.9 19.4 %fusion.16 = (f32[2048]{0:T(1024)}, bf16[2048,1024]{1,0:T(8,128)(2,1)}, bf16[2048,1024]{1,0:T(8,128)(2,1)}) fusion(bf16[16,128,1024]{2,1,0:T(8,128)(2,1)} %all-to-all-done.2, f32[2048]{0:T(1024)S(1)} %multiply_reduce_fusion.9, f32[2048]{0:T(1024)S(1)} %bitcast.128, bf16[1,1024,2048]{2,1,0:T(8,128)(2,1)} %param.35, f32[2048,2048]{1,0:T(8,128)} %fusion.27), kind=kOutput, calls=%fused_computation.29 | convolution fusion | flops 8642361344 | bytes 33579008 | tf_op jit(solution)/shard_map/dot_general | solution.py:38
  393.3 19.6 %all-to-all-start.4 = ((f32[16,1,128]{2,1,0:T(1,128)}), f32[16,1,128]{2,1,0:T(1,128)S(1)}, u32[]{:S(2)}, u32[]{:S(2)}) async-start(f32[16,1,128]{2,1,0:T(1,128)} %bitcast.21), calls=%async_computation.4 | async-start | bytes 16384 | tf_op jit(solution)/shard_map/all_to_all | solution.py:309
  413.6 5.7 all-to-all-done.4
  419.9 4.7 all-to-all-start.1
  424.6 15.1 %convolution_convert_fusion.2 = bf16[1024,2048]{1,0:T(8,128)(2,1)} fusion(f32[2048]{0:T(1024)S(1)} %fusion.71, f32[2048]{0:T(1024)S(1)} %bitcast.132, bf16[1024,1024]{0,1:T(8,128)(2,1)} %copy-done.18, bf16[1024,1024]{0,1:T(8,128)(2,1)S(1)} %copy-done.17, f32[2048,2048]{1,0:T(8,128)} %fusion.96), kind=kOutput, calls=%fused_computation.77 | convolution fusion | flops 8644460544 | bytes 25182208 | tf_op jit(solution)/shard_map/dot_general | solution.py:42
  439.7 2.9 fusion.15
  443.2 21.5 %fusion.13 = bf16[2048,2048]{1,0:T(8,128)(2,1)S(1)} fusion(f32[2048,2048]{1,0:T(8,128)} %fusion.27, bf16[2048,1024]{1,0:T(8,128)(2,1)S(1)} %bitcast.119, bf16[1,1024,2048]{2,1,0:T(8,128)(2,1)S(1)} %copy-done.70), kind=kOutput, calls=%fused_computation.21 | convolution fusion | flops 8673820672 | bytes 33554432 | tf_op jit(solution)/shard_map/dot_general | solution.py:34
  464.7 3.2 copy-done.74
  467.9 10.7 fusion.29
  478.7 40.3 %all-to-all-done.1 = bf16[16,128,1024]{2,1,0:T(8,128)(2,1)} async-done(((bf16[16,128,1024]{2,1,0:T(8,128)(2,1)}), bf16[16,128,1024]{2,1,0:T(8,128)(2,1)}, u32[]{:S(2)}, u32[]{:S(2)}) %all-to-all-start.1) | async-done | bytes 4194336 | tf_op jit(solution)/shard_map/all_to_all | solution.py:309
  519.0 28.3 %all-to-all-start.3 = ((bf16[16,128,1024]{2,1,0:T(8,128)(2,1)}), bf16[16,128,1024]{2,1,0:T(8,128)(2,1)}, u32[]{:S(2)}, u32[]{:S(2)}) async-start(bf16[16,128,1024]{2,1,0:T(8,128)(2,1)} %bitcast.117), calls=%async_computation.3 | async-start | bytes 8388608 | tf_op jit(solution)/shard_map/all_to_all | solution.py:309
  547.6 26.0 %fusion.6 = bf16[2048,2048]{1,0:T(8,128)(2,1)} fusion(f32[2048,2048]{1,0:T(8,128)} %fusion.96, bf16[1024,2048]{1,0:T(8,128)(2,1)} %param.27, f32[2048]{0:T(1024)S(1)} %fusion.71, f32[2048]{0:T(1024)S(1)} %bitcast.133, bf16[1024,1024]{0,1:T(8,128)(2,1)} %copy-done.18, bf16[1024,1024]{0,1:T(8,128)(2,1)S(1)} %copy-done.17), kind=kOutput, calls=%fused_computation.14 | convolution fusion | flops 8688500736 | bytes 33570816 | tf_op jit(solution)/shard_map/dot_general | solution.py:34
  573.6 12.8 %convolution_convert_fusion.3 = bf16[1024,2048]{1,0:T(8,128)(2,1)} fusion(bf16[2048,1024]{0,1:T(8,128)(2,1)S(1)} %copy-done.9, bf16[2048,2048]{1,0:T(8,128)(2,1)} %fusion.6), kind=kOutput, calls=%fused_computation.78 | convolution fusion | flops 8592031744 | bytes 16777216 | tf_op jit(solution)/shard_map/dot_general | solution.py:42
  593.4 13.9 %gather_fusion = bf16[2048,1024]{1,0:T(8,128)(2,1)} fusion(bf16[2048,1024]{1,0:T(8,128)(2,1)} %bitcast.11, s32[2048]{0:T(1024)S(1)} %copy-done.41), kind=kCustom, calls=%fused_computation | custom fusion | bytes 8396800 | tf_op jit(solution)/shard_map/gather | solution.py:439
  607.3 6.5 copy.52
  613.8 19.5 %all-to-all-done.3 = bf16[16,128,1024]{2,1,0:T(8,128)(2,1)} async-done(((bf16[16,128,1024]{2,1,0:T(8,128)(2,1)}), bf16[16,128,1024]{2,1,0:T(8,128)(2,1)}, u32[]{:S(2)}, u32[]{:S(2)}) %all-to-all-start.3) | async-done | bytes 4194336 | tf_op jit(solution)/shard_map/all_to_all | solution.py:309
  633.3 13.7 %gather_fusion.1 = bf16[2048,1024]{1,0:T(8,128)(2,1)} fusion(bf16[2048,1024]{1,0:T(8,128)(2,1)} %bitcast.17, s32[2048]{0:T(1024)S(1)} %copy-done.41), kind=kCustom, calls=%fused_computation.1 | custom fusion | bytes 8396800 | tf_op jit(solution)/shard_map/gather | solution.py:413
  647.0 6.5 copy.58
  653.5 13.2 %multiply_add_fusion = f32[2048,1024]{0,1:T(8,128)S(1)} fusion(bf16[2048,1024]{0,1:T(8,128)(2,1)} %copy.58, f32[2048]{0:T(1024)S(1)} %fusion.78, bf16[2048,2048]{1,0:T(8,128)(2,1)} %fusion.6, bf16[1024,2048]{1,0:T(8,128)(2,1)} %param.26), kind=kOutput, calls=%fused_computation.34 | convolution fusion | flops 8596226048 | bytes 25174016 | tf_op jit(solution)/shard_map/dot_general | solution.py:38
  666.7 3.3 copy-done.20
  673.3 19.6 %multiply_reduce_fusion.1 = (f32[2048]{0:T(1024)S(1)}, f32[2048,1024]{0,1:T(8,128)}) fusion(f32[2048]{0:T(1024)S(1)} %fusion.71, bf16[1024,1024]{0,1:T(8,128)(2,1)S(1)} %copy-done.19, bf16[1024,1024]{0,1:T(8,128)(2,1)S(1)} %copy-done.17, f32[2048]{0:T(1024)S(1)} %fusion.78, bf16[2048,1024]{0,1:T(8,128)(2,1)} %copy.52, f32[2048]{0:T(1024)S(1)} %bitcast.135, ...), kind=kOutput, calls=%fused_computation.33 | convolution fusion | flops 8652847104 | bytes 37789696 | tf_op jit(solution)/shard_map/dot_general | solution.py:38
  692.8 3.9 dynamic-slice_convert_fusion.2
  697.3 69.9 %psum.49 = f32[2,2048]{1,0:T(2,128)S(1)} all-reduce(f32[2,2048]{1,0:T(2,128)S(1)} %pad_maximum_fusion.7), channel_id=1, replica_groups=mesh['ep'=16,'tp'=2] {'tp'}, use_global_device_ids=true, to_apply=%region_22.23 | all-reduce | flops 4096 | bytes 32768 | tf_op jit(solution)/shard_map/psum | solution.py:397
  768.3 6.6 multiply_reduce_fusion.4
  776.3 5.6 fusion.84
  787.4 3.3 copy-done.11
  794.6 38.8 %collective-permute-done.5 = bf16[1024,1024]{0,1:T(8,128)(2,1)} collective-permute-done((bf16[1024,1024]{0,1:T(8,128)(2,1)}, bf16[1024,1024]{0,1:T(8,128)(2,1)}, u32[]{:S(2)}, u32[]{:S(2)}) %collective-permute-start.5) | collective-permute-done | bytes 2097184 | tf_op jit(solution)/shard_map/ppermute | solution.py:295
  840.6 67.9 %attention_backward.1 = (bf16[2048,512]{1,0:T(8,128)(2,1)S(1)}, bf16[2048,512]{1,0:T(8,128)(2,1)S(1)}, bf16[2048,512]{1,0:T(8,128)(2,1)S(1)}) custom-call(bf16[2048,1536]{1,0:T(8,128)(2,1)} %convolution_convert_fusion.q_ref.k_ref.v_ref, bf16[2048,1536]{1,0:T(8,128)(2,1)} %convolution_convert_fusion.q_ref.k_ref.v_ref, ...), custom_call_target="tpu_custom_call" | custom-call | flops 42949672960 | bytes 16777216 | tf_op jit(solution)/shard_map/attention_backward/pallas_call | solution.py:227
  910.9 7.3 convolution_convert_fusion.1
  921.0 16.5 %convolution_bitcast_fusion = f32[1,1024,2048]{2,1,0:T(8,128)} fusion(bf16[2048,1024]{1,0:T(8,128)(2,1)} %get-tuple-element.81, f32[2048,2048]{1,0:T(8,128)} %fusion.27), kind=kOutput, calls=%fused_computation.47 | convolution fusion | flops 8627683328 | bytes 29360128 | tf_op jit(solution)/shard_map/dot_general | solution.py:42
  937.5 9.4 fusion.94
  946.9 9.1 copy.62
  956.0 4.1 dynamic-slice_convert_fusion
  960.6 16.2 %convolution_bitcast_fusion.1 = f32[1,1024,2048]{2,1,0:T(8,128)} fusion(bf16[2048,1024]{1,0:T(8,128)(2,1)} %bitcast.7, bf16[2048,2048]{1,0:T(8,128)(2,1)} %copy-done.74), kind=kOutput, calls=%fused_computation.48 | convolution fusion | flops 8589934592 | bytes 20971520 | tf_op jit(solution)/shard_map/dot_general | solution.py:42
  980.9 3.9 copy.66
  984.9 6.1 multiply_reduce_fusion
  991.0 78.9 %all-reduce = (f32[1024,2]{0,1:T(2,128)}, f32[1024]{0:T(1024)}, f32[1024]{0:T(1024)}, f32[1024]{0:T(1024)}, f32[1024]{0:T(1024)}) all-reduce(f32[1024,2]{0,1:T(2,128)S(1)} %fusion.39, f32[1024]{0:T(1024)S(1)} %multiply_reduce_fusion, f32[1024]{0:T(1024)S(1)} %get-tuple-element.112, ...), channel_id=1, replica_groups=mesh['ep'=16,'tp'=2] {'ep','tp'}, use_global_device_ids=true, to_apply=%region_41.42 | all-reduce | flops 6144 | bytes 49152 | tf_op jit(solution)/shard_map/psum | solution.py:452
  1070.0 5.3 multiply_reduce_fusion.6
  1075.3 5.5 fusion.83
  1080.8 3.5 add_add_fusion.3
  1084.3 5.3 copy.67
  1091.4 33.6 %all-reduce.3.cloned.1.call-done = f32[1024,16]{0,1:T(8,128)} async-done(((f32[1024,16]{0,1:T(8,128)}), f32[1024,16]{0,1:T(8,128)}) %all-reduce.3.cloned.1.call-update) | async-done | bytes 65552 | tf_op jit(solution)/shard_map/psum | solution.py:452
  (257 shorter events, 72.6 us)
Async XLA Ops:
  8.0 155.8 %copy-start = (bf16[1024,16]{0,1:T(8,128)(2,1)S(1)}, bf16[1024,16]{0,1:T(8,128)(2,1)}, u32[]{:S(2)}) copy-start(bf16[1024,16]{0,1:T(8,128)(2,1)} %param.28) | copy-start | bytes 98308
  8.7 13.2 %copy-start.57 = (f32[1024]{0:T(1024)}, f32[1024]{0:T(1024)S(1)}, u32[]{:S(2)}) copy-start(f32[1024]{0:T(1024)S(1)} %convert_element_type.167) | copy-start | bytes 12292
  9.4 12.5 %copy-start.66 = (f32[1024]{0:T(1024)}, f32[1024]{0:T(1024)S(1)}, u32[]{:S(2)}) copy-start(f32[1024]{0:T(1024)S(1)} %convert_element_type.168) | copy-start | bytes 12292
  17.1 4.6 copy-start.25
  22.4 9.4 copy-start.31
  31.8 49.4 %copy-start.35 = (s32[2048]{0:T(1024)S(1)}, s32[2048]{0:T(1024)}, u32[]{:S(2)}) copy-start(s32[2048]{0:T(1024)} %param.21) | copy-start | bytes 24580
  31.8 49.4 %copy-start.68 = (bf16[1024]{0:T(1024)(128)(2,1)S(1)}, bf16[1024]{0:T(1024)(128)(2,1)}, u32[]{:S(2)}) copy-start(bf16[1024]{0:T(1024)(128)(2,1)} %param.32) | copy-start | bytes 6148
  31.8 49.4 %copy-start.69 = (bf16[1024]{0:T(1024)(128)(2,1)S(1)}, bf16[1024]{0:T(1024)(128)(2,1)}, u32[]{:S(2)}) copy-start(bf16[1024]{0:T(1024)(128)(2,1)} %param.33) | copy-start | bytes 6148
  77.4 71.3 %collective-permute-start = (bf16[2048,512]{1,0:T(8,128)(2,1)}, bf16[2048,512]{1,0:T(8,128)(2,1)S(1)}, u32[]{:S(2)}, u32[]{:S(2)}) collective-permute-start(bf16[2048,512]{1,0:T(8,128)(2,1)} %get-tuple-element.21.o_ref), channel_id=1, source_target_pairs={{0,1},{1,0},{2,3},{3,2},{4,5},{5,4},{6,7},{7,6},{8,9},{9,8},{10,11... | collective-permute-start | bytes 6291464 | tf_op jit(solution)/shard_map/ppermute | solution.py:345
  80.4 68.3 %collective-permute-start.1 = (bf16[1024,512]{1,0:T(8,128)(2,1)}, bf16[1024,512]{1,0:T(8,128)(2,1)S(1)}, u32[]{:S(2)}, u32[]{:S(2)}) collective-permute-start(bf16[1024,512]{1,0:T(8,128)(2,1)} %param.25), channel_id=1, source_target_pairs={{0,1},{1,0},{2,3},{3,2},{4,5},{5,4},{6,7},{7,6},{8,9},{9,8},{10,11... | collective-permute-start | bytes 3145736 | tf_op jit(solution)/shard_map/ppermute | solution.py:344
  81.2 70.9 %copy-start.44 = (f32[1024]{0:T(1024)}, f32[1024]{0:T(1024)S(1)}, u32[]{:S(2)}) copy-start(f32[1024]{0:T(1024)S(1)} %convert_element_type.171) | copy-start | bytes 12292
  86.6 62.1 %copy-start.5 = (bf16[2048,1024]{0,1:T(8,128)(2,1)S(1)}, bf16[2048,1024]{0,1:T(8,128)(2,1)}, u32[]{:S(2)}) copy-start(bf16[2048,1024]{0,1:T(8,128)(2,1)} %copy.50) | copy-start | bytes 12582916
  167.4 245.5 %copy-start.51 = (f32[2048]{0:T(1024)}, f32[2048]{0:T(1024)S(1)}, u32[]{:S(2)}) copy-start(f32[2048]{0:T(1024)S(1)} %get-tuple-element.63) | copy-start | bytes 24580
  181.1 95.3 %all-to-all-start = ((bf16[16,128,1024]{2,1,0:T(8,128)(2,1)}), bf16[16,128,1024]{2,1,0:T(8,128)(2,1)}, u32[]{:S(2)}, u32[]{:S(2)}) async-start(bf16[16,128,1024]{2,1,0:T(8,128)(2,1)} %bitcast.116), calls=%async_computation | async-start | bytes 8388608 | tf_op jit(solution)/shard_map/all_to_all | solution.py:309
  201.6 50.1 %copy-start.14 = (bf16[1024,1024]{0,1:T(8,128)(2,1)}, bf16[1024,1024]{0,1:T(8,128)(2,1)S(1)}, u32[]{:S(2)}) copy-start(bf16[1024,1024]{0,1:T(8,128)(2,1)S(1)} %copy.53) | copy-start | bytes 6291460
  201.6 48.2 %collective-permute-start.3 = (bf16[1024,1024]{0,1:T(8,128)(2,1)S(1)}, bf16[1024,1024]{0,1:T(8,128)(2,1)}, u32[]{:S(2)}, u32[]{:S(2)}) collective-permute-start(bf16[1024,1024]{0,1:T(8,128)(2,1)S(1)} %copy.53), channel_id=1, source_target_pairs={{0,1},{1,0},{2,3},{3,2},{4,5},{5,4},{6,7},{7,6},{8,9},{9,8},{10,11... | collective-permute-start | bytes 6291464 | tf_op jit(solution)/shard_map/ppermute | solution.py:295
  276.4 20.4 %copy-start.55 = (bf16[1024,2]{0,1:T(2,128)(2,1)S(1)}, bf16[1024,2]{0,1:T(2,128)(2,1)}, u32[]{:S(2)}) copy-start(bf16[1024,2]{0,1:T(2,128)(2,1)} %param.29) | copy-start | bytes 12292
  276.4 97.5 %all-to-all-start.2 = ((bf16[16,128,1024]{2,1,0:T(8,128)(2,1)}), bf16[16,128,1024]{2,1,0:T(8,128)(2,1)}, u32[]{:S(2)}, u32[]{:S(2)}) async-start(bf16[16,128,1024]{2,1,0:T(8,128)(2,1)} %bitcast.115), calls=%async_computation.2 | async-start | bytes 8388608 | tf_op jit(solution)/shard_map/all_to_all | solution.py:309
  318.4 3.8 copy-start.71
  393.3 26.0 %all-to-all-start.4 = ((f32[16,1,128]{2,1,0:T(1,128)}), f32[16,1,128]{2,1,0:T(1,128)S(1)}, u32[]{:S(2)}, u32[]{:S(2)}) async-start(f32[16,1,128]{2,1,0:T(1,128)} %bitcast.21), calls=%async_computation.4 | async-start | bytes 16384 | tf_op jit(solution)/shard_map/all_to_all | solution.py:309
  419.3 5.3 copy-start.17
  419.9 99.1 %all-to-all-start.1 = ((bf16[16,128,1024]{2,1,0:T(8,128)(2,1)}), bf16[16,128,1024]{2,1,0:T(8,128)(2,1)}, u32[]{:S(2)}, u32[]{:S(2)}) async-start(bf16[16,128,1024]{2,1,0:T(8,128)(2,1)} %bitcast.118), calls=%async_computation.1 | async-start | bytes 8388608 | tf_op jit(solution)/shard_map/all_to_all | solution.py:309
  424.6 366.5 %reduce-scatter.8.cloned.1.call-start = ((), (), s32[]{:S(2)}) async-start(), calls=%async_computation.10 | async-start | bytes 4456448 | tf_op jit(solution)/shard_map/reduce_scatter | solution.py:444
  443.2 24.8 %copy-start.72 = (bf16[1,1024,2048]{2,1,0:T(8,128)(2,1)S(1)}, bf16[1,1024,2048]{2,1,0:T(8,128)(2,1)}, u32[]{:S(2)}) copy-start(bf16[1,1024,2048]{2,1,0:T(8,128)(2,1)} %param.34) | copy-start | bytes 12582916
  519.0 28.4 %copy-start.36 = (s32[2048]{0:T(1024)S(1)}, s32[2048]{0:T(1024)}, u32[]{:S(2)}) copy-start(s32[2048]{0:T(1024)} %param.21) | copy-start | bytes 24580
  519.0 28.4 %copy-start.38 = (f32[2048]{0:T(1024)S(1)}, f32[2048]{0:T(1024)}, u32[]{:S(2)}) copy-start(f32[2048]{0:T(1024)} %copy-done.37) | copy-start | bytes 24580
  519.0 114.3 %all-to-all-start.3 = ((bf16[16,128,1024]{2,1,0:T(8,128)(2,1)}), bf16[16,128,1024]{2,1,0:T(8,128)(2,1)}, u32[]{:S(2)}, u32[]{:S(2)}) async-start(bf16[16,128,1024]{2,1,0:T(8,128)(2,1)} %bitcast.117), calls=%async_computation.3 | async-start | bytes 8388608 | tf_op jit(solution)/shard_map/all_to_all | solution.py:309
  547.3 245.5 %reduce-scatter.6.cloned.1.call-start = ((), (), s32[]{:S(2)}) async-start(), calls=%async_computation.9 | async-start | bytes 4456448 | tf_op jit(solution)/shard_map/reduce_scatter | solution.py:444
  547.4 220.0 %copy-start.33 = (pred[2048,16]{0,1:T(8,128)(4,1)}, pred[2048,16]{0,1:T(8,128)(4,1)S(1)}, u32[]{:S(2)}) copy-start(pred[2048,16]{0,1:T(8,128)(4,1)S(1)} %iota_compare_fusion.2) | copy-start | bytes 98308
  547.6 26.0 %copy-start.9 = (bf16[2048,1024]{0,1:T(8,128)(2,1)S(1)}, bf16[2048,1024]{0,1:T(8,128)(2,1)}, u32[]{:S(2)}) copy-start(bf16[2048,1024]{0,1:T(8,128)(2,1)} %add_convert_fusion) | copy-start | bytes 12582916
  586.4 503.3 %reduce-scatter.4.cloned.1.call-start = ((), (), s32[]{:S(2)}) async-start(), calls=%async_computation.8 | async-start | bytes 4456448 | tf_op jit(solution)/shard_map/reduce_scatter | solution.py:444
  587.3 180.2 %copy-start.39 = (f32[1024]{0:T(1024)}, f32[1024]{0:T(1024)S(1)}, u32[]{:S(2)}) copy-start(f32[1024]{0:T(1024)S(1)} %dynamic-slice_reduce_fusion.2) | copy-start | bytes 12292
  587.3 5.3 copy-start.65
  587.3 6.1 copy-start.41
  589.9 177.6 %copy-start.46 = (f32[1024]{0:T(1024)}, f32[1024]{0:T(1024)S(1)}, u32[]{:S(2)}) copy-start(f32[1024]{0:T(1024)S(1)} %fusion.52) | copy-start | bytes 12292
  671.7 96.5 %collective-permute-start.4 = (bf16[1024,1024]{0,1:T(8,128)(2,1)}, bf16[1024,1024]{0,1:T(8,128)(2,1)}, u32[]{:S(2)}, u32[]{:S(2)}) collective-permute-start(bf16[1024,1024]{0,1:T(8,128)(2,1)} %dynamic-slice_convert_fusion.1), channel_id=1, source_target_pairs={{0,1},{1,0},{2,3},{3,2},{4,5},{5,4},{6,7},{7,6},{8,9},{9,8},{10,11... | collective-permute-start | bytes 6291464 | tf_op jit(solution)/shard_map/ppermute | solution.py:306
  692.8 74.5 %copy-start.52 = (f32[2048]{0:T(1024)S(1)}, f32[2048]{0:T(1024)}, u32[]{:S(2)}) copy-start(f32[2048]{0:T(1024)} %copy-done.51) | copy-start | bytes 24580
  692.8 75.5 %copy-start.45 = (f32[1024]{0:T(1024)S(1)}, f32[1024]{0:T(1024)}, u32[]{:S(2)}) copy-start(f32[1024]{0:T(1024)} %copy-done.44) | copy-start | bytes 12292
  692.8 75.5 %copy-start.56 = (bf16[1024,2]{0,1:T(2,128)(2,1)S(1)}, bf16[1024,2]{0,1:T(2,128)(2,1)}, u32[]{:S(2)}) copy-start(bf16[1024,2]{0,1:T(2,128)(2,1)} %param.29) | copy-start | bytes 12292
  696.7 78.2 %collective-permute-start.2 = (bf16[1024,1024]{0,1:T(8,128)(2,1)}, bf16[1024,1024]{0,1:T(8,128)(2,1)S(1)}, u32[]{:S(2)}, u32[]{:S(2)}) collective-permute-start(bf16[1024,1024]{0,1:T(8,128)(2,1)} %dynamic-slice_convert_fusion.2), channel_id=1, source_target_pairs={{0,1},{1,0},{2,3},{3,2},{4,5},{5,4},{6,7},{7,6},{8,9},{9,8},{10,11... | collective-permute-start | bytes 6291464 | tf_op jit(solution)/shard_map/ppermute | solution.py:306
  767.3 7.6 copy-start.48
  767.5 7.5 copy-start.53
  767.5 8.8 slice-start
  768.3 8.1 slice-start.1
  768.3 8.0 copy-start.50
  776.3 5.6 copy-start.15
  781.9 4.4 copy-start.6
  785.1 48.3 %collective-permute-start.5 = (bf16[1024,1024]{0,1:T(8,128)(2,1)}, bf16[1024,1024]{0,1:T(8,128)(2,1)}, u32[]{:S(2)}, u32[]{:S(2)}) collective-permute-start(bf16[1024,1024]{0,1:T(8,128)(2,1)} %fusion.34), channel_id=1, source_target_pairs={{0,1},{1,0},{2,3},{3,2},{4,5},{5,4},{6,7},{7,6},{8,9},{9,8},{10,11... | collective-permute-start | bytes 6291464 | tf_op jit(solution)/shard_map/ppermute | solution.py:295
  794.6 41.3 %copy-start.1 = (bf16[2048,512]{1,0:T(8,128)(2,1)S(1)}, bf16[2048,512]{1,0:T(8,128)(2,1)}, u32[]{:S(2)}) copy-start(bf16[2048,512]{1,0:T(8,128)(2,1)} %get-tuple-element.21.o_ref) | copy-start | bytes 6291460
  910.9 7.3 copy-start.27
  921.0 204.0 %all-reduce.3.cloned.1.call-start = ((), (), s32[]{:S(2)}) async-start(), calls=%async_computation.11 | async-start | bytes 131072 | tf_op jit(solution)/shard_map/psum | solution.py:452
  921.0 16.5 %copy-start.28 = (bf16[2048,1536]{1,0:T(8,128)(2,1)S(1)}, bf16[2048,1536]{1,0:T(8,128)(2,1)}, u32[]{:S(2)}) copy-start(bf16[2048,1536]{1,0:T(8,128)(2,1)} %copy-done.27) | copy-start | bytes 18874372
  921.0 16.5 %copy-start.32 = (bf16[1024,1536]{1,0:T(8,128)(2,1)S(1)}, bf16[1024,1536]{1,0:T(8,128)(2,1)}, u32[]{:S(2)}) copy-start(bf16[1024,1536]{1,0:T(8,128)(2,1)} %copy-done.31) | copy-start | bytes 9437188
  960.1 16.7 %copy-start.10 = (bf16[2048,1024]{0,1:T(8,128)(2,1)S(1)}, bf16[2048,1024]{0,1:T(8,128)(2,1)}, u32[]{:S(2)}) copy-start(bf16[2048,1024]{0,1:T(8,128)(2,1)} %add_convert_fusion) | copy-start | bytes 12582916
  960.1 16.7 %copy-start.23 = (f32[2048,16]{0,1:T(8,128)S(1)}, f32[2048,16]{0,1:T(8,128)}, u32[]{:S(2)}) copy-start(f32[2048,16]{0,1:T(8,128)} %copy-done.21) | copy-start | bytes 393220
  960.1 16.7 %copy-start.34 = (pred[2048,16]{0,1:T(8,128)(4,1)S(1)}, pred[2048,16]{0,1:T(8,128)(4,1)}, u32[]{:S(2)}) copy-start(pred[2048,16]{0,1:T(8,128)(4,1)} %copy-done.33) | copy-start | bytes 98308
  960.1 16.7 %copy-start.40 = (f32[1024]{0:T(1024)S(1)}, f32[1024]{0:T(1024)}, u32[]{:S(2)}) copy-start(f32[1024]{0:T(1024)} %copy-done.39) | copy-start | bytes 12292
  960.1 16.7 %copy-start.47 = (f32[1024]{0:T(1024)S(1)}, f32[1024]{0:T(1024)}, u32[]{:S(2)}) copy-start(f32[1024]{0:T(1024)} %copy-done.46) | copy-start | bytes 12292
  960.2 16.7 %copy-start.49 = (f32[1024]{0:T(1024)S(1)}, f32[1024]{0:T(1024)}, u32[]{:S(2)}) copy-start(f32[1024]{0:T(1024)} %copy-done.48) | copy-start | bytes 12292
  960.2 16.7 %copy-start.54 = (f32[1024]{0:T(1024)S(1)}, f32[1024]{0:T(1024)}, u32[]{:S(2)}) copy-start(f32[1024]{0:T(1024)} %copy-done.53) | copy-start | bytes 12292
  960.2 109.8 %collective-permute-start.6 = (bf16[1024,1024]{0,1:T(8,128)(2,1)}, bf16[1024,1024]{0,1:T(8,128)(2,1)}, u32[]{:S(2)}, u32[]{:S(2)}) collective-permute-start(bf16[1024,1024]{0,1:T(8,128)(2,1)} %dynamic-slice_convert_fusion), channel_id=1, source_target_pairs={{0,1},{1,0},{2,3},{3,2},{4,5},{5,4},{6,7},{7,6},{8,9},{9,8},{10,11... | collective-permute-start | bytes 6291464 | tf_op jit(solution)/shard_map/ppermute | solution.py:306
  984.9 6.2 copy-start.61
  984.9 6.2 copy-start.62
  1075.3 5.5 copy-start.13
  (29 other events, 61.5 us)
Sparse Core Ops, SparseCore 0:
  439.8 102.5 reduce-scatter.7
  586.5 81.0 reduce-scatter.5
  921.1 100.9 reduce-scatter.3
Sparse Core Ops, SparseCore 1:
  978.2 146.7 all-reduce.2

commit v2 on v1

v2 whole, which is shorter than its diff:
```python
import math
from functools import partial

import jax
import jax.numpy as jnp
from jax import lax
from jax.experimental import pallas as pl
from jax.experimental.pallas import tpu as pltpu
from jax.sharding import PartitionSpec as P

HEAD_DIM = 64
PAIR = 2 * HEAD_DIM


EPS = 1e-05
NEG = -1e30
F32 = jnp.float32
BF16 = jnp.bfloat16
NT = (((1,), (1,)), ((), ()))


LANES = 128
GELU_C = math.sqrt(2.0 / math.pi)
GELU_A = 0.044715
BIG_VMEM = 62 * 1024 * 1024


def dot(left, right):
    return jnp.dot(left, right, preferred_element_type=F32)


def dot_nt(left, right):
    return lax.dot_general(left, right, NT, preferred_element_type=F32)


def normalized(values):
    middle = jnp.mean(values, axis=-1, keepdims=True)
    centred = values - middle
    rstd = lax.rsqrt(jnp.mean(centred * centred, axis=-1, keepdims=True) + EPS)
    return centred * rstd, rstd


def norm_pull(grad, normal, rstd, gain):
    q = grad * gain
    along = jnp.mean(q * normal, axis=-1, keepdims=True)
    return rstd * (q - jnp.mean(q, axis=-1, keepdims=True) - normal * along)


def gelu_and_slope(v):
    square = v * v
    t = jnp.tanh(v * (GELU_C + (GELU_C * GELU_A) * square))
    half = 0.5 + 0.5 * t
    slope = half + v * (0.5 - 0.5 * (t * t)) * (GELU_C + (3.0 * GELU_C * GELU_A) * square)
    return v * half, slope


def router_and_mix(logits, experts):
    lane = lax.broadcasted_iota(jnp.int32, logits.shape, 1)
    out = jnp.zeros_like(logits)
    for low, high in ((0, experts), (experts, experts + 2)):
        inside = (lane >= low) & (lane < high)
        top = jnp.max(jnp.where(inside, logits, NEG), axis=-1, keepdims=True)
        e = jnp.where(inside, jnp.exp(jnp.where(inside, logits - top, 0.0)), 0.0)
        out = out + e / jnp.sum(e, axis=-1, keepdims=True)
    return out


def lane_of(values, index):
    lane = lax.broadcasted_iota(jnp.int32, values.shape, 1)
    return jnp.sum(jnp.where(lane == index, values, 0.0), axis=-1, keepdims=True)


def resident(shape):
    return pl.BlockSpec(shape, lambda i, *_: (0,) * len(shape), pipeline_mode=pl.Buffered(1))


def cost(flops, bytes_accessed):
    return pl.CostEstimate(flops=flops, bytes_accessed=bytes_accessed, transcendentals=0)


def attention_forward_kernel(q_ref, k_ref, v_ref, o_ref, lse_ref, vt_ref, *, bq, bk, scale):
    qi = pl.program_id(2)

    @pl.when(qi == 0)
    def _():
        vt_ref[...] = v_ref[...].T

    lane = lax.broadcasted_iota(jnp.int32, (bq, PAIR), 1)
    q = q_ref[...] * jnp.asarray(scale, BF16)
    zero = jnp.zeros_like(q)
    halves = [jnp.where(lane < HEAD_DIM, q, zero), jnp.where(lane < HEAD_DIM, zero, q)]

    def step(j, carry, masked):
        off = pl.multiple_of(j * bk, bk)
        k = k_ref[pl.ds(off, bk), :]
        vt = vt_ref[:, pl.ds(off, bk)]
        scores = [lax.dot_general(k, half, NT, preferred_element_type=F32) for half in halves]
        if masked:
            key_pos = off + lax.broadcasted_iota(jnp.int32, (bk, bq), 0)
            query_pos = qi * bq + lax.broadcasted_iota(jnp.int32, (bk, bq), 1)
            allowed = key_pos <= query_pos
            scores = [jnp.where(allowed, s, NEG) for s in scores]
        new = []
        for h in range(2):
            m, l, acc = carry[h]
            m_new = jnp.maximum(m, jnp.max(scores[h], axis=0, keepdims=True))
            alpha = jnp.exp(m - m_new)
            p = jnp.exp(scores[h] - m_new)
            l = l * alpha + jnp.sum(p, axis=0, keepdims=True)
            part = jnp.dot(
                vt[h * HEAD_DIM : (h + 1) * HEAD_DIM], p.astype(BF16), preferred_element_type=F32
            )
            new.append((m_new, l, acc * alpha + part))
        return tuple(new)

    init = tuple(
        (jnp.full((1, bq), NEG, F32), jnp.zeros((1, bq), F32), jnp.zeros((HEAD_DIM, bq), F32))
        for _ in range(2)
    )
    full = qi * (bq // bk)
    carry = lax.fori_loop(0, full, lambda j, c: step(j, c, False), init)
    for d in range(bq // bk):
        carry = step(full + d, carry, True)
    outs = []
    for h in range(2):
        m, l, acc = carry[h]
        outs.append(acc / l)
        lse_ref[0, h : h + 1, :] = m + jnp.log(l)
    o_ref[...] = jnp.concatenate(outs, axis=0).T.astype(BF16)


def attention_forward(proj, seqs, heads, first, count, bq=512, bk=512):
    rows = proj.shape[0]
    length = rows // seqs
    pairs = heads // 2
    nq = length // bq
    flops = 2 * rows * length * count * PAIR
    return pl.pallas_call(
        partial(attention_forward_kernel, bq=bq, bk=bk, scale=HEAD_DIM**-0.5),
        grid=(seqs, count, nq),
        in_specs=[
            pl.BlockSpec((bq, PAIR), lambda s, p, i: (s * nq + i, first + p)),
            pl.BlockSpec((length, PAIR), lambda s, p, i: (s, pairs + first + p)),
            pl.BlockSpec((length, PAIR), lambda s, p, i: (s, 2 * pairs + first + p)),
        ],
        out_specs=[
            pl.BlockSpec((bq, PAIR), lambda s, p, i: (s * nq + i, p)),
            pl.BlockSpec((1, 2, bq), lambda s, p, i: (p, 0, s * nq + i)),
        ],
        out_shape=[
            jax.ShapeDtypeStruct((rows, count * PAIR), BF16),
            jax.ShapeDtypeStruct((count, 2, rows), F32),
        ],
        scratch_shapes=[pltpu.VMEM((PAIR, length), BF16)],
        cost_estimate=pl.CostEstimate(
            flops=flops * 4, bytes_accessed=8 * rows * count * PAIR, transcendentals=0
        ),
        name="attention_forward",
    )(proj, proj, proj)


def attention_backward_kernel(
    q_ref,
    k_ref,
    v_ref,
    o_ref,
    lse_ref,
    *refs,
    terms,
    bq,
    bk,
    scale,
    length,
):
    lane = lax.broadcasted_iota(jnp.int32, (length, PAIR), 1)
    first = lane < HEAD_DIM
    q = q_ref[...] * jnp.asarray(scale, BF16)
    do_refs = refs[:terms]
    dq_ref, dk_ref, dv_ref, dqt_ref, qs_ref, dos_ref, kt_ref, dl_ref = refs[terms:]
    do = do_refs[0][...]
    if terms == 2:
        do = (do.astype(F32) + do_refs[1][...].astype(F32)).astype(BF16)
    zero = jnp.zeros_like(q)
    qs_ref[0] = jnp.where(first, q, zero)
    qs_ref[1] = jnp.where(first, zero, q)
    dos_ref[0] = jnp.where(first, do, zero)
    dos_ref[1] = jnp.where(first, zero, do)
    kt_ref[...] = (k_ref[...] * jnp.asarray(scale, BF16)).T
    prod = (do.astype(F32) * o_ref[...].astype(F32)).T
    dl_ref[0:1, :] = jnp.sum(prod[:HEAD_DIM], axis=0, keepdims=True)
    dl_ref[1:2, :] = jnp.sum(prod[HEAD_DIM:], axis=0, keepdims=True)
    dqt_ref[...] = jnp.zeros_like(dqt_ref)
    nq = length // bq
    nk = length // bk

    def key_block(j, _):
        koff = pl.multiple_of(j * bk, bk)
        k = k_ref[pl.ds(koff, bk), :]
        v = v_ref[pl.ds(koff, bk), :]
        kt = kt_ref[:, pl.ds(koff, bk)]

        def step(i, carry, masked):
            dk, dv = carry
            qoff = pl.multiple_of(i * bq, bq)
            if masked:
                key_pos = koff + lax.broadcasted_iota(jnp.int32, (bk, bq), 0)
                query_pos = qoff + lax.broadcasted_iota(jnp.int32, (bk, bq), 1)
                allowed = key_pos <= query_pos
            qh = [qs_ref[h, pl.ds(qoff, bq), :] for h in range(2)]
            dh = [dos_ref[h, pl.ds(qoff, bq), :] for h in range(2)]
            scores = [lax.dot_general(k, x, NT, preferred_element_type=F32) for x in qh]
            pulls = [lax.dot_general(v, x, NT, preferred_element_type=F32) for x in dh]
            dqs = []
            for h in range(2):
                p = jnp.exp(scores[h] - lse_ref[0, h : h + 1, pl.ds(qoff, bq)])
                if masked:
                    p = jnp.where(allowed, p, 0.0)
                ds = (p * (pulls[h] - dl_ref[h : h + 1, pl.ds(qoff, bq)])).astype(BF16)
                dv = dv + jnp.dot(p.astype(BF16), dh[h], preferred_element_type=F32)
                dk = dk + jnp.dot(ds, qh[h], preferred_element_type=F32)
                dqs.append(
                    jnp.dot(
                        kt[h * HEAD_DIM : (h + 1) * HEAD_DIM], ds, preferred_element_type=F32
                    )
                )
            dqt_ref[:, pl.ds(qoff, bq)] += jnp.concatenate(dqs, axis=0)
            return dk, dv

        carry = (jnp.zeros((bk, PAIR), F32), jnp.zeros((bk, PAIR), F32))
        i0 = j * (bk // bq)
        for d in range(bk // bq):
            carry = step(i0 + d, carry, True)
        dk, dv = lax.fori_loop(i0 + bk // bq, nq, lambda i, c: step(i, c, False), carry)
        dk_ref[pl.ds(koff, bk), :] = dk.astype(BF16)
        dv_ref[pl.ds(koff, bk), :] = dv.astype(BF16)
        return 0

    lax.fori_loop(0, nk, key_block, 0)
    dq_ref[...] = dqt_ref[...].T.astype(BF16)


def attention_backward(proj, out, out_grads, lse, seqs, heads, first, bq=512, bk=512):
    rows, width = out.shape
    length = rows // seqs
    pairs = heads // 2
    count = width // PAIR

    def block(off):
        return pl.BlockSpec((length, PAIR), lambda s, p: (s, off + p))

    grad = jax.ShapeDtypeStruct((rows, width), BF16)
    terms = len(out_grads)
    return pl.pallas_call(
        partial(
            attention_backward_kernel,
            terms=terms,
            bq=bq,
            bk=bk,
            scale=HEAD_DIM**-0.5,
            length=length,
        ),
        grid=(seqs, count),
        in_specs=[
            block(first),
            block(pairs + first),
            block(2 * pairs + first),
            block(0),
            pl.BlockSpec((1, 2, length), lambda s, p: (p, 0, s)),
        ]
        + [block(0)] * terms,
        out_specs=[block(0)] * 3,
        out_shape=[grad] * 3,
        scratch_shapes=[
            pltpu.VMEM((PAIR, length), F32),
            pltpu.VMEM((2, length, PAIR), BF16),
            pltpu.VMEM((2, length, PAIR), BF16),
            pltpu.VMEM((PAIR, length), BF16),
            pltpu.VMEM((2, length), F32),
        ],
        cost_estimate=cost(20 * rows * length * width, 16 * rows * width),
        compiler_params=pltpu.CompilerParams(vmem_limit_bytes=40 * 1024 * 1024),
        name="attention_backward",
    )(proj, proj, proj, out, lse, *out_grads)


def norm_project_kernel(x_ref, gain_ref, bias_ref, wq_ref, wk_ref, wv_ref, a_ref, p_ref):
    normal, _ = normalized(x_ref[...].astype(F32))
    a = (normal * gain_ref[...] + bias_ref[...]).astype(BF16)
    a_ref[...] = a
    width = wq_ref.shape[1]
    for j, w in enumerate((wq_ref, wk_ref, wv_ref)):
        p_ref[:, j * width : (j + 1) * width] = dot(a, w[...]).astype(BF16)


def norm_project(x, gain, bias, weights, rb=512):
    rows, wide = x.shape
    width = weights[0].shape[1]
    return pl.pallas_call(
        norm_project_kernel,
        grid=(rows // rb,),
        in_specs=[pl.BlockSpec((rb, wide), lambda i: (i, 0)), resident((1, wide)), resident((1, wide))]
        + [resident((wide, width))] * 3,
        out_specs=[
            pl.BlockSpec((rb, wide), lambda i: (i, 0)),
            pl.BlockSpec((rb, 3 * width), lambda i: (i, 0)),
        ],
        out_shape=[
            jax.ShapeDtypeStruct((rows, wide), BF16),
            jax.ShapeDtypeStruct((rows, 3 * width), BF16),
        ],
        cost_estimate=cost(6 * rows * wide * width, 8 * rows * wide),
        name="norm_project",
    )(x, gain, bias, *weights)


def output_norm_kernel(*refs, parts, experts):
    x_ref, gain_ref, bias_ref, rm_ref = refs[:4]
    heads = refs[4 : 4 + parts]
    weights = refs[4 + parts : 4 + 2 * parts]
    resid_ref, f_ref, chance_ref = refs[4 + 2 * parts :]
    total = dot_nt(heads[0][...], weights[0][...])
    for h, w in zip(heads[1:], weights[1:]):
        total = total + dot_nt(h[...], w[...])
    resid = x_ref[...].astype(F32) + total
    resid_ref[...] = resid
    normal, _ = normalized(resid)
    f = (normal * gain_ref[...] + bias_ref[...]).astype(BF16)
    f_ref[...] = f
    chance_ref[...] = router_and_mix(dot(f, rm_ref[...]), experts)


def output_norm(x, gain, bias, rm, heads, weights, experts, rb=256):
    rows, wide = x.shape
    block = pl.BlockSpec((rb, wide), lambda i: (i, 0))
    weight_specs = [
        pl.BlockSpec(
            (wide, h.shape[1]), lambda i, j=j: (0, j), pipeline_mode=pl.Buffered(1)
        )
        for h, (_, j) in zip(heads, weights)
    ]
    return pl.pallas_call(
        partial(output_norm_kernel, parts=len(heads), experts=experts),
        grid=(rows // rb,),
        in_specs=[block, resident((1, wide)), resident((1, wide)), resident((wide, LANES))]
        + [pl.BlockSpec((rb, h.shape[1]), lambda i: (i, 0)) for h in heads]
        + weight_specs,
        out_specs=[block, block, pl.BlockSpec((rb, LANES), lambda i: (i, 0))],
        out_shape=[
            jax.ShapeDtypeStruct((rows, wide), F32),
            jax.ShapeDtypeStruct((rows, wide), BF16),
            jax.ShapeDtypeStruct((rows, LANES), F32),
        ],
        cost_estimate=cost(2 * rows * wide * wide, 12 * rows * wide),
        name="output_norm",
    )(x, gain, bias, rm, *heads, *[w for w, _ in weights])


def pack_kernel(place_ref, x_ref, o_ref):
    count, rows = o_ref.shape[0], x_ref.shape[0]
    slot = pl.program_id(0) * count + lax.broadcasted_iota(jnp.int32, (count, rows), 0)
    hot = jnp.where(slot == place_ref[...], 1.0, 0.0).astype(BF16)
    o_ref[...] = dot(hot, x_ref[...]).astype(BF16)


def pack(place, x, count, sb=512):
    rows, wide = x.shape
    return pl.pallas_call(
        pack_kernel,
        grid=(count // sb,),
        in_specs=[resident((1, rows)), resident((rows, wide))],
        out_specs=pl.BlockSpec((sb, wide), lambda i: (i, 0)),
        out_shape=jax.ShapeDtypeStruct((count, wide), BF16),
        cost_estimate=cost(2 * rows * wide * count, 4 * rows * wide),
        name="pack_rows",
    )(place, x)


def unpacked(place, all_ref):
    slot = lax.broadcasted_iota(jnp.int32, (place.shape[0], all_ref.shape[0]), 1)
    return dot(jnp.where(slot == place, 1.0, 0.0).astype(BF16), all_ref[...])


def nets_kernel(
    x_hbm,
    g_hbm,
    out_hbm,
    gin_hbm,
    sel_ref,
    rm_ref,
    wd1_hbm,
    wd2_hbm,
    we1_hbm,
    we2_hbm,
    y_hbm,
    dx_hbm,
    dot_hbm,
    gd1_hbm,
    gd2_hbm,
    ge1_hbm,
    ge2_hbm,
    in_hbm,
    res_hbm,
    pull_hbm,
    edot_hbm,
    pulls_hbm,
    edots_hbm,
    wd1,
    wd2,
    we1,
    we2,
    a1,
    a2,
    xb,
    gb,
    yb,
    dxb,
    dotb,
    rowb,
    ya,
    dxa,
    dyb,
    dyt,
    xt,
    w_sem,
    load_sem,
    store_sem,
    grad_sem,
    home_sem,
    local_sem,
    send_sem,
    recv_sem,
    back_send,
    back_recv,
    dot_send,
    dot_recv,
    *,
    peers,
    capacity,
    rb,
    ft,
):
    experts = peers
    me = lax.axis_index("ep")
    hidden = wd1.shape[1]
    per = rb // capacity
    quarter = peers // 4
    dense_steps = x_hbm.shape[0] // rb
    expert_steps = peers // per

    weight_copies = [
        pltpu.make_async_copy(src, dst, w_sem.at[j])
        for j, (src, dst) in enumerate(
            ((wd1_hbm, wd1), (wd2_hbm, wd2), (we1_hbm, we1), (we2_hbm, we2))
        )
    ]
    weight_copies[0].start()
    weight_copies[1].start()

    def load(t, slot):
        rows = pl.ds(pl.multiple_of(t * rb, rb), rb)
        return [
            pltpu.make_async_copy(x_hbm.at[rows, :], xb.at[slot], load_sem.at[slot, 0, 0]),
            pltpu.make_async_copy(g_hbm.at[rows, :], gb.at[slot], load_sem.at[slot, 1, 0]),
        ]

    for c in load(0, 0):
        c.start()

    barrier = pltpu.get_barrier_semaphore()
    for k in range(1, peers):
        pl.semaphore_signal(
            barrier,
            inc=1,
            device_id={"ep": jnp.bitwise_xor(me, k)},
            device_id_type=pl.DeviceIdType.MESH,
        )
    pl.semaphore_wait(barrier, peers - 1)

    def remote(src, dst, send, recv, k):
        peer = jnp.bitwise_xor(me, k)
        return pltpu.make_async_remote_copy(
            src_ref=src,
            dst_ref=dst,
            send_sem=send.at[k],
            recv_sem=recv.at[k],
            device_id={"ep": peer},
            device_id_type=pl.DeviceIdType.MESH,
        )

    def row_copy(k):
        return remote(
            out_hbm.at[jnp.bitwise_xor(me, k)], in_hbm.at[me], send_sem, recv_sem, k
        )

    def back_copy(k):
        return remote(
            pull_hbm.at[jnp.bitwise_xor(me, k)], pulls_hbm.at[me], back_send, back_recv, k
        )

    def dot_copy(k):
        return remote(
            edot_hbm.at[jnp.bitwise_xor(me, k)], edots_hbm.at[me], dot_send, dot_recv, k
        )

    far = list(range(2 * quarter, 3 * quarter))
    near = list(range(1, 2 * quarter))
    last = list(range(3 * quarter, peers))
    for k in far + near + last:
        row_copy(k).start()
    own_rows = pltpu.make_async_copy(out_hbm.at[me], in_hbm.at[me], home_sem.at[0])
    own_rows.start()
    weight_copies[2].start()
    weight_copies[3].start()

    def compute(slot, routed, w1_ref, w2_ref):
        x_ref = xb.at[slot]
        x = x_ref[...]
        g = gb[slot].astype(F32)
        chances = router_and_mix(dot(x, rm_ref[...]), experts)
        if routed:
            gate = jnp.sum(chances * sel_ref[...], axis=-1, keepdims=True)
            dy = g * lane_of(chances, experts + 1) * gate
        else:
            dy = g * lane_of(chances, experts)
        dy = dy.astype(BF16)
        dyb[...] = dy
        dyt[...] = dy.T
        xt[...] = x.T
        ya[...] = jnp.zeros_like(ya)
        dxa[...] = jnp.zeros_like(dxa)

        def step(f, _):
            cols = pl.ds(pl.multiple_of(f * ft, ft), ft)
            w1 = w1_ref[:, cols]
            w2 = w2_ref[:, cols]
            act, slope = gelu_and_slope(dot(x_ref[...], w1))
            h = act.astype(BF16)
            pre_grad = (slope * dot(dyb[...], w2)).astype(BF16)
            ya[...] += dot_nt(h, w2)
            dxa[...] += dot_nt(pre_grad, w1)
            a2[:, cols] += dot(dyt[...], h)
            a1[:, cols] += dot(xt[...], pre_grad)
            return 0

        lax.fori_loop(0, hidden // ft, step, 0)
        y = ya[...]
        yb[slot] = y.astype(BF16)
        dxb[slot] = dxa[...].astype(BF16)
        return jnp.sum(y * g, axis=1, keepdims=True)

    a1[...] = jnp.zeros_like(a1)
    a2[...] = jnp.zeros_like(a2)
    weight_copies[0].wait()
    weight_copies[1].wait()

    def dense_stores(t, slot):
        rows = pl.ds(pl.multiple_of(t * rb, rb), rb)
        return [
            pltpu.make_async_copy(yb.at[slot], y_hbm.at[rows, :], store_sem.at[slot, 0, 0]),
            pltpu.make_async_copy(dxb.at[slot], dx_hbm.at[rows, :], store_sem.at[slot, 1, 0]),
            pltpu.make_async_copy(dotb.at[slot], dot_hbm.at[rows, :], store_sem.at[slot, 2, 0]),
        ]

    def dense_step(t, _):
        slot = lax.rem(t, 2)
        for c in load(t, slot):
            c.wait()

        @pl.when(t + 1 < dense_steps)
        def _():
            for c in load(t + 1, 1 - slot):
                c.start()

        @pl.when(t >= 2)
        def _():
            for c in dense_stores(t - 2, slot):
                c.wait()

        dots = compute(slot, False, wd1, wd2)
        dotb[slot] = jnp.broadcast_to(dots, (rb, LANES))
        for c in dense_stores(t, slot):
            c.start()
        return 0

    lax.fori_loop(0, dense_steps, dense_step, 0)
    for t in range(max(0, dense_steps - 2), dense_steps):
        for c in dense_stores(t, t % 2):
            c.wait()

    wd1[...] = a1[...].astype(BF16)
    wd2[...] = a2[...].astype(BF16)
    dense_grads = [
        pltpu.make_async_copy(wd1, gd1_hbm, grad_sem.at[0]),
        pltpu.make_async_copy(wd2, gd2_hbm, grad_sem.at[1]),
    ]
    for c in dense_grads:
        c.start()
    a1[...] = jnp.zeros_like(a1)
    a2[...] = jnp.zeros_like(a2)
    weight_copies[2].wait()
    weight_copies[3].wait()
    own_rows.wait()

    def expert_step(p, _):
        base = jnp.where(p == expert_steps - 1, peers - per, (expert_steps - 2 - p) * per)
        slot = lax.rem(p, 2)
        loads = []
        for c in range(per):
            k = base + c

            @pl.when(k > 0)
            def _(k=k):
                row_copy(k).wait()

            source = jnp.bitwise_xor(me, k)
            rows = pl.ds(c * capacity, capacity)
            loads.append(
                pltpu.make_async_copy(in_hbm.at[source], xb.at[slot, rows, :], load_sem.at[slot, 0, c])
            )
            loads.append(
                pltpu.make_async_copy(gin_hbm.at[source], gb.at[slot, rows, :], load_sem.at[slot, 1, c])
            )
        for c in loads:
            c.start()
        for c in loads:
            c.wait()
        dots = compute(slot, True, we1, we2)
        across = jnp.broadcast_to(dots, (rb, LANES)).T
        stores = []
        for c in range(per):
            source = jnp.bitwise_xor(me, base + c)
            rows = pl.ds(c * capacity, capacity)
            rowb[c] = across[:8, c * capacity : (c + 1) * capacity]
            stores.append(
                pltpu.make_async_copy(yb.at[slot, rows, :], res_hbm.at[source], store_sem.at[slot, 0, c])
            )
            stores.append(
                pltpu.make_async_copy(dxb.at[slot, rows, :], pull_hbm.at[source], store_sem.at[slot, 1, c])
            )
            stores.append(
                pltpu.make_async_copy(rowb.at[c], edot_hbm.at[source], store_sem.at[slot, 2, c])
            )
        for c in stores:
            c.start()
        for c in stores:
            c.wait()
        for c in range(per):
            k = base + c

            @pl.when(k > 0)
            def _(k=k):
                back_copy(k).start()
                dot_copy(k).start()

        return 0

    lax.fori_loop(0, expert_steps, expert_step, 0)
    expert_grads = [
        pltpu.make_async_copy(a1, ge1_hbm, local_sem.at[0]),
        pltpu.make_async_copy(a2, ge2_hbm, local_sem.at[1]),
        pltpu.make_async_copy(pull_hbm.at[me], pulls_hbm.at[me], home_sem.at[1]),
        pltpu.make_async_copy(edot_hbm.at[me], edots_hbm.at[me], home_sem.at[2]),
    ]
    for c in expert_grads:
        c.start()
    for c in dense_grads + expert_grads:
        c.wait()
    for k in range(1, peers):
        back_copy(k).wait()
        dot_copy(k).wait()


def nets(x, g, out_rows, in_grads, sel, rm, dense_weights, expert_weights, rb=512, ft=512):
    rows, wide = x.shape
    hidden = dense_weights[0].shape[1]
    peers, capacity, _ = out_rows.shape
    per = rb // capacity
    anywhere = pl.BlockSpec(memory_space=pl.ANY)
    vmem = pl.BlockSpec(memory_space=pltpu.VMEM)
    sheet = jax.ShapeDtypeStruct((rows, wide), BF16)
    blocks = jax.ShapeDtypeStruct((peers, capacity, wide), BF16)
    strips = jax.ShapeDtypeStruct((peers, 8, capacity), F32)
    return pl.pallas_call(
        partial(nets_kernel, peers=peers, capacity=capacity, rb=rb, ft=ft),
        in_specs=[anywhere] * 4 + [vmem] * 2 + [anywhere] * 4,
        out_specs=[anywhere] * 13,
        out_shape=[
            sheet,
            sheet,
            jax.ShapeDtypeStruct((rows, LANES), F32),
            jax.ShapeDtypeStruct((wide, hidden), BF16),
            jax.ShapeDtypeStruct((wide, hidden), BF16),
            jax.ShapeDtypeStruct((wide, hidden), F32),
            jax.ShapeDtypeStruct((wide, hidden), F32),
            blocks,
            blocks,
            blocks,
            strips,
            blocks,
            strips,
        ],
        scratch_shapes=[pltpu.VMEM((wide, hidden), BF16)] * 4
        + [pltpu.VMEM((wide, hidden), F32)] * 2
        + [pltpu.VMEM((2, rb, wide), BF16)] * 4
        + [
            pltpu.VMEM((2, rb, LANES), F32),
            pltpu.VMEM((per, 8, capacity), F32),
            pltpu.VMEM((rb, wide), F32),
            pltpu.VMEM((rb, wide), F32),
            pltpu.VMEM((rb, wide), BF16),
            pltpu.VMEM((wide, rb), BF16),
            pltpu.VMEM((wide, rb), BF16),
            pltpu.SemaphoreType.DMA((4,)),
            pltpu.SemaphoreType.DMA((2, 2, per)),
            pltpu.SemaphoreType.DMA((2, 3, per)),
            pltpu.SemaphoreType.DMA((2,)),
            pltpu.SemaphoreType.DMA((3,)),
            pltpu.SemaphoreType.DMA((2,)),
        ]
        + [pltpu.SemaphoreType.DMA((peers,))] * 6,
        cost_estimate=cost(24 * rows * wide * hidden, 16 * rows * wide + 24 * wide * hidden),
        compiler_params=pltpu.CompilerParams(
            vmem_limit_bytes=BIG_VMEM, collective_id=0, has_side_effects=True
        ),
        name="feed_forward_nets",
    )(x, g, out_rows, in_grads, sel, rm, *dense_weights, *expert_weights)


def expert_hot(place, capacity, experts):
    lane = lax.broadcasted_iota(jnp.int32, (place.shape[0], LANES), 1)
    low = lane * capacity
    return ((place >= low) & (place < low + capacity) & (lane < experts)).astype(F32)


def ffn_pull_kernel(*refs, parts, experts, capacity):
    (
        place_ref,
        own_ref,
        dx_ref,
        chance_ref,
        first_ref,
        f_ref,
        g_ref,
        resid_ref,
        gain_ref,
        rm_ref,
        slot_ref,
        dots_ref,
    ) = refs[:12]
    weights = refs[12 : 12 + parts]
    r_ref = refs[12 + parts]
    heads = refs[13 + parts : 13 + 2 * parts]
    sums_ref, rmg_ref = refs[13 + 2 * parts :]
    place = place_ref[...]
    chances = chance_ref[...]
    hot = expert_hot(place, capacity, experts)
    gate = jnp.sum(hot * chances, axis=-1, keepdims=True)
    mix_0, mix_1 = lane_of(chances, experts), lane_of(chances, experts + 1)
    table = jnp.dot(
        hot, dots_ref[...], precision=lax.Precision.HIGHEST, preferred_element_type=F32
    )
    slot = lax.broadcasted_iota(jnp.int32, table.shape, 1)
    number = jnp.sum(hot * lax.broadcasted_iota(jnp.int32, hot.shape, 1).astype(F32), axis=-1)
    inside = place - number.astype(jnp.int32)[:, None] * capacity
    second = jnp.sum(jnp.where(slot == inside, table, 0.0), axis=-1, keepdims=True)
    first = lane_of(first_ref[...], 0)
    grad_0, grad_1 = first, gate * second
    inner = mix_0 * grad_0 + mix_1 * grad_1
    lane = lax.broadcasted_iota(jnp.int32, chances.shape, 1)
    low = (mix_1 * second * gate) * (hot - chances)
    low = jnp.where(lane == experts, mix_0 * (grad_0 - inner), low)
    low = jnp.where(lane == experts + 1, mix_1 * (grad_1 - inner), low)
    low = jnp.where(lane > experts + 1, 0.0, low).astype(BF16)
    grad = dx_ref[...].astype(F32) + unpacked(place, slot_ref) + dot_nt(low, rm_ref[...])
    normal, rstd = normalized(resid_ref[...])
    r = norm_pull(grad, normal, rstd, gain_ref[...]) + own_ref[...] * g_ref[...].astype(F32)
    r = r.astype(BF16)
    r_ref[...] = r
    for h, w in zip(heads, weights):
        h[...] = dot(r, w[...]).astype(BF16)

    @pl.when(pl.program_id(0) == 0)
    def _():
        sums_ref[...] = jnp.zeros_like(sums_ref)
        rmg_ref[...] = jnp.zeros_like(rmg_ref)

    sums_ref[0:1, :] += jnp.sum(grad * normal, axis=0, keepdims=True)
    sums_ref[1:2, :] += jnp.sum(grad, axis=0, keepdims=True)
    rmg_ref[...] += dot(low.T, f_ref[...])


def ffn_pull(
    place, own, dx, chances, first, f, g, resid, gain, rm, slot_rows, dots, weights, experts, rb=256
):
    rows, wide = dx.shape
    capacity = dots.shape[1]
    dots = jnp.pad(dots, ((0, LANES - experts), (0, 0)))
    block = pl.BlockSpec((rb, wide), lambda i: (i, 0))
    narrow = pl.BlockSpec((rb, LANES), lambda i: (i, 0))
    col = pl.BlockSpec((rb, 1), lambda i: (i, 0))
    head_specs = [pl.BlockSpec((rb, size), lambda i: (i, 0)) for _, _, size in weights]
    return pl.pallas_call(
        partial(ffn_pull_kernel, parts=len(weights), experts=experts, capacity=capacity),
        grid=(rows // rb,),
        in_specs=[col, col, block, narrow, narrow, block, block, block]
        + [resident((1, wide)), resident((wide, LANES))]
        + [resident(slot_rows.shape), resident(dots.shape)]
        + [
            pl.BlockSpec((wide, size), lambda i, j=j: (0, j), pipeline_mode=pl.Buffered(1))
            for _, j, size in weights
        ],
        out_specs=[block] + head_specs + [resident((8, wide)), resident((LANES, wide))],
        out_shape=[jax.ShapeDtypeStruct((rows, wide), BF16)]
        + [jax.ShapeDtypeStruct((rows, size), BF16) for _, _, size in weights]
        + [jax.ShapeDtypeStruct((8, wide), F32), jax.ShapeDtypeStruct((LANES, wide), F32)],
        cost_estimate=cost(6 * rows * wide * wide, 16 * rows * wide),
        compiler_params=pltpu.CompilerParams(vmem_limit_bytes=48 * 1024 * 1024),
        name="ffn_norm_pull",
    )(
        place,
        own,
        dx,
        chances,
        first,
        f,
        g,
        resid,
        gain,
        rm,
        slot_rows,
        dots,
        *[w for w, _, _ in weights],
    )


def outer_kernel(left_ref, *refs, parts):
    rights = refs[:parts]
    o_ref, acc_ref = refs[parts:]

    @pl.when(pl.program_id(0) == 0)
    def _():
        acc_ref[...] = jnp.zeros_like(acc_ref)

    left = left_ref[...].T
    at = 0
    for r in rights:
        width = r.shape[1]
        acc_ref[:, at : at + width] += dot(left, r[...])
        at += width

    @pl.when(pl.program_id(0) == pl.num_programs(0) - 1)
    def _():
        o_ref[...] = acc_ref[...].astype(BF16)


def outer(left, rights, rb=512):
    rows, wide = left.shape
    total = sum(r.shape[1] for r in rights)
    return pl.pallas_call(
        partial(outer_kernel, parts=len(rights)),
        grid=(rows // rb,),
        in_specs=[pl.BlockSpec((rb, wide), lambda i: (i, 0))]
        + [pl.BlockSpec((rb, r.shape[1]), lambda i: (i, 0)) for r in rights],
        out_specs=resident((wide, total)),
        out_shape=jax.ShapeDtypeStruct((wide, total), BF16),
        scratch_shapes=[pltpu.VMEM((wide, total), F32)],
        cost_estimate=cost(2 * rows * wide * total, 2 * rows * (wide + total)),
        name="outer_product",
    )(left, *rights)


def attn_pull_kernel(at_ref, x_ref, r_ref, gain_ref, *refs, groups):
    grads = refs[: 3 * groups]
    weights = refs[3 * groups : 3 * groups + 3]
    t_ref, sums_ref = refs[3 * groups + 3 :]
    del at_ref
    total = None
    for k in range(3):
        at = 0
        for j in range(groups):
            d = grads[k * groups + j]
            width = d.shape[1]
            part = dot_nt(d[...], weights[k][:, at : at + width])
            total = part if total is None else total + part
            at += width
    normal, rstd = normalized(x_ref[...].astype(F32))
    t = norm_pull(total, normal, rstd, gain_ref[...]) + r_ref[...].astype(F32)
    t_ref[...] = t.astype(t_ref.dtype)

    @pl.when(pl.program_id(0) == 0)
    def _():
        sums_ref[...] = jnp.zeros_like(sums_ref)

    sums_ref[0:1, :] += jnp.sum(total * normal, axis=0, keepdims=True)
    sums_ref[1:2, :] += jnp.sum(total, axis=0, keepdims=True)


def attn_pull(first_row, count, x, r, gain, grads, weights, out_type, rb=256):
    wide = x.shape[1]
    groups = len(grads) // 3

    def rows(width):
        return pl.BlockSpec((rb, width), lambda i, at: (at[0] + i, 0))

    return pl.pallas_call(
        partial(attn_pull_kernel, groups=groups),
        grid_spec=pltpu.PrefetchScalarGridSpec(
            num_scalar_prefetch=1,
            grid=(count // rb,),
            in_specs=[rows(wide), rows(wide), resident((1, wide))]
            + [rows(d.shape[1]) for d in grads]
            + [resident(w.shape) for w in weights],
            out_specs=[pl.BlockSpec((rb, wide), lambda i, at: (i, 0)), resident((8, wide))],
        ),
        out_shape=[
            jax.ShapeDtypeStruct((count, wide), out_type),
            jax.ShapeDtypeStruct((8, wide), F32),
        ],
        cost_estimate=cost(6 * count * wide * weights[0].shape[1], 10 * count * wide),
        name="attention_norm_pull",
    )((first_row // rb).astype(jnp.int32).reshape(1), x, r, gain, *grads, *weights)


def combine_kernel(place_ref, y_ref, chance_ref, slot_ref, o_ref, *, experts, capacity):
    place = place_ref[...]
    chances = chance_ref[...]
    gate = jnp.sum(expert_hot(place, capacity, experts) * chances, axis=-1, keepdims=True)
    moe = unpacked(place, slot_ref) * (lane_of(chances, experts + 1) * gate)
    o_ref[...] = (lane_of(chances, experts) * y_ref[...].astype(F32) + moe).astype(BF16)


def combine(place, y, coef, slot_rows, experts, rb=256):
    rows, wide = y.shape
    block = pl.BlockSpec((rb, wide), lambda i: (i, 0))
    return pl.pallas_call(
        partial(combine_kernel, experts=experts, capacity=slot_rows.shape[0] // experts),
        grid=(rows // rb,),
        in_specs=[
            pl.BlockSpec((rb, 1), lambda i: (i, 0)),
            block,
            pl.BlockSpec((rb, LANES), lambda i: (i, 0)),
        ]
        + [resident(slot_rows.shape)],
        out_specs=block,
        out_shape=jax.ShapeDtypeStruct((rows, wide), BF16),
        cost_estimate=cost(4 * rows * wide * wide, 8 * rows * wide),
        name="combine_nets",
    )(place, y, coef, slot_rows)


def on_device(
    sizes,
    tokens,
    out_grad,
    lengths,
    expert_ids,
    w_query,
    w_key,
    w_value,
    w_output,
    w_hidden,
    w_return,
    router,
    mix_weight,
    gain_attn,
    bias_attn,
    gain_ffn,
    bias_ffn,
    expert_in,
    expert_out,
):
    tp, ep = sizes
    shard_rows = out_grad.shape[0]
    all_rows = tokens.shape[0]
    model_width = tokens.shape[1]
    experts = router.shape[1]
    capacity = all_rows // experts
    seq_count = lengths.shape[0]
    seq_len = all_rows // seq_count
    local_width = w_query.shape[1]
    local_heads = local_width // HEAD_DIM
    pairs = local_heads // 2
    splits = 2 if pairs % 2 == 0 else 1
    each = pairs // splits
    tp_index = lax.axis_index("tp")
    ep_index = lax.axis_index("ep")
    first_row = tp_index * shard_rows
    swap = [(0, 1), (1, 0)]

    def shard_of(values, axis=0):
        return lax.dynamic_slice_in_dim(values, first_row, shard_rows, axis)

    def swapped(values):
        return lax.ppermute(values, "tp", swap)

    def exchange(values):
        return lax.all_to_all(values, "ep", split_axis=0, concat_axis=0, tiled=True)

    def after(values, *others):
        return lax.optimization_barrier((values, others))[0]

    def summed_over(values, axis, size):
        step = 1
        while step < size:
            values = values + lax.ppermute(values, axis, [(i, i ^ step) for i in range(size)])
            step *= 2
        return values

    def over_sequences(values):
        return lax.psum_scatter(values, "ep", scatter_dimension=0, tiled=True).astype(F32)

    def halved_over_sequences(values):
        step = 1
        while step < ep:
            width = values.shape[-1]
            split = values.reshape(-1, 2, values.shape[0] // (ep // step), width)
            bit = (ep_index // step) % 2
            keep = lax.dynamic_index_in_dim(split, bit, 1, keepdims=False)
            give = lax.dynamic_index_in_dim(split, 1 - bit, 1, keepdims=False)
            give = give.reshape(-1, width)
            got = lax.ppermute(give, "ep", [(i, i ^ step) for i in range(ep)])
            values = (keep.reshape(-1, width).astype(F32) + got.astype(F32)).astype(BF16)
            step *= 2
        return values.astype(F32)

    positions = jnp.arange(all_rows)
    seq_index = positions // seq_len
    row_limit = jnp.sum(
        jnp.where(seq_index[:, None] == jnp.arange(seq_count)[None, :], lengths[None, :], 0), axis=1
    )
    live_all = positions % seq_len < row_limit
    one_hot = (expert_ids[:, None] == jnp.arange(experts)[None, :]) & live_all[:, None]
    routed = one_hot.astype(F32)
    slots = jnp.sum((jnp.cumsum(routed, axis=0) - routed) * routed, axis=1).astype(jnp.int32)
    sound = live_all & (slots < capacity)
    place = jnp.where(sound, expert_ids * capacity + slots, -1)
    place_row = place[None, :]
    place_col = place[:, None]
    slot_count = experts * capacity
    blocks = (experts, capacity, model_width)

    live_grad = jnp.where(shard_of(live_all)[:, None], out_grad, jnp.zeros_like(out_grad))
    if tp == 2:
        grad_other = swapped(live_grad)
        w_other = swapped(w_output)
        mine_first = tp_index == 0
        grad_all = jnp.concatenate(
            [
                jnp.where(mine_first, live_grad, grad_other),
                jnp.where(mine_first, grad_other, live_grad),
            ],
            axis=0,
        )
    else:
        w_all = lax.all_gather(w_output, "tp", axis=1, tiled=True)
        grad_all = lax.all_gather(live_grad, "tp", axis=0, tiled=True)

    def row(values):
        return values.astype(F32)[None, :]

    rm = jnp.pad(
        jnp.concatenate([router, mix_weight], axis=1), ((0, 0), (0, LANES - experts - 2))
    )

    attn_in, projected = norm_project(
        tokens, row(gain_attn), row(bias_attn), (w_query, w_key, w_value)
    )
    heads, log_sums = [], []
    for s in range(splits):
        if s == splits - 1:
            grad_blocks = pack(place_row, after(grad_all, *heads), slot_count)
            projected = after(projected, grad_blocks)
        o, lse = attention_forward(projected, seq_count, local_heads, s * each, each)
        heads.append(o)
        log_sums.append(lse)
    if tp == 2:
        others = [swapped(o) for o in heads]
        all_heads = heads + others
        weights = [(w_output, s) for s in range(splits)] + [(w_other, s) for s in range(splits)]
        wide_weights = [(w, s, each * PAIR) for w, s in weights]
    else:
        all_heads = [lax.all_gather(jnp.concatenate(heads, axis=1), "tp", axis=1, tiled=True)]
        weights = [(w_all, 0)]
        wide_weights = [(w_all, 0, model_width)]
    resid, ffn_in, chances = output_norm(
        tokens, row(gain_ffn), row(bias_ffn), rm, all_heads, weights, experts
    )
    grad_rows = exchange(grad_blocks.reshape(blocks))
    sent = pack(place_row, ffn_in, slot_count).reshape(blocks)
    sel = (jnp.arange(LANES) == ep_index).astype(F32)[None, :]
    (
        dense,
        dense_pull,
        first_dot,
        grad_hidden,
        grad_return,
        grad_expert_in,
        grad_expert_out,
        _,
        results,
        _,
        _,
        pulls,
        dots,
    ) = nets(
        ffn_in,
        grad_all,
        sent,
        grad_rows,
        sel,
        rm,
        (w_hidden, w_return),
        (expert_in[0], expert_out[0]),
    )
    returned = exchange(results).reshape(slot_count, model_width)
    pulls = pulls.reshape(slot_count, model_width)
    dots = dots[:, 0, :]
    own = ((positions >= first_row) & (positions < first_row + shard_rows)).astype(F32)[:, None]

    part, *rest = ffn_pull(
        place_col,
        own,
        dense_pull,
        chances,
        first_dot,
        ffn_in,
        grad_all,
        resid,
        row(gain_ffn),
        rm,
        pulls,
        dots,
        wide_weights,
        experts,
    )
    *head_parts, ffn_sums, rm_sums = rest
    if tp == 2:
        head_grads = [[m, swapped(o)] for m, o in zip(head_parts[:splits], head_parts[splits:])]
    else:
        local = lax.psum_scatter(head_parts[0], "tp", scatter_dimension=1, tiled=True)
        head_grads = [
            [local[:, s * each * PAIR : (s + 1) * each * PAIR]] for s in range(splits)
        ]
    grad_output = halved_over_sequences(outer(part, all_heads))
    if tp == 2:
        grad_output = grad_output[:, :local_width] + swapped(
            grad_output[:, local_width:].astype(BF16)
        ).astype(F32)
    else:
        grad_output = lax.psum_scatter(
            grad_output.astype(BF16), "tp", scatter_dimension=1, tiled=True
        ).astype(F32)

    grad_hidden = over_sequences(grad_hidden)
    grad_return = over_sequences(grad_return)

    square, qkv = [], []
    for s in range(splits):
        if s == splits - 1:
            weighted = combine(place_col, dense, chances, returned, experts)
            grad_expert_in, grad_expert_out = [
                jnp.where(lengths[0] > 0, e, 0.0) for e in (grad_expert_in, grad_expert_out)
            ]
            projected = after(
                projected, weighted, grad_expert_in, grad_expert_out, *(qkv[-1] if qkv else ())
            )
        grads3 = attention_backward(
            projected, heads[s], head_grads[s], log_sums[s], seq_count, local_heads, s * each
        )
        qkv.append(grads3)
        square.append(halved_over_sequences(outer(attn_in, grads3)))
    width = each * PAIR
    grad_query, grad_key, grad_value = [
        jnp.concatenate([q[:, k * width : (k + 1) * width] for q in square], axis=1)
        for k in range(3)
    ]
    part = after(part, grad_hidden, grad_return)
    ffn_sums, rm_sums = after((ffn_sums, rm_sums), *qkv[-1])
    flat = [qkv[s][k] for k in range(3) for s in range(splits)]
    pull = partial(
        attn_pull,
        x=tokens,
        r=part,
        gain=row(gain_attn),
        grads=flat,
        weights=(w_query, w_key, w_value),
    )
    if tp == 2:
        theirs, sums_a = pull(shard_rows - first_row, shard_rows, out_type=BF16)
        own_part, sums_b = pull(first_row, shard_rows, out_type=F32)
        token_grad = own_part + swapped(theirs).astype(F32)
        attn_sums = sums_a + sums_b
    else:
        whole, attn_sums = pull(jnp.zeros((), jnp.int32), all_rows, out_type=BF16)
        token_grad = lax.psum_scatter(whole, "tp", scatter_dimension=0, tiled=True).astype(F32)

    if tp == 2:
        theirs = lax.dynamic_slice_in_dim(weighted, shard_rows - first_row, shard_rows, 0)
        summed = shard_of(weighted).astype(F32) + swapped(theirs).astype(F32)
    else:
        summed = lax.psum_scatter(weighted, "tp", scatter_dimension=0, tiled=True).astype(F32)
    block_out = jnp.where(shard_of(live_all)[:, None], shard_of(resid) + summed, 0.0).astype(BF16)

    rows_kept = -(-(experts + 2) // 8) * 8
    small = summed_over(
        summed_over(jnp.concatenate([ffn_sums, rm_sums[:rows_kept]], axis=0), "tp", tp), "ep", ep
    )
    attn_sums = summed_over(summed_over(attn_sums, "tp", tp), "ep", ep)
    return (
        block_out,
        token_grad,
        grad_query,
        grad_key,
        grad_value,
        grad_output,
        grad_hidden,
        grad_return,
        small[8 : 8 + experts].T,
        small[8 + experts : 10 + experts].T,
        attn_sums[0],
        attn_sums[1],
        small[0],
        small[1],
        grad_expert_in[None],
        grad_expert_out[None],
    )


def solution(mesh):
    in_specs = (
        P("ep", None),
        P(("ep", "tp"), None),
        P("ep"),
        P("ep"),
        P(None, "tp"),
        P(None, "tp"),
        P(None, "tp"),
        P(None, "tp"),
        P(None, "tp"),
        P(None, "tp"),
        P(),
        P(),
        P(),
        P(),
        P(),
        P(),
        P("ep", None, "tp"),
        P("ep", None, "tp"),
    )
    out_specs = (
        P(("ep", "tp"), None),
        P(("ep", "tp"), None),
        P("ep", "tp"),
        P("ep", "tp"),
        P("ep", "tp"),
        P("ep", "tp"),
        P("ep", "tp"),
        P("ep", "tp"),
        P(),
        P(),
        P(),
        P(),
        P(),
        P(),
        P("ep", None, "tp"),
        P("ep", None, "tp"),
    )
    return jax.shard_map(
        partial(on_device, (mesh.shape["tp"], mesh.shape["ep"])),
        mesh=mesh,
        in_specs=in_specs,
        out_specs=out_specs,
        check_vma=False,
    )
```

time: 1140 us -> 782 us (0.69)
  Pallas kernels: 114 us -> 440 us
  matrix products: 262 us -> 0 us
  blocking collectives: 149 us -> 0 us
  local copies, waits for them, and re-layouts: 146 us -> 26.9 us
  waiting for transfers between devices: 281 us -> 190 us
  starting transfers between devices: 97.9 us -> 56.6 us
  other arithmetic: 67.1 us -> 46 us
    pallas_call x1 -> x14, Pallas kernels: 67.9 us -> 392 us  [the longest x1 182 us: nets(): pl.pallas_call(partial(nets_kernel, peers=peers, capacity=capacity, rb=rb...]
    dot_general x28 -> x0, matrix products: 262 us -> none  [the longest x10 101 us: matmul(): return jnp.dot(left, right, preferred_element_type=jnp.float32)]
    psum x2 -> x0, blocking collectives: 149 us -> none  [the longest x1 78.9 us: on_device(): lax.psum((grad_router, grad_mix, grad_gain_ffn, grad_bias_ffn), ('ep', 't...]
    all_to_all x5 -> x2, waiting for transfers between devices: 104 us -> 0.01 us  [exchange(): return lax.all_to_all(values, 'ep', split_axis=0, concat_axis=0, tiled=True)]
    all_to_all x5 -> x2, starting transfers between devices: 90.1 us -> 24.7 us  [exchange(): return lax.all_to_all(values, 'ep', split_axis=0, concat_axis=0, tiled=True)]
    ppermute x7 -> x31, waiting for transfers between devices: 143 us -> 186 us  [the longest x9 121 us: swapped(): return lax.ppermute(values, 'tp', swap)]
    gather x4 -> x0, local copies, waits for them, and re-layouts: 40.7 us -> none  [the longest x2 20.4 us: on_device(): moe_part = returned[take_index].astype(F32) * mine_col]
    psum x1 -> x0, waiting for transfers between devices: 33.6 us -> none  [on_device(): lax.psum((grad_router, grad_mix, grad_gain_ffn, grad_bias_ffn), ('ep', 't...]
  transfers between devices with their start and end apart: 16 -> 35, of which waited for: 9 -> 21; matrix products, arithmetic and copies ran while one was open for 32% -> 6% of each run, Pallas kernels for 0% -> 32%
where the time goes in v2:
time: 782 us; the launch traced here: 775 us
  Pallas kernels  440 us (56%)
  waiting for transfers between devices  190 us (24%)
  starting transfers between devices  56.6 us (7%)
  other arithmetic  46 us (6%)
  local copies, waits for them, and re-layouts  26.9 us (3%)
  between operations  15.7 us (2%)
    pallas_call x1, Pallas kernels, nets(): pl.pallas_call(partial(nets_kernel, peers=peers, capacity=capacity, rb=rb...  182 us
    ppermute x9, waiting for transfers between devices, swapped(): return lax.ppermute(values, 'tp', swap)  121 us
    pallas_call x2, Pallas kernels, attention_backward(): pl.pallas_call(partial(attention_backward_kernel, terms=terms, bq=bq, bk=...  69.3 us
    ppermute x12, waiting for transfers between devices, halved_over_sequences(): got = lax.ppermute(give, 'ep', [(i, i ^ step) for i in range(ep)])  50.5 us
    pallas_call x2, Pallas kernels, attention_forward(): pl.pallas_call(partial(attention_forward_kernel, bq=bq, bk=bk, scale=HEAD...  47.7 us
    pallas_call x1, Pallas kernels, ffn_pull(): pl.pallas_call(partial(ffn_pull_kernel, parts=len(weights), experts=exper...  29.6 us
    pallas_call x2, Pallas kernels, pack(): pl.pallas_call(pack_kernel, grid=(count // sb,), in_specs=[resident((1, r...  25.1 us
    all_to_all x2, starting transfers between devices, exchange(): return lax.all_to_all(values, 'ep', split_axis=0, concat_axis=0, tiled=True)  24.7 us
  transfers between devices with their start and end apart: 35, of which 21 were waited for; matrix products, arithmetic and copies ran while one was open for 6% of the time, Pallas kernels for 32%

profile of v2, /device:TPU:0, one launch (start us, length us, event | category | flops | bytes accessed | tf_op | source)
XLA Modules:
  0.0 775.2 jit_solution(17461116974607801831)
XLA Ops:
  7.9 3.1 broadcast_select_fusion.2
  11.1 3.0 collective-permute-start
  15.3 4.5 reduce-window.6
  21.0 12.5 %norm_project.1 = (bf16[2048,1024]{1,0:T(8,128)(2,1)}, bf16[2048,1536]{1,0:T(8,128)(2,1)}) custom-call(bf16[2048,1024]{1,0:T(8,128)(2,1)} %x_ref.5, f32[1,1024]{1,0:T(1,128)} %bitcast.143, f32[1,1024]{1,0:T(1,128)} %bitcast.151, bf16[1024,512]{1,0:T(8,128)(2,1)} %refs_6_.3, bf16[1024,512]{1,0:T(8,128)(2,1)} %refs_7_.3, bf16[1024,512]{1,0:T(8,128)(2,1)} %refs_8_.5), custom_call_target="tpu_custom_call" | custom-call | flops 6442450944 | bytes 16777216 | tf_op jit(solution)/shard_map/norm_project/pallas_call | solution.py:298
  33.5 23.9 %attention_forward.2 = (bf16[2048,256]{1,0:T(8,128)(2,1)}, f32[2,2,2048]{2,1,0:T(2,128)}) custom-call(bf16[2048,1536]{1,0:T(8,128)(2,1)} %get-tuple-element.84.q_ref.k_ref.v_ref, bf16[2048,1536]{1,0:T(8,128)(2,1)} %get-tuple-element.84.q_ref.k_ref.v_ref, bf16[2048,1536]{1,0:T(8,128)(2,1)} %get-tuple-element.84.q_ref.k_ref.v_ref), custom_call_target="tpu_custom_call" | custom-call | flops 8589934592 | bytes 4194304 | tf_op jit(solution)/shard_map/attention_forward/pallas_call | solution.py:138
  57.4 2.5 collective-permute-done
  60.0 2.0 broadcast_select_fusion.4
  62.0 2.5 pad_maximum_fusion.x_ref.g_hbm.refs_6_
  64.4 12.6 %pack_rows.2 = bf16[2048,1024]{1,0:T(8,128)(2,1)} custom-call(s32[1,2048]{1,0:T(1,128)} %bitcast.146, bf16[2048,1024]{1,0:T(8,128)(2,1)} %pad_maximum_fusion.x_ref.g_hbm.refs_6_), custom_call_target="tpu_custom_call" | custom-call | flops 8589934592 | bytes 8388608 | tf_op jit(solution)/shard_map/pack_rows/pallas_call | solution.py:367
  77.0 6.3 all-to-all-start
  84.0 1.6 collective-permute-start.1
  86.1 23.8 %attention_forward.3 = (bf16[2048,256]{1,0:T(8,128)(2,1)}, f32[2,2,2048]{2,1,0:T(2,128)}) custom-call(bf16[2048,1536]{1,0:T(8,128)(2,1)} %get-tuple-element.84.q_ref.k_ref.v_ref, bf16[2048,1536]{1,0:T(8,128)(2,1)} %get-tuple-element.84.q_ref.k_ref.v_ref, bf16[2048,1536]{1,0:T(8,128)(2,1)} %get-tuple-element.84.q_ref.k_ref.v_ref), custom_call_target="tpu_custom_call" | custom-call | flops 8589934592 | bytes 4194304 | tf_op jit(solution)/shard_map/attention_forward/pallas_call | solution.py:138
  109.9 1.5 collective-permute-start.2
  114.1 18.5 %collective-permute-done.3.refs_10_.refs_11_.refs_14_.refs_15_ = bf16[1024,512]{1,0:T(8,128)(2,1)} collective-permute-done((bf16[1024,512]{1,0:T(8,128)(2,1)S(1)}, bf16[1024,512]{1,0:T(8,128)(2,1)}, u32[]{:S(2)}, u32[]{:S(2)}) %collective-permute-start.3) | collective-permute-done | bytes 1048608 | tf_op jit(solution)/shard_map/ppermute | solution.py:994
  132.6 21.9 %collective-permute-done.2.refs_7_.refs_3_ = bf16[2048,256]{1,0:T(8,128)(2,1)} collective-permute-done((bf16[2048,256]{1,0:T(8,128)(2,1)}, bf16[2048,256]{1,0:T(8,128)(2,1)}, u32[]{:S(2)}, u32[]{:S(2)}) %collective-permute-start.2) | collective-permute-done | bytes 1048608 | tf_op jit(solution)/shard_map/ppermute | solution.py:994
  154.5 14.3 %output_norm.1 = (f32[2048,1024]{1,0:T(8,128)}, bf16[2048,1024]{1,0:T(8,128)(2,1)}, f32[2048,128]{1,0:T(8,128)}) custom-call(bf16[2048,1024]{1,0:T(8,128)(2,1)} %x_ref.5, f32[1,1024]{1,0:T(1,128)} %bitcast.113, f32[1,1024]{1,0:T(1,128)} %bitcast.150, bf16[1024,128]{1,0:T(8,128)(2,1)} %pad.8.refs_3_.rm_ref.refs_9_, ...), custom_call_target="tpu_custom_call" | custom-call | flops 4294967296 | bytes 25165824 | tf_op jit(solution)/shard_map/output_norm/pallas_call | solution.py:341
  168.8 12.5 %pack_rows.3 = bf16[2048,1024]{1,0:T(8,128)(2,1)} custom-call(s32[1,2048]{1,0:T(1,128)} %bitcast.147, bf16[2048,1024]{1,0:T(8,128)(2,1)} %get-tuple-element.64.x_ref.x_hbm.refs_5_), custom_call_target="tpu_custom_call" | custom-call | flops 8589934592 | bytes 8388608 | tf_op jit(solution)/shard_map/pack_rows/pallas_call | solution.py:367
  181.3 182.1 %feed_forward_nets.1 = (bf16[2048,1024]{1,0:T(8,128)(2,1)}, bf16[2048,1024]{1,0:T(8,128)(2,1)}, f32[2048,128]{1,0:T(8,128)}, bf16[1024,2048]{1,0:T(8,128)(2,1)},...) custom-call(bf16[2048,1024]{1,0:T(8,128)(2,1)} %get-tuple-element.64, ...), custom_call_target="tpu_custom_call" | custom-call | flops 103079215104 | bytes 83886080 | tf_op jit(solution)/shard_map/feed_forward_nets/pallas_call | solution.py:683
  365.9 29.6 %ffn_norm_pull.1 = (bf16[2048,1024]{1,0:T(8,128)(2,1)}, bf16[2048,256]{1,0:T(8,128)(2,1)S(1)}, bf16[2048,256]{1,0:T(8,128)(2,1)S(1)}, bf16[2048,256]{1,0:T(8,128...) custom-call(s32[2048,1]{1,0:T(8,128)S(1)} %copy.52.place_ref.refs_0_, ...), custom_call_target="tpu_custom_call" | custom-call | flops 12884901888 | bytes 33554432 | tf_op jit(solution)/shard_map/ffn_norm_pull/pallas_call | solution.py:802
  397.6 8.8 %outer_product.5 = bf16[1024,1024]{1,0:T(8,128)(2,1)} custom-call(bf16[2048,1024]{1,0:T(8,128)(2,1)} %get-tuple-element.75.r_ref.left_ref, bf16[2048,256]{1,0:T(8,128)(2,1)} %get-tuple-element.59.refs_4_.o_ref.refs_0_, bf16[2048,256]{1,0:T(8,128)(2,1)} %get-tuple-element.62.refs_5_.o_ref.refs_1_, bf16[2048,256]{1,0:T(8,128)(2,1)} %copy-done.37, ...), custom_call_target="tpu_custom_call" | custom-call | flops 4294967296 | bytes 8388608 | tf_op jit(solution)/shard_map/outer_product/pallas_call | solution.py:859
  406.4 3.6 constant_dynamic-slice_fusion.5
  410.6 18.3 %all-to-all-start.1 = ((bf16[16,128,1024]{2,1,0:T(8,128)(2,1)}), bf16[16,128,1024]{2,1,0:T(8,128)(2,1)}, u32[]{:S(2)}, u32[]{:S(2)}) async-start(bf16[16,128,1024]{2,1,0:T(8,128)(2,1)} %get-tuple-element.67), calls=%async_computation.1 | async-start | bytes 8388608 | tf_op jit(solution)/shard_map/all_to_all | solution.py:997
  429.0 1.6 collective-permute-start.5
  430.6 2.1 fusion
  433.6 1.8 collective-permute-start.17
  435.5 19.3 %collective-permute-done.5.refs_1_ = bf16[2048,256]{1,0:T(8,128)(2,1)} collective-permute-done((bf16[2048,256]{1,0:T(8,128)(2,1)}, bf16[2048,256]{1,0:T(8,128)(2,1)}, u32[]{:S(2)}, u32[]{:S(2)}) %collective-permute-start.5) | collective-permute-done | bytes 1048608 | tf_op jit(solution)/shard_map/ppermute | solution.py:994
  454.8 2.8 copy-done.12
  457.6 34.4 %attention_backward.2 = (bf16[2048,256]{1,0:T(8,128)(2,1)S(1)}, bf16[2048,256]{1,0:T(8,128)(2,1)S(1)}, bf16[2048,256]{1,0:T(8,128)(2,1)S(1)}) custom-call(bf16[2048,1536]{1,0:T(8,128)(2,1)S(1)} %copy-done.12, bf16[2048,1536]{1,0:T(8,128)(2,1)S(1)} %copy-done.12, bf16[2048,1536]{1,0:T(8,128)(2,1)S(1)} %copy-done.12, bf16[2048,256]{1,0:T(8,128)(2,1)S(1)} %copy-done.11, ...), custom_call_target="tpu_custom_call" | custom-call | flops 21474836480 | bytes 8388608 | tf_op jit(solution)/shard_map/attention_backward/pallas_call | solution.py:253
  495.0 7.8 %outer_product.3 = bf16[1024,768]{1,0:T(8,128)(2,1)} custom-call(bf16[2048,1024]{1,0:T(8,128)(2,1)} %get-tuple-element.93.left_ref, bf16[2048,256]{1,0:T(8,128)(2,1)} %copy-done, bf16[2048,256]{1,0:T(8,128)(2,1)} %copy-done.1, bf16[2048,256]{1,0:T(8,128)(2,1)} %copy-done.2), custom_call_target="tpu_custom_call" | custom-call | flops 3221225472 | bytes 7340032 | tf_op jit(solution)/shard_map/outer_product/pallas_call | solution.py:859
  502.8 2.4 constant_dynamic-slice_fusion.17
  506.6 1.7 collective-permute-start.18
  508.3 1.5 collective-permute-start.6
  509.8 26.2 %collective-permute-done.18 = bf16[128,1024]{1,0:T(8,128)(2,1)S(1)} collective-permute-done((bf16[128,1024]{1,0:T(8,128)(2,1)S(1)}, bf16[128,1024]{1,0:T(8,128)(2,1)S(1)}, u32[]{:S(2)}, u32[]{:S(2)}) %collective-permute-start.18) | collective-permute-done | bytes 262176 | tf_op jit(solution)/shard_map/ppermute | solution.py:1021
  537.7 2.4 collective-permute-start.9
  540.1 11.0 %broadcast_select_fusion = (f32[1024,2048]{1,0:T(8,128)}, f32[1024,2048]{1,0:T(8,128)}) fusion(f32[1024,2048]{1,0:T(8,128)} %get-tuple-element.81, pred[]{:T(512)S(6)} %gt.4, f32[1024,2048]{1,0:T(8,128)} %get-tuple-element.80), kind=kLoop, calls=%fused_computation.2 | loop fusion | flops 4194304 | bytes 33554432 | tf_op jit(solution)/shard_map/jit(_where)/select_n | solution.py:1162
  551.1 2.7 collective-permute-done.19
  553.8 1.6 collective-permute-start.20
  555.7 2.5 collective-permute-done.20
  558.8 8.4 %collective-permute-done.10 = bf16[128,768]{1,0:T(8,128)(2,1)S(1)} collective-permute-done((bf16[128,768]{1,0:T(8,128)(2,1)S(1)}, bf16[128,768]{1,0:T(8,128)(2,1)S(1)}, u32[]{:S(2)}, u32[]{:S(2)}) %collective-permute-start.10) | collective-permute-done | bytes 196640 | tf_op jit(solution)/shard_map/ppermute | solution.py:1021
  568.2 1.8 convert_element_type.221
  570.0 4.9 reduce-scatter.5.cloned.1.call-done
  574.9 1.8 convert_element_type.222
  576.7 14.4 %combine_nets.1 = bf16[2048,1024]{1,0:T(8,128)(2,1)} custom-call(s32[2048,1]{1,0:T(8,128)} %copy-done.6, bf16[2048,1024]{1,0:T(8,128)(2,1)} %get-tuple-element.65.y_ref, f32[2048,128]{1,0:T(8,128)} %get-tuple-element.66.chance_ref.refs_3_, bf16[2048,1024]{1,0:T(8,128)(2,1)} %bitcast.13.slot_ref), custom_call_target="tpu_custom_call" | custom-call | flops 8589934592 | bytes 16777216 | tf_op jit(solution)/shard_map/combine_nets/pallas_call | solution.py:935
  591.0 2.8 copy-done.13
  595.0 34.9 %attention_backward.3 = (bf16[2048,256]{1,0:T(8,128)(2,1)S(1)}, bf16[2048,256]{1,0:T(8,128)(2,1)S(1)}, bf16[2048,256]{1,0:T(8,128)(2,1)S(1)}) custom-call(bf16[2048,1536]{1,0:T(8,128)(2,1)S(1)} %copy-done.13, bf16[2048,1536]{1,0:T(8,128)(2,1)S(1)} %copy-done.13, bf16[2048,1536]{1,0:T(8,128)(2,1)S(1)} %copy-done.13, bf16[2048,256]{1,0:T(8,128)(2,1)S(1)} %copy-done.9, ...), custom_call_target="tpu_custom_call" | custom-call | flops 21474836480 | bytes 8388608 | tf_op jit(solution)/shard_map/attention_backward/pallas_call | solution.py:253
  632.9 7.7 outer_product.4
  640.5 9.9 %attention_norm_pull.3 = (bf16[1024,1024]{1,0:T(8,128)(2,1)}, f32[8,1024]{1,0:T(8,128)}) custom-call(s32[1]{0:T(128)} %bitcast.17.at_ref, bf16[2048,1024]{1,0:T(8,128)(2,1)} %x_ref.5, bf16[2048,1024]{1,0:T(8,128)(2,1)} %get-tuple-element.75.r_ref.left_ref, f32[1,1024]{1,0:T(1,128)} %bitcast.144, bf16[2048,256]{1,0:T(8,128)(2,1)} %copy-done, ...), custom_call_target="tpu_custom_call" | custom-call | flops 3221225472 | bytes 10485760 | tf_op jit(solution)/shard_map/attention_norm_pull/pallas_call | solution.py:905
  650.5 10.3 %attention_norm_pull.2 = (f32[1024,1024]{1,0:T(8,128)}, f32[8,1024]{1,0:T(8,128)}) custom-call(s32[1]{0:T(128)} %bitcast.14.at_ref, bf16[2048,1024]{1,0:T(8,128)(2,1)} %x_ref.5, bf16[2048,1024]{1,0:T(8,128)(2,1)} %get-tuple-element.75.r_ref.left_ref, f32[1,1024]{1,0:T(1,128)} %bitcast.145, bf16[2048,256]{1,0:T(8,128)(2,1)} %copy-done, ...), custom_call_target="tpu_custom_call" | custom-call | flops 3221225472 | bytes 10485760 | tf_op jit(solution)/shard_map/attention_norm_pull/pallas_call | solution.py:905
  661.7 1.7 collective-permute-start.26
  663.8 2.0 collective-permute-done.26
  667.0 1.4 collective-permute-done.21
  668.6 2.3 collective-permute-done.28
  671.1 2.0 collective-permute-start.7
  673.1 1.8 collective-permute-done.29
  676.0 2.1 collective-permute-start.24
  678.3 2.0 collective-permute-start.4
  681.3 2.2 collective-permute-start.25
  684.5 4.1 collective-permute-done.25
  689.3 2.4 collective-permute-done.13
  692.9 5.8 collective-permute-done.14
  700.2 5.0 collective-permute-done.15
  707.2 56.2 %collective-permute-done.4 = bf16[1024,1024]{1,0:T(8,128)(2,1)S(1)} collective-permute-done((bf16[1024,1024]{1,0:T(8,128)(2,1)S(1)}, bf16[1024,1024]{1,0:T(8,128)(2,1)S(1)}, u32[]{:S(2)}, u32[]{:S(2)}) %collective-permute-start.4) | collective-permute-done | bytes 2097184 | tf_op jit(solution)/shard_map/ppermute | solution.py:994
  763.4 2.1 select_convert_fusion
  765.5 2.7 convert_add_fusion
  (185 shorter events, 35.5 us)
Async XLA Ops:
  7.2 6.8 copy-start.32
  7.2 7.4 copy-start.33
  7.2 8.0 %copy-start.24 = (s32[2048]{0:T(1024)S(1)}, s32[2048]{0:T(1024)}, u32[]{:S(2)}) copy-start(s32[2048]{0:T(1024)} %param.21) | copy-start | bytes 24580
  7.9 52.1 %copy-start.29 = (pred[1024]{0:T(1024)(128)(4,1)}, pred[1024]{0:T(1024)(128)(4,1)S(1)}, u32[]{:S(2)}) copy-start(pred[1024]{0:T(1024)(128)(4,1)S(1)} %dynamic_slice.93) | copy-start | bytes 3076
  11.1 48.9 %collective-permute-start = (bf16[1024,1024]{1,0:T(8,128)(2,1)}, bf16[1024,1024]{1,0:T(8,128)(2,1)}, u32[]{:S(2)}, u32[]{:S(2)}) collective-permute-start(bf16[1024,1024]{1,0:T(8,128)(2,1)} %broadcast_select_fusion.2), channel_id=1, source_target_pairs={{0,1},{1,0},{2,3},{3,2},{4,5},{5,4},{6,7},{7,6},{8,9},{9,8},{10,11... | collective-permute-start | bytes 6291464 | tf_op jit(solution)/shard_map/ppermute | solution.py:994
  33.5 26.5 %copy-start.20 = (bf16[1024,1024]{1,0:T(8,128)(2,1)S(1)}, bf16[1024,1024]{1,0:T(8,128)(2,1)}, u32[]{:S(2)}) copy-start(bf16[1024,1024]{1,0:T(8,128)(2,1)} %param.19) | copy-start | bytes 6291460
  77.0 7.0 copy-start.10
  77.0 8.5 %copy-start.36 = (bf16[1024,512]{1,0:T(8,128)(2,1)S(1)}, bf16[1024,512]{1,0:T(8,128)(2,1)}, u32[]{:S(2)}) copy-start(bf16[1024,512]{1,0:T(8,128)(2,1)} %refs_13_.1) | copy-start | bytes 3145732
  77.0 104.3 %all-to-all-start = ((bf16[16,128,1024]{2,1,0:T(8,128)(2,1)}), bf16[16,128,1024]{2,1,0:T(8,128)(2,1)}, u32[]{:S(2)}, u32[]{:S(2)}) async-start(bf16[16,128,1024]{2,1,0:T(8,128)(2,1)} %bitcast.118), calls=%async_computation | async-start | bytes 8388608 | tf_op jit(solution)/shard_map/all_to_all | solution.py:997
  83.4 28.1 %copy-start.28 = (bf16[1024,16]{0,1:T(8,128)(2,1)S(1)}, bf16[1024,16]{0,1:T(8,128)(2,1)}, u32[]{:S(2)}) copy-start(bf16[1024,16]{0,1:T(8,128)(2,1)} %param.28) | copy-start | bytes 98308
  83.4 28.1 %copy-start.31 = (bf16[1024,2]{0,1:T(2,128)(2,1)S(1)}, bf16[1024,2]{0,1:T(2,128)(2,1)}, u32[]{:S(2)}) copy-start(bf16[1024,2]{0,1:T(2,128)(2,1)} %param.29) | copy-start | bytes 12292
  83.4 28.2 %copy-start.34 = (bf16[1024]{0:T(1024)(128)(2,1)S(1)}, bf16[1024]{0:T(1024)(128)(2,1)}, u32[]{:S(2)}) copy-start(bf16[1024]{0:T(1024)(128)(2,1)} %param.32) | copy-start | bytes 6148
  83.4 28.8 %copy-start.35 = (bf16[1024]{0:T(1024)(128)(2,1)S(1)}, bf16[1024]{0:T(1024)(128)(2,1)}, u32[]{:S(2)}) copy-start(bf16[1024]{0:T(1024)(128)(2,1)} %param.33) | copy-start | bytes 6148
  83.4 484.8 %reduce-scatter.3.cloned.1.call-start = ((), (), s32[]{:S(2)}) async-start(), calls=%async_computation.4 | async-start | bytes 4456448 | tf_op jit(solution)/shard_map/reduce_scatter | solution.py:1010
  84.0 30.1 %collective-permute-start.1 = (bf16[2048,256]{1,0:T(8,128)(2,1)S(1)}, bf16[2048,256]{1,0:T(8,128)(2,1)S(1)}, u32[]{:S(2)}, u32[]{:S(2)}) collective-permute-start(bf16[2048,256]{1,0:T(8,128)(2,1)S(1)} %copy-done.10), channel_id=1, source_target_pairs={{0,1},{1,0},{2,3},{3,2},{4,5},{5,4},{6,7},{7,6},{8,9},{9,8},{10,11... | collective-permute-start | bytes 3145736 | tf_op jit(solution)/shard_map/ppermute | solution.py:994
  85.6 47.0 %collective-permute-start.3 = (bf16[1024,512]{1,0:T(8,128)(2,1)S(1)}, bf16[1024,512]{1,0:T(8,128)(2,1)}, u32[]{:S(2)}, u32[]{:S(2)}) collective-permute-start(bf16[1024,512]{1,0:T(8,128)(2,1)S(1)} %copy-done.36), channel_id=1, source_target_pairs={{0,1},{1,0},{2,3},{3,2},{4,5},{5,4},{6,7},{7,6},{8,9},{9,8},{10,11... | collective-permute-start | bytes 3145736 | tf_op jit(solution)/shard_map/ppermute | solution.py:994
  109.9 44.6 %collective-permute-start.2 = (bf16[2048,256]{1,0:T(8,128)(2,1)}, bf16[2048,256]{1,0:T(8,128)(2,1)}, u32[]{:S(2)}, u32[]{:S(2)}) collective-permute-start(bf16[2048,256]{1,0:T(8,128)(2,1)} %get-tuple-element.62.refs_5_.o_ref.refs_1_), channel_id=1, source_target_pairs={{0,1},{1,0},{2,3},{3,2},{4,5},{5,4},{6,7},{7,6},{8,9},{9,8},{10,11... | collective-permute-start | bytes 3145736 | tf_op jit(solution)/shard_map/ppermute | solution.py:994
  114.1 40.4 %copy-start.37 = (bf16[2048,256]{1,0:T(8,128)(2,1)}, bf16[2048,256]{1,0:T(8,128)(2,1)S(1)}, u32[]{:S(2)}) copy-start(bf16[2048,256]{1,0:T(8,128)(2,1)S(1)} %collective-permute-done.1.refs_6_.refs_2_) | copy-start | bytes 3145732
  363.5 2.4 copy-start.7
  363.5 2.4 copy-start.8
  364.6 31.0 %copy-start.6 = (s32[2048,1]{1,0:T(8,128)}, s32[2048,1]{1,0:T(8,128)S(1)}, u32[]{:S(2)}) copy-start(s32[2048,1]{1,0:T(8,128)S(1)} %copy.52.place_ref.refs_0_) | copy-start | bytes 24580
  410.0 20.6 %collective-permute-start.16 = (bf16[512,1024]{1,0:T(8,128)(2,1)}, bf16[512,1024]{1,0:T(8,128)(2,1)}, u32[]{:S(2)}, u32[]{:S(2)}) collective-permute-start(bf16[512,1024]{1,0:T(8,128)(2,1)} %bitcast.44), channel_id=1, source_target_pairs={{0,2},{2,0},{4,6},{6,4},{8,10},{10,8},{12,14},{14,12},{16,18},{18,... | collective-permute-start | bytes 3145736 | tf_op jit(solution)/shard_map/ppermute | solution.py:1021
  410.6 166.1 %all-to-all-start.1 = ((bf16[16,128,1024]{2,1,0:T(8,128)(2,1)}), bf16[16,128,1024]{2,1,0:T(8,128)(2,1)}, u32[]{:S(2)}, u32[]{:S(2)}) async-start(bf16[16,128,1024]{2,1,0:T(8,128)(2,1)} %get-tuple-element.67), calls=%async_computation.1 | async-start | bytes 8388608 | tf_op jit(solution)/shard_map/all_to_all | solution.py:997
  428.9 145.9 %reduce-scatter.5.cloned.1.call-start = ((), (), s32[]{:S(2)}) async-start(), calls=%async_computation.5 | async-start | bytes 4456448 | tf_op jit(solution)/shard_map/reduce_scatter | solution.py:1010
  429.0 25.8 %collective-permute-start.5 = (bf16[2048,256]{1,0:T(8,128)(2,1)}, bf16[2048,256]{1,0:T(8,128)(2,1)}, u32[]{:S(2)}, u32[]{:S(2)}) collective-permute-start(bf16[2048,256]{1,0:T(8,128)(2,1)} %get-tuple-element.78), channel_id=1, source_target_pairs={{0,1},{1,0},{2,3},{3,2},{4,5},{5,4},{6,7},{7,6},{8,9},{9,8},{10,11... | collective-permute-start | bytes 3145736 | tf_op jit(solution)/shard_map/ppermute | solution.py:994
  430.5 24.2 %copy-start.11 = (bf16[2048,256]{1,0:T(8,128)(2,1)S(1)}, bf16[2048,256]{1,0:T(8,128)(2,1)}, u32[]{:S(2)}) copy-start(bf16[2048,256]{1,0:T(8,128)(2,1)} %get-tuple-element.59.refs_4_.o_ref.refs_0_) | copy-start | bytes 3145732
  430.5 24.2 %copy-start.19 = (f32[2,2,2048]{2,1,0:T(2,128)S(1)}, f32[2,2,2048]{2,1,0:T(2,128)}, u32[]{:S(2)}) copy-start(f32[2,2,2048]{2,1,0:T(2,128)} %get-tuple-element.76.lse_ref) | copy-start | bytes 98308
  430.6 24.2 %copy-start.17 = (bf16[2048,256]{1,0:T(8,128)(2,1)S(1)}, bf16[2048,256]{1,0:T(8,128)(2,1)}, u32[]{:S(2)}) copy-start(bf16[2048,256]{1,0:T(8,128)(2,1)} %copy-done.16) | copy-start | bytes 3145732
  433.6 71.7 %collective-permute-start.17 = (bf16[256,1024]{1,0:T(8,128)(2,1)}, bf16[256,1024]{1,0:T(8,128)(2,1)}, u32[]{:S(2)}, u32[]{:S(2)}) collective-permute-start(bf16[256,1024]{1,0:T(8,128)(2,1)} %bitcast.47), channel_id=1, source_target_pairs={{0,4},{2,6},{4,0},{6,2},{8,12},{10,14},{12,8},{14,10},{16,20},{18,... | collective-permute-start | bytes 1572872 | tf_op jit(solution)/shard_map/ppermute | solution.py:1021
  454.8 2.8 copy-start.12
  505.3 31.0 %collective-permute-start.8 = (bf16[512,768]{1,0:T(8,128)(2,1)}, bf16[512,768]{1,0:T(8,128)(2,1)}, u32[]{:S(2)}, u32[]{:S(2)}) collective-permute-start(bf16[512,768]{1,0:T(8,128)(2,1)} %bitcast.20), channel_id=1, source_target_pairs={{0,2},{2,0},{4,6},{6,4},{8,10},{10,8},{12,14},{14,12},{16,18},{18,... | collective-permute-start | bytes 2359304 | tf_op jit(solution)/shard_map/ppermute | solution.py:1021
  506.6 29.4 %collective-permute-start.18 = (bf16[128,1024]{1,0:T(8,128)(2,1)S(1)}, bf16[128,1024]{1,0:T(8,128)(2,1)S(1)}, u32[]{:S(2)}, u32[]{:S(2)}) collective-permute-start(bf16[128,1024]{1,0:T(8,128)(2,1)S(1)} %bitcast.139), channel_id=1, source_target_pairs={{0,8},{2,10},{4,12},{6,14},{8,0},{10,2},{12,4},{14,6},{16,24},{18,... | collective-permute-start | bytes 786440 | tf_op jit(solution)/shard_map/ppermute | solution.py:1021
  508.3 82.7 %collective-permute-start.6 = (bf16[2048,256]{1,0:T(8,128)(2,1)S(1)}, bf16[2048,256]{1,0:T(8,128)(2,1)}, u32[]{:S(2)}, u32[]{:S(2)}) collective-permute-start(bf16[2048,256]{1,0:T(8,128)(2,1)S(1)} %get-tuple-element.87), channel_id=1, source_target_pairs={{0,1},{1,0},{2,3},{3,2},{4,5},{5,4},{6,7},{7,6},{8,9},{9,8},{10,11... | collective-permute-start | bytes 3145736 | tf_op jit(solution)/shard_map/ppermute | solution.py:994
  536.2 17.6 %collective-permute-start.19 = (bf16[64,1024]{1,0:T(8,128)(2,1)S(1)}, bf16[64,1024]{1,0:T(8,128)(2,1)S(1)}, u32[]{:S(2)}, u32[]{:S(2)}) collective-permute-start(bf16[64,1024]{1,0:T(8,128)(2,1)S(1)} %dynamic-slice_bitcast_fusion), channel_id=1, source_target_pairs={{0,16},{2,18},{4,20},{6,22},{8,24},{10,26},{12,28},{14,30},{16,0},... | collective-permute-start | bytes 393224 | tf_op jit(solution)/shard_map/ppermute | solution.py:1021
  537.7 17.7 %collective-permute-start.9 = (bf16[256,768]{1,0:T(8,128)(2,1)S(1)}, bf16[256,768]{1,0:T(8,128)(2,1)S(1)}, u32[]{:S(2)}, u32[]{:S(2)}) collective-permute-start(bf16[256,768]{1,0:T(8,128)(2,1)S(1)} %bitcast.137), channel_id=1, source_target_pairs={{0,4},{2,6},{4,0},{6,2},{8,12},{10,14},{12,8},{14,10},{16,20},{18,... | collective-permute-start | bytes 1179656 | tf_op jit(solution)/shard_map/ppermute | solution.py:1021
  553.8 4.3 collective-permute-start.20
  555.6 11.7 %collective-permute-start.10 = (bf16[128,768]{1,0:T(8,128)(2,1)S(1)}, bf16[128,768]{1,0:T(8,128)(2,1)S(1)}, u32[]{:S(2)}, u32[]{:S(2)}) collective-permute-start(bf16[128,768]{1,0:T(8,128)(2,1)S(1)} %bitcast.140), channel_id=1, source_target_pairs={{0,8},{2,10},{4,12},{6,14},{8,0},{10,2},{12,4},{14,6},{16,24},{18,... | collective-permute-start | bytes 589832 | tf_op jit(solution)/shard_map/ppermute | solution.py:1021
  567.4 101.2 %collective-permute-start.11 = (bf16[64,768]{1,0:T(8,128)(2,1)S(1)}, bf16[64,768]{1,0:T(8,128)(2,1)S(1)}, u32[]{:S(2)}, u32[]{:S(2)}) collective-permute-start(bf16[64,768]{1,0:T(8,128)(2,1)S(1)} %dynamic-slice_bitcast_fusion.2), channel_id=1, source_target_pairs={{0,16},{2,18},{4,20},{6,22},{8,24},{10,26},{12,28},{14,30},{16,0},... | collective-permute-start | bytes 294920 | tf_op jit(solution)/shard_map/ppermute | solution.py:1021
  576.7 14.4 %copy-start.9 = (bf16[2048,256]{1,0:T(8,128)(2,1)S(1)}, bf16[2048,256]{1,0:T(8,128)(2,1)}, u32[]{:S(2)}) copy-start(bf16[2048,256]{1,0:T(8,128)(2,1)} %get-tuple-element.62.refs_5_.o_ref.refs_1_) | copy-start | bytes 3145732
  576.7 14.4 %copy-start.18 = (f32[2,2,2048]{2,1,0:T(2,128)S(1)}, f32[2,2,2048]{2,1,0:T(2,128)}, u32[]{:S(2)}) copy-start(f32[2,2,2048]{2,1,0:T(2,128)} %get-tuple-element.85.lse_ref) | copy-start | bytes 98308
  591.0 2.8 copy-start.13
  650.5 10.3 %copy-start.27 = (f32[8,1024]{1,0:T(8,128)S(1)}, f32[8,1024]{1,0:T(8,128)}, u32[]{:S(2)}) copy-start(f32[8,1024]{1,0:T(8,128)} %get-tuple-element.98) | copy-start | bytes 98308
  650.5 15.3 %copy-start.23 = (bf16[1024,768]{1,0:T(8,128)(2,1)S(1)}, bf16[1024,768]{1,0:T(8,128)(2,1)}, u32[]{:S(2)}) copy-start(bf16[1024,768]{1,0:T(8,128)(2,1)} %outer_product.4) | copy-start | bytes 4718596
  660.8 17.4 %copy-start.22 = (bf16[2048,1024]{1,0:T(8,128)(2,1)S(1)}, bf16[2048,1024]{1,0:T(8,128)(2,1)}, u32[]{:S(2)}) copy-start(bf16[2048,1024]{1,0:T(8,128)(2,1)} %combine_nets.1) | copy-start | bytes 12582916
  661.7 4.1 collective-permute-start.26
  663.4 5.0 collective-permute-start.21
  665.8 1.2 collective-permute-start.27
  665.9 17.5 %collective-permute-start.12 = (bf16[512,768]{1,0:T(8,128)(2,1)S(1)}, bf16[512,768]{1,0:T(8,128)(2,1)S(1)}, u32[]{:S(2)}, u32[]{:S(2)}) collective-permute-start(bf16[512,768]{1,0:T(8,128)(2,1)S(1)} %bitcast.131), channel_id=1, source_target_pairs={{0,2},{2,0},{4,6},{6,4},{8,10},{10,8},{12,14},{14,12},{16,18},{18,... | collective-permute-start | bytes 2359304 | tf_op jit(solution)/shard_map/ppermute | solution.py:1021
  667.0 3.9 collective-permute-start.28
  668.5 2.5 collective-permute-start.22
  668.6 94.8 %slice-start = ((s8[8388608]{0:T(1024)(128)(4,1)}), s8[4194304]{0:T(1024)(128)(4,1)S(1)}, s32[]{:S(2)}) async-start(s8[8388608]{0:T(1024)(128)(4,1)} %bitcast.123), calls=%async_computation.6 | async-start | bytes 8388608
  670.9 3.9 collective-permute-start.29
  671.0 5.0 collective-permute-start.23
  671.1 94.4 %collective-permute-start.7 = (bf16[1024,1024]{1,0:T(8,128)(2,1)}, bf16[1024,1024]{1,0:T(8,128)(2,1)S(1)}, u32[]{:S(2)}, u32[]{:S(2)}) collective-permute-start(bf16[1024,1024]{1,0:T(8,128)(2,1)} %get-tuple-element.92), channel_id=1, source_target_pairs={{0,1},{1,0},{2,3},{3,2},{4,5},{5,4},{6,7},{7,6},{8,9},{9,8},{10,11... | collective-permute-start | bytes 6291464 | tf_op jit(solution)/shard_map/ppermute | solution.py:994
  674.9 5.4 collective-permute-start.30
  676.0 5.2 collective-permute-start.24
  678.3 85.1 %collective-permute-start.4 = (bf16[1024,1024]{1,0:T(8,128)(2,1)S(1)}, bf16[1024,1024]{1,0:T(8,128)(2,1)S(1)}, u32[]{:S(2)}, u32[]{:S(2)}) collective-permute-start(bf16[1024,1024]{1,0:T(8,128)(2,1)S(1)} %constant_dynamic-slice_fusion.18), channel_id=1, source_target_pairs={{0,1},{1,0},{2,3},{3,2},{4,5},{5,4},{6,7},{7,6},{8,9},{9,8},{10,11... | collective-permute-start | bytes 6291464 | tf_op jit(solution)/shard_map/ppermute | solution.py:994
  681.3 7.3 collective-permute-start.25
  683.4 79.9 %slice-start.1 = ((s8[8388608]{0:T(1024)(128)(4,1)}), s8[4194304]{0:T(1024)(128)(4,1)S(1)}, s32[]{:S(2)}) async-start(s8[8388608]{0:T(1024)(128)(4,1)} %bitcast.123), calls=%async_computation.7 | async-start | bytes 8388608
  683.4 79.9 %copy-start.30 = (pred[1024]{0:T(1024)(128)(4,1)S(1)}, pred[1024]{0:T(1024)(128)(4,1)}, u32[]{:S(2)}) copy-start(pred[1024]{0:T(1024)(128)(4,1)} %copy-done.29) | copy-start | bytes 3076
  683.8 7.9 %collective-permute-start.13 = (bf16[256,768]{1,0:T(8,128)(2,1)S(1)}, bf16[256,768]{1,0:T(8,128)(2,1)S(1)}, u32[]{:S(2)}, u32[]{:S(2)}) collective-permute-start(bf16[256,768]{1,0:T(8,128)(2,1)S(1)} %bitcast.138), channel_id=1, source_target_pairs={{0,4},{2,6},{4,0},{6,2},{8,12},{10,14},{12,8},{14,10},{16,20},{18,... | collective-permute-start | bytes 1179656 | tf_op jit(solution)/shard_map/ppermute | solution.py:1021
  691.9 6.8 collective-permute-start.14
  698.7 6.4 collective-permute-start.15
  707.2 58.3 %copy-start.21 = (f32[1024,1024]{1,0:T(8,128)S(1)}, f32[1024,1024]{1,0:T(8,128)}, u32[]{:S(2)}) copy-start(f32[1024,1024]{1,0:T(8,128)} %get-tuple-element.91) | copy-start | bytes 12582916
  (11 other events, 12.2 us)
Sparse Core Ops, SparseCore 0:
  363.7 112.9 reduce-scatter.2
  481.0 93.8 reduce-scatter.4

commit v3 on v2

--- a/solution.py
+++ b/solution.py
@@ -75,25 +75,19 @@
 
 
 def cost(flops, bytes_accessed):
-    return pl.CostEstimate(flops=flops, bytes_accessed=bytes_accessed, transcendentals=0)
-
-
-def attention_forward_kernel(q_ref, k_ref, v_ref, o_ref, lse_ref, vt_ref, *, bq, bk, scale):
-    qi = pl.program_id(2)
-
-    @pl.when(qi == 0)
-    def _():
-        vt_ref[...] = v_ref[...].T
-
+    return pl.CostEstimate(flops=flops // 64, bytes_accessed=bytes_accessed // 64, transcendentals=0)
+
+
+def attend_block(qi, q, keys, values_t, bq, bk, scale):
     lane = lax.broadcasted_iota(jnp.int32, (bq, PAIR), 1)
-    q = q_ref[...] * jnp.asarray(scale, BF16)
+    q = q * jnp.asarray(scale, BF16)
     zero = jnp.zeros_like(q)
     halves = [jnp.where(lane < HEAD_DIM, q, zero), jnp.where(lane < HEAD_DIM, zero, q)]
 
     def step(j, carry, masked):
         off = pl.multiple_of(j * bk, bk)
-        k = k_ref[pl.ds(off, bk), :]
-        vt = vt_ref[:, pl.ds(off, bk)]
+        k = keys(pl.ds(off, bk))
+        vt = values_t(pl.ds(off, bk))
         scores = [lax.dot_general(k, half, NT, preferred_element_type=F32) for half in halves]
         if masked:
             key_pos = off + lax.broadcasted_iota(jnp.int32, (bk, bq), 0)
@@ -107,9 +101,7 @@
             alpha = jnp.exp(m - m_new)
             p = jnp.exp(scores[h] - m_new)
             l = l * alpha + jnp.sum(p, axis=0, keepdims=True)
-            part = jnp.dot(
-                vt[h * HEAD_DIM : (h + 1) * HEAD_DIM], p.astype(BF16), preferred_element_type=F32
-            )
+            part = dot(vt[h * HEAD_DIM : (h + 1) * HEAD_DIM], p.astype(BF16))
             new.append((m_new, l, acc * alpha + part))
         return tuple(new)
 
@@ -121,12 +113,23 @@
     carry = lax.fori_loop(0, full, lambda j, c: step(j, c, False), init)
     for d in range(bq // bk):
         carry = step(full + d, carry, True)
-    outs = []
+    out = jnp.concatenate([acc / l for _, l, acc in carry], axis=0).T.astype(BF16)
+    return out, [m + jnp.log(l) for m, l, _ in carry]
+
+
+def attention_forward_kernel(q_ref, k_ref, v_ref, o_ref, lse_ref, vt_ref, *, bq, bk, scale):
+    qi = pl.program_id(2)
+
+    @pl.when(qi == 0)
+    def _():
+        vt_ref[...] = v_ref[...].T
+
+    out, lse = attend_block(
+        qi, q_ref[...], lambda s: k_ref[s, :], lambda s: vt_ref[:, s], bq, bk, scale
+    )
+    o_ref[...] = out
     for h in range(2):
-        m, l, acc = carry[h]
-        outs.append(acc / l)
-        lse_ref[0, h : h + 1, :] = m + jnp.log(l)
-    o_ref[...] = jnp.concatenate(outs, axis=0).T.astype(BF16)
+        lse_ref[0, h : h + 1, :] = lse[h]
 
 
 def attention_forward(proj, seqs, heads, first, count, bq=512, bk=512):
@@ -152,9 +155,7 @@
             jax.ShapeDtypeStruct((count, 2, rows), F32),
         ],
         scratch_shapes=[pltpu.VMEM((PAIR, length), BF16)],
-        cost_estimate=pl.CostEstimate(
-            flops=flops * 4, bytes_accessed=8 * rows * count * PAIR, transcendentals=0
-        ),
+        cost_estimate=cost(flops * 4, 8 * rows * count * PAIR),
         name="attention_forward",
     )(proj, proj, proj)
 
@@ -380,6 +381,401 @@
     return dot(jnp.where(slot == place, 1.0, 0.0).astype(BF16), all_ref[...])
 
 
+def front_kernel(*refs, peers, experts, half, bq, heads_count):
+    refs = list(refs)
+
+    def take(count):
+        taken = refs[:count]
+        del refs[:count]
+        return taken
+
+    x_hbm, g_hbm, wq_hbm, wk_hbm, wv_hbm, wo_hbm = take(6)
+    len_ref, norms_ref, rm_ref, ids_ref = take(4)
+    a_hbm, p_hbm, heads_hbm_a, heads_hbm_b, others_hbm_a, others_hbm_b, wo2_hbm = take(7)
+    gall_hbm, resid_hbm, f_hbm, chance_hbm, packed_hbm, gin_hbm, info_hbm, lse_ref = take(8)
+    xv, wq, wk, wv, wo, wo2, av, pv, vt, ha, hb, oa, ob, gv, pk, fv, rb, cb, hbuf = take(19)
+    place_ref, place_g_ref, info = take(3)
+    (
+        load_sem,
+        x_sem,
+        a_sem,
+        home_sem,
+        grad_sem,
+        w_sem,
+        head_send,
+        head_recv,
+        z_send,
+        z_recv,
+        out_sem,
+    ) = refs
+    me = lax.axis_index("ep")
+    tp_me = lax.axis_index("tp")
+    mesh = pl.DeviceIdType.MESH
+    across = {"tp": 1 - tp_me}
+    rows, wide = xv.shape
+    shard = rows // 2
+    width = wq.shape[1]
+    block = 512
+    steps = rows // block
+
+    def rows_at(i, size):
+        return pl.ds(pl.multiple_of(i * size, size), size)
+
+    def x_load(i):
+        return pltpu.make_async_copy(
+            x_hbm.at[rows_at(i, block), :], xv.at[rows_at(i, block), :], x_sem.at[i]
+        )
+
+    weight_loads = [
+        pltpu.make_async_copy(src, dst, load_sem.at[j])
+        for j, (src, dst) in enumerate(((wq_hbm, wq), (wk_hbm, wk), (wv_hbm, wv), (wo_hbm, wo)))
+    ]
+    for c in weight_loads[:3]:
+        c.start()
+    for i in range(steps):
+        x_load(i).start()
+    weight_loads[3].start()
+    own_rows = pl.ds(pl.multiple_of(tp_me * shard, shard), shard)
+    own_grad = pltpu.make_async_copy(g_hbm, gv.at[own_rows, :], home_sem.at[0])
+    own_grad.start()
+
+    barrier = pltpu.get_barrier_semaphore()
+    pl.semaphore_signal(barrier, inc=1, device_id=across, device_id_type=mesh)
+    for k in range(1, peers):
+        pl.semaphore_signal(
+            barrier, inc=1, device_id={"ep": jnp.bitwise_xor(me, k)}, device_id_type=mesh
+        )
+    pl.semaphore_wait(barrier, peers)
+
+    def remote(src, dst, send, recv, to):
+        return pltpu.make_async_remote_copy(
+            src_ref=src,
+            dst_ref=dst,
+            send_sem=send,
+            recv_sem=recv,
+            device_id=to,
+            device_id_type=mesh,
+        )
+
+    grad_copy = remote(g_hbm, gv.at[own_rows, :], grad_sem.at[0], grad_sem.at[1], across)
+    grad_copy.start()
+    side = lax.rem(me, 2)
+    part = wide // 2
+    half_rows = pl.ds(pl.multiple_of(side * part, part), part)
+    w_copy = remote(
+        wo_hbm.at[half_rows, :], wo2.at[half_rows, :], w_sem.at[0], w_sem.at[1], across
+    )
+    w_copy.start()
+    w_pass = remote(
+        wo2.at[half_rows, :],
+        wo2.at[half_rows, :],
+        w_sem.at[2],
+        w_sem.at[3],
+        {"ep": jnp.bitwise_xor(me, 1)},
+    )
+
+    for c in weight_loads[:3]:
+        c.wait()
+
+    def a_store(i):
+        return [
+            pltpu.make_async_copy(
+                av.at[rows_at(i, block), :], a_hbm.at[rows_at(i, block), :], a_sem.at[i, 0]
+            ),
+            pltpu.make_async_copy(
+                pv.at[rows_at(i, block), :], p_hbm.at[rows_at(i, block), :], a_sem.at[i, 1]
+            ),
+        ]
+
+    def project(i, _):
+        at = rows_at(i, block)
+        x_load(i).wait()
+        normal, _ = normalized(xv[at, :].astype(F32))
+        a = (normal * norms_ref[0:1, :] + norms_ref[1:2, :]).astype(BF16)
+        av[at, :] = a
+        for j, w in enumerate((wq, wk, wv)):
+            pv[at, j * width : (j + 1) * width] = dot(a, w[...]).astype(BF16)
+        for c in a_store(i):
+            c.start()
+        return 0
+
+    lax.fori_loop(0, steps, project, 0)
+
+    pairs = heads_count // 2
+
+    def attend(pair, out_ref, col):
+        vt[...] = pv[:, 2 * width + pair * PAIR : 2 * width + (pair + 1) * PAIR].T
+
+        def q_step(i, _):
+            at = rows_at(i, bq)
+            q = pv[at, pair * PAIR : (pair + 1) * PAIR]
+            out, lse = attend_block(
+                i,
+                q,
+                lambda s: pv[s, width + pair * PAIR : width + (pair + 1) * PAIR],
+                lambda s: vt[:, s],
+                bq,
+                bq,
+                HEAD_DIM**-0.5,
+            )
+            out_ref[at, col : col + PAIR] = out
+            for h in range(2):
+                lse_ref[pair, h : h + 1, at] = lse[h]
+            return 0
+
+        lax.fori_loop(0, rows // bq, q_step, 0)
+
+    def is_live(position):
+        count = len_ref.shape[0]
+        length = rows // count
+        inside = None
+        for s in range(count):
+            here = (position >= s * length) & (position < s * length + len_ref[s])
+            inside = here if inside is None else inside | here
+        return inside
+
+    span = 256
+    run = jnp.zeros((experts, 1), F32)
+    triangle = jnp.where(
+        lax.broadcasted_iota(jnp.int32, (span, span), 0)
+        < lax.broadcasted_iota(jnp.int32, (span, span), 1),
+        1.0,
+        0.0,
+    ).astype(BF16)
+    capacity = 2 * half
+    for b in range(rows // span):
+        at = slice(b * span, (b + 1) * span)
+        ids = ids_ref[:, at]
+        live = is_live(b * span + lax.broadcasted_iota(jnp.int32, (1, span), 1))
+        hot = (lax.broadcasted_iota(jnp.int32, (experts, span), 0) == ids) & live
+        hot = jnp.where(hot, 1.0, 0.0)
+        before = dot(hot.astype(BF16), triangle) + run
+        run = run + jnp.sum(hot, axis=1, keepdims=True)
+        slot = jnp.sum(before * hot, axis=0, keepdims=True).astype(jnp.int32)
+        sound = live & (slot < capacity)
+        place = jnp.where(sound, ids * capacity + slot, -1)
+        inside = slot - tp_me * half
+        mine = sound & (inside >= 0) & (inside < half)
+        place_g = jnp.where(mine, ids * half + inside, -1)
+        place_ref[:, at] = place
+        place_g_ref[:, at] = place_g
+        line = lax.broadcasted_iota(jnp.int32, (LANES, span), 0)
+        both = jnp.where(line == 0, place.astype(F32), place_g.astype(F32))
+        info[at, :] = both.T
+    info_store = pltpu.make_async_copy(info, info_hbm, home_sem.at[4])
+    info_store.start()
+
+    def head_copy(j, src, dst):
+        return remote(src, dst, head_send.at[j], head_recv.at[j], across)
+
+    first = pairs // 2
+    for pair in range(first):
+        attend(pair, ha, pair * PAIR)
+    copy_a = head_copy(0, ha, oa)
+    copy_a.start()
+    for pair in range(first, pairs - 1):
+        attend(pair, hb, (pair - first) * PAIR)
+
+    own_grad.wait()
+    grad_copy.wait()
+
+    def mask(i, _):
+        at = rows_at(i, block)
+        live = is_live(i * block + lax.broadcasted_iota(jnp.int32, (block, wide), 0))
+        gv[at, :] = jnp.where(live, gv[at, :], jnp.zeros((block, wide), BF16))
+        return 0
+
+    lax.fori_loop(0, steps, mask, 0)
+    gall_store = pltpu.make_async_copy(gv, gall_hbm, home_sem.at[1])
+    gall_store.start()
+
+    def pack_g(i, _):
+        slot = i * block + lax.broadcasted_iota(jnp.int32, (block, rows), 0)
+        hot = jnp.where(slot == place_g_ref[...], 1.0, 0.0).astype(BF16)
+        pk[rows_at(i, block), :] = dot(hot, gv[...]).astype(BF16)
+        return 0
+
+    lax.fori_loop(0, peers * half // block, pack_g, 0)
+
+    def z_copy(k):
+        peer = jnp.bitwise_xor(me, k)
+        return remote(
+            pk.at[rows_at(peer, half), :], gin_hbm.at[me], z_send.at[k], z_recv.at[k], {"ep": peer}
+        )
+
+    for k in list(range(peers // 2, peers)) + list(range(1, peers // 2)):
+        z_copy(k).start()
+    gin_own = pltpu.make_async_copy(pk.at[rows_at(me, half), :], gin_hbm.at[me], home_sem.at[2])
+    gin_own.start()
+    w_copy.wait()
+    w_pass.start()
+    attend(pairs - 1, hb, (pairs - 1 - first) * PAIR)
+    copy_b = head_copy(1, hb, ob)
+    copy_b.start()
+    weight_loads[3].wait()
+    w_pass.wait()
+    stores = [
+        pltpu.make_async_copy(ha, heads_hbm_a, out_sem.at[0]),
+        pltpu.make_async_copy(hb, heads_hbm_b, out_sem.at[1]),
+        pltpu.make_async_copy(wo2, wo2_hbm, out_sem.at[2]),
+    ]
+    for c in stores:
+        c.start()
+    copy_a.wait()
+    copy_b.wait()
+    stores_others = [
+        pltpu.make_async_copy(oa, others_hbm_a, out_sem.at[3]),
+        pltpu.make_async_copy(ob, others_hbm_b, out_sem.at[4]),
+    ]
+    for c in stores_others:
+        c.start()
+    small = rb.shape[1]
+    cut = first * PAIR
+
+    def norm_stores(i, slot):
+        at = rows_at(i, small)
+        return [
+            pltpu.make_async_copy(rb.at[slot], resid_hbm.at[at, :], out_sem.at[5 + slot]),
+            pltpu.make_async_copy(cb.at[slot], chance_hbm.at[at, :], out_sem.at[7 + slot]),
+        ]
+
+    def norm_step(i, _):
+        at = rows_at(i, small)
+        slot = lax.rem(i, 2)
+
+        @pl.when(i >= 2)
+        def _():
+            for c in norm_stores(i - 2, slot):
+                c.wait()
+
+        total = dot_nt(ha[at, :], wo[:, :cut]) + dot_nt(hb[at, :], wo[:, cut:])
+        total = total + (dot_nt(oa[at, :], wo2[:, :cut]) + dot_nt(ob[at, :], wo2[:, cut:]))
+        resid = xv[at, :].astype(F32) + total
+        rb[slot] = resid
+        normal, _ = normalized(resid)
+        f = (normal * norms_ref[2:3, :] + norms_ref[3:4, :]).astype(BF16)
+        fv[at, :] = f
+        cb[slot] = router_and_mix(dot(f, rm_ref[...]), experts)
+        for c in norm_stores(i, slot):
+            c.start()
+        return 0
+
+    count = rows // small
+    lax.fori_loop(0, count, norm_step, 0)
+    f_store = pltpu.make_async_copy(fv, f_hbm, home_sem.at[3])
+    f_store.start()
+    for i in range(count - 2, count):
+        for c in norm_stores(i, i % 2):
+            c.wait()
+
+    def packed_store(i, slot):
+        return pltpu.make_async_copy(
+            hbuf.at[slot], packed_hbm.at[rows_at(i, block), :], out_sem.at[5 + slot]
+        )
+
+    def pack_h(i, _):
+        slot = lax.rem(i, 2)
+
+        @pl.when(i >= 2)
+        def _():
+            packed_store(i - 2, slot).wait()
+
+        at = i * block + lax.broadcasted_iota(jnp.int32, (block, rows), 0)
+        hot = jnp.where(at == place_ref[...], 1.0, 0.0).astype(BF16)
+        hbuf[slot] = dot(hot, fv[...]).astype(BF16)
+        packed_store(i, slot).start()
+        return 0
+
+    packs = packed_hbm.shape[0] // block
+    lax.fori_loop(0, packs, pack_h, 0)
+    for i in range(packs - 2, packs):
+        packed_store(i, i % 2).wait()
+    for c in [gall_store, gin_own, f_store, info_store] + stores + stores_others:
+        c.wait()
+    for i in range(steps):
+        for c in a_store(i):
+            c.wait()
+    for k in range(1, peers):
+        z_copy(k).wait()
+
+
+def front(x, g, weights, lengths, norms, rm, ids, peers, experts, capacity, bq=512):
+    rows, wide = x.shape
+    width = weights[0].shape[1]
+    half = capacity // 2
+    cut = width // 2
+    anywhere = pl.BlockSpec(memory_space=pl.ANY)
+    vmem = pl.BlockSpec(memory_space=pltpu.VMEM)
+
+    def like(*shape, kind=BF16):
+        return jax.ShapeDtypeStruct(shape, kind)
+
+    return pl.pallas_call(
+        partial(
+            front_kernel,
+            peers=peers,
+            experts=experts,
+            half=half,
+            bq=bq,
+            heads_count=width // HEAD_DIM,
+        ),
+        in_specs=[anywhere] * 6 + [pl.BlockSpec(memory_space=pltpu.SMEM)] + [vmem] * 3,
+        out_specs=[anywhere] * 14 + [vmem],
+        out_shape=[
+            like(rows, wide),
+            like(rows, 3 * width),
+            like(rows, cut),
+            like(rows, cut),
+            like(rows, cut),
+            like(rows, cut),
+            like(wide, width),
+            like(rows, wide),
+            like(rows, wide, kind=F32),
+            like(rows, wide),
+            like(rows, LANES, kind=F32),
+            like(experts * capacity, wide),
+            like(peers, half, wide),
+            like(rows, LANES, kind=F32),
+            like(width // PAIR, 2, rows, kind=F32),
+        ],
+        scratch_shapes=[pltpu.VMEM((rows, wide), BF16)]
+        + [pltpu.VMEM((wide, width), BF16)] * 5
+        + [
+            pltpu.VMEM((rows, wide), BF16),
+            pltpu.VMEM((rows, 3 * width), BF16),
+            pltpu.VMEM((PAIR, rows), BF16),
+        ]
+        + [pltpu.VMEM((rows, cut), BF16)] * 4
+        + [
+            pltpu.VMEM((rows, wide), BF16),
+            pltpu.VMEM((peers * half, wide), BF16),
+            pltpu.VMEM((rows, wide), BF16),
+            pltpu.VMEM((2, 256, wide), F32),
+            pltpu.VMEM((2, 256, LANES), F32),
+            pltpu.VMEM((2, 512, wide), BF16),
+            pltpu.VMEM((1, rows), jnp.int32),
+            pltpu.VMEM((1, rows), jnp.int32),
+            pltpu.VMEM((rows, LANES), F32),
+            pltpu.SemaphoreType.DMA((4,)),
+            pltpu.SemaphoreType.DMA((rows // 512,)),
+            pltpu.SemaphoreType.DMA((rows // 512, 2)),
+            pltpu.SemaphoreType.DMA((5,)),
+            pltpu.SemaphoreType.DMA((2,)),
+            pltpu.SemaphoreType.DMA((4,)),
+            pltpu.SemaphoreType.DMA((2,)),
+            pltpu.SemaphoreType.DMA((2,)),
+            pltpu.SemaphoreType.DMA((peers,)),
+            pltpu.SemaphoreType.DMA((peers,)),
+            pltpu.SemaphoreType.DMA((9,)),
+        ],
+        cost_estimate=cost(20 * rows * wide * wide, 30 * rows * wide),
+        compiler_params=pltpu.CompilerParams(
+            vmem_limit_bytes=BIG_VMEM, collective_id=2, has_side_effects=True
+        ),
+        name="layer_front",
+    )(x, g, *weights, lengths, norms, rm, ids)
+
+
 def nets_kernel(
     x_hbm,
     g_hbm,
@@ -404,6 +800,7 @@
     edot_hbm,
     pulls_hbm,
     edots_hbm,
+    gin2_hbm,
     wd1,
     wd2,
     we1,
@@ -433,11 +830,19 @@
     back_recv,
     dot_send,
     dot_recv,
+    relay_sem,
+    swap_send,
+    swap_recv,
+    keep,
+    give,
+    got,
+    stage,
     *,
     peers,
     capacity,
     rb,
     ft,
+    relayed,
 ):
     experts = peers
     me = lax.axis_index("ep")
@@ -474,7 +879,24 @@
             device_id={"ep": jnp.bitwise_xor(me, k)},
             device_id_type=pl.DeviceIdType.MESH,
         )
-    pl.semaphore_wait(barrier, peers - 1)
+    tp_me = lax.axis_index("tp")
+    across = {"tp": 1 - tp_me}
+    half = capacity // 2
+    if relayed:
+        pl.semaphore_signal(
+            barrier, inc=1, device_id=across, device_id_type=pl.DeviceIdType.MESH
+        )
+    pl.semaphore_wait(barrier, peers if relayed else peers - 1)
+    relay = pltpu.make_async_remote_copy(
+        src_ref=gin_hbm,
+        dst_ref=gin2_hbm,
+        send_sem=relay_sem.at[0],
+        recv_sem=relay_sem.at[1],
+        device_id=across,
+        device_id_type=pl.DeviceIdType.MESH,
+    )
+    if relayed:
+        relay.start()
 
     def remote(src, dst, send, recv, k):
         peer = jnp.bitwise_xor(me, k)
@@ -502,10 +924,9 @@
             edot_hbm.at[jnp.bitwise_xor(me, k)], edots_hbm.at[me], dot_send, dot_recv, k
         )
 
-    far = list(range(2 * quarter, 3 * quarter))
+    far = list(range(2 * quarter, peers))
     near = list(range(1, 2 * quarter))
-    last = list(range(3 * quarter, peers))
-    for k in far + near + last:
+    for k in far[:quarter] + near[quarter - 1 :] + far[quarter:] + near[: quarter - 1]:
         row_copy(k).start()
     own_rows = pltpu.make_async_copy(out_hbm.at[me], in_hbm.at[me], home_sem.at[0])
     own_rows.start()
@@ -543,10 +964,7 @@
             return 0
 
         lax.fori_loop(0, hidden // ft, step, 0)
-        y = ya[...]
-        yb[slot] = y.astype(BF16)
-        dxb[slot] = dxa[...].astype(BF16)
-        return jnp.sum(y * g, axis=1, keepdims=True)
+        return jnp.sum(ya[...] * gb[slot].astype(F32), axis=1, keepdims=True)
 
     a1[...] = jnp.zeros_like(a1)
     a2[...] = jnp.zeros_like(a2)
@@ -577,6 +995,8 @@
                 c.wait()
 
         dots = compute(slot, False, wd1, wd2)
+        yb[slot] = ya[...].astype(BF16)
+        dxb[slot] = dxa[...].astype(BF16)
         dotb[slot] = jnp.broadcast_to(dots, (rb, LANES))
         for c in dense_stores(t, slot):
             c.start()
@@ -600,9 +1020,57 @@
     weight_copies[2].wait()
     weight_copies[3].wait()
     own_rows.wait()
+    if relayed:
+        relay.wait()
+
+    def first_of(p):
+        if expert_steps != 4:
+            return (expert_steps - 1 - p) * per
+        return jnp.where(p < 2, 2 + p, 3 - p) * per
+
+    def swap_copy(p, j):
+        slot = lax.rem(p, 2)
+        return pltpu.make_async_remote_copy(
+            src_ref=give.at[slot, j],
+            dst_ref=got.at[slot, j],
+            send_sem=swap_send.at[slot, j],
+            recv_sem=swap_recv.at[slot, j],
+            device_id=across,
+            device_id_type=pl.DeviceIdType.MESH,
+        )
+
+    def send_back(p, size, sources):
+        base = first_of(p)
+        stores = []
+        for c in range(per):
+            source = jnp.bitwise_xor(me, base + c)
+            rows = pl.ds(c * size, size)
+            for j, to in ((0, pull_hbm), (1, res_hbm)):
+                stores.append(
+                    pltpu.make_async_copy(
+                        sources[j].at[rows, :], to.at[source], store_sem.at[0, j, c]
+                    )
+                )
+        for c in stores:
+            c.start()
+        for c in stores:
+            c.wait()
+        for c in range(per):
+            k = base + c
+
+            @pl.when(k > 0)
+            def _(k=k):
+                back_copy(k).start()
+
+    def finish(p):
+        slot = lax.rem(p, 2)
+        for j in range(2):
+            swap_copy(p, j).wait()
+            stage[j] = (keep[j] + got[slot, j].astype(F32)).astype(BF16)
+        send_back(p, half, (stage.at[0], stage.at[1]))
 
     def expert_step(p, _):
-        base = jnp.where(p == expert_steps - 1, peers - per, (expert_steps - 2 - p) * per)
+        base = first_of(p)
         slot = lax.rem(p, 2)
         loads = []
         for c in range(per):
@@ -617,28 +1085,51 @@
             loads.append(
                 pltpu.make_async_copy(in_hbm.at[source], xb.at[slot, rows, :], load_sem.at[slot, 0, c])
             )
-            loads.append(
-                pltpu.make_async_copy(gin_hbm.at[source], gb.at[slot, rows, :], load_sem.at[slot, 1, c])
-            )
+            if relayed:
+                for j, src, which in ((1, gin_hbm, tp_me), (2, gin2_hbm, 1 - tp_me)):
+                    at = pl.ds(pl.multiple_of(c * capacity + which * half, half), half)
+                    loads.append(
+                        pltpu.make_async_copy(
+                            src.at[source], gb.at[slot, at, :], load_sem.at[slot, j, c]
+                        )
+                    )
+            else:
+                loads.append(
+                    pltpu.make_async_copy(
+                        gin_hbm.at[source], gb.at[slot, rows, :], load_sem.at[slot, 1, c]
+                    )
+                )
         for c in loads:
             c.start()
         for c in loads:
             c.wait()
         dots = compute(slot, True, we1, we2)
-        across = jnp.broadcast_to(dots, (rb, LANES)).T
+        if relayed:
+
+            @pl.when(p > 0)
+            def _():
+                finish(p - 1)
+
+            for j, total in ((0, dxa), (1, ya)):
+                for c in range(per):
+                    rows = slice(c * half, (c + 1) * half)
+                    at = pl.ds(pl.multiple_of(c * capacity + tp_me * half, half), half)
+                    other = pl.ds(pl.multiple_of(c * capacity + (1 - tp_me) * half, half), half)
+                    keep[j, rows, :] = total[at, :]
+                    give[slot, j, rows, :] = total[other, :].astype(BF16)
+                swap_copy(p, j).start()
+        else:
+            yb[slot] = ya[...].astype(BF16)
+            dxb[slot] = dxa[...].astype(BF16)
+            send_back(p, capacity, (dxb.at[slot], yb.at[slot]))
+        across_dots = jnp.broadcast_to(dots, (rb, LANES)).T
         stores = []
         for c in range(per):
-            source = jnp.bitwise_xor(me, base + c)
-            rows = pl.ds(c * capacity, capacity)
-            rowb[c] = across[:8, c * capacity : (c + 1) * capacity]
+            rowb[c] = across_dots[:8, c * capacity : (c + 1) * capacity]
             stores.append(
-                pltpu.make_async_copy(yb.at[slot, rows, :], res_hbm.at[source], store_sem.at[slot, 0, c])
-            )
-            stores.append(
-                pltpu.make_async_copy(dxb.at[slot, rows, :], pull_hbm.at[source], store_sem.at[slot, 1, c])
-            )
-            stores.append(
-                pltpu.make_async_copy(rowb.at[c], edot_hbm.at[source], store_sem.at[slot, 2, c])
+                pltpu.make_async_copy(
+                    rowb.at[c], edot_hbm.at[jnp.bitwise_xor(me, base + c)], store_sem.at[1, 2, c]
+                )
             )
         for c in stores:
             c.start()
@@ -649,12 +1140,13 @@
 
             @pl.when(k > 0)
             def _(k=k):
-                back_copy(k).start()
                 dot_copy(k).start()
 
         return 0
 
     lax.fori_loop(0, expert_steps, expert_step, 0)
+    if relayed:
+        finish(expert_steps - 1)
     expert_grads = [
         pltpu.make_async_copy(a1, ge1_hbm, local_sem.at[0]),
         pltpu.make_async_copy(a2, ge2_hbm, local_sem.at[1]),
@@ -678,12 +1170,15 @@
     anywhere = pl.BlockSpec(memory_space=pl.ANY)
     vmem = pl.BlockSpec(memory_space=pltpu.VMEM)
     sheet = jax.ShapeDtypeStruct((rows, wide), BF16)
+    relayed = in_grads.shape[1] < capacity
     blocks = jax.ShapeDtypeStruct((peers, capacity, wide), BF16)
+    backs = jax.ShapeDtypeStruct(in_grads.shape, BF16)
+    part = (rb * in_grads.shape[1] // capacity, wide) if relayed else (16, wide)
     strips = jax.ShapeDtypeStruct((peers, 8, capacity), F32)
     return pl.pallas_call(
-        partial(nets_kernel, peers=peers, capacity=capacity, rb=rb, ft=ft),
+        partial(nets_kernel, peers=peers, capacity=capacity, rb=rb, ft=ft, relayed=relayed),
         in_specs=[anywhere] * 4 + [vmem] * 2 + [anywhere] * 4,
-        out_specs=[anywhere] * 13,
+        out_specs=[anywhere] * 14,
         out_shape=[
             sheet,
             sheet,
@@ -693,11 +1188,12 @@
             jax.ShapeDtypeStruct((wide, hidden), F32),
             jax.ShapeDtypeStruct((wide, hidden), F32),
             blocks,
-            blocks,
-            blocks,
+            backs,
+            backs,
             strips,
-            blocks,
+            backs,
             strips,
+            backs,
         ],
         scratch_shapes=[pltpu.VMEM((wide, hidden), BF16)] * 4
         + [pltpu.VMEM((wide, hidden), F32)] * 2
@@ -711,13 +1207,22 @@
             pltpu.VMEM((wide, rb), BF16),
             pltpu.VMEM((wide, rb), BF16),
             pltpu.SemaphoreType.DMA((4,)),
-            pltpu.SemaphoreType.DMA((2, 2, per)),
+            pltpu.SemaphoreType.DMA((2, 3, per)),
             pltpu.SemaphoreType.DMA((2, 3, per)),
             pltpu.SemaphoreType.DMA((2,)),
             pltpu.SemaphoreType.DMA((3,)),
             pltpu.SemaphoreType.DMA((2,)),
         ]
-        + [pltpu.SemaphoreType.DMA((peers,))] * 6,
+        + [pltpu.SemaphoreType.DMA((peers,))] * 6
+        + [
+            pltpu.SemaphoreType.DMA((2,)),
+            pltpu.SemaphoreType.DMA((2, 2)),
+            pltpu.SemaphoreType.DMA((2, 2)),
+            pltpu.VMEM((2, *part), F32),
+            pltpu.VMEM((2, 2, *part), BF16),
+            pltpu.VMEM((2, 2, *part), BF16),
+            pltpu.VMEM((2, *part), BF16),
+        ],
         cost_estimate=cost(24 * rows * wide * hidden, 16 * rows * wide + 24 * wide * hidden),
         compiler_params=pltpu.CompilerParams(
             vmem_limit_bytes=BIG_VMEM, collective_id=0, has_side_effects=True
@@ -732,10 +1237,9 @@
     return ((place >= low) & (place < low + capacity) & (lane < experts)).astype(F32)
 
 
-def ffn_pull_kernel(*refs, parts, experts, capacity):
+def ffn_pull_kernel(*refs, parts, experts, capacity, shard):
     (
-        place_ref,
-        own_ref,
+        info_ref,
         dx_ref,
         chance_ref,
         first_ref,
@@ -746,12 +1250,17 @@
         rm_ref,
         slot_ref,
         dots_ref,
-    ) = refs[:12]
-    weights = refs[12 : 12 + parts]
-    r_ref = refs[12 + parts]
-    heads = refs[13 + parts : 13 + 2 * parts]
-    sums_ref, rmg_ref = refs[13 + 2 * parts :]
-    place = place_ref[...]
+    ) = refs[:11]
+    weights = refs[11 : 11 + parts]
+    r_ref = refs[11 + parts]
+    heads = refs[12 + parts : 12 + 2 * parts]
+    sums_ref, rmg_ref = refs[12 + 2 * parts :]
+    place = info_ref[:, 0:1].astype(jnp.int32)
+    here = info_ref[:, 1:2].astype(jnp.int32)
+    size = info_ref.shape[0]
+    row = pl.program_id(0) * size + lax.broadcasted_iota(jnp.int32, (size, 1), 0)
+    row = row - lax.axis_index("tp") * shard
+    own = ((row >= 0) & (row < shard)).astype(F32)
     chances = chance_ref[...]
     hot = expert_hot(place, capacity, experts)
     gate = jnp.sum(hot * chances, axis=-1, keepdims=True)
@@ -771,9 +1280,9 @@
     low = jnp.where(lane == experts, mix_0 * (grad_0 - inner), low)
     low = jnp.where(lane == experts + 1, mix_1 * (grad_1 - inner), low)
     low = jnp.where(lane > experts + 1, 0.0, low).astype(BF16)
-    grad = dx_ref[...].astype(F32) + unpacked(place, slot_ref) + dot_nt(low, rm_ref[...])
+    grad = dx_ref[...].astype(F32) + unpacked(here, slot_ref) + dot_nt(low, rm_ref[...])
     normal, rstd = normalized(resid_ref[...])
-    r = norm_pull(grad, normal, rstd, gain_ref[...]) + own_ref[...] * g_ref[...].astype(F32)
+    r = norm_pull(grad, normal, rstd, gain_ref[2:3, :]) + own * g_ref[...].astype(F32)
     r = r.astype(BF16)
     r_ref[...] = r
     for h, w in zip(heads, weights):
@@ -790,20 +1299,21 @@
 
 
 def ffn_pull(
-    place, own, dx, chances, first, f, g, resid, gain, rm, slot_rows, dots, weights, experts, rb=256
+    info, dx, chances, first, f, g, resid, gain, rm, slot_rows, dots, weights, experts, shard, rb=256
 ):
     rows, wide = dx.shape
     capacity = dots.shape[1]
     dots = jnp.pad(dots, ((0, LANES - experts), (0, 0)))
     block = pl.BlockSpec((rb, wide), lambda i: (i, 0))
     narrow = pl.BlockSpec((rb, LANES), lambda i: (i, 0))
-    col = pl.BlockSpec((rb, 1), lambda i: (i, 0))
     head_specs = [pl.BlockSpec((rb, size), lambda i: (i, 0)) for _, _, size in weights]
     return pl.pallas_call(
-        partial(ffn_pull_kernel, parts=len(weights), experts=experts, capacity=capacity),
+        partial(
+            ffn_pull_kernel, parts=len(weights), experts=experts, capacity=capacity, shard=shard
+        ),
         grid=(rows // rb,),
-        in_specs=[col, col, block, narrow, narrow, block, block, block]
-        + [resident((1, wide)), resident((wide, LANES))]
+        in_specs=[narrow, block, narrow, narrow, block, block, block]
+        + [resident(gain.shape), resident((wide, LANES))]
         + [resident(slot_rows.shape), resident(dots.shape)]
         + [
             pl.BlockSpec((wide, size), lambda i, j=j: (0, j), pipeline_mode=pl.Buffered(1))
@@ -817,8 +1327,7 @@
         compiler_params=pltpu.CompilerParams(vmem_limit_bytes=48 * 1024 * 1024),
         name="ffn_norm_pull",
     )(
-        place,
-        own,
+        info,
         dx,
         chances,
         first,
@@ -921,22 +1430,23 @@
     )((first_row // rb).astype(jnp.int32).reshape(1), x, r, gain, *grads, *weights)
 
 
-def combine_kernel(place_ref, y_ref, chance_ref, slot_ref, o_ref, *, experts, capacity):
-    place = place_ref[...]
+def combine_kernel(info_ref, y_ref, chance_ref, slot_ref, o_ref, *, experts, capacity):
+    place = info_ref[:, 0:1].astype(jnp.int32)
+    here = info_ref[:, 1:2].astype(jnp.int32)
     chances = chance_ref[...]
     gate = jnp.sum(expert_hot(place, capacity, experts) * chances, axis=-1, keepdims=True)
-    moe = unpacked(place, slot_ref) * (lane_of(chances, experts + 1) * gate)
+    moe = unpacked(here, slot_ref) * (lane_of(chances, experts + 1) * gate)
     o_ref[...] = (lane_of(chances, experts) * y_ref[...].astype(F32) + moe).astype(BF16)
 
 
-def combine(place, y, coef, slot_rows, experts, rb=256):
+def combine(info, y, coef, slot_rows, experts, capacity, rb=256):
     rows, wide = y.shape
     block = pl.BlockSpec((rb, wide), lambda i: (i, 0))
     return pl.pallas_call(
-        partial(combine_kernel, experts=experts, capacity=slot_rows.shape[0] // experts),
+        partial(combine_kernel, experts=experts, capacity=capacity),
         grid=(rows // rb,),
         in_specs=[
-            pl.BlockSpec((rb, 1), lambda i: (i, 0)),
+            pl.BlockSpec((rb, LANES), lambda i: (i, 0)),
             block,
             pl.BlockSpec((rb, LANES), lambda i: (i, 0)),
         ]
@@ -945,7 +1455,285 @@
         out_shape=jax.ShapeDtypeStruct((rows, wide), BF16),
         cost_estimate=cost(4 * rows * wide * wide, 8 * rows * wide),
         name="combine_nets",
-    )(place, y, coef, slot_rows)
+    )(info, y, coef, slot_rows)
+
+
+class Halving:
+    def __init__(self, total, gives, gots, send, recv, me, size):
+        self.total, self.gives, self.gots = total, gives, gots
+        self.send, self.recv, self.me, self.size = send, recv, me, size
+        self.rows = total.shape[0] // size
+
+    def block(self, index):
+        return pl.ds(pl.multiple_of(index * self.rows, self.rows), self.rows)
+
+    def copy(self, s):
+        return pltpu.make_async_remote_copy(
+            src_ref=self.gives[s],
+            dst_ref=self.gots[s],
+            send_sem=self.send.at[s],
+            recv_sem=self.recv.at[s],
+            device_id={"ep": jnp.bitwise_xor(self.me, 1 << s)},
+            device_id_type=pl.DeviceIdType.MESH,
+        )
+
+    def bit(self, s):
+        return lax.rem(lax.div(self.me, 1 << s), 2)
+
+    def start(self, s):
+        for i in range(self.size >> (s + 1)):
+            at = slice(i * self.rows, (i + 1) * self.rows)
+            self.gives[s][at, :] = self.total[self.block(2 * i + 1 - self.bit(s)), :].astype(BF16)
+        self.copy(s).start()
+
+    def finish(self, s):
+        self.copy(s).wait()
+        for i in range(self.size >> (s + 1)):
+            at = slice(i * self.rows, (i + 1) * self.rows)
+            self.total[at, :] = self.total[self.block(2 * i + self.bit(s)), :] + self.gots[s][at, :].astype(F32)
+
+
+def tail_kernel(*refs, groups, size, rb, small_rows):
+    refs = list(refs)
+
+    def take(count):
+        taken = refs[:count]
+        del refs[:count]
+        return taken
+
+    x_hbm, r_hbm, a_hbm, out_hbm = take(4)
+    grads_hbm = take(3 * groups)
+    small_ref, gain_ref = take(2)
+    weights = take(3)
+    own_hbm, got_hbm, square_ref, outsum_ref, total_ref = take(5)
+    xv, rv, av = take(3)
+    grads = take(3 * groups)
+    gov, acc, goacc, give_rows, own_buf = take(5)
+    steps = size.bit_length() - 1
+    hops = steps + 1
+    gives, gots = take(steps), take(steps)
+    go_gives, go_gots = take(steps), take(steps)
+    small_gives, small_gots = take(hops), take(hops)
+    (
+        load_sem,
+        own_sem,
+        row_send,
+        row_recv,
+        half_send,
+        half_recv,
+        go_send,
+        go_recv,
+        small_send,
+        small_recv,
+        out_sem,
+        out_give,
+        out_got,
+    ) = refs
+    me = lax.axis_index("ep")
+    tp_me = lax.axis_index("tp")
+    rows = x_hbm.shape[0]
+    shard = rows // 2
+    count = shard // rb
+
+    sources = [x_hbm, r_hbm, *grads_hbm, a_hbm, out_hbm]
+    targets = [xv, rv, *grads, av, gov]
+    loads = [
+        pltpu.make_async_copy(src, dst, load_sem.at[j])
+        for j, (src, dst) in enumerate(zip(sources, targets))
+    ]
+    loads[-1].start()
+    for c in loads[:-1]:
+        c.start()
+
+    barrier = pltpu.get_barrier_semaphore()
+    mesh = pl.DeviceIdType.MESH
+    pl.semaphore_signal(barrier, inc=1, device_id={"tp": 1 - tp_me}, device_id_type=mesh)
+    for s in range(steps):
+        pl.semaphore_signal(
+            barrier, inc=1, device_id={"ep": jnp.bitwise_xor(me, 1 << s)}, device_id_type=mesh
+        )
+    pl.semaphore_wait(barrier, hops)
+
+    qkv = Halving(acc, gives, gots, half_send, half_recv, me, size)
+    go = Halving(goacc, go_gives, go_gots, go_send, go_recv, me, size)
+
+    loads[-1].wait()
+    goacc[...] = gov[...].astype(F32)
+    go.start(0)
+    for c in loads[:-2]:
+        c.wait()
+
+    total_ref[:small_rows, :] = small_ref[...]
+    total_ref[small_rows:, :] = jnp.zeros_like(total_ref[small_rows:, :])
+
+    def pulled(at):
+        total = None
+        for k in range(3):
+            col = 0
+            for j in range(groups):
+                d = grads[k * groups + j][at, :]
+                width = d.shape[1]
+                part = dot_nt(d, weights[k][:, col : col + width])
+                total = part if total is None else total + part
+                col += width
+        normal, rstd = normalized(xv[at, :].astype(F32))
+        total_ref[small_rows : small_rows + 1, :] += jnp.sum(total * normal, axis=0, keepdims=True)
+        total_ref[small_rows + 1 : small_rows + 2, :] += jnp.sum(total, axis=0, keepdims=True)
+        return norm_pull(total, normal, rstd, gain_ref[0:1, :]) + rv[at, :].astype(F32)
+
+    def row_copy(b):
+        at = pl.ds(pl.multiple_of(b * rb, rb), rb)
+        return pltpu.make_async_remote_copy(
+            src_ref=give_rows.at[at, :],
+            dst_ref=got_hbm.at[at, :],
+            send_sem=row_send.at[b],
+            recv_sem=row_recv.at[b],
+            device_id={"tp": 1 - tp_me},
+            device_id_type=mesh,
+        )
+
+    def theirs(b, _):
+        at = pl.ds(pl.multiple_of((1 - tp_me) * shard + b * rb, rb), rb)
+        give_rows[pl.ds(pl.multiple_of(b * rb, rb), rb), :] = pulled(at).astype(BF16)
+        row_copy(b).start()
+        return 0
+
+    lax.fori_loop(0, count, theirs, 0)
+    go.finish(0)
+    go.start(1)
+
+    loads[-2].wait()
+    acc[...] = jnp.zeros_like(acc)
+
+    def outer_step(b, _):
+        at = pl.ds(pl.multiple_of(b * 512, 512), 512)
+        left = av[at, :].T
+        col = 0
+        for g in grads:
+            width = g.shape[1]
+            acc[:, col : col + width] += dot(left, g[at, :])
+            col += width
+        return 0
+
+    lax.fori_loop(0, rows // 512, outer_step, 0)
+    qkv.start(0)
+    for s in range(1, steps):
+        go.finish(s)
+        if s + 1 < steps:
+            go.start(s + 1)
+        if s == 1:
+            qkv.finish(0)
+            qkv.start(1)
+
+    own_width = outsum_ref.shape[1]
+    out_give[...] = goacc[: goacc.shape[0] // size, own_width:].astype(BF16)
+    out_copy = pltpu.make_async_remote_copy(
+        src_ref=out_give,
+        dst_ref=out_got,
+        send_sem=out_sem.at[0],
+        recv_sem=out_sem.at[1],
+        device_id={"tp": 1 - tp_me},
+        device_id_type=mesh,
+    )
+    out_copy.start()
+
+    def own_copy(b):
+        at = pl.ds(pl.multiple_of(b * rb, rb), rb)
+        return pltpu.make_async_copy(own_buf.at[at, :], own_hbm.at[at, :], own_sem.at[b])
+
+    def own_step(b, _):
+        at = pl.ds(pl.multiple_of(tp_me * shard + b * rb, rb), rb)
+        own_buf[pl.ds(pl.multiple_of(b * rb, rb), rb), :] = pulled(at)
+        own_copy(b).start()
+        return 0
+
+    lax.fori_loop(0, count, own_step, 0)
+
+    def small_copy(s):
+        peer = {"tp": 1 - tp_me} if s == 0 else {"ep": jnp.bitwise_xor(me, 1 << (s - 1))}
+        return pltpu.make_async_remote_copy(
+            src_ref=small_gives[s],
+            dst_ref=small_gots[s],
+            send_sem=small_send.at[s],
+            recv_sem=small_recv.at[s],
+            device_id=peer,
+            device_id_type=mesh,
+        )
+
+    for s in range(hops):
+        small_gives[s][...] = total_ref[...]
+        small_copy(s).start()
+        if 0 < s < steps:
+            qkv.finish(s)
+            if s + 1 < steps:
+                qkv.start(s + 1)
+        small_copy(s).wait()
+        total_ref[...] += small_gots[s][...]
+    square_ref[...] = acc[: acc.shape[0] // size, :]
+    out_copy.wait()
+    outsum_ref[...] = goacc[: goacc.shape[0] // size, :own_width] + out_got[...].astype(F32)
+    for b in range(count):
+        own_copy(b).wait()
+        row_copy(b).wait()
+
+
+def tail(x, r, a, out_part, grads, small, gain, weights, size, rb=256):
+    rows, wide = x.shape
+    shard = rows // 2
+    groups = len(grads) // 3
+    total = sum(g.shape[1] for g in grads)
+    out_width = out_part.shape[1]
+    small_rows = small.shape[0]
+    steps = size.bit_length() - 1
+    kept = wide // size
+    anywhere = pl.BlockSpec(memory_space=pl.ANY)
+    vmem = pl.BlockSpec(memory_space=pltpu.VMEM)
+
+    def halves(width):
+        return [pltpu.VMEM((wide >> (s + 1), width), BF16) for s in range(steps)]
+
+    return pl.pallas_call(
+        partial(tail_kernel, groups=groups, size=size, rb=rb, small_rows=small_rows),
+        in_specs=[anywhere] * (4 + 3 * groups) + [vmem] * 5,
+        out_specs=[anywhere, anywhere, vmem, vmem, vmem],
+        out_shape=[
+            jax.ShapeDtypeStruct((shard, wide), F32),
+            jax.ShapeDtypeStruct((shard, wide), BF16),
+            jax.ShapeDtypeStruct((kept, total), F32),
+            jax.ShapeDtypeStruct((kept, out_width // 2), F32),
+            jax.ShapeDtypeStruct((small_rows + 8, wide), F32),
+        ],
+        scratch_shapes=[pltpu.VMEM((rows, wide), BF16)] * 3
+        + [pltpu.VMEM(g.shape, BF16) for g in grads]
+        + [
+            pltpu.VMEM((wide, out_width), BF16),
+            pltpu.VMEM((wide, total), F32),
+            pltpu.VMEM((wide, out_width), F32),
+            pltpu.VMEM((shard, wide), BF16),
+            pltpu.VMEM((shard, wide), F32),
+        ]
+        + halves(total) * 2
+        + halves(out_width) * 2
+        + [pltpu.VMEM((small_rows + 8, wide), F32)] * (2 * (steps + 1))
+        + [
+            pltpu.SemaphoreType.DMA((5 + 3 * groups,)),
+            pltpu.SemaphoreType.DMA((shard // rb,)),
+            pltpu.SemaphoreType.DMA((shard // rb,)),
+            pltpu.SemaphoreType.DMA((shard // rb,)),
+        ]
+        + [pltpu.SemaphoreType.DMA((steps,))] * 4
+        + [pltpu.SemaphoreType.DMA((steps + 1,))] * 2
+        + [
+            pltpu.SemaphoreType.DMA((2,)),
+            pltpu.VMEM((kept, out_width // 2), BF16),
+            pltpu.VMEM((kept, out_width // 2), BF16),
+        ],
+        cost_estimate=cost(12 * rows * wide * total // 3, 16 * rows * wide),
+        compiler_params=pltpu.CompilerParams(
+            vmem_limit_bytes=BIG_VMEM, collective_id=1, has_side_effects=True
+        ),
+        name="backward_tail",
+    )(x, r, a, out_part, *grads, small, gain, *weights)
 
 
 def on_device(
@@ -1007,21 +1795,7 @@
         return values
 
     def over_sequences(values):
-        return lax.psum_scatter(values, "ep", scatter_dimension=0, tiled=True).astype(F32)
-
-    def halved_over_sequences(values):
-        step = 1
-        while step < ep:
-            width = values.shape[-1]
-            split = values.reshape(-1, 2, values.shape[0] // (ep // step), width)
-            bit = (ep_index // step) % 2
-            keep = lax.dynamic_index_in_dim(split, bit, 1, keepdims=False)
-            give = lax.dynamic_index_in_dim(split, 1 - bit, 1, keepdims=False)
-            give = give.reshape(-1, width)
-            got = lax.ppermute(give, "ep", [(i, i ^ step) for i in range(ep)])
-            values = (keep.reshape(-1, width).astype(F32) + got.astype(F32)).astype(BF16)
-            step *= 2
-        return values.astype(F32)
+        return lax.psum_scatter(values, "ep", scatter_dimension=0, tiled=True)
 
     positions = jnp.arange(all_rows)
     seq_index = positions // seq_len
@@ -1029,64 +1803,70 @@
         jnp.where(seq_index[:, None] == jnp.arange(seq_count)[None, :], lengths[None, :], 0), axis=1
     )
     live_all = positions % seq_len < row_limit
-    one_hot = (expert_ids[:, None] == jnp.arange(experts)[None, :]) & live_all[:, None]
-    routed = one_hot.astype(F32)
-    slots = jnp.sum((jnp.cumsum(routed, axis=0) - routed) * routed, axis=1).astype(jnp.int32)
-    sound = live_all & (slots < capacity)
-    place = jnp.where(sound, expert_ids * capacity + slots, -1)
-    place_row = place[None, :]
-    place_col = place[:, None]
     slot_count = experts * capacity
     blocks = (experts, capacity, model_width)
-
-    live_grad = jnp.where(shard_of(live_all)[:, None], out_grad, jnp.zeros_like(out_grad))
-    if tp == 2:
-        grad_other = swapped(live_grad)
-        w_other = swapped(w_output)
-        mine_first = tp_index == 0
-        grad_all = jnp.concatenate(
-            [
-                jnp.where(mine_first, live_grad, grad_other),
-                jnp.where(mine_first, grad_other, live_grad),
-            ],
-            axis=0,
-        )
-    else:
-        w_all = lax.all_gather(w_output, "tp", axis=1, tiled=True)
-        grad_all = lax.all_gather(live_grad, "tp", axis=0, tiled=True)
-
-    def row(values):
-        return values.astype(F32)[None, :]
 
     rm = jnp.pad(
         jnp.concatenate([router, mix_weight], axis=1), ((0, 0), (0, LANES - experts - 2))
     )
-
-    attn_in, projected = norm_project(
-        tokens, row(gain_attn), row(bias_attn), (w_query, w_key, w_value)
-    )
-    heads, log_sums = [], []
-    for s in range(splits):
-        if s == splits - 1:
-            grad_blocks = pack(place_row, after(grad_all, *heads), slot_count)
-            projected = after(projected, grad_blocks)
-        o, lse = attention_forward(projected, seq_count, local_heads, s * each, each)
-        heads.append(o)
-        log_sums.append(lse)
+    norms = jnp.stack([gain_attn, bias_attn, gain_ffn, bias_ffn]).astype(F32)
+    projections = (w_query, w_key, w_value)
     if tp == 2:
-        others = [swapped(o) for o in heads]
-        all_heads = heads + others
-        weights = [(w_output, s) for s in range(splits)] + [(w_other, s) for s in range(splits)]
+        (
+            attn_in,
+            projected,
+            *heads,
+            w_other,
+            grad_all,
+            resid,
+            ffn_in,
+            chances,
+            packed,
+            grad_rows,
+            info,
+            lse,
+        ) = front(
+            tokens,
+            out_grad,
+            (*projections, w_output),
+            lengths,
+            norms,
+            rm,
+            expert_ids[None, :],
+            ep,
+            experts,
+            capacity,
+        )
+        all_heads = heads
+        heads = heads[:2]
+        log_sums = [lse[s * each : (s + 1) * each] for s in range(splits)]
+        weights = [(w_output, s) for s in range(2)] + [(w_other, s) for s in range(2)]
         wide_weights = [(w, s, each * PAIR) for w, s in weights]
     else:
+        one_hot = (expert_ids[:, None] == jnp.arange(experts)[None, :]) & live_all[:, None]
+        routed = one_hot.astype(F32)
+        slots = jnp.sum((jnp.cumsum(routed, axis=0) - routed) * routed, axis=1).astype(jnp.int32)
+        sound = live_all & (slots < capacity)
+        place = jnp.where(sound, expert_ids * capacity + slots, -1)
+        place_row = place[None, :]
+        info = jnp.broadcast_to(place[:, None], (all_rows, LANES)).astype(F32)
+        live_grad = jnp.where(shard_of(live_all)[:, None], out_grad, jnp.zeros_like(out_grad))
+        w_all = lax.all_gather(w_output, "tp", axis=1, tiled=True)
+        grad_all = lax.all_gather(live_grad, "tp", axis=0, tiled=True)
+        grad_rows = exchange(pack(place_row, grad_all, slot_count).reshape(blocks))
+        attn_in, projected = norm_project(tokens, norms[0:1], norms[1:2], projections)
+        heads, log_sums = [], []
+        for s in range(splits):
+            o, lse = attention_forward(projected, seq_count, local_heads, s * each, each)
+            heads.append(o)
+            log_sums.append(lse)
         all_heads = [lax.all_gather(jnp.concatenate(heads, axis=1), "tp", axis=1, tiled=True)]
-        weights = [(w_all, 0)]
         wide_weights = [(w_all, 0, model_width)]
-    resid, ffn_in, chances = output_norm(
-        tokens, row(gain_ffn), row(bias_ffn), rm, all_heads, weights, experts
-    )
-    grad_rows = exchange(grad_blocks.reshape(blocks))
-    sent = pack(place_row, ffn_in, slot_count).reshape(blocks)
+        resid, ffn_in, chances = output_norm(
+            tokens, norms[2:3], norms[3:4], rm, all_heads, [(w_all, 0)], experts
+        )
+        packed = pack(place_row, ffn_in, slot_count)
+
     sel = (jnp.arange(LANES) == ep_index).astype(F32)[None, :]
     (
         dense,
@@ -1102,36 +1882,35 @@
         _,
         pulls,
         dots,
+        _,
     ) = nets(
         ffn_in,
         grad_all,
-        sent,
+        packed.reshape(blocks),
         grad_rows,
         sel,
         rm,
         (w_hidden, w_return),
         (expert_in[0], expert_out[0]),
     )
-    returned = exchange(results).reshape(slot_count, model_width)
-    pulls = pulls.reshape(slot_count, model_width)
+    returned = exchange(results).reshape(-1, model_width)
+    pulls = pulls.reshape(-1, model_width)
     dots = dots[:, 0, :]
-    own = ((positions >= first_row) & (positions < first_row + shard_rows)).astype(F32)[:, None]
-
     part, *rest = ffn_pull(
-        place_col,
-        own,
+        info,
         dense_pull,
         chances,
         first_dot,
         ffn_in,
         grad_all,
         resid,
-        row(gain_ffn),
+        norms,
         rm,
         pulls,
         dots,
         wide_weights,
         experts,
+        shard_rows,
     )
     *head_parts, ffn_sums, rm_sums = rest
     if tp == 2:
@@ -1141,71 +1920,67 @@
         head_grads = [
             [local[:, s * each * PAIR : (s + 1) * each * PAIR]] for s in range(splits)
         ]
-    grad_output = halved_over_sequences(outer(part, all_heads))
-    if tp == 2:
-        grad_output = grad_output[:, :local_width] + swapped(
-            grad_output[:, local_width:].astype(BF16)
-        ).astype(F32)
-    else:
-        grad_output = lax.psum_scatter(
-            grad_output.astype(BF16), "tp", scatter_dimension=1, tiled=True
-        ).astype(F32)
-
+    out_part = outer(part, all_heads)
+    part = after(part, out_part)
     grad_hidden = over_sequences(grad_hidden)
     grad_return = over_sequences(grad_return)
 
     square, qkv = [], []
     for s in range(splits):
         if s == splits - 1:
-            weighted = combine(place_col, dense, chances, returned, experts)
+            if qkv:
+                dense, qkv[-1], head_grads[s], out_part = lax.optimization_barrier(
+                    (dense, qkv[-1], head_grads[s], out_part)
+                )
+            weighted = combine(info, dense, chances, returned, experts, capacity)
             grad_expert_in, grad_expert_out = [
                 jnp.where(lengths[0] > 0, e, 0.0) for e in (grad_expert_in, grad_expert_out)
             ]
-            projected = after(
-                projected, weighted, grad_expert_in, grad_expert_out, *(qkv[-1] if qkv else ())
+            projected, weighted, grad_expert_in, grad_expert_out = lax.optimization_barrier(
+                (projected, weighted, grad_expert_in, grad_expert_out)
             )
         grads3 = attention_backward(
             projected, heads[s], head_grads[s], log_sums[s], seq_count, local_heads, s * each
         )
         qkv.append(grads3)
-        square.append(halved_over_sequences(outer(attn_in, grads3)))
-    width = each * PAIR
-    grad_query, grad_key, grad_value = [
-        jnp.concatenate([q[:, k * width : (k + 1) * width] for q in square], axis=1)
-        for k in range(3)
-    ]
-    part = after(part, grad_hidden, grad_return)
-    ffn_sums, rm_sums = after((ffn_sums, rm_sums), *qkv[-1])
     flat = [qkv[s][k] for k in range(3) for s in range(splits)]
-    pull = partial(
-        attn_pull,
-        x=tokens,
-        r=part,
-        gain=row(gain_attn),
-        grads=flat,
-        weights=(w_query, w_key, w_value),
-    )
+    rows_kept = -(-(experts + 2) // 8) * 8
+    small = jnp.concatenate([ffn_sums, rm_sums[:rows_kept]], axis=0)
+    theirs = lax.dynamic_slice_in_dim(weighted, shard_rows - first_row, shard_rows, 0)
     if tp == 2:
-        theirs, sums_a = pull(shard_rows - first_row, shard_rows, out_type=BF16)
-        own_part, sums_b = pull(first_row, shard_rows, out_type=F32)
-        token_grad = own_part + swapped(theirs).astype(F32)
-        attn_sums = sums_a + sums_b
+        summed = shard_of(weighted).astype(F32) + swapped(theirs).astype(F32)
+        block_out = jnp.where(shard_of(live_all)[:, None], shard_of(resid) + summed, 0.0).astype(BF16)
+        part, block_out = lax.optimization_barrier((part, block_out))
+        own_part, got, square, grad_output, small = tail(
+            tokens,
+            part,
+            attn_in,
+            out_part,
+            flat,
+            small,
+            norms,
+            projections,
+            ep,
+        )
+        token_grad = own_part + got.astype(F32)
+        attn_sums = small[8 + rows_kept :]
     else:
-        whole, attn_sums = pull(jnp.zeros((), jnp.int32), all_rows, out_type=BF16)
+        whole, attn_sums = attn_pull(
+            jnp.zeros((), jnp.int32), all_rows, tokens, part, norms[0:1], flat, projections, BF16
+        )
         token_grad = lax.psum_scatter(whole, "tp", scatter_dimension=0, tiled=True).astype(F32)
-
-    if tp == 2:
-        theirs = lax.dynamic_slice_in_dim(weighted, shard_rows - first_row, shard_rows, 0)
-        summed = shard_of(weighted).astype(F32) + swapped(theirs).astype(F32)
-    else:
         summed = lax.psum_scatter(weighted, "tp", scatter_dimension=0, tiled=True).astype(F32)
-    block_out = jnp.where(shard_of(live_all)[:, None], shard_of(resid) + summed, 0.0).astype(BF16)
-
-    rows_kept = -(-(experts + 2) // 8) * 8
-    small = summed_over(
-        summed_over(jnp.concatenate([ffn_sums, rm_sums[:rows_kept]], axis=0), "tp", tp), "ep", ep
-    )
-    attn_sums = summed_over(summed_over(attn_sums, "tp", tp), "ep", ep)
+        block_out = jnp.where(shard_of(live_all)[:, None], shard_of(resid) + summed, 0.0).astype(BF16)
+        square = over_sequences(outer(attn_in, flat))
+        grad_output = lax.psum_scatter(
+            over_sequences(out_part).astype(BF16), "tp", scatter_dimension=1, tiled=True
+        ).astype(F32)
+        small = summed_over(summed_over(small, "tp", tp), "ep", ep)
+        attn_sums = summed_over(summed_over(attn_sums, "tp", tp), "ep", ep)
+    grad_hidden, grad_return, square = lax.optimization_barrier((grad_hidden, grad_return, square))
+    grad_query, grad_key, grad_value = jnp.split(square.astype(F32), 3, axis=1)
+
+
     return (
         block_out,
         token_grad,
@@ -1213,8 +1988,8 @@
         grad_key,
         grad_value,
         grad_output,
-        grad_hidden,
-        grad_return,
+        grad_hidden.astype(F32),
+        grad_return.astype(F32),
         small[8 : 8 + experts].T,
         small[8 + experts : 10 + experts].T,
         attn_sums[0],

time: 782 us -> 626 us (0.80)
  waiting for transfers between devices: 190 us -> 9.44 us
  Pallas kernels: 440 us -> 530 us
  starting transfers between devices: 56.6 us -> 9.57 us
  other arithmetic: 46 us -> 30.1 us
    ppermute x9 -> x3, waiting for transfers between devices: 121 us -> 8.72 us  [swapped(): return lax.ppermute(values, 'tp', swap)]
    pallas_call x9 -> x3, Pallas kernels: 134 us -> 234 us  [the longest x1 136 us: front(): pl.pallas_call(partial(front_kernel, peers=peers, experts=experts, half=h...]
    ppermute x22 -> x0, waiting for transfers between devices: 64.6 us -> none  [the longest x12 50.5 us: halved_over_sequences(): got = lax.ppermute(give, 'ep', [(i, i ^ step) for i in range(ep)])]
    all_to_all x2 -> x1, starting transfers between devices: 24.7 us -> 5.72 us  [exchange(): return lax.all_to_all(values, 'ep', split_axis=0, concat_axis=0, tiled=True)]
    ppermute x22 -> x0, starting transfers between devices: 16.1 us -> none  [the longest x12 9.38 us: halved_over_sequences(): got = lax.ppermute(give, 'ep', [(i, i ^ step) for i in range(ep)])]
    pallas_call x3 -> x1, Pallas kernels: 24.3 us -> 8.82 us  [outer(): pl.pallas_call(partial(outer_kernel, parts=len(rights)), grid=(rows // rb...]
    pallas_call x1, Pallas kernels: 182 us -> 195 us  [nets(): pl.pallas_call(partial(nets_kernel, peers=peers, capacity=capacity, rb=rb...]
    ppermute x9 -> x3, starting transfers between devices: 15.1 us -> 3.78 us  [swapped(): return lax.ppermute(values, 'tp', swap)]
  transfers between devices with their start and end apart: 35 -> 6, of which waited for: 21 -> 2; matrix products, arithmetic and copies ran while one was open for 6% -> 5% of each run, Pallas kernels for 32% -> 32%
where the time goes in v3:
time: 626 us; the launch traced here: 616 us
  Pallas kernels  530 us (85%)
  other arithmetic  30.1 us (5%)
  local copies, waits for them, and re-layouts  21.1 us (3%)
  between operations  15.4 us (2%)
  starting transfers between devices  9.57 us (2%)
  waiting for transfers between devices  9.44 us (2%)
    pallas_call x1, Pallas kernels, nets(): pl.pallas_call(partial(nets_kernel, peers=peers, capacity=capacity, rb=rb...  195 us
    pallas_call x1, Pallas kernels, front(): pl.pallas_call(partial(front_kernel, peers=peers, experts=experts, half=h...  136 us
    pallas_call x1, Pallas kernels, tail(): pl.pallas_call(partial(tail_kernel, groups=groups, size=size, rb=rb, smal...  87 us
    pallas_call x2, Pallas kernels, attention_backward(): pl.pallas_call(partial(attention_backward_kernel, terms=terms, bq=bq, bk=...  68.3 us
    pallas_call x1, Pallas kernels, ffn_pull(): pl.pallas_call(partial(ffn_pull_kernel, parts=len(weights), experts=exper...  24.4 us
    select_n x1, other arithmetic, on_device(): jnp.where(lengths[0] > 0, e, 0.0)  13 us
  transfers between devices with their start and end apart: 6, of which 2 were waited for; matrix products, arithmetic and copies ran while one was open for 5% of the time, Pallas kernels for 32%

profile of v3, /device:TPU:0, one launch (start us, length us, event | category | flops | bytes accessed | tf_op | source)
XLA Modules:
  0.0 615.6 jit_solution(10912844003467902886)
XLA Ops:
  7.2 0.0 reduce-scatter.3.cloned.1.call-start
  7.2 0.8 pad_maximum_fusion.1
  8.0 0.2 copy.37
  8.2 0.7 stack.15
  8.9 0.7 stack.16
  9.6 0.7 stack.17
  10.3 0.7 stack.18
  11.6 0.5 compare_convert_fusion.sel_ref
  12.1 0.8 pad.8.refs_8_.rm_ref
  12.9 0.6 maximum_convert_fusion.refs_7_.refs_11_
  13.5 135.7 %layer_front.1 = (bf16[2048,1024]{1,0:T(8,128)(2,1)}, bf16[2048,1536]{1,0:T(8,128)(2,1)}, bf16[2048,256]{1,0:T(8,128)(2,1)}, bf16[2048,256]{1,0:T(8,128)(2,1)}, ...) custom-call(bf16[2048,1024]{1,0:T(8,128)(2,1)} %refs_0_.3, ...), custom_call_target="tpu_custom_call" | custom-call | flops 671088640 | bytes 983040 | tf_op jit(solution)/shard_map/layer_front/pallas_call | solution.py:713
  149.2 194.6 %feed_forward_nets.1 = (bf16[2048,1024]{1,0:T(8,128)(2,1)}, bf16[2048,1024]{1,0:T(8,128)(2,1)}, f32[2048,128]{1,0:T(8,128)}, bf16[1024,2048]{1,0:T(8,128)(2,1)},...) custom-call(bf16[2048,1024]{1,0:T(8,128)(2,1)} %get-tuple-element.77, ...), custom_call_target="tpu_custom_call" | custom-call | flops 1610612736 | bytes 1310720 | tf_op jit(solution)/shard_map/feed_forward_nets/pallas_call | solution.py:1178
  343.7 0.0 reduce-scatter.3.cloned.1.call-update
  343.8 0.0 copy-start.19
  343.8 0.0 copy-start.1
  343.8 0.0 copy-start.2
  343.8 0.0 copy-start.13
  343.8 5.7 all-to-all-start
  349.5 0.0 reduce-scatter.5.cloned.1.call-start
  349.6 0.7 reduce-scatter.5.cloned.1.call-update
  350.3 0.0 copy-done.19
  350.3 0.0 copy-done.1
  350.3 0.0 copy-done.2
  350.4 0.0 copy-done.13
  350.4 24.4 %ffn_norm_pull.1 = (bf16[2048,1024]{1,0:T(8,128)(2,1)}, bf16[2048,256]{1,0:T(8,128)(2,1)S(1)}, bf16[2048,256]{1,0:T(8,128)(2,1)S(1)}, bf16[2048,256]{1,0:T(8,128...) custom-call(f32[2048,128]{1,0:T(8,128)S(1)} %copy-done.2, ...), custom_call_target="tpu_custom_call" | custom-call | flops 201326592 | bytes 524288 | tf_op jit(solution)/shard_map/ffn_norm_pull/pallas_call | solution.py:1310
  374.8 1.0 copy-done.8
  375.7 0.8 copy-done.14
  376.5 1.7 collective-permute-start
  378.2 0.4 collective-permute-start.1
  378.6 8.8 %outer_product.1.refs_3_ = bf16[1024,1024]{1,0:T(8,128)(2,1)} custom-call(bf16[2048,1024]{1,0:T(8,128)(2,1)} %get-tuple-element.110.left_ref.refs_1_, bf16[2048,256]{1,0:T(8,128)(2,1)} %get-tuple-element.89.refs_0_.o_ref, bf16[2048,256]{1,0:T(8,128)(2,1)} %get-tuple-element.90.refs_1_.o_ref, bf16[2048,256]{1,0:T(8,128)(2,1)} %get-tuple-element.91.refs_2_, ...), custom_call_target="tpu_custom_call" | custom-call | flops 67108864 | bytes 131072 | tf_op jit(solution)/shard_map/outer_product/pallas_call | solution.py:1368
  387.4 0.0 copy-done.18
  387.4 0.0 slice-start
  387.4 0.0 slice-start.1
  387.4 0.0 copy-start.4
  387.4 13.0 %broadcast_select_fusion = (f32[1024,2048]{1,0:T(8,128)}, f32[1024,2048]{1,0:T(8,128)}) fusion(f32[1024,2048]{1,0:T(8,128)} %get-tuple-element.107, pred[]{:T(512)S(6)} %gt.4, f32[1024,2048]{1,0:T(8,128)} %get-tuple-element.106), kind=kLoop, calls=%fused_computation.2 | loop fusion | flops 4194304 | bytes 33554432 | tf_op jit(solution)/shard_map/jit(_where)/select_n | solution.py:1937
  400.5 2.3 collective-permute-done.refs_1_
  402.7 0.0 slice-done.1
  402.8 34.0 %attention_backward.2 = (bf16[2048,256]{1,0:T(8,128)(2,1)S(1)}, bf16[2048,256]{1,0:T(8,128)(2,1)S(1)}, bf16[2048,256]{1,0:T(8,128)(2,1)S(1)}) custom-call(bf16[2048,1536]{1,0:T(8,128)(2,1)S(1)} %bitcast.22, bf16[2048,1536]{1,0:T(8,128)(2,1)S(1)} %bitcast.22, bf16[2048,1536]{1,0:T(8,128)(2,1)S(1)} %bitcast.22, bf16[2048,256]{1,0:T(8,128)(2,1)S(1)} %copy-done.4, ...), custom_call_target="tpu_custom_call" | custom-call | flops 335544320 | bytes 131072 | tf_op jit(solution)/shard_map/attention_backward/pallas_call | solution.py:254
  436.8 1.0 copy-done.5
  437.8 1.0 copy-done.6
  438.8 0.9 copy-done.7
  439.8 0.0 collective-permute-done.1.refs_1_
  439.8 0.0 all-to-all-done
  439.8 11.2 %combine_nets.1 = bf16[2048,1024]{1,0:T(8,128)(2,1)} custom-call(f32[2048,128]{1,0:T(8,128)} %get-tuple-element.76.refs_0_.info_ref, bf16[2048,1024]{1,0:T(8,128)(2,1)} %get-tuple-element.104.y_ref, f32[2048,128]{1,0:T(8,128)} %get-tuple-element.82.refs_2_.chance_ref, bf16[1024,1024]{1,0:T(8,128)(2,1)} %bitcast.7.slot_ref), custom_call_target="tpu_custom_call" | custom-call | flops 134217728 | bytes 262144 | tf_op jit(solution)/shard_map/combine_nets/pallas_call | solution.py:1445
  451.0 3.3 constant_dynamic-slice_fusion
  454.2 1.7 collective-permute-start.2
  456.0 0.9 slice.36
  456.9 0.7 pad_maximum_fusion.refs_10_
  457.6 2.8 copy-done
  460.3 34.3 %attention_backward.3 = (bf16[2048,256]{1,0:T(8,128)(2,1)S(1)}, bf16[2048,256]{1,0:T(8,128)(2,1)S(1)}, bf16[2048,256]{1,0:T(8,128)(2,1)S(1)}) custom-call(bf16[2048,1536]{1,0:T(8,128)(2,1)S(1)} %copy-done, bf16[2048,1536]{1,0:T(8,128)(2,1)S(1)} %copy-done, bf16[2048,1536]{1,0:T(8,128)(2,1)S(1)} %copy-done, bf16[2048,256]{1,0:T(8,128)(2,1)S(1)} %copy-done.3, ...), custom_call_target="tpu_custom_call" | custom-call | flops 335544320 | bytes 131072 | tf_op jit(solution)/shard_map/attention_backward/pallas_call | solution.py:254
  494.6 0.0 copy-start.10
  494.6 0.0 copy-start.11
  494.6 0.0 copy-start.12
  494.7 6.4 %collective-permute-done.2 = bf16[1024,1024]{1,0:T(8,128)(2,1)} collective-permute-done((bf16[1024,1024]{1,0:T(8,128)(2,1)}, bf16[1024,1024]{1,0:T(8,128)(2,1)}, u32[]{:S(2)}, u32[]{:S(2)}) %collective-permute-start.2) | collective-permute-done | bytes 2097184 | tf_op jit(solution)/shard_map/ppermute | solution.py:1782
  501.1 5.0 select_convert_fusion
  506.1 87.0 %backward_tail.1 = (f32[1024,1024]{1,0:T(8,128)}, bf16[1024,1024]{1,0:T(8,128)(2,1)}, f32[64,1536]{1,0:T(8,128)}, f32[64,512]{1,0:T(8,128)}, f32[40,1024]{1,0:T(8,128)}) custom-call(bf16[2048,1024]{1,0:T(8,128)(2,1)} %refs_0_.3, bf16[2048,1024]{1,0:T(8,128)(2,1)} %get-tuple-element.110.left_ref.refs_1_, bf16[2048,1024]{1,0:T(8,128)(2,1)} %get-tuple-element.111.refs_2_, ...), custom_call_target="tpu_custom_call" | custom-call | flops 201326592 | bytes 524288 | tf_op jit(solution)/shard_map/backward_tail/pallas_call | solution.py:1695
  593.1 1.4 slice_bitcast_fusion.2
  594.5 1.4 fusion.4
  595.9 1.5 slice_bitcast_fusion
  597.4 6.0 convert_add_fusion
  603.4 1.8 convert_element_type.41
  605.1 1.8 convert_element_type.42
  606.9 0.8 fusion.3
  607.7 0.7 copy.41
  (31 shorter events, 0.1 us)
Async XLA Ops:
  7.2 596.2 %reduce-scatter.3.cloned.1.call-start = ((), (), s32[]{:S(2)}) async-start(), calls=%async_computation.3 | async-start | bytes 4456448 | tf_op jit(solution)/shard_map/reduce_scatter | solution.py:1798
  343.8 6.5 %copy-start.19 = (f32[16,8,128]{2,1,0:T(8,128)S(1)}, f32[16,8,128]{2,1,0:T(8,128)}, u32[]{:S(2)}) copy-start(f32[16,8,128]{2,1,0:T(8,128)} %get-tuple-element.86) | copy-start | bytes 196612
  343.8 6.6 %copy-start.1 = (bf16[1024,128]{1,0:T(8,128)(2,1)S(1)}, bf16[1024,128]{1,0:T(8,128)(2,1)}, u32[]{:S(2)}) copy-start(bf16[1024,128]{1,0:T(8,128)(2,1)} %pad.8.refs_8_.rm_ref) | copy-start | bytes 786436
  343.8 6.6 %copy-start.2 = (f32[2048,128]{1,0:T(8,128)S(1)}, f32[2048,128]{1,0:T(8,128)}, u32[]{:S(2)}) copy-start(f32[2048,128]{1,0:T(8,128)} %get-tuple-element.76.refs_0_.info_ref) | copy-start | bytes 3145732
  343.8 6.6 %copy-start.13 = (f32[4,1024]{1,0:T(4,128)S(1)}, f32[4,1024]{1,0:T(4,128)}, u32[]{:S(2)}) copy-start(f32[4,1024]{1,0:T(4,128)} %maximum_convert_fusion.refs_7_.refs_11_) | copy-start | bytes 49156
  343.8 96.0 %all-to-all-start = ((bf16[16,64,1024]{2,1,0:T(8,128)(2,1)}), bf16[16,64,1024]{2,1,0:T(8,128)(2,1)}, u32[]{:S(2)}, u32[]{:S(2)}) async-start(bf16[16,64,1024]{2,1,0:T(8,128)(2,1)} %get-tuple-element.105), calls=%async_computation | async-start | bytes 4194304 | tf_op jit(solution)/shard_map/all_to_all | solution.py:1785
  349.5 253.8 %reduce-scatter.5.cloned.1.call-start = ((), (), s32[]{:S(2)}) async-start(), calls=%async_computation.4 | async-start | bytes 4456448 | tf_op jit(solution)/shard_map/reduce_scatter | solution.py:1798
  374.8 1.0 copy-start.8
  375.7 0.8 copy-start.14
  376.5 26.2 %collective-permute-start = (bf16[2048,256]{1,0:T(8,128)(2,1)}, bf16[2048,256]{1,0:T(8,128)(2,1)S(1)}, u32[]{:S(2)}, u32[]{:S(2)}) collective-permute-start(bf16[2048,256]{1,0:T(8,128)(2,1)} %get-tuple-element.98), channel_id=1, source_target_pairs={{0,1},{1,0},{2,3},{3,2},{4,5},{5,4},{6,7},{7,6},{8,9},{9,8},{10,11... | collective-permute-start | bytes 3145736 | tf_op jit(solution)/shard_map/ppermute | solution.py:1782
  378.2 61.6 %collective-permute-start.1 = (bf16[2048,256]{1,0:T(8,128)(2,1)}, bf16[2048,256]{1,0:T(8,128)(2,1)S(1)}, u32[]{:S(2)}, u32[]{:S(2)}) collective-permute-start(bf16[2048,256]{1,0:T(8,128)(2,1)} %get-tuple-element.103), channel_id=1, source_target_pairs={{0,1},{1,0},{2,3},{3,2},{4,5},{5,4},{6,7},{7,6},{8,9},{9,8},{10,11... | collective-permute-start | bytes 3145736 | tf_op jit(solution)/shard_map/ppermute | solution.py:1782
  378.6 8.8 %copy-start.18 = (f32[4,2,2048]{2,1,0:T(2,128)S(1)}, f32[4,2,2048]{2,1,0:T(2,128)}, u32[]{:S(2)}) copy-start(f32[4,2,2048]{2,1,0:T(2,128)} %get-tuple-element.96) | copy-start | bytes 196612
  387.4 15.3 %slice-start = ((s8[6291456]{0:T(1024)(128)(4,1)}), s8[4194304]{0:T(1024)(128)(4,1)S(1)}, s32[]{:S(2)}) async-start(s8[6291456]{0:T(1024)(128)(4,1)} %bitcast.21), calls=%async_computation.5 | async-start | bytes 8388608
  387.4 15.3 %slice-start.1 = ((s8[6291456]{0:T(1024)(128)(4,1)}), s8[2097152]{0:T(1024)(128)(4,1)S(1)}, s32[]{:S(2)}) async-start(s8[6291456]{0:T(1024)(128)(4,1)} %bitcast.21), calls=%async_computation.6 | async-start | bytes 4194304
  387.4 15.3 %copy-start.4 = (bf16[2048,256]{1,0:T(8,128)(2,1)S(1)}, bf16[2048,256]{1,0:T(8,128)(2,1)}, u32[]{:S(2)}) copy-start(bf16[2048,256]{1,0:T(8,128)(2,1)} %get-tuple-element.89.refs_0_.o_ref) | copy-start | bytes 3145732
  387.4 15.3 %copy-start.9 = (bf16[2048,256]{1,0:T(8,128)(2,1)S(1)}, bf16[2048,256]{1,0:T(8,128)(2,1)}, u32[]{:S(2)}) copy-start(bf16[2048,256]{1,0:T(8,128)(2,1)} %copy-done.8) | copy-start | bytes 3145732
  436.8 1.0 copy-start.5
  437.8 1.0 copy-start.6
  438.8 0.9 copy-start.7
  451.0 6.6 %copy-start.3 = (bf16[2048,256]{1,0:T(8,128)(2,1)S(1)}, bf16[2048,256]{1,0:T(8,128)(2,1)}, u32[]{:S(2)}) copy-start(bf16[2048,256]{1,0:T(8,128)(2,1)} %get-tuple-element.90.refs_1_.o_ref) | copy-start | bytes 3145732
  454.2 46.9 %collective-permute-start.2 = (bf16[1024,1024]{1,0:T(8,128)(2,1)}, bf16[1024,1024]{1,0:T(8,128)(2,1)}, u32[]{:S(2)}, u32[]{:S(2)}) collective-permute-start(bf16[1024,1024]{1,0:T(8,128)(2,1)} %constant_dynamic-slice_fusion), channel_id=1, source_target_pairs={{0,1},{1,0},{2,3},{3,2},{4,5},{5,4},{6,7},{7,6},{8,9},{9,8},{10,11... | collective-permute-start | bytes 6291464 | tf_op jit(solution)/shard_map/ppermute | solution.py:1782
  457.6 2.8 copy-start
  460.3 40.8 %copy-start.15 = (bf16[2048,1024]{1,0:T(8,128)(2,1)S(1)}, bf16[2048,1024]{1,0:T(8,128)(2,1)}, u32[]{:S(2)}) copy-start(bf16[2048,1024]{1,0:T(8,128)(2,1)} %combine_nets.1) | copy-start | bytes 12582916
  494.6 11.5 %copy-start.10 = (bf16[2048,256]{1,0:T(8,128)(2,1)}, bf16[2048,256]{1,0:T(8,128)(2,1)S(1)}, u32[]{:S(2)}) copy-start(bf16[2048,256]{1,0:T(8,128)(2,1)S(1)} %get-tuple-element.117.refs_5_) | copy-start | bytes 3145732
  494.6 11.4 %copy-start.11 = (bf16[2048,256]{1,0:T(8,128)(2,1)}, bf16[2048,256]{1,0:T(8,128)(2,1)S(1)}, u32[]{:S(2)}) copy-start(bf16[2048,256]{1,0:T(8,128)(2,1)S(1)} %get-tuple-element.119.refs_7_) | copy-start | bytes 3145732
  494.6 11.4 %copy-start.12 = (bf16[2048,256]{1,0:T(8,128)(2,1)}, bf16[2048,256]{1,0:T(8,128)(2,1)S(1)}, u32[]{:S(2)}) copy-start(bf16[2048,256]{1,0:T(8,128)(2,1)S(1)} %get-tuple-element.121.refs_9_) | copy-start | bytes 3145732
  597.4 9.6 %copy-start.16 = (f32[64,1536]{1,0:T(8,128)S(1)}, f32[64,1536]{1,0:T(8,128)}, u32[]{:S(2)}) copy-start(f32[64,1536]{1,0:T(8,128)} %get-tuple-element.129) | copy-start | bytes 1179652
  597.4 10.3 %copy-start.17 = (f32[64,512]{1,0:T(8,128)S(1)}, f32[64,512]{1,0:T(8,128)}, u32[]{:S(2)}) copy-start(f32[64,512]{1,0:T(8,128)} %get-tuple-element.170) | copy-start | bytes 393220
Sparse Core Ops, SparseCore 0:
  343.9 87.9 reduce-scatter.2
  436.2 71.3 reduce-scatter.4

commit v4 on v3

--- a/solution.py
+++ b/solution.py
@@ -168,6 +168,7 @@
     lse_ref,
     *refs,
     terms,
+    carried,
     bq,
     bk,
     scale,
@@ -177,7 +178,26 @@
     first = lane < HEAD_DIM
     q = q_ref[...] * jnp.asarray(scale, BF16)
     do_refs = refs[:terms]
-    dq_ref, dk_ref, dv_ref, dqt_ref, qs_ref, dos_ref, kt_ref, dl_ref = refs[terms:]
+    refs = refs[terms:]
+    if carried:
+        from_hbm, dq_ref, dk_ref, dv_ref, to_hbm, *refs, held, carry_sem = refs
+        way_in = pltpu.make_async_copy(from_hbm, held, carry_sem.at[0])
+        way_out = pltpu.make_async_copy(held, to_hbm, carry_sem.at[1])
+        at = pl.program_id(0) * pl.num_programs(1) + pl.program_id(1)
+        final = pl.num_programs(0) * pl.num_programs(1) - 1
+
+        @pl.when(at == 0)
+        def _():
+            way_in.start()
+
+        @pl.when(at == final)
+        def _():
+            way_in.wait()
+            way_out.start()
+
+    else:
+        dq_ref, dk_ref, dv_ref, *refs = refs
+    dqt_ref, qs_ref, dos_ref, kt_ref, dl_ref = refs
     do = do_refs[0][...]
     if terms == 2:
         do = (do.astype(F32) + do_refs[1][...].astype(F32)).astype(BF16)
@@ -238,13 +258,18 @@
 
     lax.fori_loop(0, nk, key_block, 0)
     dq_ref[...] = dqt_ref[...].T.astype(BF16)
-
-
-def attention_backward(proj, out, out_grads, lse, seqs, heads, first, bq=512, bk=512):
-    rows, width = out.shape
+    if carried:
+
+        @pl.when(at == final)
+        def _():
+            way_out.wait()
+
+
+def attention_backward(proj, out, out_grads, lse, seqs, heads, first, count, carry=(), bq=512, bk=512):
+    rows = out.shape[0]
     length = rows // seqs
     pairs = heads // 2
-    count = width // PAIR
+    width = count * PAIR
 
     def block(off):
         return pl.BlockSpec((length, PAIR), lambda s, p: (s, off + p))
@@ -255,6 +280,7 @@
         partial(
             attention_backward_kernel,
             terms=terms,
+            carried=bool(carry),
             bq=bq,
             bk=bk,
             scale=HEAD_DIM**-0.5,
@@ -265,23 +291,25 @@
             block(first),
             block(pairs + first),
             block(2 * pairs + first),
-            block(0),
-            pl.BlockSpec((1, 2, length), lambda s, p: (p, 0, s)),
+            block(first),
+            pl.BlockSpec((1, 2, length), lambda s, p: (first + p, 0, s)),
         ]
-        + [block(0)] * terms,
-        out_specs=[block(0)] * 3,
-        out_shape=[grad] * 3,
+        + [block(0)] * terms
+        + [pl.BlockSpec(memory_space=pl.ANY) for _ in carry],
+        out_specs=[block(0)] * 3 + [pl.BlockSpec(memory_space=pl.ANY) for _ in carry],
+        out_shape=[grad] * 3 + [jax.ShapeDtypeStruct(c.shape, c.dtype) for c in carry],
         scratch_shapes=[
             pltpu.VMEM((PAIR, length), F32),
             pltpu.VMEM((2, length, PAIR), BF16),
             pltpu.VMEM((2, length, PAIR), BF16),
             pltpu.VMEM((PAIR, length), BF16),
             pltpu.VMEM((2, length), F32),
-        ],
+        ]
+        + [s for c in carry for s in (pltpu.VMEM(c.shape, c.dtype), pltpu.SemaphoreType.DMA((2,)))],
         cost_estimate=cost(20 * rows * length * width, 16 * rows * width),
-        compiler_params=pltpu.CompilerParams(vmem_limit_bytes=40 * 1024 * 1024),
+        compiler_params=pltpu.CompilerParams(vmem_limit_bytes=52 * 1024 * 1024),
         name="attention_backward",
-    )(proj, proj, proj, out, lse, *out_grads)
+    )(proj, proj, proj, out, lse, *out_grads, *carry)
 
 
 def norm_project_kernel(x_ref, gain_ref, bias_ref, wq_ref, wk_ref, wv_ref, a_ref, p_ref):
@@ -381,7 +409,7 @@
     return dot(jnp.where(slot == place, 1.0, 0.0).astype(BF16), all_ref[...])
 
 
-def front_kernel(*refs, peers, experts, half, bq, heads_count):
+def front_kernel(*refs, peers, experts, half, heads_count):
     refs = list(refs)
 
     def take(count):
@@ -391,9 +419,9 @@
 
     x_hbm, g_hbm, wq_hbm, wk_hbm, wv_hbm, wo_hbm = take(6)
     len_ref, norms_ref, rm_ref, ids_ref = take(4)
-    a_hbm, p_hbm, heads_hbm_a, heads_hbm_b, others_hbm_a, others_hbm_b, wo2_hbm = take(7)
+    a_hbm, p_hbm, heads_hbm, others_hbm, wo2_hbm = take(5)
     gall_hbm, resid_hbm, f_hbm, chance_hbm, packed_hbm, gin_hbm, info_hbm, lse_ref = take(8)
-    xv, wq, wk, wv, wo, wo2, av, pv, vt, ha, hb, oa, ob, gv, pk, fv, rb, cb, hbuf = take(19)
+    xv, wq, wk, wv, wo, wo2, av, pv, vt, hv, ov, gv, pk, fv, rb, cb, hbuf, pa = take(18)
     place_ref, place_g_ref, info = take(3)
     (
         load_sem,
@@ -402,6 +430,8 @@
         home_sem,
         grad_sem,
         w_sem,
+        w_send,
+        w_recv,
         head_send,
         head_recv,
         z_send,
@@ -457,22 +487,20 @@
             device_id_type=mesh,
         )
 
+    def w_rows(index):
+        return wo2.at[rows_at(index, wide // peers), :]
+
+    w_copy = remote(
+        wo_hbm.at[rows_at(me, wide // peers), :], w_rows(me), w_sem.at[0], w_sem.at[1], across
+    )
+    w_copy.start()
     grad_copy = remote(g_hbm, gv.at[own_rows, :], grad_sem.at[0], grad_sem.at[1], across)
     grad_copy.start()
-    side = lax.rem(me, 2)
-    part = wide // 2
-    half_rows = pl.ds(pl.multiple_of(side * part, part), part)
-    w_copy = remote(
-        wo_hbm.at[half_rows, :], wo2.at[half_rows, :], w_sem.at[0], w_sem.at[1], across
-    )
-    w_copy.start()
-    w_pass = remote(
-        wo2.at[half_rows, :],
-        wo2.at[half_rows, :],
-        w_sem.at[2],
-        w_sem.at[3],
-        {"ep": jnp.bitwise_xor(me, 1)},
-    )
+
+    def w_pass(k):
+        return remote(
+            w_rows(me), w_rows(me), w_send.at[k], w_recv.at[k], {"ep": jnp.bitwise_xor(me, k)}
+        )
 
     for c in weight_loads[:3]:
         c.wait()
@@ -487,7 +515,7 @@
             ),
         ]
 
-    def project(i, _):
+    def project(i):
         at = rows_at(i, block)
         x_load(i).wait()
         normal, _ = normalized(xv[at, :].astype(F32))
@@ -497,33 +525,40 @@
             pv[at, j * width : (j + 1) * width] = dot(a, w[...]).astype(BF16)
         for c in a_store(i):
             c.start()
-        return 0
-
-    lax.fori_loop(0, steps, project, 0)
 
     pairs = heads_count // 2
 
-    def attend(pair, out_ref, col):
-        vt[...] = pv[:, 2 * width + pair * PAIR : 2 * width + (pair + 1) * PAIR].T
-
-        def q_step(i, _):
-            at = rows_at(i, bq)
-            q = pv[at, pair * PAIR : (pair + 1) * PAIR]
+    def head_copy(i):
+        at = rows_at(i, block)
+        return remote(hv.at[at, :], ov.at[at, :], head_send.at[i], head_recv.at[i], across)
+
+    def attend(i, _):
+        project(i)
+        at = rows_at(i, block)
+        for pair in range(pairs):
+            cols = [slice(j * width + pair * PAIR, j * width + (pair + 1) * PAIR) for j in range(3)]
+            vt[pair, :, at] = pv[at, cols[2]].T
             out, lse = attend_block(
                 i,
-                q,
-                lambda s: pv[s, width + pair * PAIR : width + (pair + 1) * PAIR],
-                lambda s: vt[:, s],
-                bq,
-                bq,
+                pv[at, cols[0]],
+                lambda s, cols=cols: pv[s, cols[1]],
+                lambda s, pair=pair: vt[pair, :, s],
+                block,
+                block,
                 HEAD_DIM**-0.5,
             )
-            out_ref[at, col : col + PAIR] = out
+            hv[at, pair * PAIR : (pair + 1) * PAIR] = out
             for h in range(2):
                 lse_ref[pair, h : h + 1, at] = lse[h]
-            return 0
-
-        lax.fori_loop(0, rows // bq, q_step, 0)
+        head_copy(i).start()
+
+        @pl.when(i == 0)
+        def _():
+            w_copy.wait()
+            for k in range(1, peers):
+                w_pass(k).start()
+
+        return 0
 
     def is_live(position):
         count = len_ref.shape[0]
@@ -565,16 +600,7 @@
     info_store = pltpu.make_async_copy(info, info_hbm, home_sem.at[4])
     info_store.start()
 
-    def head_copy(j, src, dst):
-        return remote(src, dst, head_send.at[j], head_recv.at[j], across)
-
-    first = pairs // 2
-    for pair in range(first):
-        attend(pair, ha, pair * PAIR)
-    copy_a = head_copy(0, ha, oa)
-    copy_a.start()
-    for pair in range(first, pairs - 1):
-        attend(pair, hb, (pair - first) * PAIR)
+    lax.fori_loop(0, steps - 1, attend, 0)
 
     own_grad.wait()
     grad_copy.wait()
@@ -607,49 +633,39 @@
         z_copy(k).start()
     gin_own = pltpu.make_async_copy(pk.at[rows_at(me, half), :], gin_hbm.at[me], home_sem.at[2])
     gin_own.start()
-    w_copy.wait()
-    w_pass.start()
-    attend(pairs - 1, hb, (pairs - 1 - first) * PAIR)
-    copy_b = head_copy(1, hb, ob)
-    copy_b.start()
+    lax.fori_loop(steps - 1, steps, attend, 0)
     weight_loads[3].wait()
-    w_pass.wait()
+    for k in range(1, peers):
+        w_pass(k).wait()
     stores = [
-        pltpu.make_async_copy(ha, heads_hbm_a, out_sem.at[0]),
-        pltpu.make_async_copy(hb, heads_hbm_b, out_sem.at[1]),
-        pltpu.make_async_copy(wo2, wo2_hbm, out_sem.at[2]),
+        pltpu.make_async_copy(hv, heads_hbm, out_sem.at[0]),
+        pltpu.make_async_copy(wo2, wo2_hbm, out_sem.at[1]),
     ]
     for c in stores:
         c.start()
-    copy_a.wait()
-    copy_b.wait()
-    stores_others = [
-        pltpu.make_async_copy(oa, others_hbm_a, out_sem.at[3]),
-        pltpu.make_async_copy(ob, others_hbm_b, out_sem.at[4]),
-    ]
-    for c in stores_others:
-        c.start()
     small = rb.shape[1]
-    cut = first * PAIR
 
     def norm_stores(i, slot):
         at = rows_at(i, small)
         return [
-            pltpu.make_async_copy(rb.at[slot], resid_hbm.at[at, :], out_sem.at[5 + slot]),
-            pltpu.make_async_copy(cb.at[slot], chance_hbm.at[at, :], out_sem.at[7 + slot]),
+            pltpu.make_async_copy(rb.at[slot], resid_hbm.at[at, :], out_sem.at[3 + slot]),
+            pltpu.make_async_copy(cb.at[slot], chance_hbm.at[at, :], out_sem.at[5 + slot]),
         ]
 
     def norm_step(i, _):
         at = rows_at(i, small)
         slot = lax.rem(i, 2)
+
+        @pl.when(slot == 0)
+        def _():
+            head_copy(i // 2).wait()
 
         @pl.when(i >= 2)
         def _():
             for c in norm_stores(i - 2, slot):
                 c.wait()
 
-        total = dot_nt(ha[at, :], wo[:, :cut]) + dot_nt(hb[at, :], wo[:, cut:])
-        total = total + (dot_nt(oa[at, :], wo2[:, :cut]) + dot_nt(ob[at, :], wo2[:, cut:]))
+        total = dot_nt(hv[at, :], wo[...]) + dot_nt(ov[at, :], wo2[...])
         resid = xv[at, :].astype(F32) + total
         rb[slot] = resid
         normal, _ = normalized(resid)
@@ -660,37 +676,52 @@
             c.start()
         return 0
 
+    def packed_part(i, first, size):
+        at = i * block + lax.broadcasted_iota(jnp.int32, (block, size), 0)
+        hot = jnp.where(at == place_ref[:, first : first + size], 1.0, 0.0).astype(BF16)
+        return dot(hot, fv[first : first + size, :])
+
     count = rows // small
-    lax.fori_loop(0, count, norm_step, 0)
-    f_store = pltpu.make_async_copy(fv, f_hbm, home_sem.at[3])
-    f_store.start()
+    packs = packed_hbm.shape[0] // block
+    lax.fori_loop(0, count // 2, norm_step, 0)
+
+    def pack_low(i, _):
+        pa[rows_at(i, block), :] = packed_part(i, 0, rows // 2).astype(BF16)
+        return 0
+
+    lax.fori_loop(0, packs, pack_low, 0)
+    lax.fori_loop(count // 2, count, norm_step, 0)
+    stores_late = [
+        pltpu.make_async_copy(ov, others_hbm, out_sem.at[2]),
+        pltpu.make_async_copy(fv, f_hbm, home_sem.at[3]),
+    ]
+    for c in stores_late:
+        c.start()
+
+    def packed_store(i, slot):
+        return pltpu.make_async_copy(
+            hbuf.at[slot], packed_hbm.at[rows_at(i, block), :], out_sem.at[7 + slot]
+        )
+
+    def pack_high(i, _):
+        slot = lax.rem(i, 2)
+
+        @pl.when(i >= 2)
+        def _():
+            packed_store(i - 2, slot).wait()
+
+        both = packed_part(i, rows // 2, rows // 2) + pa[rows_at(i, block), :].astype(F32)
+        hbuf[slot] = both.astype(BF16)
+        packed_store(i, slot).start()
+        return 0
+
+    lax.fori_loop(0, packs, pack_high, 0)
+    for i in range(packs - 2, packs):
+        packed_store(i, i % 2).wait()
     for i in range(count - 2, count):
         for c in norm_stores(i, i % 2):
             c.wait()
-
-    def packed_store(i, slot):
-        return pltpu.make_async_copy(
-            hbuf.at[slot], packed_hbm.at[rows_at(i, block), :], out_sem.at[5 + slot]
-        )
-
-    def pack_h(i, _):
-        slot = lax.rem(i, 2)
-
-        @pl.when(i >= 2)
-        def _():
-            packed_store(i - 2, slot).wait()
-
-        at = i * block + lax.broadcasted_iota(jnp.int32, (block, rows), 0)
-        hot = jnp.where(at == place_ref[...], 1.0, 0.0).astype(BF16)
-        hbuf[slot] = dot(hot, fv[...]).astype(BF16)
-        packed_store(i, slot).start()
-        return 0
-
-    packs = packed_hbm.shape[0] // block
-    lax.fori_loop(0, packs, pack_h, 0)
-    for i in range(packs - 2, packs):
-        packed_store(i, i % 2).wait()
-    for c in [gall_store, gin_own, f_store, info_store] + stores + stores_others:
+    for c in [gall_store, gin_own, info_store] + stores + stores_late:
         c.wait()
     for i in range(steps):
         for c in a_store(i):
@@ -699,11 +730,10 @@
         z_copy(k).wait()
 
 
-def front(x, g, weights, lengths, norms, rm, ids, peers, experts, capacity, bq=512):
+def front(x, g, weights, lengths, norms, rm, ids, peers, experts, capacity):
     rows, wide = x.shape
     width = weights[0].shape[1]
     half = capacity // 2
-    cut = width // 2
     anywhere = pl.BlockSpec(memory_space=pl.ANY)
     vmem = pl.BlockSpec(memory_space=pltpu.VMEM)
 
@@ -716,18 +746,15 @@
             peers=peers,
             experts=experts,
             half=half,
-            bq=bq,
             heads_count=width // HEAD_DIM,
         ),
         in_specs=[anywhere] * 6 + [pl.BlockSpec(memory_space=pltpu.SMEM)] + [vmem] * 3,
-        out_specs=[anywhere] * 14 + [vmem],
+        out_specs=[anywhere] * 12 + [vmem],
         out_shape=[
             like(rows, wide),
             like(rows, 3 * width),
-            like(rows, cut),
-            like(rows, cut),
-            like(rows, cut),
-            like(rows, cut),
+            like(rows, width),
+            like(rows, width),
             like(wide, width),
             like(rows, wide),
             like(rows, wide, kind=F32),
@@ -743,16 +770,17 @@
         + [
             pltpu.VMEM((rows, wide), BF16),
             pltpu.VMEM((rows, 3 * width), BF16),
-            pltpu.VMEM((PAIR, rows), BF16),
-        ]
-        + [pltpu.VMEM((rows, cut), BF16)] * 4
-        + [
+            pltpu.VMEM((width // PAIR, PAIR, rows), BF16),
+            pltpu.VMEM((rows, width), BF16),
+            pltpu.VMEM((rows, width), BF16),
+
             pltpu.VMEM((rows, wide), BF16),
             pltpu.VMEM((peers * half, wide), BF16),
             pltpu.VMEM((rows, wide), BF16),
             pltpu.VMEM((2, 256, wide), F32),
             pltpu.VMEM((2, 256, LANES), F32),
             pltpu.VMEM((2, 512, wide), BF16),
+            pltpu.VMEM((experts * capacity, wide), BF16),
             pltpu.VMEM((1, rows), jnp.int32),
             pltpu.VMEM((1, rows), jnp.int32),
             pltpu.VMEM((rows, LANES), F32),
@@ -761,9 +789,11 @@
             pltpu.SemaphoreType.DMA((rows // 512, 2)),
             pltpu.SemaphoreType.DMA((5,)),
             pltpu.SemaphoreType.DMA((2,)),
-            pltpu.SemaphoreType.DMA((4,)),
             pltpu.SemaphoreType.DMA((2,)),
-            pltpu.SemaphoreType.DMA((2,)),
+            pltpu.SemaphoreType.DMA((peers,)),
+            pltpu.SemaphoreType.DMA((peers,)),
+            pltpu.SemaphoreType.DMA((rows // 512,)),
+            pltpu.SemaphoreType.DMA((rows // 512,)),
             pltpu.SemaphoreType.DMA((peers,)),
             pltpu.SemaphoreType.DMA((peers,)),
             pltpu.SemaphoreType.DMA((9,)),
@@ -836,7 +866,8 @@
     keep,
     give,
     got,
-    stage,
+    hv,
+    pv,
     *,
     peers,
     capacity,
@@ -861,14 +892,14 @@
     weight_copies[0].start()
     weight_copies[1].start()
 
-    def load(t, slot):
+    def load(t):
         rows = pl.ds(pl.multiple_of(t * rb, rb), rb)
         return [
-            pltpu.make_async_copy(x_hbm.at[rows, :], xb.at[slot], load_sem.at[slot, 0, 0]),
-            pltpu.make_async_copy(g_hbm.at[rows, :], gb.at[slot], load_sem.at[slot, 1, 0]),
+            pltpu.make_async_copy(x_hbm.at[rows, :], xb, load_sem.at[0, 0]),
+            pltpu.make_async_copy(g_hbm.at[rows, :], gb, load_sem.at[1, 0]),
         ]
 
-    for c in load(0, 0):
+    for c in load(0):
         c.start()
 
     barrier = pltpu.get_barrier_semaphore()
@@ -933,10 +964,9 @@
     weight_copies[2].start()
     weight_copies[3].start()
 
-    def compute(slot, routed, w1_ref, w2_ref):
-        x_ref = xb.at[slot]
-        x = x_ref[...]
-        g = gb[slot].astype(F32)
+    def outputs(routed, w1_ref, w2_ref):
+        x = xb[...]
+        g = gb[...].astype(F32)
         chances = router_and_mix(dot(x, rm_ref[...]), experts)
         if routed:
             gate = jnp.sum(chances * sel_ref[...], axis=-1, keepdims=True)
@@ -947,76 +977,111 @@
         dyb[...] = dy
         dyt[...] = dy.T
         xt[...] = x.T
-        ya[...] = jnp.zeros_like(ya)
-        dxa[...] = jnp.zeros_like(dxa)
-
-        def step(f, _):
+
+        def products(f, _):
             cols = pl.ds(pl.multiple_of(f * ft, ft), ft)
             w1 = w1_ref[:, cols]
             w2 = w2_ref[:, cols]
-            act, slope = gelu_and_slope(dot(x_ref[...], w1))
+            act, slope = gelu_and_slope(dot(xb[...], w1))
             h = act.astype(BF16)
             pre_grad = (slope * dot(dyb[...], w2)).astype(BF16)
+            hv[:, cols] = h
+            pv[:, cols] = pre_grad
             ya[...] += dot_nt(h, w2)
             dxa[...] += dot_nt(pre_grad, w1)
-            a2[:, cols] += dot(dyt[...], h)
-            a1[:, cols] += dot(xt[...], pre_grad)
             return 0
 
-        lax.fori_loop(0, hidden // ft, step, 0)
-        return jnp.sum(ya[...] * gb[slot].astype(F32), axis=1, keepdims=True)
-
-    a1[...] = jnp.zeros_like(a1)
-    a2[...] = jnp.zeros_like(a2)
+        ya[...] = jnp.zeros_like(ya)
+        dxa[...] = jnp.zeros_like(dxa)
+        lax.fori_loop(0, hidden // ft, products, 0)
+
+    def row_dots():
+        return jnp.sum(ya[...] * gb[...].astype(F32), axis=1, keepdims=True)
+
+    def gradients(first, last=None):
+        wide_step = ft
+
+        def at(f):
+            return pl.ds(pl.multiple_of(f * wide_step, wide_step), wide_step)
+
+        def put(f, _):
+            a2[:, at(f)] = dot(dyt[...], hv[:, at(f)])
+            a1[:, at(f)] = dot(xt[...], pv[:, at(f)])
+            return 0
+
+        def add(f, _):
+            a2[:, at(f)] += dot(dyt[...], hv[:, at(f)])
+            a1[:, at(f)] += dot(xt[...], pv[:, at(f)])
+            return 0
+
+        def round_off(f, _):
+            wd2[:, at(f)] = (a2[:, at(f)] + dot(dyt[...], hv[:, at(f)])).astype(BF16)
+            wd1[:, at(f)] = (a1[:, at(f)] + dot(xt[...], pv[:, at(f)])).astype(BF16)
+            return 0
+
+        @pl.when(first)
+        def _():
+            lax.fori_loop(0, hidden // wide_step, put, 0)
+
+        if last is None:
+            middle = jnp.logical_not(first)
+        else:
+            middle = jnp.logical_not(first | last)
+
+            @pl.when(last)
+            def _():
+                lax.fori_loop(0, hidden // wide_step, round_off, 0)
+
+        @pl.when(middle)
+        def _():
+            lax.fori_loop(0, hidden // wide_step, add, 0)
+
     weight_copies[0].wait()
     weight_copies[1].wait()
 
     def dense_stores(t, slot):
         rows = pl.ds(pl.multiple_of(t * rb, rb), rb)
         return [
-            pltpu.make_async_copy(yb.at[slot], y_hbm.at[rows, :], store_sem.at[slot, 0, 0]),
-            pltpu.make_async_copy(dxb.at[slot], dx_hbm.at[rows, :], store_sem.at[slot, 1, 0]),
+            pltpu.make_async_copy(yb, y_hbm.at[rows, :], store_sem.at[slot, 0, 0]),
+            pltpu.make_async_copy(dxb, dx_hbm.at[rows, :], store_sem.at[slot, 1, 0]),
             pltpu.make_async_copy(dotb.at[slot], dot_hbm.at[rows, :], store_sem.at[slot, 2, 0]),
         ]
 
     def dense_step(t, _):
         slot = lax.rem(t, 2)
-        for c in load(t, slot):
+        for c in load(t):
             c.wait()
+        outputs(False, wd1, wd2)
+
+        @pl.when(t >= 1)
+        def _():
+            for c in dense_stores(t - 1, 1 - slot):
+                c.wait()
+
+        yb[...] = ya[...].astype(BF16)
+        dxb[...] = dxa[...].astype(BF16)
+        dotb[slot] = jnp.broadcast_to(row_dots(), (rb, LANES))
 
         @pl.when(t + 1 < dense_steps)
         def _():
-            for c in load(t + 1, 1 - slot):
+            for c in load(t + 1):
                 c.start()
 
-        @pl.when(t >= 2)
-        def _():
-            for c in dense_stores(t - 2, slot):
-                c.wait()
-
-        dots = compute(slot, False, wd1, wd2)
-        yb[slot] = ya[...].astype(BF16)
-        dxb[slot] = dxa[...].astype(BF16)
-        dotb[slot] = jnp.broadcast_to(dots, (rb, LANES))
         for c in dense_stores(t, slot):
             c.start()
+        gradients(t == 0, t == dense_steps - 1)
         return 0
 
     lax.fori_loop(0, dense_steps, dense_step, 0)
-    for t in range(max(0, dense_steps - 2), dense_steps):
-        for c in dense_stores(t, t % 2):
-            c.wait()
-
-    wd1[...] = a1[...].astype(BF16)
-    wd2[...] = a2[...].astype(BF16)
+    for c in dense_stores(dense_steps - 1, (dense_steps - 1) % 2):
+        c.wait()
+
     dense_grads = [
         pltpu.make_async_copy(wd1, gd1_hbm, grad_sem.at[0]),
         pltpu.make_async_copy(wd2, gd2_hbm, grad_sem.at[1]),
     ]
     for c in dense_grads:
         c.start()
-    a1[...] = jnp.zeros_like(a1)
-    a2[...] = jnp.zeros_like(a2)
     weight_copies[2].wait()
     weight_copies[3].wait()
     own_rows.wait()
@@ -1026,7 +1091,7 @@
     def first_of(p):
         if expert_steps != 4:
             return (expert_steps - 1 - p) * per
-        return jnp.where(p < 2, 2 + p, 3 - p) * per
+        return jnp.where(p == 0, 2, jnp.where(p == 1, 1, jnp.where(p == 2, 3, 0))) * per
 
     def swap_copy(p, j):
         slot = lax.rem(p, 2)
@@ -1039,76 +1104,99 @@
             device_id_type=pl.DeviceIdType.MESH,
         )
 
-    def send_back(p, size, sources):
-        base = first_of(p)
-        stores = []
+    size = half if relayed else capacity
+
+    def back_stores(p, j, source_ref):
+        to = (pull_hbm, res_hbm)[j]
+        return [
+            pltpu.make_async_copy(
+                source_ref.at[pl.ds(c * size, size), :],
+                to.at[jnp.bitwise_xor(me, first_of(p) + c)],
+                store_sem.at[0, j, c],
+            )
+            for c in range(per)
+        ]
+
+    def dot_stores(p):
+        return [
+            pltpu.make_async_copy(
+                rowb.at[c], edot_hbm.at[jnp.bitwise_xor(me, first_of(p) + c)], store_sem.at[1, 2, c]
+            )
+            for c in range(per)
+        ]
+
+    def to_peers(p, copy):
         for c in range(per):
-            source = jnp.bitwise_xor(me, base + c)
-            rows = pl.ds(c * size, size)
-            for j, to in ((0, pull_hbm), (1, res_hbm)):
-                stores.append(
-                    pltpu.make_async_copy(
-                        sources[j].at[rows, :], to.at[source], store_sem.at[0, j, c]
-                    )
-                )
-        for c in stores:
-            c.start()
-        for c in stores:
-            c.wait()
-        for c in range(per):
-            k = base + c
+            k = first_of(p) + c
 
             @pl.when(k > 0)
             def _(k=k):
-                back_copy(k).start()
-
-    def finish(p):
-        slot = lax.rem(p, 2)
-        for j in range(2):
-            swap_copy(p, j).wait()
-            stage[j] = (keep[j] + got[slot, j].astype(F32)).astype(BF16)
-        send_back(p, half, (stage.at[0], stage.at[1]))
-
-    def expert_step(p, _):
-        base = first_of(p)
-        slot = lax.rem(p, 2)
-        loads = []
+                copy(k).start()
+
+    def sum_shares(p, j):
+        swap_copy(p, j).wait()
+        stage = (dxb, yb)[j]
+        stage[: per * half, :] = (keep[j] + got[lax.rem(p, 2), j].astype(F32)).astype(BF16)
+        for c in back_stores(p, j, stage):
+            c.start()
+
+    def stored(p, j, source_ref):
+        for c in back_stores(p, j, source_ref):
+            c.wait()
+
+    def fetch(p):
         for c in range(per):
-            k = base + c
+            k = first_of(p) + c
 
             @pl.when(k > 0)
             def _(k=k):
                 row_copy(k).wait()
 
-            source = jnp.bitwise_xor(me, k)
+        for c in fetches(p):
+            c.start()
+
+    def fetches(p):
+        loads = []
+        for c in range(per):
+            source = jnp.bitwise_xor(me, first_of(p) + c)
             rows = pl.ds(c * capacity, capacity)
             loads.append(
-                pltpu.make_async_copy(in_hbm.at[source], xb.at[slot, rows, :], load_sem.at[slot, 0, c])
+                pltpu.make_async_copy(in_hbm.at[source], xb.at[rows, :], load_sem.at[0, c])
             )
             if relayed:
                 for j, src, which in ((1, gin_hbm, tp_me), (2, gin2_hbm, 1 - tp_me)):
                     at = pl.ds(pl.multiple_of(c * capacity + which * half, half), half)
                     loads.append(
                         pltpu.make_async_copy(
-                            src.at[source], gb.at[slot, at, :], load_sem.at[slot, j, c]
+                            src.at[source], gb.at[at, :], load_sem.at[j, c]
                         )
                     )
             else:
                 loads.append(
                     pltpu.make_async_copy(
-                        gin_hbm.at[source], gb.at[slot, rows, :], load_sem.at[slot, 1, c]
+                        gin_hbm.at[source], gb.at[rows, :], load_sem.at[1, c]
                     )
                 )
-        for c in loads:
+        return loads
+
+    fetch(0)
+
+    def expert_step(p, _):
+        slot = lax.rem(p, 2)
+        for c in fetches(p):
+            c.wait()
+        outputs(True, we1, we2)
+        across_dots = jnp.broadcast_to(row_dots(), (rb, LANES)).T
+        for c in range(per):
+            rowb[c] = across_dots[:8, c * capacity : (c + 1) * capacity]
+        for c in dot_stores(p):
             c.start()
-        for c in loads:
-            c.wait()
-        dots = compute(slot, True, we1, we2)
         if relayed:
 
             @pl.when(p > 0)
             def _():
-                finish(p - 1)
+                for j in range(2):
+                    sum_shares(p - 1, j)
 
             for j, total in ((0, dxa), (1, ya)):
                 for c in range(per):
@@ -1119,43 +1207,51 @@
                     give[slot, j, rows, :] = total[other, :].astype(BF16)
                 swap_copy(p, j).start()
         else:
-            yb[slot] = ya[...].astype(BF16)
-            dxb[slot] = dxa[...].astype(BF16)
-            send_back(p, capacity, (dxb.at[slot], yb.at[slot]))
-        across_dots = jnp.broadcast_to(dots, (rb, LANES)).T
-        stores = []
-        for c in range(per):
-            rowb[c] = across_dots[:8, c * capacity : (c + 1) * capacity]
-            stores.append(
-                pltpu.make_async_copy(
-                    rowb.at[c], edot_hbm.at[jnp.bitwise_xor(me, base + c)], store_sem.at[1, 2, c]
-                )
-            )
-        for c in stores:
-            c.start()
-        for c in stores:
+            dxb[...] = dxa[...].astype(BF16)
+            yb[...] = ya[...].astype(BF16)
+            for j, source_ref in ((0, dxb), (1, yb)):
+                for c in back_stores(p, j, source_ref):
+                    c.start()
+
+        @pl.when(p + 1 < expert_steps)
+        def _():
+            fetch(p + 1)
+
+        gradients(p == 0)
+        for c in dot_stores(p):
             c.wait()
-        for c in range(per):
-            k = base + c
-
-            @pl.when(k > 0)
-            def _(k=k):
-                dot_copy(k).start()
-
+        to_peers(p, dot_copy)
+        if relayed:
+
+            @pl.when(p > 0)
+            def _():
+                for j in range(2):
+                    stored(p - 1, j, (dxb, yb)[j])
+                to_peers(p - 1, back_copy)
+        else:
+            for j, source_ref in ((0, dxb), (1, yb)):
+                stored(p, j, source_ref)
+            to_peers(p, back_copy)
         return 0
 
     lax.fori_loop(0, expert_steps, expert_step, 0)
-    if relayed:
-        finish(expert_steps - 1)
     expert_grads = [
         pltpu.make_async_copy(a1, ge1_hbm, local_sem.at[0]),
         pltpu.make_async_copy(a2, ge2_hbm, local_sem.at[1]),
-        pltpu.make_async_copy(pull_hbm.at[me], pulls_hbm.at[me], home_sem.at[1]),
         pltpu.make_async_copy(edot_hbm.at[me], edots_hbm.at[me], home_sem.at[2]),
     ]
     for c in expert_grads:
         c.start()
-    for c in dense_grads + expert_grads:
+    if relayed:
+        final = expert_steps - 1
+        sum_shares(final, 0)
+        stored(final, 0, dxb)
+        to_peers(final, back_copy)
+        sum_shares(final, 1)
+        stored(final, 1, yb)
+    own_back = pltpu.make_async_copy(pull_hbm.at[me], pulls_hbm.at[me], home_sem.at[1])
+    own_back.start()
+    for c in dense_grads + expert_grads + [own_back]:
         c.wait()
     for k in range(1, peers):
         back_copy(k).wait()
@@ -1197,7 +1293,7 @@
         ],
         scratch_shapes=[pltpu.VMEM((wide, hidden), BF16)] * 4
         + [pltpu.VMEM((wide, hidden), F32)] * 2
-        + [pltpu.VMEM((2, rb, wide), BF16)] * 4
+        + [pltpu.VMEM((rb, wide), BF16)] * 4
         + [
             pltpu.VMEM((2, rb, LANES), F32),
             pltpu.VMEM((per, 8, capacity), F32),
@@ -1207,7 +1303,7 @@
             pltpu.VMEM((wide, rb), BF16),
             pltpu.VMEM((wide, rb), BF16),
             pltpu.SemaphoreType.DMA((4,)),
-            pltpu.SemaphoreType.DMA((2, 3, per)),
+            pltpu.SemaphoreType.DMA((3, per)),
             pltpu.SemaphoreType.DMA((2, 3, per)),
             pltpu.SemaphoreType.DMA((2,)),
             pltpu.SemaphoreType.DMA((3,)),
@@ -1221,11 +1317,12 @@
             pltpu.VMEM((2, *part), F32),
             pltpu.VMEM((2, 2, *part), BF16),
             pltpu.VMEM((2, 2, *part), BF16),
-            pltpu.VMEM((2, *part), BF16),
+            pltpu.VMEM((rb, hidden), BF16),
+            pltpu.VMEM((rb, hidden), BF16),
         ],
         cost_estimate=cost(24 * rows * wide * hidden, 16 * rows * wide + 24 * wide * hidden),
         compiler_params=pltpu.CompilerParams(
-            vmem_limit_bytes=BIG_VMEM, collective_id=0, has_side_effects=True
+            vmem_limit_bytes=67043328, collective_id=0, has_side_effects=True
         ),
         name="feed_forward_nets",
     )(x, g, out_rows, in_grads, sel, rm, *dense_weights, *expert_weights)
@@ -1237,7 +1334,7 @@
     return ((place >= low) & (place < low + capacity) & (lane < experts)).astype(F32)
 
 
-def ffn_pull_kernel(*refs, parts, experts, capacity, shard):
+def ffn_pull_kernel(*refs, parts, experts, capacity, shard, sent):
     (
         info_ref,
         dx_ref,
@@ -1253,12 +1350,36 @@
     ) = refs[:11]
     weights = refs[11 : 11 + parts]
     r_ref = refs[11 + parts]
-    heads = refs[12 + parts : 12 + 2 * parts]
-    sums_ref, rmg_ref = refs[12 + 2 * parts :]
+    heads = list(refs[12 + parts : 12 + 2 * parts])
+    sums_ref, rmg_ref = refs[12 + 2 * parts : 14 + 2 * parts]
+    size = info_ref.shape[0]
+    step = pl.program_id(0)
+    if sent is not None:
+        give, send_sem, recv_sem = refs[14 + 2 * parts :]
+        got = heads[sent]
+        across = {"tp": 1 - lax.axis_index("tp")}
+        mesh = pl.DeviceIdType.MESH
+
+        def share(b):
+            at = pl.ds(pl.multiple_of(b * size, size), size)
+            return pltpu.make_async_remote_copy(
+                src_ref=give.at[at, :],
+                dst_ref=got.at[at, :],
+                send_sem=send_sem.at[b],
+                recv_sem=recv_sem.at[b],
+                device_id=across,
+                device_id_type=mesh,
+            )
+
+        @pl.when(step == 0)
+        def _():
+            barrier = pltpu.get_barrier_semaphore()
+            pl.semaphore_signal(barrier, inc=1, device_id=across, device_id_type=mesh)
+            pl.semaphore_wait(barrier, 1)
+
     place = info_ref[:, 0:1].astype(jnp.int32)
     here = info_ref[:, 1:2].astype(jnp.int32)
-    size = info_ref.shape[0]
-    row = pl.program_id(0) * size + lax.broadcasted_iota(jnp.int32, (size, 1), 0)
+    row = step * size + lax.broadcasted_iota(jnp.int32, (size, 1), 0)
     row = row - lax.axis_index("tp") * shard
     own = ((row >= 0) & (row < shard)).astype(F32)
     chances = chance_ref[...]
@@ -1285,8 +1406,13 @@
     r = norm_pull(grad, normal, rstd, gain_ref[2:3, :]) + own * g_ref[...].astype(F32)
     r = r.astype(BF16)
     r_ref[...] = r
-    for h, w in zip(heads, weights):
-        h[...] = dot(r, w[...]).astype(BF16)
+    if sent is not None:
+        at = pl.ds(pl.multiple_of(step * size, size), size)
+        give[at, :] = dot(r, weights[sent][...]).astype(BF16)
+        share(step).start()
+    for j, (h, w) in enumerate(zip(heads, weights)):
+        if j != sent:
+            h[...] = dot(r, w[...]).astype(BF16)
 
     @pl.when(pl.program_id(0) == 0)
     def _():
@@ -1296,20 +1422,57 @@
     sums_ref[0:1, :] += jnp.sum(grad * normal, axis=0, keepdims=True)
     sums_ref[1:2, :] += jnp.sum(grad, axis=0, keepdims=True)
     rmg_ref[...] += dot(low.T, f_ref[...])
+    if sent is not None:
+
+        @pl.when(step == pl.num_programs(0) - 1)
+        def _():
+            for b in range(give.shape[0] // size):
+                share(b).wait()
 
 
 def ffn_pull(
-    info, dx, chances, first, f, g, resid, gain, rm, slot_rows, dots, weights, experts, shard, rb=256
+    info,
+    dx,
+    chances,
+    first,
+    f,
+    g,
+    resid,
+    gain,
+    rm,
+    slot_rows,
+    dots,
+    weights,
+    experts,
+    shard,
+    sent=None,
+    rb=256,
 ):
     rows, wide = dx.shape
     capacity = dots.shape[1]
     dots = jnp.pad(dots, ((0, LANES - experts), (0, 0)))
     block = pl.BlockSpec((rb, wide), lambda i: (i, 0))
     narrow = pl.BlockSpec((rb, LANES), lambda i: (i, 0))
-    head_specs = [pl.BlockSpec((rb, size), lambda i: (i, 0)) for _, _, size in weights]
+    head_specs = [
+        pl.BlockSpec(memory_space=pl.ANY) if j == sent else pl.BlockSpec((rb, size), lambda i: (i, 0))
+        for j, (_, _, size) in enumerate(weights)
+    ]
+    scratch, extra = [], {}
+    if sent is not None:
+        scratch = [
+            pltpu.VMEM((rows, weights[sent][2]), BF16),
+            pltpu.SemaphoreType.DMA((rows // rb,)),
+            pltpu.SemaphoreType.DMA((rows // rb,)),
+        ]
+        extra = dict(collective_id=3, has_side_effects=True)
     return pl.pallas_call(
         partial(
-            ffn_pull_kernel, parts=len(weights), experts=experts, capacity=capacity, shard=shard
+            ffn_pull_kernel,
+            parts=len(weights),
+            experts=experts,
+            capacity=capacity,
+            shard=shard,
+            sent=sent,
         ),
         grid=(rows // rb,),
         in_specs=[narrow, block, narrow, narrow, block, block, block]
@@ -1323,8 +1486,9 @@
         out_shape=[jax.ShapeDtypeStruct((rows, wide), BF16)]
         + [jax.ShapeDtypeStruct((rows, size), BF16) for _, _, size in weights]
         + [jax.ShapeDtypeStruct((8, wide), F32), jax.ShapeDtypeStruct((LANES, wide), F32)],
+        scratch_shapes=scratch,
         cost_estimate=cost(6 * rows * wide * wide, 16 * rows * wide),
-        compiler_params=pltpu.CompilerParams(vmem_limit_bytes=48 * 1024 * 1024),
+        compiler_params=pltpu.CompilerParams(vmem_limit_bytes=48 * 1024 * 1024, **extra),
         name="ffn_norm_pull",
     )(
         info,
@@ -1459,9 +1623,10 @@
 
 
 class Halving:
-    def __init__(self, total, gives, gots, send, recv, me, size):
+    def __init__(self, total, gives, gots, send, recv, me, size, order):
         self.total, self.gives, self.gots = total, gives, gots
         self.send, self.recv, self.me, self.size = send, recv, me, size
+        self.order = order
         self.rows = total.shape[0] // size
 
     def block(self, index):
@@ -1473,24 +1638,37 @@
             dst_ref=self.gots[s],
             send_sem=self.send.at[s],
             recv_sem=self.recv.at[s],
-            device_id={"ep": jnp.bitwise_xor(self.me, 1 << s)},
+            device_id={"ep": jnp.bitwise_xor(self.me, 1 << self.order[s])},
             device_id_type=pl.DeviceIdType.MESH,
         )
 
+    def halves(self, s):
+        place = sum(1 for b in self.order[s:] if b < self.order[s])
+        low = (1 << place) - 1
+        return [((i >> place) << (place + 1) | (i & low)) for i in range(self.size >> (s + 1))], 1 << place
+
     def bit(self, s):
-        return lax.rem(lax.div(self.me, 1 << s), 2)
+        return lax.rem(lax.div(self.me, 1 << self.order[s]), 2)
 
     def start(self, s):
-        for i in range(self.size >> (s + 1)):
-            at = slice(i * self.rows, (i + 1) * self.rows)
-            self.gives[s][at, :] = self.total[self.block(2 * i + 1 - self.bit(s)), :].astype(BF16)
+        places, step = self.halves(s)
+        for i, at in enumerate(places):
+            rows = slice(i * self.rows, (i + 1) * self.rows)
+            self.gives[s][rows, :] = self.total[self.block(at + (1 - self.bit(s)) * step), :].astype(BF16)
         self.copy(s).start()
 
     def finish(self, s):
         self.copy(s).wait()
-        for i in range(self.size >> (s + 1)):
-            at = slice(i * self.rows, (i + 1) * self.rows)
-            self.total[at, :] = self.total[self.block(2 * i + self.bit(s)), :] + self.gots[s][at, :].astype(F32)
+        places, step = self.halves(s)
+        for i, at in enumerate(places):
+            rows = slice(i * self.rows, (i + 1) * self.rows)
+            kept = self.total[self.block(at + self.bit(s) * step), :]
+            self.total[rows, :] = kept + self.gots[s][rows, :].astype(F32)
+
+    def step(self, s):
+        self.finish(s)
+        if s + 1 < len(self.order):
+            self.start(s + 1)
 
 
 def tail_kernel(*refs, groups, size, rb, small_rows):
@@ -1508,10 +1686,11 @@
     own_hbm, got_hbm, square_ref, outsum_ref, total_ref = take(5)
     xv, rv, av = take(3)
     grads = take(3 * groups)
-    gov, acc, goacc, give_rows, own_buf = take(5)
+    gov, acc_a, acc_b, goacc, give_rows, own_buf = take(6)
     steps = size.bit_length() - 1
     hops = steps + 1
     gives, gots = take(steps), take(steps)
+    gives_b, gots_b = take(steps), take(steps)
     go_gives, go_gots = take(steps), take(steps)
     small_gives, small_gots = take(hops), take(hops)
     (
@@ -1521,6 +1700,8 @@
         row_recv,
         half_send,
         half_recv,
+        half_send_b,
+        half_recv_b,
         go_send,
         go_recv,
         small_send,
@@ -1535,15 +1716,25 @@
     shard = rows // 2
     count = shard // rb
 
-    sources = [x_hbm, r_hbm, *grads_hbm, a_hbm, out_hbm]
-    targets = [xv, rv, *grads, av, gov]
-    loads = [
-        pltpu.make_async_copy(src, dst, load_sem.at[j])
-        for j, (src, dst) in enumerate(zip(sources, targets))
-    ]
-    loads[-1].start()
-    for c in loads[:-1]:
+    out_load = pltpu.make_async_copy(out_hbm, gov, load_sem.at[0, 0])
+    a_load = pltpu.make_async_copy(a_hbm, av, load_sem.at[1, 0])
+
+    def loads(which, line):
+        at = pl.ds(pl.multiple_of(which * shard, shard), shard)
+        return [
+            pltpu.make_async_copy(
+                src.at[at, :], dst.at[at, :], load_sem.at[line, j + 1]
+            )
+            for j, (src, dst) in enumerate(zip([x_hbm, r_hbm, *grads_hbm], [xv, rv, *grads]))
+        ]
+
+    theirs_loads, own_loads = loads(1 - tp_me, 0), loads(tp_me, 1)
+    for c in theirs_loads:
         c.start()
+    out_load.start()
+    for c in own_loads:
+        c.start()
+    a_load.start()
 
     barrier = pltpu.get_barrier_semaphore()
     mesh = pl.DeviceIdType.MESH
@@ -1554,13 +1745,15 @@
         )
     pl.semaphore_wait(barrier, hops)
 
-    qkv = Halving(acc, gives, gots, half_send, half_recv, me, size)
-    go = Halving(goacc, go_gives, go_gots, go_send, go_recv, me, size)
-
-    loads[-1].wait()
-    goacc[...] = gov[...].astype(F32)
-    go.start(0)
-    for c in loads[:-2]:
+    order = list(range(steps))
+    other_order = [0, 2, 1] + order[3:] if steps > 2 else order
+    qkv = [
+        Halving(acc_a, gives, gots, half_send, half_recv, me, size, order),
+        Halving(acc_b, gives_b, gots_b, half_send_b, half_recv_b, me, size, other_order),
+    ]
+    go = Halving(goacc, go_gives, go_gots, go_send, go_recv, me, size, order)
+
+    for c in theirs_loads:
         c.wait()
 
     total_ref[:small_rows, :] = small_ref[...]
@@ -1598,44 +1791,32 @@
         row_copy(b).start()
         return 0
 
-    lax.fori_loop(0, count, theirs, 0)
-    go.finish(0)
-    go.start(1)
-
-    loads[-2].wait()
-    acc[...] = jnp.zeros_like(acc)
+    lax.fori_loop(0, count // 2, theirs, 0)
+    out_load.wait()
+    goacc[...] = gov[...].astype(F32)
+    go.start(0)
+    for c in own_loads + [a_load]:
+        c.wait()
+    cut = len(grads) // 2
+    for acc in (acc_a, acc_b):
+        acc[...] = jnp.zeros_like(acc)
 
     def outer_step(b, _):
         at = pl.ds(pl.multiple_of(b * 512, 512), 512)
         left = av[at, :].T
-        col = 0
-        for g in grads:
-            width = g.shape[1]
-            acc[:, col : col + width] += dot(left, g[at, :])
-            col += width
+        for acc, some in ((acc_a, grads[:cut]), (acc_b, grads[cut:])):
+            col = 0
+            for g in some:
+                width = g.shape[1]
+                acc[:, col : col + width] += dot(left, g[at, :])
+                col += width
         return 0
 
     lax.fori_loop(0, rows // 512, outer_step, 0)
-    qkv.start(0)
-    for s in range(1, steps):
-        go.finish(s)
-        if s + 1 < steps:
-            go.start(s + 1)
-        if s == 1:
-            qkv.finish(0)
-            qkv.start(1)
-
-    own_width = outsum_ref.shape[1]
-    out_give[...] = goacc[: goacc.shape[0] // size, own_width:].astype(BF16)
-    out_copy = pltpu.make_async_remote_copy(
-        src_ref=out_give,
-        dst_ref=out_got,
-        send_sem=out_sem.at[0],
-        recv_sem=out_sem.at[1],
-        device_id={"tp": 1 - tp_me},
-        device_id_type=mesh,
-    )
-    out_copy.start()
+    for chain in qkv:
+        chain.start(0)
+    go.step(0)
+    lax.fori_loop(count // 2, count, theirs, 0)
 
     def own_copy(b):
         at = pl.ds(pl.multiple_of(b * rb, rb), rb)
@@ -1647,7 +1828,11 @@
         own_copy(b).start()
         return 0
 
-    lax.fori_loop(0, count, own_step, 0)
+    for chain in qkv:
+        chain.step(0)
+    lax.fori_loop(0, count // 2, own_step, 0)
+    go.step(1)
+    lax.fori_loop(count // 2, count, own_step, 0)
 
     def small_copy(s):
         peer = {"tp": 1 - tp_me} if s == 0 else {"ep": jnp.bitwise_xor(me, 1 << (s - 1))}
@@ -1663,13 +1848,29 @@
     for s in range(hops):
         small_gives[s][...] = total_ref[...]
         small_copy(s).start()
+        if s + 2 < steps:
+            go.step(s + 2)
         if 0 < s < steps:
-            qkv.finish(s)
-            if s + 1 < steps:
-                qkv.start(s + 1)
+            for chain in qkv:
+                chain.step(s)
         small_copy(s).wait()
         total_ref[...] += small_gots[s][...]
-    square_ref[...] = acc[: acc.shape[0] // size, :]
+        if s == max(0, steps - 3):
+            own_width = outsum_ref.shape[1]
+            out_give[...] = goacc[: goacc.shape[0] // size, own_width:].astype(BF16)
+            out_copy = pltpu.make_async_remote_copy(
+                src_ref=out_give,
+                dst_ref=out_got,
+                send_sem=out_sem.at[0],
+                recv_sem=out_sem.at[1],
+                device_id={"tp": 1 - tp_me},
+                device_id_type=mesh,
+            )
+            out_copy.start()
+    col = 0
+    for acc in (acc_a, acc_b):
+        square_ref[:, col : col + acc.shape[1]] = acc[: acc.shape[0] // size, :]
+        col += acc.shape[1]
     out_copy.wait()
     outsum_ref[...] = goacc[: goacc.shape[0] // size, :own_width] + out_got[...].astype(F32)
     for b in range(count):
@@ -1707,21 +1908,22 @@
         + [pltpu.VMEM(g.shape, BF16) for g in grads]
         + [
             pltpu.VMEM((wide, out_width), BF16),
-            pltpu.VMEM((wide, total), F32),
+            pltpu.VMEM((wide, total // 2), F32),
+            pltpu.VMEM((wide, total // 2), F32),
             pltpu.VMEM((wide, out_width), F32),
             pltpu.VMEM((shard, wide), BF16),
             pltpu.VMEM((shard, wide), F32),
         ]
-        + halves(total) * 2
+        + halves(total // 2) * 4
         + halves(out_width) * 2
         + [pltpu.VMEM((small_rows + 8, wide), F32)] * (2 * (steps + 1))
         + [
-            pltpu.SemaphoreType.DMA((5 + 3 * groups,)),
+            pltpu.SemaphoreType.DMA((2, 3 + 3 * groups)),
             pltpu.SemaphoreType.DMA((shard // rb,)),
             pltpu.SemaphoreType.DMA((shard // rb,)),
             pltpu.SemaphoreType.DMA((shard // rb,)),
         ]
-        + [pltpu.SemaphoreType.DMA((steps,))] * 4
+        + [pltpu.SemaphoreType.DMA((steps,))] * 6
         + [pltpu.SemaphoreType.DMA((steps + 1,))] * 2
         + [
             pltpu.SemaphoreType.DMA((2,)),
@@ -1734,6 +1936,60 @@
         ),
         name="backward_tail",
     )(x, r, a, out_part, *grads, small, gain, *weights)
+
+
+def results_kernel(
+    own_ref,
+    got_ref,
+    square_ref,
+    small_ref,
+    h_ref,
+    r_ref,
+    token_ref,
+    q_ref,
+    k_ref,
+    v_ref,
+    gh_ref,
+    gr_ref,
+    router_ref,
+    mix_ref,
+    gain1_ref,
+    bias1_ref,
+    gain2_ref,
+    bias2_ref,
+):
+    token_ref[...] = own_ref[...] + got_ref[...].astype(F32)
+
+    @pl.when(pl.program_id(0) == 0)
+    def _():
+        width = q_ref.shape[1]
+        for j, ref in enumerate((q_ref, k_ref, v_ref)):
+            ref[...] = square_ref[:, j * width : (j + 1) * width]
+        gh_ref[...] = h_ref[...].astype(F32)
+        gr_ref[...] = r_ref[...].astype(F32)
+        experts = router_ref.shape[0]
+        router_ref[...] = small_ref[8 : 8 + experts, :]
+        mix_ref[...] = small_ref[8 + experts : 10 + experts, :]
+        end = small_ref.shape[0] - 8
+        for ref, at in ((gain1_ref, end), (bias1_ref, end + 1), (gain2_ref, 0), (bias2_ref, 1)):
+            ref[...] = small_ref[at : at + 1, :]
+
+
+def results(own, got, square, small, gh, gr, experts, rb=256):
+    rows, wide = own.shape
+    kept, width = square.shape[0], square.shape[1] // 3
+    block = pl.BlockSpec((rb, wide), lambda i: (i, 0))
+    shapes = [(kept, width)] * 3 + [gh.shape, gr.shape, (experts, wide), (2, wide)] + [(1, wide)] * 4
+    return pl.pallas_call(
+        results_kernel,
+        grid=(rows // rb,),
+        in_specs=[block, block] + [resident(v.shape) for v in (square, small, gh, gr)],
+        out_specs=[block] + [resident(s) for s in shapes],
+        out_shape=[jax.ShapeDtypeStruct((rows, wide), F32)]
+        + [jax.ShapeDtypeStruct(s, F32) for s in shapes],
+        cost_estimate=cost(rows * wide, 12 * rows * wide),
+        name="results",
+    )(own, got, square, small, gh, gr)
 
 
 def on_device(
@@ -1815,7 +2071,8 @@
         (
             attn_in,
             projected,
-            *heads,
+            heads,
+            others,
             w_other,
             grad_all,
             resid,
@@ -1837,11 +2094,8 @@
             experts,
             capacity,
         )
-        all_heads = heads
-        heads = heads[:2]
-        log_sums = [lse[s * each : (s + 1) * each] for s in range(splits)]
-        weights = [(w_output, s) for s in range(2)] + [(w_other, s) for s in range(2)]
-        wide_weights = [(w, s, each * PAIR) for w, s in weights]
+        all_heads = [heads, others]
+        wide_weights = [(w, s, each * PAIR) for w in (w_output, w_other) for s in range(splits)]
     else:
         one_hot = (expert_ids[:, None] == jnp.arange(experts)[None, :]) & live_all[:, None]
         routed = one_hot.astype(F32)
@@ -1855,12 +2109,8 @@
         grad_all = lax.all_gather(live_grad, "tp", axis=0, tiled=True)
         grad_rows = exchange(pack(place_row, grad_all, slot_count).reshape(blocks))
         attn_in, projected = norm_project(tokens, norms[0:1], norms[1:2], projections)
-        heads, log_sums = [], []
-        for s in range(splits):
-            o, lse = attention_forward(projected, seq_count, local_heads, s * each, each)
-            heads.append(o)
-            log_sums.append(lse)
-        all_heads = [lax.all_gather(jnp.concatenate(heads, axis=1), "tp", axis=1, tiled=True)]
+        heads, lse = attention_forward(projected, seq_count, local_heads, 0, pairs)
+        all_heads = [lax.all_gather(heads, "tp", axis=1, tiled=True)]
         wide_weights = [(w_all, 0, model_width)]
         resid, ffn_in, chances = output_norm(
             tokens, norms[2:3], norms[3:4], rm, all_heads, [(w_all, 0)], experts
@@ -1877,7 +2127,7 @@
         grad_expert_in,
         grad_expert_out,
         _,
-        results,
+        sums_back,
         _,
         _,
         pulls,
@@ -1893,7 +2143,7 @@
         (w_hidden, w_return),
         (expert_in[0], expert_out[0]),
     )
-    returned = exchange(results).reshape(-1, model_width)
+    returned = exchange(sums_back).reshape(-1, model_width)
     pulls = pulls.reshape(-1, model_width)
     dots = dots[:, 0, :]
     part, *rest = ffn_pull(
@@ -1911,10 +2161,14 @@
         wide_weights,
         experts,
         shard_rows,
+        sent=splits if tp == 2 else None,
     )
     *head_parts, ffn_sums, rm_sums = rest
     if tp == 2:
-        head_grads = [[m, swapped(o)] for m, o in zip(head_parts[:splits], head_parts[splits:])]
+        head_grads = [
+            [m, o if s == 0 else swapped(o)]
+            for s, (m, o) in enumerate(zip(head_parts[:splits], head_parts[splits:]))
+        ]
     else:
         local = lax.psum_scatter(head_parts[0], "tp", scatter_dimension=1, tiled=True)
         head_grads = [
@@ -1925,7 +2179,8 @@
     grad_hidden = over_sequences(grad_hidden)
     grad_return = over_sequences(grad_return)
 
-    square, qkv = [], []
+    qkv = []
+    expert_grads = [grad_expert_in, grad_expert_out]
     for s in range(splits):
         if s == splits - 1:
             if qkv:
@@ -1933,14 +2188,17 @@
                     (dense, qkv[-1], head_grads[s], out_part)
                 )
             weighted = combine(info, dense, chances, returned, experts, capacity)
-            grad_expert_in, grad_expert_out = [
-                jnp.where(lengths[0] > 0, e, 0.0) for e in (grad_expert_in, grad_expert_out)
-            ]
-            projected, weighted, grad_expert_in, grad_expert_out = lax.optimization_barrier(
-                (projected, weighted, grad_expert_in, grad_expert_out)
-            )
-        grads3 = attention_backward(
-            projected, heads[s], head_grads[s], log_sums[s], seq_count, local_heads, s * each
+            projected, weighted = lax.optimization_barrier((projected, weighted))
+        *grads3, expert_grads[s] = attention_backward(
+            projected,
+            heads,
+            head_grads[s],
+            lse,
+            seq_count,
+            local_heads,
+            s * each,
+            each,
+            (expert_grads[s],),
         )
         qkv.append(grads3)
     flat = [qkv[s][k] for k in range(3) for s in range(splits)]
@@ -1962,8 +2220,18 @@
             projections,
             ep,
         )
-        token_grad = own_part + got.astype(F32)
-        attn_sums = small[8 + rows_kept :]
+        (
+            token_grad,
+            grad_query,
+            grad_key,
+            grad_value,
+            grad_hidden,
+            grad_return,
+            grad_router,
+            grad_mix,
+            *vectors,
+        ) = results(own_part, got, square, small, grad_hidden, grad_return, experts)
+        vectors = [v[0] for v in vectors]
     else:
         whole, attn_sums = attn_pull(
             jnp.zeros((), jnp.int32), all_rows, tokens, part, norms[0:1], flat, projections, BF16
@@ -1977,10 +2245,10 @@
         ).astype(F32)
         small = summed_over(summed_over(small, "tp", tp), "ep", ep)
         attn_sums = summed_over(summed_over(attn_sums, "tp", tp), "ep", ep)
-    grad_hidden, grad_return, square = lax.optimization_barrier((grad_hidden, grad_return, square))
-    grad_query, grad_key, grad_value = jnp.split(square.astype(F32), 3, axis=1)
-
-
+        grad_query, grad_key, grad_value = jnp.split(square.astype(F32), 3, axis=1)
+        grad_hidden, grad_return = grad_hidden.astype(F32), grad_return.astype(F32)
+        grad_router, grad_mix = small[8 : 8 + experts], small[8 + experts : 10 + experts]
+        vectors = [attn_sums[0], attn_sums[1], small[0], small[1]]
     return (
         block_out,
         token_grad,
@@ -1988,16 +2256,13 @@
         grad_key,
         grad_value,
         grad_output,
-        grad_hidden.astype(F32),
-        grad_return.astype(F32),
-        small[8 : 8 + experts].T,
-        small[8 + experts : 10 + experts].T,
-        attn_sums[0],
-        attn_sums[1],
-        small[0],
-        small[1],
-        grad_expert_in[None],
-        grad_expert_out[None],
+        grad_hidden,
+        grad_return,
+        grad_router.T,
+        grad_mix.T,
+        *vectors,
+        expert_grads[0][None],
+        expert_grads[1][None],
     )
 
 

time: 626 us -> 568 us (0.907)
  other arithmetic: 30.1 us -> 7.54 us
  Pallas kernels: 530 us -> 510 us
  local copies, waits for them, and re-layouts: 21.1 us -> 10.2 us
    pallas_call x1, Pallas kernels: 136 us -> 112 us  [front(): pl.pallas_call(partial(front_kernel, peers=peers, experts=experts, half=h...]
    select_n x1 -> x0, other arithmetic: 13 us -> none  [on_device(): jnp.where(lengths[0] > 0, e, 0.0)]
    pallas_call x2 -> x3, Pallas kernels: 68.3 us -> 78.6 us  [the longest x2 72.5 us: attention_backward(): pl.pallas_call(partial(attention_backward_kernel, terms=terms, carried=bo...]
    pallas_call x1, Pallas kernels: 24.4 us -> 32.9 us  [ffn_pull(): pl.pallas_call(partial(ffn_pull_kernel, parts=len(weights), experts=exper...]
    pallas_call x1, Pallas kernels: 195 us -> 187 us  [nets(): pl.pallas_call(partial(nets_kernel, peers=peers, capacity=capacity, rb=rb...]
    pallas_call x1, Pallas kernels: 87 us -> 80.5 us  [tail(): pl.pallas_call(partial(tail_kernel, groups=groups, size=size, rb=rb, smal...]
  transfers between devices with their start and end apart: 6 -> 5, of which waited for: 2 -> 1; matrix products, arithmetic and copies ran while one was open for 5% -> 1% of each run, Pallas kernels for 32% -> 37%
where the time goes in v4:
time: 568 us; the launch traced here: 559 us
  Pallas kernels  510 us (90%)
  between operations  15.1 us (3%)
  local copies, waits for them, and re-layouts  10.2 us (2%)
  waiting for transfers between devices  9.04 us (2%)
  other arithmetic  7.54 us (1%)
  starting transfers between devices  6.82 us (1%)
    pallas_call x1, Pallas kernels, nets(): pl.pallas_call(partial(nets_kernel, peers=peers, capacity=capacity, rb=rb...  187 us
    pallas_call x1, Pallas kernels, front(): pl.pallas_call(partial(front_kernel, peers=peers, experts=experts, half=h...  112 us
    pallas_call x1, Pallas kernels, tail(): pl.pallas_call(partial(tail_kernel, groups=groups, size=size, rb=rb, smal...  80.5 us
    pallas_call x2, Pallas kernels, attention_backward(): pl.pallas_call(partial(attention_backward_kernel, terms=terms, carried=bo...  72.5 us
    pallas_call x1, Pallas kernels, ffn_pull(): pl.pallas_call(partial(ffn_pull_kernel, parts=len(weights), experts=exper...  32.9 us
  transfers between devices with their start and end apart: 5, of which 1 were waited for; matrix products, arithmetic and copies ran while one was open for 1% of the time, Pallas kernels for 37%

profile of v4, /device:TPU:0, one launch (start us, length us, event | category | flops | bytes accessed | tf_op | source)
XLA Modules:
  0.0 559.1 jit_solution(1518524221562548708)
XLA Ops:
  7.2 0.0 reduce-scatter.3.cloned.1.call-start
  7.2 0.8 pad_maximum_fusion.1
  8.0 0.2 copy.37
  8.2 0.7 stack.15
  8.9 0.7 stack.16
  9.6 0.7 stack.17
  10.3 0.7 stack.18
  11.6 0.5 compare_convert_fusion.sel_ref
  12.1 0.8 pad.8.refs_8_.rm_ref
  12.9 0.6 maximum_convert_fusion.refs_7_.refs_11_
  13.5 111.6 %layer_front.1 = (bf16[2048,1024]{1,0:T(8,128)(2,1)}, bf16[2048,1536]{1,0:T(8,128)(2,1)}, bf16[2048,512]{1,0:T(8,128)(2,1)}, bf16[2048,512]{1,0:T(8,128)(2,1)}, ...) custom-call(bf16[2048,1024]{1,0:T(8,128)(2,1)} %refs_0_.3, ...), custom_call_target="tpu_custom_call" | custom-call | flops 671088640 | bytes 983040 | tf_op jit(solution)/shard_map/layer_front/pallas_call | solution.py:743
  125.1 187.1 %feed_forward_nets.1 = (bf16[2048,1024]{1,0:T(8,128)(2,1)}, bf16[2048,1024]{1,0:T(8,128)(2,1)}, f32[2048,128]{1,0:T(8,128)}, bf16[1024,2048]{1,0:T(8,128)(2,1)},...) custom-call(bf16[2048,1024]{1,0:T(8,128)(2,1)} %get-tuple-element.84, ...), custom_call_target="tpu_custom_call" | custom-call | flops 1610612736 | bytes 1310720 | tf_op jit(solution)/shard_map/feed_forward_nets/pallas_call | solution.py:1274
  312.2 0.0 reduce-scatter.3.cloned.1.call-update
  312.2 0.0 copy-start.11
  312.2 0.0 copy-start
  312.3 0.0 copy-start.1
  312.3 0.0 copy-start.7
  312.3 4.7 all-to-all-start
  317.0 0.0 reduce-scatter.5.cloned.1.call-start
  317.0 0.7 reduce-scatter.5.cloned.1.call-update
  317.7 0.0 copy-done.11
  317.8 0.0 copy-done
  317.8 0.0 copy-done.1
  317.8 0.0 copy-done.7
  317.8 32.9 %ffn_norm_pull.1 = (bf16[2048,1024]{1,0:T(8,128)(2,1)}, bf16[2048,256]{1,0:T(8,128)(2,1)S(1)}, bf16[2048,256]{1,0:T(8,128)(2,1)S(1)}, bf16[2048,256]{1,0:T(8,128...) custom-call(f32[2048,128]{1,0:T(8,128)S(1)} %copy-done.1, ...), custom_call_target="tpu_custom_call" | custom-call | flops 201326592 | bytes 524288 | tf_op jit(solution)/shard_map/ffn_norm_pull/pallas_call | solution.py:1468
  350.7 0.0 copy-start.2
  350.7 1.0 copy-done.2
  351.7 0.0 copy-start.3
  351.7 1.0 copy-done.3
  352.7 0.0 copy-start.4
  352.7 1.0 copy-done.4
  353.6 0.9 collective-permute-start
  354.5 0.0 copy-start.8
  354.5 8.8 %outer_product.1.refs_3_ = bf16[1024,1024]{1,0:T(8,128)(2,1)} custom-call(bf16[2048,1024]{1,0:T(8,128)(2,1)} %get-tuple-element.114.left_ref.refs_1_, bf16[2048,512]{1,0:T(8,128)(2,1)} %get-tuple-element.96.refs_0_.o_ref, bf16[2048,512]{1,0:T(8,128)(2,1)} %get-tuple-element.97.refs_1_), custom_call_target="tpu_custom_call" | custom-call | flops 67108864 | bytes 131072 | tf_op jit(solution)/shard_map/outer_product/pallas_call | solution.py:1532
  363.3 0.0 copy-done.8
  363.3 35.8 %attention_backward.2 = (bf16[2048,256]{1,0:T(8,128)(2,1)S(1)}, bf16[2048,256]{1,0:T(8,128)(2,1)}, bf16[2048,256]{1,0:T(8,128)(2,1)}, f32[1024,2048]{1,0:T(8,128)}) custom-call(bf16[2048,1536]{1,0:T(8,128)(2,1)} %get-tuple-element.118.q_ref.k_ref.v_ref, bf16[2048,1536]{1,0:T(8,128)(2,1)} %get-tuple-element.118.q_ref.k_ref.v_ref, ...), custom_call_target="tpu_custom_call" | custom-call | flops 335544320 | bytes 131072 | tf_op jit(solution)/shard_map/attention_backward/pallas_call | solution.py:279
  399.1 0.0 copy-start.5
  399.1 1.0 copy-done.5
  400.1 0.0 collective-permute-done.refs_1_
  400.1 0.0 all-to-all-done
  400.1 11.0 %combine_nets.1 = bf16[2048,1024]{1,0:T(8,128)(2,1)} custom-call(f32[2048,128]{1,0:T(8,128)} %get-tuple-element.83.refs_0_.info_ref, bf16[2048,1024]{1,0:T(8,128)(2,1)} %get-tuple-element.110.y_ref, f32[2048,128]{1,0:T(8,128)} %get-tuple-element.89.refs_2_.chance_ref, bf16[1024,1024]{1,0:T(8,128)(2,1)} %bitcast.7.slot_ref), custom_call_target="tpu_custom_call" | custom-call | flops 134217728 | bytes 262144 | tf_op jit(solution)/shard_map/combine_nets/pallas_call | solution.py:1609
  411.1 1.9 constant_dynamic-slice_fusion
  412.9 1.2 collective-permute-start.1
  414.1 0.7 pad_maximum_fusion.refs_10_
  414.8 0.0 copy-start.9
  414.8 36.7 %attention_backward.3 = (bf16[2048,256]{1,0:T(8,128)(2,1)S(1)}, bf16[2048,256]{1,0:T(8,128)(2,1)}, bf16[2048,256]{1,0:T(8,128)(2,1)}, f32[1024,2048]{1,0:T(8,128)}) custom-call(bf16[2048,1536]{1,0:T(8,128)(2,1)} %get-tuple-element.118.q_ref.k_ref.v_ref, bf16[2048,1536]{1,0:T(8,128)(2,1)} %get-tuple-element.118.q_ref.k_ref.v_ref, ...), custom_call_target="tpu_custom_call" | custom-call | flops 335544320 | bytes 131072 | tf_op jit(solution)/shard_map/attention_backward/pallas_call | solution.py:279
  451.5 0.0 copy-start.6
  451.5 8.3 %collective-permute-done.1 = bf16[1024,1024]{1,0:T(8,128)(2,1)} collective-permute-done((bf16[1024,1024]{1,0:T(8,128)(2,1)S(1)}, bf16[1024,1024]{1,0:T(8,128)(2,1)}, u32[]{:S(2)}, u32[]{:S(2)}) %collective-permute-start.1) | collective-permute-done | bytes 2097184 | tf_op jit(solution)/shard_map/ppermute | solution.py:2038
  459.8 0.0 copy-done.9
  459.8 4.9 select_convert_fusion
  464.7 0.0 copy-done.6
  464.7 80.5 %backward_tail.1 = (f32[1024,1024]{1,0:T(8,128)}, bf16[1024,1024]{1,0:T(8,128)(2,1)}, f32[64,1536]{1,0:T(8,128)}, f32[64,512]{1,0:T(8,128)}, f32[40,1024]{1,0:T(8,128)}) custom-call(bf16[2048,1024]{1,0:T(8,128)(2,1)} %refs_0_.3, bf16[2048,1024]{1,0:T(8,128)(2,1)} %get-tuple-element.114.left_ref.refs_1_, bf16[2048,1024]{1,0:T(8,128)(2,1)} %get-tuple-element.115.refs_2_, ...), custom_call_target="tpu_custom_call" | custom-call | flops 201326592 | bytes 524288 | tf_op jit(solution)/shard_map/backward_tail/pallas_call | solution.py:1896
  545.2 0.0 copy-start.10
  545.2 0.0 reduce-scatter.3.cloned.1.call-done.h_ref
  545.3 0.0 reduce-scatter.5.cloned.1.call-done.r_ref
  545.3 6.1 %results.1 = (f32[1024,1024]{1,0:T(8,128)}, f32[64,512]{1,0:T(8,128)}, f32[64,512]{1,0:T(8,128)}, f32[64,512]{1,0:T(8,128)}, f32[64,2048]{1,0:T(8,128)}, /*index...) custom-call(f32[1024,1024]{1,0:T(8,128)} %get-tuple-element.129.own_, ...), custom_call_target="tpu_custom_call" | custom-call | flops 16384 | bytes 196608 | tf_op jit(solution)/shard_map/results/pallas_call | solution.py:1983
  551.4 0.0 copy-done.10
  551.4 0.7 copy.41
  (6 shorter events, 0.1 us)
Async XLA Ops:
  7.2 538.1 %reduce-scatter.3.cloned.1.call-start = ((), (), s32[]{:S(2)}) async-start(), calls=%async_computation.3 | async-start | bytes 4456448 | tf_op jit(solution)/shard_map/reduce_scatter | solution.py:2054
  312.2 5.5 copy-start.11
  312.2 5.5 copy-start
  312.3 5.5 copy-start.1
  312.3 5.5 copy-start.7
  312.3 87.8 %all-to-all-start = ((bf16[16,64,1024]{2,1,0:T(8,128)(2,1)}), bf16[16,64,1024]{2,1,0:T(8,128)(2,1)}, u32[]{:S(2)}, u32[]{:S(2)}) async-start(bf16[16,64,1024]{2,1,0:T(8,128)(2,1)} %get-tuple-element.111), calls=%async_computation | async-start | bytes 4194304 | tf_op jit(solution)/shard_map/all_to_all | solution.py:2041
  317.0 228.3 %reduce-scatter.5.cloned.1.call-start = ((), (), s32[]{:S(2)}) async-start(), calls=%async_computation.4 | async-start | bytes 4456448 | tf_op jit(solution)/shard_map/reduce_scatter | solution.py:2054
  350.7 1.0 copy-start.2
  351.7 1.0 copy-start.3
  352.7 1.0 copy-start.4
  353.6 46.5 %collective-permute-start = (bf16[2048,256]{1,0:T(8,128)(2,1)S(1)}, bf16[2048,256]{1,0:T(8,128)(2,1)}, u32[]{:S(2)}, u32[]{:S(2)}) collective-permute-start(bf16[2048,256]{1,0:T(8,128)(2,1)S(1)} %get-tuple-element.109), channel_id=1, source_target_pairs={{0,1},{1,0},{2,3},{3,2},{4,5},{5,4},{6,7},{7,6},{8,9},{9,8},{10,11... | collective-permute-start | bytes 3145736 | tf_op jit(solution)/shard_map/ppermute | solution.py:2038
  354.5 8.8 %copy-start.8 = (f32[4,2,2048]{2,1,0:T(2,128)S(1)}, f32[4,2,2048]{2,1,0:T(2,128)}, u32[]{:S(2)}) copy-start(f32[4,2,2048]{2,1,0:T(2,128)} %get-tuple-element.101.lse_ref) | copy-start | bytes 196612
  399.1 1.0 copy-start.5
  412.9 46.9 %collective-permute-start.1 = (bf16[1024,1024]{1,0:T(8,128)(2,1)S(1)}, bf16[1024,1024]{1,0:T(8,128)(2,1)}, u32[]{:S(2)}, u32[]{:S(2)}) collective-permute-start(bf16[1024,1024]{1,0:T(8,128)(2,1)S(1)} %constant_dynamic-slice_fusion), channel_id=1, source_target_pairs={{0,1},{1,0},{2,3},{3,2},{4,5},{5,4},{6,7},{7,6},{8,9},{9,8},{10,11... | collective-permute-start | bytes 6291464 | tf_op jit(solution)/shard_map/ppermute | solution.py:2038
  414.8 45.0 %copy-start.9 = (bf16[2048,1024]{1,0:T(8,128)(2,1)S(1)}, bf16[2048,1024]{1,0:T(8,128)(2,1)}, u32[]{:S(2)}) copy-start(bf16[2048,1024]{1,0:T(8,128)(2,1)} %combine_nets.1) | copy-start | bytes 12582916
  451.5 13.2 %copy-start.6 = (bf16[2048,256]{1,0:T(8,128)(2,1)}, bf16[2048,256]{1,0:T(8,128)(2,1)S(1)}, u32[]{:S(2)}) copy-start(bf16[2048,256]{1,0:T(8,128)(2,1)S(1)} %get-tuple-element.122.refs_5_) | copy-start | bytes 3145732
  545.2 6.2 %copy-start.10 = (f32[64,512]{1,0:T(8,128)S(1)}, f32[64,512]{1,0:T(8,128)}, u32[]{:S(2)}) copy-start(f32[64,512]{1,0:T(8,128)} %get-tuple-element.173) | copy-start | bytes 393220
Sparse Core Ops, SparseCore 0:
  312.4 86.1 reduce-scatter.2
  402.9 71.4 reduce-scatter.4

commit v5 on v4

--- a/solution.py
+++ b/solution.py
@@ -220,38 +220,43 @@
         v = v_ref[pl.ds(koff, bk), :]
         kt = kt_ref[:, pl.ds(koff, bk)]
 
-        def step(i, carry, masked):
-            dk, dv = carry
-            qoff = pl.multiple_of(i * bq, bq)
+        def tile(qoff, wide, tall, masked):
+            qoff = pl.multiple_of(qoff, wide)
+            cols = pl.ds(qoff, wide)
             if masked:
-                key_pos = koff + lax.broadcasted_iota(jnp.int32, (bk, bq), 0)
-                query_pos = qoff + lax.broadcasted_iota(jnp.int32, (bk, bq), 1)
+                key_pos = koff + lax.broadcasted_iota(jnp.int32, (tall, wide), 0)
+                query_pos = qoff + lax.broadcasted_iota(jnp.int32, (tall, wide), 1)
                 allowed = key_pos <= query_pos
-            qh = [qs_ref[h, pl.ds(qoff, bq), :] for h in range(2)]
-            dh = [dos_ref[h, pl.ds(qoff, bq), :] for h in range(2)]
-            scores = [lax.dot_general(k, x, NT, preferred_element_type=F32) for x in qh]
-            pulls = [lax.dot_general(v, x, NT, preferred_element_type=F32) for x in dh]
-            dqs = []
+            qh = [qs_ref[h, cols, :] for h in range(2)]
+            dh = [dos_ref[h, cols, :] for h in range(2)]
+            scores = [lax.dot_general(k[:tall], x, NT, preferred_element_type=F32) for x in qh]
+            pulls = [lax.dot_general(v[:tall], x, NT, preferred_element_type=F32) for x in dh]
+            dk, dv, dqs = 0.0, 0.0, []
             for h in range(2):
-                p = jnp.exp(scores[h] - lse_ref[0, h : h + 1, pl.ds(qoff, bq)])
+                p = jnp.exp(scores[h] - lse_ref[0, h : h + 1, cols])
                 if masked:
                     p = jnp.where(allowed, p, 0.0)
-                ds = (p * (pulls[h] - dl_ref[h : h + 1, pl.ds(qoff, bq)])).astype(BF16)
-                dv = dv + jnp.dot(p.astype(BF16), dh[h], preferred_element_type=F32)
-                dk = dk + jnp.dot(ds, qh[h], preferred_element_type=F32)
-                dqs.append(
-                    jnp.dot(
-                        kt[h * HEAD_DIM : (h + 1) * HEAD_DIM], ds, preferred_element_type=F32
-                    )
-                )
-            dqt_ref[:, pl.ds(qoff, bq)] += jnp.concatenate(dqs, axis=0)
+                ds = (p * (pulls[h] - dl_ref[h : h + 1, cols])).astype(BF16)
+                dv = dv + dot(p.astype(BF16), dh[h])
+                dk = dk + dot(ds, qh[h])
+                dqs.append(dot(kt[h * HEAD_DIM : (h + 1) * HEAD_DIM, :tall], ds))
+            dqt_ref[:, cols] += jnp.concatenate(dqs, axis=0)
             return dk, dv
 
-        carry = (jnp.zeros((bk, PAIR), F32), jnp.zeros((bk, PAIR), F32))
+        def step(i, carry):
+            dk, dv = tile(i * bq, bq, bk, False)
+            return carry[0] + dk, carry[1] + dv
+
+        half = bk // 2
+        dk, dv = tile(koff + half, half, bk, True)
+        dk_0, dv_0 = tile(koff, half, half, True)
+        rest = jnp.zeros((bk - half, PAIR), F32)
+        carry = (
+            dk + jnp.concatenate([dk_0, rest], axis=0),
+            dv + jnp.concatenate([dv_0, rest], axis=0),
+        )
         i0 = j * (bk // bq)
-        for d in range(bk // bq):
-            carry = step(i0 + d, carry, True)
-        dk, dv = lax.fori_loop(i0 + bk // bq, nq, lambda i, c: step(i, c, False), carry)
+        dk, dv = lax.fori_loop(i0 + bk // bq, nq, step, carry)
         dk_ref[pl.ds(koff, bk), :] = dk.astype(BF16)
         dv_ref[pl.ds(koff, bk), :] = dv.astype(BF16)
         return 0
@@ -532,34 +537,6 @@
         at = rows_at(i, block)
         return remote(hv.at[at, :], ov.at[at, :], head_send.at[i], head_recv.at[i], across)
 
-    def attend(i, _):
-        project(i)
-        at = rows_at(i, block)
-        for pair in range(pairs):
-            cols = [slice(j * width + pair * PAIR, j * width + (pair + 1) * PAIR) for j in range(3)]
-            vt[pair, :, at] = pv[at, cols[2]].T
-            out, lse = attend_block(
-                i,
-                pv[at, cols[0]],
-                lambda s, cols=cols: pv[s, cols[1]],
-                lambda s, pair=pair: vt[pair, :, s],
-                block,
-                block,
-                HEAD_DIM**-0.5,
-            )
-            hv[at, pair * PAIR : (pair + 1) * PAIR] = out
-            for h in range(2):
-                lse_ref[pair, h : h + 1, at] = lse[h]
-        head_copy(i).start()
-
-        @pl.when(i == 0)
-        def _():
-            w_copy.wait()
-            for k in range(1, peers):
-                w_pass(k).start()
-
-        return 0
-
     def is_live(position):
         count = len_ref.shape[0]
         length = rows // count
@@ -600,10 +577,8 @@
     info_store = pltpu.make_async_copy(info, info_hbm, home_sem.at[4])
     info_store.start()
 
-    lax.fori_loop(0, steps - 1, attend, 0)
-
-    own_grad.wait()
-    grad_copy.wait()
+    gall_store = pltpu.make_async_copy(gv, gall_hbm, home_sem.at[1])
+    gin_own = pltpu.make_async_copy(pk.at[rows_at(me, half), :], gin_hbm.at[me], home_sem.at[2])
 
     def mask(i, _):
         at = rows_at(i, block)
@@ -611,29 +586,58 @@
         gv[at, :] = jnp.where(live, gv[at, :], jnp.zeros((block, wide), BF16))
         return 0
 
-    lax.fori_loop(0, steps, mask, 0)
-    gall_store = pltpu.make_async_copy(gv, gall_hbm, home_sem.at[1])
-    gall_store.start()
-
     def pack_g(i, _):
         slot = i * block + lax.broadcasted_iota(jnp.int32, (block, rows), 0)
         hot = jnp.where(slot == place_g_ref[...], 1.0, 0.0).astype(BF16)
         pk[rows_at(i, block), :] = dot(hot, gv[...]).astype(BF16)
         return 0
 
-    lax.fori_loop(0, peers * half // block, pack_g, 0)
-
     def z_copy(k):
         peer = jnp.bitwise_xor(me, k)
         return remote(
             pk.at[rows_at(peer, half), :], gin_hbm.at[me], z_send.at[k], z_recv.at[k], {"ep": peer}
         )
 
-    for k in list(range(peers // 2, peers)) + list(range(1, peers // 2)):
-        z_copy(k).start()
-    gin_own = pltpu.make_async_copy(pk.at[rows_at(me, half), :], gin_hbm.at[me], home_sem.at[2])
-    gin_own.start()
-    lax.fori_loop(steps - 1, steps, attend, 0)
+    def send_gradient():
+        own_grad.wait()
+        grad_copy.wait()
+        lax.fori_loop(0, steps, mask, 0)
+        gall_store.start()
+        lax.fori_loop(0, peers * half // block, pack_g, 0)
+        for k in list(range(peers // 2, peers)) + list(range(1, peers // 2)):
+            z_copy(k).start()
+        gin_own.start()
+
+    def attend(i, _):
+        project(i)
+        at = rows_at(i, block)
+        for pair in range(pairs):
+            cols = [slice(j * width + pair * PAIR, j * width + (pair + 1) * PAIR) for j in range(3)]
+            vt[pair, :, at] = pv[at, cols[2]].T
+            out, lse = attend_block(
+                i,
+                pv[at, cols[0]],
+                lambda s, cols=cols: pv[s, cols[1]],
+                lambda s, pair=pair: vt[pair, :, s],
+                block,
+                block,
+                HEAD_DIM**-0.5,
+            )
+            hv[at, pair * PAIR : (pair + 1) * PAIR] = out
+            for h in range(2):
+                lse_ref[pair, h : h + 1, at] = lse[h]
+        head_copy(i).start()
+
+        @pl.when(i == 0)
+        def _():
+            w_copy.wait()
+            for k in range(1, peers):
+                w_pass(k).start()
+
+        pl.when(i == steps - 2)(send_gradient)
+        return 0
+
+    lax.fori_loop(0, steps, attend, 0)
     weight_loads[3].wait()
     for k in range(1, peers):
         w_pass(k).wait()
@@ -1334,7 +1338,7 @@
     return ((place >= low) & (place < low + capacity) & (lane < experts)).astype(F32)
 
 
-def ffn_pull_kernel(*refs, parts, experts, capacity, shard, sent):
+def ffn_pull_kernel(*refs, parts, experts, capacity, shard, sent, outs):
     (
         info_ref,
         dx_ref,
@@ -1348,14 +1352,19 @@
         slot_ref,
         dots_ref,
     ) = refs[:11]
-    weights = refs[11 : 11 + parts]
-    r_ref = refs[11 + parts]
-    heads = list(refs[12 + parts : 12 + 2 * parts])
-    sums_ref, rmg_ref = refs[12 + 2 * parts : 14 + 2 * parts]
+    heads_out = refs[11 : 11 + outs]
+    refs = refs[11 + outs :]
+    weights = refs[:parts]
+    r_ref = refs[parts]
+    heads = list(refs[1 + parts : 1 + 2 * parts])
+    sums_ref, rmg_ref, outer_ref, outer_acc = (
+        *refs[1 + 2 * parts : 4 + 2 * parts],
+        refs[4 + 2 * parts],
+    )
     size = info_ref.shape[0]
     step = pl.program_id(0)
     if sent is not None:
-        give, send_sem, recv_sem = refs[14 + 2 * parts :]
+        give, send_sem, recv_sem = refs[5 + 2 * parts :]
         got = heads[sent]
         across = {"tp": 1 - lax.axis_index("tp")}
         mesh = pl.DeviceIdType.MESH
@@ -1418,10 +1427,21 @@
     def _():
         sums_ref[...] = jnp.zeros_like(sums_ref)
         rmg_ref[...] = jnp.zeros_like(rmg_ref)
+        outer_acc[...] = jnp.zeros_like(outer_acc)
 
     sums_ref[0:1, :] += jnp.sum(grad * normal, axis=0, keepdims=True)
     sums_ref[1:2, :] += jnp.sum(grad, axis=0, keepdims=True)
     rmg_ref[...] += dot(low.T, f_ref[...])
+    left = r.T
+    col = 0
+    for h in heads_out:
+        outer_acc[:, col : col + h.shape[1]] += dot(left, h[...])
+        col += h.shape[1]
+
+    @pl.when(step == pl.num_programs(0) - 1)
+    def _():
+        outer_ref[...] = outer_acc[...].astype(BF16)
+
     if sent is not None:
 
         @pl.when(step == pl.num_programs(0) - 1)
@@ -1442,6 +1462,7 @@
     rm,
     slot_rows,
     dots,
+    heads,
     weights,
     experts,
     shard,
@@ -1457,9 +1478,10 @@
         pl.BlockSpec(memory_space=pl.ANY) if j == sent else pl.BlockSpec((rb, size), lambda i: (i, 0))
         for j, (_, _, size) in enumerate(weights)
     ]
-    scratch, extra = [], {}
+    outer_width = sum(h.shape[1] for h in heads)
+    scratch, extra = [pltpu.VMEM((wide, outer_width), F32)], {}
     if sent is not None:
-        scratch = [
+        scratch += [
             pltpu.VMEM((rows, weights[sent][2]), BF16),
             pltpu.SemaphoreType.DMA((rows // rb,)),
             pltpu.SemaphoreType.DMA((rows // rb,)),
@@ -1473,22 +1495,27 @@
             capacity=capacity,
             shard=shard,
             sent=sent,
+            outs=len(heads),
         ),
         grid=(rows // rb,),
         in_specs=[narrow, block, narrow, narrow, block, block, block]
         + [resident(gain.shape), resident((wide, LANES))]
         + [resident(slot_rows.shape), resident(dots.shape)]
+        + [pl.BlockSpec((rb, h.shape[1]), lambda i: (i, 0)) for h in heads]
         + [
             pl.BlockSpec((wide, size), lambda i, j=j: (0, j), pipeline_mode=pl.Buffered(1))
             for _, j, size in weights
         ],
-        out_specs=[block] + head_specs + [resident((8, wide)), resident((LANES, wide))],
+        out_specs=[block]
+        + head_specs
+        + [resident((8, wide)), resident((LANES, wide)), resident((wide, outer_width))],
         out_shape=[jax.ShapeDtypeStruct((rows, wide), BF16)]
         + [jax.ShapeDtypeStruct((rows, size), BF16) for _, _, size in weights]
-        + [jax.ShapeDtypeStruct((8, wide), F32), jax.ShapeDtypeStruct((LANES, wide), F32)],
+        + [jax.ShapeDtypeStruct((8, wide), F32), jax.ShapeDtypeStruct((LANES, wide), F32)]
+        + [jax.ShapeDtypeStruct((wide, outer_width), BF16)],
         scratch_shapes=scratch,
         cost_estimate=cost(6 * rows * wide * wide, 16 * rows * wide),
-        compiler_params=pltpu.CompilerParams(vmem_limit_bytes=48 * 1024 * 1024, **extra),
+        compiler_params=pltpu.CompilerParams(vmem_limit_bytes=56 * 1024 * 1024, **extra),
         name="ffn_norm_pull",
     )(
         info,
@@ -1502,6 +1529,7 @@
         rm,
         slot_rows,
         dots,
+        *heads,
         *[w for w, _, _ in weights],
     )
 
@@ -1594,32 +1622,50 @@
     )((first_row // rb).astype(jnp.int32).reshape(1), x, r, gain, *grads, *weights)
 
 
-def combine_kernel(info_ref, y_ref, chance_ref, slot_ref, o_ref, *, experts, capacity):
+def combine_kernel(
+    at_ref, info_ref, y_ref, chance_ref, slot_ref, other_ref, own_ref, *, experts, capacity
+):
+    del at_ref
     place = info_ref[:, 0:1].astype(jnp.int32)
     here = info_ref[:, 1:2].astype(jnp.int32)
     chances = chance_ref[...]
     gate = jnp.sum(expert_hot(place, capacity, experts) * chances, axis=-1, keepdims=True)
     moe = unpacked(here, slot_ref) * (lane_of(chances, experts + 1) * gate)
-    o_ref[...] = (lane_of(chances, experts) * y_ref[...].astype(F32) + moe).astype(BF16)
-
-
-def combine(info, y, coef, slot_rows, experts, capacity, rb=256):
+    total = (lane_of(chances, experts) * y_ref[...].astype(F32) + moe).astype(BF16)
+    first = pl.program_id(0) < pl.num_programs(0) // 2
+
+    @pl.when(first)
+    def _():
+        other_ref[...] = total
+
+    @pl.when(jnp.logical_not(first))
+    def _():
+        own_ref[...] = total
+
+
+def combine(first_row, info, y, coef, slot_rows, experts, capacity, rb=256):
     rows, wide = y.shape
-    block = pl.BlockSpec((rb, wide), lambda i: (i, 0))
+    half = rows // rb // 2
+
+    def block(width):
+        return pl.BlockSpec((rb, width), lambda i, at: (lax.rem(at[0] + half + i, 2 * half), 0))
+
+    part = jax.ShapeDtypeStruct((rows // 2, wide), BF16)
     return pl.pallas_call(
         partial(combine_kernel, experts=experts, capacity=capacity),
-        grid=(rows // rb,),
-        in_specs=[
-            pl.BlockSpec((rb, LANES), lambda i: (i, 0)),
-            block,
-            pl.BlockSpec((rb, LANES), lambda i: (i, 0)),
-        ]
-        + [resident(slot_rows.shape)],
-        out_specs=block,
-        out_shape=jax.ShapeDtypeStruct((rows, wide), BF16),
+        grid_spec=pltpu.PrefetchScalarGridSpec(
+            num_scalar_prefetch=1,
+            grid=(2 * half,),
+            in_specs=[block(LANES), block(wide), block(LANES), resident(slot_rows.shape)],
+            out_specs=[
+                pl.BlockSpec((rb, wide), lambda i, _: (jnp.minimum(i, half - 1), 0)),
+                pl.BlockSpec((rb, wide), lambda i, _: (jnp.maximum(i - half, 0), 0)),
+            ],
+        ),
+        out_shape=[part, part],
         cost_estimate=cost(4 * rows * wide * wide, 8 * rows * wide),
         name="combine_nets",
-    )(info, y, coef, slot_rows)
+    )((first_row // rb).astype(jnp.int32).reshape(1), info, y, coef, slot_rows)
 
 
 class Halving:
@@ -1801,21 +1847,23 @@
     for acc in (acc_a, acc_b):
         acc[...] = jnp.zeros_like(acc)
 
-    def outer_step(b, _):
-        at = pl.ds(pl.multiple_of(b * 512, 512), 512)
-        left = av[at, :].T
-        for acc, some in ((acc_a, grads[:cut]), (acc_b, grads[cut:])):
+    for acc, some, chain in ((acc_a, grads[:cut], qkv[0]), (acc_b, grads[cut:], qkv[1])):
+
+        def outer_step(b, _, acc=acc, some=some):
+            at = pl.ds(pl.multiple_of(b * 512, 512), 512)
+            left = av[at, :].T
             col = 0
             for g in some:
                 width = g.shape[1]
                 acc[:, col : col + width] += dot(left, g[at, :])
                 col += width
-        return 0
-
-    lax.fori_loop(0, rows // 512, outer_step, 0)
-    for chain in qkv:
+            return 0
+
+        lax.fori_loop(0, rows // 512, outer_step, 0)
         chain.start(0)
-    go.step(0)
+        if chain is qkv[0]:
+            go.step(0)
+    qkv[0].step(0)
     lax.fori_loop(count // 2, count, theirs, 0)
 
     def own_copy(b):
@@ -1828,10 +1876,10 @@
         own_copy(b).start()
         return 0
 
-    for chain in qkv:
-        chain.step(0)
+    qkv[1].step(0)
     lax.fori_loop(0, count // 2, own_step, 0)
     go.step(1)
+    qkv[0].step(1)
     lax.fori_loop(count // 2, count, own_step, 0)
 
     def small_copy(s):
@@ -1850,9 +1898,11 @@
         small_copy(s).start()
         if s + 2 < steps:
             go.step(s + 2)
-        if 0 < s < steps:
-            for chain in qkv:
-                chain.step(s)
+        if s == 1:
+            qkv[1].step(1)
+            qkv[0].step(2)
+        if s == 2:
+            qkv[1].step(2)
         small_copy(s).wait()
         total_ref[...] += small_gots[s][...]
         if s == max(0, steps - 3):
@@ -1867,6 +1917,9 @@
                 device_id_type=mesh,
             )
             out_copy.start()
+    for chain in qkv:
+        for s in range(3, steps):
+            chain.step(s)
     col = 0
     for acc in (acc_a, acc_b):
         square_ref[:, col : col + acc.shape[1]] = acc[: acc.shape[0] // size, :]
@@ -1939,13 +1992,19 @@
 
 
 def results_kernel(
+    at_ref,
+    len_ref,
     own_ref,
     got_ref,
+    resid_ref,
+    mine_ref,
+    theirs_ref,
     square_ref,
     small_ref,
     h_ref,
     r_ref,
     token_ref,
+    block_ref,
     q_ref,
     k_ref,
     v_ref,
@@ -1957,8 +2016,18 @@
     bias1_ref,
     gain2_ref,
     bias2_ref,
+    *,
+    length,
 ):
     token_ref[...] = own_ref[...] + got_ref[...].astype(F32)
+    size = own_ref.shape[0]
+    position = (at_ref[0] + pl.program_id(0)) * size + lax.broadcasted_iota(jnp.int32, own_ref.shape, 0)
+    live = None
+    for s in range(len_ref.shape[0]):
+        inside = (position >= s * length) & (position < s * length + len_ref[s])
+        live = inside if live is None else live | inside
+    nets_sum = mine_ref[...].astype(F32) + theirs_ref[...].astype(F32)
+    block_ref[...] = jnp.where(live, resid_ref[...] + nets_sum, 0.0).astype(BF16)
 
     @pl.when(pl.program_id(0) == 0)
     def _():
@@ -1975,21 +2044,38 @@
             ref[...] = small_ref[at : at + 1, :]
 
 
-def results(own, got, square, small, gh, gr, experts, rb=256):
+def results(first_row, lengths, own, got, resid, weighted, theirs, square, small, gh, gr, experts, rb=256):
     rows, wide = own.shape
     kept, width = square.shape[0], square.shape[1] // 3
-    block = pl.BlockSpec((rb, wide), lambda i: (i, 0))
+    block = pl.BlockSpec((rb, wide), lambda i, *_: (i, 0))
+    shifted = pl.BlockSpec((rb, wide), lambda i, at, _: (at[0] + i, 0))
     shapes = [(kept, width)] * 3 + [gh.shape, gr.shape, (experts, wide), (2, wide)] + [(1, wide)] * 4
     return pl.pallas_call(
-        results_kernel,
-        grid=(rows // rb,),
-        in_specs=[block, block] + [resident(v.shape) for v in (square, small, gh, gr)],
-        out_specs=[block] + [resident(s) for s in shapes],
-        out_shape=[jax.ShapeDtypeStruct((rows, wide), F32)]
+        partial(results_kernel, length=resid.shape[0] // lengths.shape[0]),
+        grid_spec=pltpu.PrefetchScalarGridSpec(
+            num_scalar_prefetch=2,
+            grid=(rows // rb,),
+            in_specs=[block, block, shifted, block, block]
+            + [resident(v.shape) for v in (square, small, gh, gr)],
+            out_specs=[block, block] + [resident(s) for s in shapes],
+        ),
+        out_shape=[jax.ShapeDtypeStruct((rows, wide), F32), jax.ShapeDtypeStruct((rows, wide), BF16)]
         + [jax.ShapeDtypeStruct(s, F32) for s in shapes],
-        cost_estimate=cost(rows * wide, 12 * rows * wide),
+        cost_estimate=cost(rows * wide, 22 * rows * wide),
         name="results",
-    )(own, got, square, small, gh, gr)
+    )(
+        (first_row // rb).astype(jnp.int32).reshape(1),
+        lengths,
+        own,
+        got,
+        resid,
+        weighted,
+        theirs,
+        square,
+        small,
+        gh,
+        gr,
+    )
 
 
 def on_device(
@@ -2065,7 +2151,8 @@
     rm = jnp.pad(
         jnp.concatenate([router, mix_weight], axis=1), ((0, 0), (0, LANES - experts - 2))
     )
-    norms = jnp.stack([gain_attn, bias_attn, gain_ffn, bias_ffn]).astype(F32)
+    norms = jnp.concatenate([gain_attn, bias_attn, gain_ffn, bias_ffn]).astype(F32)
+    norms = norms.reshape(4, model_width)
     projections = (w_query, w_key, w_value)
     if tp == 2:
         (
@@ -2158,12 +2245,13 @@
         rm,
         pulls,
         dots,
+        all_heads,
         wide_weights,
         experts,
         shard_rows,
         sent=splits if tp == 2 else None,
     )
-    *head_parts, ffn_sums, rm_sums = rest
+    *head_parts, ffn_sums, rm_sums, out_part = rest
     if tp == 2:
         head_grads = [
             [m, o if s == 0 else swapped(o)]
@@ -2174,8 +2262,6 @@
         head_grads = [
             [local[:, s * each * PAIR : (s + 1) * each * PAIR]] for s in range(splits)
         ]
-    out_part = outer(part, all_heads)
-    part = after(part, out_part)
     grad_hidden = over_sequences(grad_hidden)
     grad_return = over_sequences(grad_return)
 
@@ -2184,10 +2270,12 @@
     for s in range(splits):
         if s == splits - 1:
             if qkv:
-                dense, qkv[-1], head_grads[s], out_part = lax.optimization_barrier(
-                    (dense, qkv[-1], head_grads[s], out_part)
+                dense, qkv[-1], head_grads[s] = lax.optimization_barrier(
+                    (dense, qkv[-1], head_grads[s])
                 )
-            weighted = combine(info, dense, chances, returned, experts, capacity)
+            weighted = combine(
+                first_row if tp == 2 else jnp.zeros((), jnp.int32), info, dense, chances, returned, experts, capacity
+            )
             projected, weighted = lax.optimization_barrier((projected, weighted))
         *grads3, expert_grads[s] = attention_backward(
             projected,
@@ -2204,11 +2292,8 @@
     flat = [qkv[s][k] for k in range(3) for s in range(splits)]
     rows_kept = -(-(experts + 2) // 8) * 8
     small = jnp.concatenate([ffn_sums, rm_sums[:rows_kept]], axis=0)
-    theirs = lax.dynamic_slice_in_dim(weighted, shard_rows - first_row, shard_rows, 0)
     if tp == 2:
-        summed = shard_of(weighted).astype(F32) + swapped(theirs).astype(F32)
-        block_out = jnp.where(shard_of(live_all)[:, None], shard_of(resid) + summed, 0.0).astype(BF16)
-        part, block_out = lax.optimization_barrier((part, block_out))
+        theirs = swapped(weighted[0])
         own_part, got, square, grad_output, small = tail(
             tokens,
             part,
@@ -2222,6 +2307,7 @@
         )
         (
             token_grad,
+            block_out,
             grad_query,
             grad_key,
             grad_value,
@@ -2230,13 +2316,27 @@
             grad_router,
             grad_mix,
             *vectors,
-        ) = results(own_part, got, square, small, grad_hidden, grad_return, experts)
+        ) = results(
+            first_row,
+            lengths,
+            own_part,
+            got,
+            resid,
+            weighted[1],
+            theirs,
+            square,
+            small,
+            grad_hidden,
+            grad_return,
+            experts,
+        )
         vectors = [v[0] for v in vectors]
     else:
         whole, attn_sums = attn_pull(
             jnp.zeros((), jnp.int32), all_rows, tokens, part, norms[0:1], flat, projections, BF16
         )
         token_grad = lax.psum_scatter(whole, "tp", scatter_dimension=0, tiled=True).astype(F32)
+        weighted = jnp.concatenate(weighted[::-1], axis=0)
         summed = lax.psum_scatter(weighted, "tp", scatter_dimension=0, tiled=True).astype(F32)
         block_out = jnp.where(shard_of(live_all)[:, None], shard_of(resid) + summed, 0.0).astype(BF16)
         square = over_sequences(outer(attn_in, flat))

time: 568 us -> 552 us (0.972)
  waiting for transfers between devices: 9.04 us -> 0.75 us
    ppermute x2, waiting for transfers between devices: 8.28 us -> 0.01 us  [swapped(): return lax.ppermute(values, 'tp', swap)]
    pallas_call x1, Pallas kernels: 32.9 us -> 39.1 us  [ffn_pull(): pl.pallas_call(partial(ffn_pull_kernel, parts=len(weights), experts=exper...]
    pallas_call x2 -> x1, Pallas kernels: 14.9 us -> 9.34 us  [results(): pl.pallas_call(partial(results_kernel, length=resid.shape[0] // lengths.s...]
  transfers between devices with their start and end apart: 5 -> 5, of which waited for: 1 -> 0; matrix products, arithmetic and copies ran while one was open for 1% -> 0% of each run, Pallas kernels for 37% -> 37%
where the time goes in v5:
time: 552 us; the launch traced here: 542 us
  Pallas kernels  510 us (92%)
  between operations  15.3 us (3%)
  local copies, waits for them, and re-layouts  7.12 us (1%)
  starting transfers between devices  6.75 us (1%)
    pallas_call x1, Pallas kernels, nets(): pl.pallas_call(partial(nets_kernel, peers=peers, capacity=capacity, rb=rb...  187 us
    pallas_call x1, Pallas kernels, front(): pl.pallas_call(partial(front_kernel, peers=peers, experts=experts, half=h...  112 us
    pallas_call x1, Pallas kernels, tail(): pl.pallas_call(partial(tail_kernel, groups=groups, size=size, rb=rb, smal...  80.7 us
    pallas_call x2, Pallas kernels, attention_backward(): pl.pallas_call(partial(attention_backward_kernel, terms=terms, carried=bo...  70.6 us
    pallas_call x1, Pallas kernels, ffn_pull(): pl.pallas_call(partial(ffn_pull_kernel, parts=len(weights), experts=exper...  39.1 us
    pallas_call x1, Pallas kernels, combine(): pl.pallas_call(partial(combine_kernel, experts=experts, capacity=capacity...  11.3 us
  transfers between devices with their start and end apart: 5, of which 0 were waited for; matrix products, arithmetic and copies ran while one was open for 0% of the time, Pallas kernels for 37%

profile of v5, /device:TPU:0, one launch (start us, length us, event | category | flops | bytes accessed | tf_op | source)
XLA Modules:
  0.0 542.5 jit_solution(11141762951122917485)
XLA Ops:
  7.2 0.0 reduce-scatter.3.cloned.1.call-start
  7.9 0.5 compare_convert_fusion.sel_ref
  8.4 0.7 maximum_convert_fusion
  9.1 0.6 reshape.63.refs_7_.refs_11_
  9.7 0.8 pad_maximum_fusion.1
  10.5 0.2 copy.37
  10.7 0.8 pad.8.refs_8_.rm_ref
  11.5 111.6 %layer_front.1 = (bf16[2048,1024]{1,0:T(8,128)(2,1)}, bf16[2048,1536]{1,0:T(8,128)(2,1)}, bf16[2048,512]{1,0:T(8,128)(2,1)}, bf16[2048,512]{1,0:T(8,128)(2,1)}, ...) custom-call(bf16[2048,1024]{1,0:T(8,128)(2,1)} %refs_0_.3, ...), custom_call_target="tpu_custom_call" | custom-call | flops 671088640 | bytes 983040 | tf_op jit(solution)/shard_map/layer_front/pallas_call | solution.py:747
  123.1 187.2 %feed_forward_nets.1 = (bf16[2048,1024]{1,0:T(8,128)(2,1)}, bf16[2048,1024]{1,0:T(8,128)(2,1)}, f32[2048,128]{1,0:T(8,128)}, bf16[1024,2048]{1,0:T(8,128)(2,1)},...) custom-call(bf16[2048,1024]{1,0:T(8,128)(2,1)} %get-tuple-element.85, ...), custom_call_target="tpu_custom_call" | custom-call | flops 1610612736 | bytes 1310720 | tf_op jit(solution)/shard_map/feed_forward_nets/pallas_call | solution.py:1278
  310.3 0.0 reduce-scatter.3.cloned.1.call-update
  310.4 0.0 reduce-scatter.5.cloned.1.call-start
  310.4 0.0 copy-start.6
  310.4 0.7 reduce-scatter.5.cloned.1.call-update
  311.1 4.6 all-to-all-start
  315.7 0.0 copy-done.6
  315.8 0.6 pad.9.refs_10_
  316.4 0.0 copy-start.2
  316.4 39.1 %ffn_norm_pull.1 = (bf16[2048,1024]{1,0:T(8,128)(2,1)}, bf16[2048,256]{1,0:T(8,128)(2,1)}, bf16[2048,256]{1,0:T(8,128)(2,1)}, bf16[2048,256]{1,0:T(8,128)(2,1)},...) custom-call(f32[2048,128]{1,0:T(8,128)} %get-tuple-element.84.refs_0_.info_ref, ...), custom_call_target="tpu_custom_call" | custom-call | flops 201326592 | bytes 524288 | tf_op jit(solution)/shard_map/ffn_norm_pull/pallas_call | solution.py:1490
  355.5 0.6 collective-permute-start
  356.1 0.0 copy-done.2
  356.1 35.1 %attention_backward.2 = (bf16[2048,256]{1,0:T(8,128)(2,1)S(1)}, bf16[2048,256]{1,0:T(8,128)(2,1)}, bf16[2048,256]{1,0:T(8,128)(2,1)}, f32[1024,2048]{1,0:T(8,128)}) custom-call(bf16[2048,1536]{1,0:T(8,128)(2,1)} %get-tuple-element.117.q_ref.k_ref.v_ref, bf16[2048,1536]{1,0:T(8,128)(2,1)} %get-tuple-element.117.q_ref.k_ref.v_ref, ...), custom_call_target="tpu_custom_call" | custom-call | flops 335544320 | bytes 131072 | tf_op jit(solution)/shard_map/attention_backward/pallas_call | solution.py:284
  391.2 0.0 copy-start
  391.2 1.0 copy-done
  392.2 0.0 collective-permute-done.refs_1_
  392.2 0.0 copy-start.4
  392.2 0.0 all-to-all-done
  392.2 0.0 copy-start.3
  392.2 1.3 copy-done.3
  393.6 0.0 copy-start.7
  393.6 11.3 %combine_nets.1 = (bf16[1024,1024]{1,0:T(8,128)(2,1)}, bf16[1024,1024]{1,0:T(8,128)(2,1)}) custom-call(s32[1]{0:T(128)} %bitcast.at_ref, f32[2048,128]{1,0:T(8,128)} %get-tuple-element.84.refs_0_.info_ref, bf16[2048,1024]{1,0:T(8,128)(2,1)} %get-tuple-element.113.y_ref, f32[2048,128]{1,0:T(8,128)} %get-tuple-element.90.refs_2_.chance_ref, ...), custom_call_target="tpu_custom_call" | custom-call | flops 134217728 | bytes 262144 | tf_op jit(solution)/shard_map/combine_nets/pallas_call | solution.py:1654
  404.9 1.4 collective-permute-start.1
  406.3 0.9 slice.7
  407.2 0.0 copy-done.7
  407.2 0.7 pad_maximum_fusion.refs_10_
  407.9 0.0 copy-done.4
  407.9 35.5 %attention_backward.3 = (bf16[2048,256]{1,0:T(8,128)(2,1)S(1)}, bf16[2048,256]{1,0:T(8,128)(2,1)}, bf16[2048,256]{1,0:T(8,128)(2,1)}, f32[1024,2048]{1,0:T(8,128)}) custom-call(bf16[2048,1536]{1,0:T(8,128)(2,1)} %get-tuple-element.117.q_ref.k_ref.v_ref, bf16[2048,1536]{1,0:T(8,128)(2,1)} %get-tuple-element.117.q_ref.k_ref.v_ref, ...), custom_call_target="tpu_custom_call" | custom-call | flops 335544320 | bytes 131072 | tf_op jit(solution)/shard_map/attention_backward/pallas_call | solution.py:284
  443.4 0.0 copy-start.1
  443.4 1.0 copy-done.1
  444.4 80.7 %backward_tail.1 = (f32[1024,1024]{1,0:T(8,128)}, bf16[1024,1024]{1,0:T(8,128)(2,1)}, f32[64,1536]{1,0:T(8,128)}, f32[64,512]{1,0:T(8,128)}, f32[40,1024]{1,0:T(8,128)}) custom-call(bf16[2048,1024]{1,0:T(8,128)(2,1)} %refs_0_.3, bf16[2048,1024]{1,0:T(8,128)(2,1)} %get-tuple-element.98.refs_1_, bf16[2048,1024]{1,0:T(8,128)(2,1)} %get-tuple-element.99.refs_2_, ...), custom_call_target="tpu_custom_call" | custom-call | flops 201326592 | bytes 524288 | tf_op jit(solution)/shard_map/backward_tail/pallas_call | solution.py:1949
  525.1 0.0 collective-permute-done.1.theirs_ref
  525.1 0.0 reduce-scatter.3.cloned.1.call-done.h_ref
  525.2 0.0 reduce-scatter.5.cloned.1.call-done.r_ref
  525.2 0.0 copy-start.5
  525.2 9.3 %results.1 = (f32[1024,1024]{1,0:T(8,128)}, bf16[1024,1024]{1,0:T(8,128)(2,1)}, f32[64,512]{1,0:T(8,128)}, f32[64,512]{1,0:T(8,128)}, f32[64,512]{1,0:T(8,128)},...) custom-call(s32[1]{0:T(128)} %bitcast.at_ref, ...), custom_call_target="tpu_custom_call" | custom-call | flops 16384 | bytes 360448 | tf_op jit(solution)/shard_map/results/pallas_call | solution.py:2053
  534.5 0.0 copy-done.5
  534.6 0.7 copy.41
  (2 shorter events, 0.0 us)
Async XLA Ops:
  7.2 518.0 %reduce-scatter.3.cloned.1.call-start = ((), (), s32[]{:S(2)}) async-start(), calls=%async_computation.3 | async-start | bytes 4456448 | tf_op jit(solution)/shard_map/reduce_scatter | solution.py:2140
  310.4 214.8 %reduce-scatter.5.cloned.1.call-start = ((), (), s32[]{:S(2)}) async-start(), calls=%async_computation.4 | async-start | bytes 4456448 | tf_op jit(solution)/shard_map/reduce_scatter | solution.py:2140
  310.4 5.3 copy-start.6
  311.1 81.1 %all-to-all-start = ((bf16[16,64,1024]{2,1,0:T(8,128)(2,1)}), bf16[16,64,1024]{2,1,0:T(8,128)(2,1)S(1)}, u32[]{:S(2)}, u32[]{:S(2)}) async-start(bf16[16,64,1024]{2,1,0:T(8,128)(2,1)} %get-tuple-element.114), calls=%async_computation | async-start | bytes 4194304 | tf_op jit(solution)/shard_map/all_to_all | solution.py:2127
  316.4 39.7 %copy-start.2 = (f32[4,2,2048]{2,1,0:T(2,128)S(1)}, f32[4,2,2048]{2,1,0:T(2,128)}, u32[]{:S(2)}) copy-start(f32[4,2,2048]{2,1,0:T(2,128)} %get-tuple-element.103.lse_ref) | copy-start | bytes 196612
  355.5 36.8 %collective-permute-start = (bf16[2048,256]{1,0:T(8,128)(2,1)}, bf16[2048,256]{1,0:T(8,128)(2,1)S(1)}, u32[]{:S(2)}, u32[]{:S(2)}) collective-permute-start(bf16[2048,256]{1,0:T(8,128)(2,1)} %get-tuple-element.111), channel_id=1, source_target_pairs={{0,1},{1,0},{2,3},{3,2},{4,5},{5,4},{6,7},{7,6},{8,9},{9,8},{10,11... | collective-permute-start | bytes 3145736 | tf_op jit(solution)/shard_map/ppermute | solution.py:2124
  391.2 1.0 copy-start
  392.2 15.7 %copy-start.4 = (bf16[2048,256]{1,0:T(8,128)(2,1)}, bf16[2048,256]{1,0:T(8,128)(2,1)S(1)}, u32[]{:S(2)}) copy-start(bf16[2048,256]{1,0:T(8,128)(2,1)S(1)} %collective-permute-done.refs_1_) | copy-start | bytes 3145732
  392.2 1.3 copy-start.3
  393.6 13.6 %copy-start.7 = (f32[8,1024]{1,0:T(8,128)S(1)}, f32[8,1024]{1,0:T(8,128)}, u32[]{:S(2)}) copy-start(f32[8,1024]{1,0:T(8,128)} %get-tuple-element.126) | copy-start | bytes 98308
  404.9 120.3 %collective-permute-start.1 = (bf16[1024,1024]{1,0:T(8,128)(2,1)}, bf16[1024,1024]{1,0:T(8,128)(2,1)}, u32[]{:S(2)}, u32[]{:S(2)}) collective-permute-start(bf16[1024,1024]{1,0:T(8,128)(2,1)} %get-tuple-element.131), channel_id=1, source_target_pairs={{0,1},{1,0},{2,3},{3,2},{4,5},{5,4},{6,7},{7,6},{8,9},{9,8},{10,11... | collective-permute-start | bytes 6291464 | tf_op jit(solution)/shard_map/ppermute | solution.py:2124
  443.4 1.0 copy-start.1
  525.2 9.4 %copy-start.5 = (f32[64,512]{1,0:T(8,128)S(1)}, f32[64,512]{1,0:T(8,128)}, u32[]{:S(2)}) copy-start(f32[64,512]{1,0:T(8,128)} %get-tuple-element.173) | copy-start | bytes 393220
Sparse Core Ops, SparseCore 0:
  310.5 86.4 reduce-scatter.2
  401.3 74.8 reduce-scatter.4

commit v6 on v5

--- a/solution.py
+++ b/solution.py
@@ -169,6 +169,7 @@
     *refs,
     terms,
     carried,
+    filled,
     bq,
     bk,
     scale,
@@ -179,25 +180,33 @@
     q = q_ref[...] * jnp.asarray(scale, BF16)
     do_refs = refs[:terms]
     refs = refs[terms:]
-    if carried:
-        from_hbm, dq_ref, dk_ref, dv_ref, to_hbm, *refs, held, carry_sem = refs
-        way_in = pltpu.make_async_copy(from_hbm, held, carry_sem.at[0])
-        way_out = pltpu.make_async_copy(held, to_hbm, carry_sem.at[1])
-        at = pl.program_id(0) * pl.num_programs(1) + pl.program_id(1)
-        final = pl.num_programs(0) * pl.num_programs(1) - 1
-
-        @pl.when(at == 0)
-        def _():
+    from_refs = refs[:carried]
+    dq_ref, dk_ref, dv_ref = refs[carried + filled : carried + filled + 3]
+    refs = refs[carried + filled + 3 :]
+    to_refs = refs[:carried]
+    dqt_ref, qs_ref, dos_ref, kt_ref, dl_ref = refs[carried : carried + 5]
+    held = refs[carried + 5 :]
+    at = pl.program_id(0) * pl.num_programs(1) + pl.program_id(1)
+    final = pl.num_programs(0) * pl.num_programs(1) - 1
+    ways = [
+        (
+            pltpu.make_async_copy(from_refs[c], held[2 * c], held[2 * c + 1].at[0]),
+            pltpu.make_async_copy(held[2 * c], to_refs[c], held[2 * c + 1].at[1]),
+        )
+        for c in range(carried)
+    ]
+
+    @pl.when(at == 0)
+    def _():
+        for way_in, _ in ways:
             way_in.start()
 
-        @pl.when(at == final)
-        def _():
+    @pl.when(at == final)
+    def _():
+        for way_in, way_out in ways:
             way_in.wait()
             way_out.start()
 
-    else:
-        dq_ref, dk_ref, dv_ref, *refs = refs
-    dqt_ref, qs_ref, dos_ref, kt_ref, dl_ref = refs
     do = do_refs[0][...]
     if terms == 2:
         do = (do.astype(F32) + do_refs[1][...].astype(F32)).astype(BF16)
@@ -267,14 +276,15 @@
 
         @pl.when(at == final)
         def _():
-            way_out.wait()
-
-
-def attention_backward(proj, out, out_grads, lse, seqs, heads, first, count, carry=(), bq=512, bk=512):
+            for _, way_out in ways:
+                way_out.wait()
+
+
+def attention_backward(proj, out, out_grads, lse, seqs, heads, first, count, place=0, into=(), carry=(), bq=512, bk=512):
     rows = out.shape[0]
     length = rows // seqs
     pairs = heads // 2
-    width = count * PAIR
+    width = out_grads[0].shape[1]
 
     def block(off):
         return pl.BlockSpec((length, PAIR), lambda s, p: (s, off + p))
@@ -285,7 +295,8 @@
         partial(
             attention_backward_kernel,
             terms=terms,
-            carried=bool(carry),
+            carried=len(carry),
+            filled=len(into),
             bq=bq,
             bk=bk,
             scale=HEAD_DIM**-0.5,
@@ -299,9 +310,10 @@
             block(first),
             pl.BlockSpec((1, 2, length), lambda s, p: (first + p, 0, s)),
         ]
-        + [block(0)] * terms
-        + [pl.BlockSpec(memory_space=pl.ANY) for _ in carry],
-        out_specs=[block(0)] * 3 + [pl.BlockSpec(memory_space=pl.ANY) for _ in carry],
+        + [block(place)] * terms
+        + [pl.BlockSpec(memory_space=pl.ANY) for _ in (*carry, *into)],
+        input_output_aliases={5 + terms + len(carry) + j: j for j in range(len(into))},
+        out_specs=[block(place)] * 3 + [pl.BlockSpec(memory_space=pl.ANY) for _ in carry],
         out_shape=[grad] * 3 + [jax.ShapeDtypeStruct(c.shape, c.dtype) for c in carry],
         scratch_shapes=[
             pltpu.VMEM((PAIR, length), F32),
@@ -311,10 +323,10 @@
             pltpu.VMEM((2, length), F32),
         ]
         + [s for c in carry for s in (pltpu.VMEM(c.shape, c.dtype), pltpu.SemaphoreType.DMA((2,)))],
-        cost_estimate=cost(20 * rows * length * width, 16 * rows * width),
+        cost_estimate=cost(20 * rows * length * count * PAIR, 16 * rows * width),
         compiler_params=pltpu.CompilerParams(vmem_limit_bytes=52 * 1024 * 1024),
         name="attention_backward",
-    )(proj, proj, proj, out, lse, *out_grads, *carry)
+    )(proj, proj, proj, out, lse, *out_grads, *carry, *into)
 
 
 def norm_project_kernel(x_ref, gain_ref, bias_ref, wq_ref, wk_ref, wv_ref, a_ref, p_ref):
@@ -1467,7 +1479,7 @@
     experts,
     shard,
     sent=None,
-    rb=256,
+    rb=512,
 ):
     rows, wide = dx.shape
     capacity = dots.shape[1]
@@ -1643,7 +1655,7 @@
         own_ref[...] = total
 
 
-def combine(first_row, info, y, coef, slot_rows, experts, capacity, rb=256):
+def combine(first_row, info, y, coef, slot_rows, experts, capacity, rb=512):
     rows, wide = y.shape
     half = rows // rb // 2
 
@@ -1688,32 +1700,69 @@
             device_id_type=pl.DeviceIdType.MESH,
         )
 
-    def halves(self, s):
-        place = sum(1 for b in self.order[s:] if b < self.order[s])
-        low = (1 << place) - 1
-        return [((i >> place) << (place + 1) | (i & low)) for i in range(self.size >> (s + 1))], 1 << place
-
     def bit(self, s):
         return lax.rem(lax.div(self.me, 1 << self.order[s]), 2)
 
+    def each(self, s, body):
+        place = sum(1 for b in self.order[s:] if b < self.order[s])
+        low = 1 << place
+
+        def step(i, _):
+            body(self.block(i), lax.div(i, low) * (2 * low) + lax.rem(i, low), low)
+            return 0
+
+        lax.fori_loop(0, self.size >> (s + 1), step, 0)
+
     def start(self, s):
-        places, step = self.halves(s)
-        for i, at in enumerate(places):
-            rows = slice(i * self.rows, (i + 1) * self.rows)
-            self.gives[s][rows, :] = self.total[self.block(at + (1 - self.bit(s)) * step), :].astype(BF16)
+        def give(rows, at, step):
+            other = self.total[self.block(at + (1 - self.bit(s)) * step), :]
+            self.gives[s][rows, :] = other.astype(BF16)
+
+        self.each(s, give)
         self.copy(s).start()
 
     def finish(self, s):
         self.copy(s).wait()
-        places, step = self.halves(s)
-        for i, at in enumerate(places):
-            rows = slice(i * self.rows, (i + 1) * self.rows)
+
+        def keep(rows, at, step):
             kept = self.total[self.block(at + self.bit(s) * step), :]
             self.total[rows, :] = kept + self.gots[s][rows, :].astype(F32)
+
+        self.each(s, keep)
 
     def step(self, s):
         self.finish(s)
         if s + 1 < len(self.order):
+            self.start(s + 1)
+
+
+class Rounds:
+    def __init__(self, total, gives, gots, send, recv, me, tp_me):
+        self.total, self.gives, self.gots = total, gives, gots
+        self.send, self.recv, self.me, self.tp_me = send, recv, me, tp_me
+
+    def copy(self, s):
+        peer = {"tp": 1 - self.tp_me} if s == 0 else {"ep": jnp.bitwise_xor(self.me, 1 << (s - 1))}
+        return pltpu.make_async_remote_copy(
+            src_ref=self.gives[s],
+            dst_ref=self.gots[s],
+            send_sem=self.send.at[s],
+            recv_sem=self.recv.at[s],
+            device_id=peer,
+            device_id_type=pl.DeviceIdType.MESH,
+        )
+
+    def start(self, s):
+        self.gives[s][...] = self.total[...]
+        self.copy(s).start()
+
+    def finish(self, s):
+        self.copy(s).wait()
+        self.total[...] += self.gots[s][...]
+
+    def step(self, s):
+        self.finish(s)
+        if s + 1 < len(self.gives):
             self.start(s + 1)
 
 
@@ -1739,6 +1788,7 @@
     gives_b, gots_b = take(steps), take(steps)
     go_gives, go_gots = take(steps), take(steps)
     small_gives, small_gots = take(hops), take(hops)
+    late_gives, late_gots = take(hops), take(hops)
     (
         load_sem,
         own_sem,
@@ -1752,6 +1802,8 @@
         go_recv,
         small_send,
         small_recv,
+        late_send,
+        late_recv,
         out_sem,
         out_give,
         out_got,
@@ -1798,12 +1850,19 @@
         Halving(acc_b, gives_b, gots_b, half_send_b, half_recv_b, me, size, other_order),
     ]
     go = Halving(goacc, go_gives, go_gots, go_send, go_recv, me, size, order)
+    early = Rounds(
+        total_ref.at[:small_rows, :], small_gives, small_gots, small_send, small_recv, me, tp_me
+    )
+    late = Rounds(
+        total_ref.at[small_rows:, :], late_gives, late_gots, late_send, late_recv, me, tp_me
+    )
 
     for c in theirs_loads:
         c.wait()
 
     total_ref[:small_rows, :] = small_ref[...]
-    total_ref[small_rows:, :] = jnp.zeros_like(total_ref[small_rows:, :])
+    total_ref[small_rows:, :] = jnp.zeros((8, total_ref.shape[1]), F32)
+    early.start(0)
 
     def pulled(at):
         total = None
@@ -1841,6 +1900,7 @@
     out_load.wait()
     goacc[...] = gov[...].astype(F32)
     go.start(0)
+    early.step(0)
     for c in own_loads + [a_load]:
         c.wait()
     cut = len(grads) // 2
@@ -1863,7 +1923,9 @@
         chain.start(0)
         if chain is qkv[0]:
             go.step(0)
+            early.step(1)
     qkv[0].step(0)
+    early.step(2)
     lax.fori_loop(count // 2, count, theirs, 0)
 
     def own_copy(b):
@@ -1877,25 +1939,16 @@
         return 0
 
     qkv[1].step(0)
+    early.step(3)
     lax.fori_loop(0, count // 2, own_step, 0)
     go.step(1)
     qkv[0].step(1)
+    for s in range(4, hops):
+        early.step(s)
     lax.fori_loop(count // 2, count, own_step, 0)
 
-    def small_copy(s):
-        peer = {"tp": 1 - tp_me} if s == 0 else {"ep": jnp.bitwise_xor(me, 1 << (s - 1))}
-        return pltpu.make_async_remote_copy(
-            src_ref=small_gives[s],
-            dst_ref=small_gots[s],
-            send_sem=small_send.at[s],
-            recv_sem=small_recv.at[s],
-            device_id=peer,
-            device_id_type=mesh,
-        )
-
     for s in range(hops):
-        small_gives[s][...] = total_ref[...]
-        small_copy(s).start()
+        late.start(s)
         if s + 2 < steps:
             go.step(s + 2)
         if s == 1:
@@ -1903,8 +1956,7 @@
             qkv[0].step(2)
         if s == 2:
             qkv[1].step(2)
-        small_copy(s).wait()
-        total_ref[...] += small_gots[s][...]
+        late.finish(s)
         if s == max(0, steps - 3):
             own_width = outsum_ref.shape[1]
             out_give[...] = goacc[: goacc.shape[0] // size, own_width:].astype(BF16)
@@ -1969,7 +2021,8 @@
         ]
         + halves(total // 2) * 4
         + halves(out_width) * 2
-        + [pltpu.VMEM((small_rows + 8, wide), F32)] * (2 * (steps + 1))
+        + [pltpu.VMEM((small_rows, wide), F32)] * (2 * (steps + 1))
+        + [pltpu.VMEM((8, wide), F32)] * (2 * (steps + 1))
         + [
             pltpu.SemaphoreType.DMA((2, 3 + 3 * groups)),
             pltpu.SemaphoreType.DMA((shard // rb,)),
@@ -1977,7 +2030,7 @@
             pltpu.SemaphoreType.DMA((shard // rb,)),
         ]
         + [pltpu.SemaphoreType.DMA((steps,))] * 6
-        + [pltpu.SemaphoreType.DMA((steps + 1,))] * 2
+        + [pltpu.SemaphoreType.DMA((steps + 1,))] * 4
         + [
             pltpu.SemaphoreType.DMA((2,)),
             pltpu.VMEM((kept, out_width // 2), BF16),
@@ -2265,30 +2318,38 @@
     grad_hidden = over_sequences(grad_hidden)
     grad_return = over_sequences(grad_return)
 
-    qkv = []
     expert_grads = [grad_expert_in, grad_expert_out]
-    for s in range(splits):
-        if s == splits - 1:
-            if qkv:
-                dense, qkv[-1], head_grads[s] = lax.optimization_barrier(
-                    (dense, qkv[-1], head_grads[s])
-                )
-            weighted = combine(
-                first_row if tp == 2 else jnp.zeros((), jnp.int32), info, dense, chances, returned, experts, capacity
-            )
-            projected, weighted = lax.optimization_barrier((projected, weighted))
-        *grads3, expert_grads[s] = attention_backward(
-            projected,
-            heads,
-            head_grads[s],
-            lse,
-            seq_count,
-            local_heads,
-            s * each,
-            each,
-            (expert_grads[s],),
-        )
-        qkv.append(grads3)
+    pull_heads = partial(
+        attention_backward, out=heads, lse=lse, seqs=seq_count, heads=local_heads
+    )
+    if tp == 2 and each > 1:
+        first_qkv = pull_heads(projected, out_grads=head_grads[0], first=0, count=1)
+        dense, first_qkv = lax.optimization_barrier((dense, first_qkv))
+        weighted = combine(first_row, info, dense, chances, returned, experts, capacity)
+        projected, weighted, head_grads[1] = lax.optimization_barrier(
+            (projected, weighted, head_grads[1])
+        )
+        first_qkv = pull_heads(
+            projected, out_grads=head_grads[0], first=1, count=each - 1, place=1, into=first_qkv
+        )
+        *second_qkv, expert_grads[0], expert_grads[1] = pull_heads(
+            projected, out_grads=head_grads[1], first=each, count=each, carry=expert_grads
+        )
+        qkv = [first_qkv, second_qkv]
+    else:
+        weighted = combine(
+            first_row if tp == 2 else jnp.zeros((), jnp.int32),
+            info,
+            dense,
+            chances,
+            returned,
+            experts,
+            capacity,
+        )
+        qkv = [
+            pull_heads(projected, out_grads=head_grads[s], first=s * each, count=each)
+            for s in range(splits)
+        ]
     flat = [qkv[s][k] for k in range(3) for s in range(splits)]
     rows_kept = -(-(experts + 2) // 8) * 8
     small = jnp.concatenate([ffn_sums, rm_sums[:rows_kept]], axis=0)

time: 552 us -> 552 us (level)
    pallas_call x2 -> x3, Pallas kernels: 70.6 us -> 73 us  [attention_backward(): pl.pallas_call(partial(attention_backward_kernel, terms=terms, carried=le...]
where the time goes in v6:
time: 552 us; the launch traced here: 542 us
  Pallas kernels  511 us (93%)
  between operations  15.3 us (3%)
  starting transfers between devices  6.87 us (1%)
    pallas_call x1, Pallas kernels, nets(): pl.pallas_call(partial(nets_kernel, peers=peers, capacity=capacity, rb=rb...  187 us
    pallas_call x1, Pallas kernels, front(): pl.pallas_call(partial(front_kernel, peers=peers, experts=experts, half=h...  112 us
    pallas_call x1, Pallas kernels, tail(): pl.pallas_call(partial(tail_kernel, groups=groups, size=size, rb=rb, smal...  80.7 us
    pallas_call x3, Pallas kernels, attention_backward(): pl.pallas_call(partial(attention_backward_kernel, terms=terms, carried=le...  73 us
    pallas_call x1, Pallas kernels, ffn_pull(): pl.pallas_call(partial(ffn_pull_kernel, parts=len(weights), experts=exper...  39.1 us
  transfers between devices with their start and end apart: 5, of which 0 were waited for; matrix products, arithmetic and copies ran while one was open for 0% of the time, Pallas kernels for 37%

profile of v6, /device:TPU:0, one launch (start us, length us, event | category | flops | bytes accessed | tf_op | source)
XLA Modules:
  0.0 541.6 jit_solution(1394446373917205244)
XLA Ops:
  7.2 0.0 reduce-scatter.3.cloned.1.call-start
  7.2 0.8 pad_maximum_fusion.1
  8.0 0.2 copy.40
  8.2 0.7 maximum_convert_fusion
  8.9 0.6 reshape.66.refs_7_.refs_11_
  10.2 0.5 compare_convert_fusion.sel_ref
  10.7 0.8 pad.8.refs_8_.rm_ref
  11.5 111.6 %layer_front.1 = (bf16[2048,1024]{1,0:T(8,128)(2,1)}, bf16[2048,1536]{1,0:T(8,128)(2,1)}, bf16[2048,512]{1,0:T(8,128)(2,1)}, bf16[2048,512]{1,0:T(8,128)(2,1)}, ...) custom-call(bf16[2048,1024]{1,0:T(8,128)(2,1)} %refs_0_.3, ...), custom_call_target="tpu_custom_call" | custom-call | flops 671088640 | bytes 983040 | tf_op jit(solution)/shard_map/layer_front/pallas_call | solution.py:759
  123.1 187.2 %feed_forward_nets.1 = (bf16[2048,1024]{1,0:T(8,128)(2,1)}, bf16[2048,1024]{1,0:T(8,128)(2,1)}, f32[2048,128]{1,0:T(8,128)}, bf16[1024,2048]{1,0:T(8,128)(2,1)},...) custom-call(bf16[2048,1024]{1,0:T(8,128)(2,1)} %get-tuple-element.88, ...), custom_call_target="tpu_custom_call" | custom-call | flops 1610612736 | bytes 1310720 | tf_op jit(solution)/shard_map/feed_forward_nets/pallas_call | solution.py:1290
  310.3 0.0 reduce-scatter.3.cloned.1.call-update
  310.3 0.0 reduce-scatter.5.cloned.1.call-start
  310.4 0.0 copy-start.5
  310.4 0.7 reduce-scatter.5.cloned.1.call-update
  311.1 4.6 all-to-all-start
  315.8 0.0 copy-done.5
  315.8 0.6 pad.9.refs_10_
  316.4 0.0 copy-start.2
  316.4 39.1 %ffn_norm_pull.1 = (bf16[2048,1024]{1,0:T(8,128)(2,1)}, bf16[2048,256]{1,0:T(8,128)(2,1)}, bf16[2048,256]{1,0:T(8,128)(2,1)}, bf16[2048,256]{1,0:T(8,128)(2,1)},...) custom-call(f32[2048,128]{1,0:T(8,128)} %get-tuple-element.87.refs_0_.info_ref, ...), custom_call_target="tpu_custom_call" | custom-call | flops 201326592 | bytes 524288 | tf_op jit(solution)/shard_map/ffn_norm_pull/pallas_call | solution.py:1502
  355.5 1.1 collective-permute-start
  356.6 0.0 copy-done.2
  356.6 18.6 %attention_backward.3 = (bf16[2048,256]{1,0:T(8,128)(2,1)S(1)}, bf16[2048,256]{1,0:T(8,128)(2,1)}, bf16[2048,256]{1,0:T(8,128)(2,1)}) custom-call(bf16[2048,1536]{1,0:T(8,128)(2,1)} %get-tuple-element.118.q_ref.k_ref.v_ref, bf16[2048,1536]{1,0:T(8,128)(2,1)} %get-tuple-element.118.q_ref.k_ref.v_ref, bf16[2048,1536]{1,0:T(8,128)(2,1)} %get-tuple-element.118.q_ref.k_ref.v_ref, ...), custom_call_target="tpu_custom_call" | custom-call | flops 167772160 | bytes 131072 | tf_op jit(solution)/shard_map/attention_backward/pallas_call | solution.py:294
  375.2 0.0 all-to-all-done
  375.2 0.0 copy-start.6
  375.2 10.2 %combine_nets.1 = (bf16[1024,1024]{1,0:T(8,128)(2,1)}, bf16[1024,1024]{1,0:T(8,128)(2,1)}) custom-call(s32[1]{0:T(128)} %bitcast.7.at_ref, f32[2048,128]{1,0:T(8,128)} %get-tuple-element.87.refs_0_.info_ref, bf16[2048,1024]{1,0:T(8,128)(2,1)} %get-tuple-element.112.y_ref, f32[2048,128]{1,0:T(8,128)} %get-tuple-element.93.refs_2_.chance_ref, ...), custom_call_target="tpu_custom_call" | custom-call | flops 134217728 | bytes 262144 | tf_op jit(solution)/shard_map/combine_nets/pallas_call | solution.py:1666
  385.5 0.0 collective-permute-done.refs_1_
  385.5 0.0 copy-start.3
  385.5 1.0 collective-permute-start.1
  386.6 0.9 slice.7
  387.5 0.0 copy-done.6
  387.5 0.7 pad_maximum_fusion.refs_10_
  388.1 18.6 %attention_backward.4 = (bf16[2048,256]{1,0:T(8,128)(2,1)S(1)}, bf16[2048,256]{1,0:T(8,128)(2,1)}, bf16[2048,256]{1,0:T(8,128)(2,1)}) custom-call(bf16[2048,1536]{1,0:T(8,128)(2,1)} %get-tuple-element.118.q_ref.k_ref.v_ref, bf16[2048,1536]{1,0:T(8,128)(2,1)} %get-tuple-element.118.q_ref.k_ref.v_ref, ...), custom_call_target="tpu_custom_call", output_to_operand_aliasing={{0}: (7, {}), {1}: (8, {}), {2}: (9, {})} | custom-call | flops 167772160 | bytes 131072 | tf_op jit(solution)/shard_map/attention_backward/pallas_call | solution.py:294
  406.8 0.0 copy-done.3
  406.8 0.0 copy-start
  406.8 35.7 %attention_backward.5 = (bf16[2048,256]{1,0:T(8,128)(2,1)S(1)}, bf16[2048,256]{1,0:T(8,128)(2,1)}, bf16[2048,256]{1,0:T(8,128)(2,1)}, f32[1024,2048]{1,0:T(8,128)}, f32[1024,2048]{1,0:T(8,128)}) custom-call(bf16[2048,1536]{1,0:T(8,128)(2,1)} %get-tuple-element.118.q_ref.k_ref.v_ref, bf16[2048,1536]{1,0:T(8,128)(2,1)} %get-tuple-element.118.q_ref.k_ref.v_ref, ...), custom_call_target="tpu_custom_call" | custom-call | flops 335544320 | bytes 131072 | tf_op jit(solution)/shard_map/attention_backward/pallas_call | solution.py:294
  442.5 0.0 copy-done
  442.5 0.0 copy-start.1
  442.5 1.0 copy-done.1
  443.5 80.7 %backward_tail.1 = (f32[1024,1024]{1,0:T(8,128)}, bf16[1024,1024]{1,0:T(8,128)(2,1)}, f32[64,1536]{1,0:T(8,128)}, f32[64,512]{1,0:T(8,128)}, f32[40,1024]{1,0:T(8,128)}) custom-call(bf16[2048,1024]{1,0:T(8,128)(2,1)} %refs_0_.3, bf16[2048,1024]{1,0:T(8,128)(2,1)} %get-tuple-element.101.refs_1_, bf16[2048,1024]{1,0:T(8,128)(2,1)} %get-tuple-element.102.refs_2_, ...), custom_call_target="tpu_custom_call" | custom-call | flops 201326592 | bytes 524288 | tf_op jit(solution)/shard_map/backward_tail/pallas_call | solution.py:2001
  524.3 0.0 collective-permute-done.1.theirs_ref
  524.3 0.0 reduce-scatter.3.cloned.1.call-done.h_ref
  524.3 0.0 reduce-scatter.5.cloned.1.call-done.r_ref
  524.3 0.0 copy-start.4
  524.3 9.3 %results.1 = (f32[1024,1024]{1,0:T(8,128)}, bf16[1024,1024]{1,0:T(8,128)(2,1)}, f32[64,512]{1,0:T(8,128)}, f32[64,512]{1,0:T(8,128)}, f32[64,512]{1,0:T(8,128)},...) custom-call(s32[1]{0:T(128)} %bitcast.at_ref, ...), custom_call_target="tpu_custom_call" | custom-call | flops 16384 | bytes 360448 | tf_op jit(solution)/shard_map/results/pallas_call | solution.py:2106
  533.7 0.0 copy-done.4
  533.7 0.7 copy.47
  (2 shorter events, 0.0 us)
Async XLA Ops:
  7.2 517.1 %reduce-scatter.3.cloned.1.call-start = ((), (), s32[]{:S(2)}) async-start(), calls=%async_computation.3 | async-start | bytes 4456448 | tf_op jit(solution)/shard_map/reduce_scatter | solution.py:2193
  310.3 214.0 %reduce-scatter.5.cloned.1.call-start = ((), (), s32[]{:S(2)}) async-start(), calls=%async_computation.4 | async-start | bytes 4456448 | tf_op jit(solution)/shard_map/reduce_scatter | solution.py:2193
  310.4 5.4 copy-start.5
  311.1 64.1 %all-to-all-start = ((bf16[16,64,1024]{2,1,0:T(8,128)(2,1)}), bf16[16,64,1024]{2,1,0:T(8,128)(2,1)}, u32[]{:S(2)}, u32[]{:S(2)}) async-start(bf16[16,64,1024]{2,1,0:T(8,128)(2,1)} %get-tuple-element.113), calls=%async_computation | async-start | bytes 4194304 | tf_op jit(solution)/shard_map/all_to_all | solution.py:2180
  316.4 40.2 %copy-start.2 = (f32[4,2,2048]{2,1,0:T(2,128)S(1)}, f32[4,2,2048]{2,1,0:T(2,128)}, u32[]{:S(2)}) copy-start(f32[4,2,2048]{2,1,0:T(2,128)} %get-tuple-element.106.lse_ref) | copy-start | bytes 196612
  355.5 30.0 %collective-permute-start = (bf16[2048,256]{1,0:T(8,128)(2,1)}, bf16[2048,256]{1,0:T(8,128)(2,1)S(1)}, u32[]{:S(2)}, u32[]{:S(2)}) collective-permute-start(bf16[2048,256]{1,0:T(8,128)(2,1)} %get-tuple-element.117), channel_id=1, source_target_pairs={{0,1},{1,0},{2,3},{3,2},{4,5},{5,4},{6,7},{7,6},{8,9},{9,8},{10,11... | collective-permute-start | bytes 3145736 | tf_op jit(solution)/shard_map/ppermute | solution.py:2177
  375.2 12.2 %copy-start.6 = (f32[8,1024]{1,0:T(8,128)S(1)}, f32[8,1024]{1,0:T(8,128)}, u32[]{:S(2)}) copy-start(f32[8,1024]{1,0:T(8,128)} %get-tuple-element.132) | copy-start | bytes 98308
  385.5 21.3 %copy-start.3 = (bf16[2048,256]{1,0:T(8,128)(2,1)}, bf16[2048,256]{1,0:T(8,128)(2,1)S(1)}, u32[]{:S(2)}) copy-start(bf16[2048,256]{1,0:T(8,128)(2,1)S(1)} %collective-permute-done.refs_1_) | copy-start | bytes 3145732
  385.5 138.7 %collective-permute-start.1 = (bf16[1024,1024]{1,0:T(8,128)(2,1)}, bf16[1024,1024]{1,0:T(8,128)(2,1)}, u32[]{:S(2)}, u32[]{:S(2)}) collective-permute-start(bf16[1024,1024]{1,0:T(8,128)(2,1)} %get-tuple-element.137), channel_id=1, source_target_pairs={{0,1},{1,0},{2,3},{3,2},{4,5},{5,4},{6,7},{7,6},{8,9},{9,8},{10,11... | collective-permute-start | bytes 6291464 | tf_op jit(solution)/shard_map/ppermute | solution.py:2177
  406.8 35.8 %copy-start = (bf16[2048,256]{1,0:T(8,128)(2,1)}, bf16[2048,256]{1,0:T(8,128)(2,1)S(1)}, u32[]{:S(2)}) copy-start(bf16[2048,256]{1,0:T(8,128)(2,1)S(1)} %get-tuple-element.122.refs_4_) | copy-start | bytes 3145732
  442.5 1.0 copy-start.1
  524.3 9.4 %copy-start.4 = (f32[64,512]{1,0:T(8,128)S(1)}, f32[64,512]{1,0:T(8,128)}, u32[]{:S(2)}) copy-start(f32[64,512]{1,0:T(8,128)} %get-tuple-element.179) | copy-start | bytes 393220
Sparse Core Ops, SparseCore 0:
  310.5 86.5 reduce-scatter.2
  401.4 71.4 reduce-scatter.4

commit v7 on v5

--- a/solution.py
+++ b/solution.py
@@ -1467,7 +1467,7 @@
     experts,
     shard,
     sent=None,
-    rb=256,
+    rb=512,
 ):
     rows, wide = dx.shape
     capacity = dots.shape[1]
@@ -1643,7 +1643,7 @@
         own_ref[...] = total
 
 
-def combine(first_row, info, y, coef, slot_rows, experts, capacity, rb=256):
+def combine(first_row, info, y, coef, slot_rows, experts, capacity, rb=512):
     rows, wide = y.shape
     half = rows // rb // 2
 
@@ -1688,32 +1688,69 @@
             device_id_type=pl.DeviceIdType.MESH,
         )
 
-    def halves(self, s):
-        place = sum(1 for b in self.order[s:] if b < self.order[s])
-        low = (1 << place) - 1
-        return [((i >> place) << (place + 1) | (i & low)) for i in range(self.size >> (s + 1))], 1 << place
-
     def bit(self, s):
         return lax.rem(lax.div(self.me, 1 << self.order[s]), 2)
 
+    def each(self, s, body):
+        place = sum(1 for b in self.order[s:] if b < self.order[s])
+        low = 1 << place
+
+        def step(i, _):
+            body(self.block(i), lax.div(i, low) * (2 * low) + lax.rem(i, low), low)
+            return 0
+
+        lax.fori_loop(0, self.size >> (s + 1), step, 0)
+
     def start(self, s):
-        places, step = self.halves(s)
-        for i, at in enumerate(places):
-            rows = slice(i * self.rows, (i + 1) * self.rows)
-            self.gives[s][rows, :] = self.total[self.block(at + (1 - self.bit(s)) * step), :].astype(BF16)
+        def give(rows, at, step):
+            other = self.total[self.block(at + (1 - self.bit(s)) * step), :]
+            self.gives[s][rows, :] = other.astype(BF16)
+
+        self.each(s, give)
         self.copy(s).start()
 
     def finish(self, s):
         self.copy(s).wait()
-        places, step = self.halves(s)
-        for i, at in enumerate(places):
-            rows = slice(i * self.rows, (i + 1) * self.rows)
+
+        def keep(rows, at, step):
             kept = self.total[self.block(at + self.bit(s) * step), :]
             self.total[rows, :] = kept + self.gots[s][rows, :].astype(F32)
+
+        self.each(s, keep)
 
     def step(self, s):
         self.finish(s)
         if s + 1 < len(self.order):
+            self.start(s + 1)
+
+
+class Rounds:
+    def __init__(self, total, gives, gots, send, recv, me, tp_me):
+        self.total, self.gives, self.gots = total, gives, gots
+        self.send, self.recv, self.me, self.tp_me = send, recv, me, tp_me
+
+    def copy(self, s):
+        peer = {"tp": 1 - self.tp_me} if s == 0 else {"ep": jnp.bitwise_xor(self.me, 1 << (s - 1))}
+        return pltpu.make_async_remote_copy(
+            src_ref=self.gives[s],
+            dst_ref=self.gots[s],
+            send_sem=self.send.at[s],
+            recv_sem=self.recv.at[s],
+            device_id=peer,
+            device_id_type=pl.DeviceIdType.MESH,
+        )
+
+    def start(self, s):
+        self.gives[s][...] = self.total[...]
+        self.copy(s).start()
+
+    def finish(self, s):
+        self.copy(s).wait()
+        self.total[...] += self.gots[s][...]
+
+    def step(self, s):
+        self.finish(s)
+        if s + 1 < len(self.gives):
             self.start(s + 1)
 
 
@@ -1739,6 +1776,7 @@
     gives_b, gots_b = take(steps), take(steps)
     go_gives, go_gots = take(steps), take(steps)
     small_gives, small_gots = take(hops), take(hops)
+    late_gives, late_gots = take(hops), take(hops)
     (
         load_sem,
         own_sem,
@@ -1752,6 +1790,8 @@
         go_recv,
         small_send,
         small_recv,
+        late_send,
+        late_recv,
         out_sem,
         out_give,
         out_got,
@@ -1798,12 +1838,19 @@
         Halving(acc_b, gives_b, gots_b, half_send_b, half_recv_b, me, size, other_order),
     ]
     go = Halving(goacc, go_gives, go_gots, go_send, go_recv, me, size, order)
+    early = Rounds(
+        total_ref.at[:small_rows, :], small_gives, small_gots, small_send, small_recv, me, tp_me
+    )
+    late = Rounds(
+        total_ref.at[small_rows:, :], late_gives, late_gots, late_send, late_recv, me, tp_me
+    )
 
     for c in theirs_loads:
         c.wait()
 
     total_ref[:small_rows, :] = small_ref[...]
-    total_ref[small_rows:, :] = jnp.zeros_like(total_ref[small_rows:, :])
+    total_ref[small_rows:, :] = jnp.zeros((8, total_ref.shape[1]), F32)
+    early.start(0)
 
     def pulled(at):
         total = None
@@ -1841,6 +1888,7 @@
     out_load.wait()
     goacc[...] = gov[...].astype(F32)
     go.start(0)
+    early.step(0)
     for c in own_loads + [a_load]:
         c.wait()
     cut = len(grads) // 2
@@ -1863,7 +1911,9 @@
         chain.start(0)
         if chain is qkv[0]:
             go.step(0)
+            early.step(1)
     qkv[0].step(0)
+    early.step(2)
     lax.fori_loop(count // 2, count, theirs, 0)
 
     def own_copy(b):
@@ -1877,25 +1927,16 @@
         return 0
 
     qkv[1].step(0)
+    early.step(3)
     lax.fori_loop(0, count // 2, own_step, 0)
     go.step(1)
     qkv[0].step(1)
+    for s in range(4, hops):
+        early.step(s)
     lax.fori_loop(count // 2, count, own_step, 0)
 
-    def small_copy(s):
-        peer = {"tp": 1 - tp_me} if s == 0 else {"ep": jnp.bitwise_xor(me, 1 << (s - 1))}
-        return pltpu.make_async_remote_copy(
-            src_ref=small_gives[s],
-            dst_ref=small_gots[s],
-            send_sem=small_send.at[s],
-            recv_sem=small_recv.at[s],
-            device_id=peer,
-            device_id_type=mesh,
-        )
-
     for s in range(hops):
-        small_gives[s][...] = total_ref[...]
-        small_copy(s).start()
+        late.start(s)
         if s + 2 < steps:
             go.step(s + 2)
         if s == 1:
@@ -1903,8 +1944,7 @@
             qkv[0].step(2)
         if s == 2:
             qkv[1].step(2)
-        small_copy(s).wait()
-        total_ref[...] += small_gots[s][...]
+        late.finish(s)
         if s == max(0, steps - 3):
             own_width = outsum_ref.shape[1]
             out_give[...] = goacc[: goacc.shape[0] // size, own_width:].astype(BF16)
@@ -1969,7 +2009,8 @@
         ]
         + halves(total // 2) * 4
         + halves(out_width) * 2
-        + [pltpu.VMEM((small_rows + 8, wide), F32)] * (2 * (steps + 1))
+        + [pltpu.VMEM((small_rows, wide), F32)] * (2 * (steps + 1))
+        + [pltpu.VMEM((8, wide), F32)] * (2 * (steps + 1))
         + [
             pltpu.SemaphoreType.DMA((2, 3 + 3 * groups)),
             pltpu.SemaphoreType.DMA((shard // rb,)),
@@ -1977,7 +2018,7 @@
             pltpu.SemaphoreType.DMA((shard // rb,)),
         ]
         + [pltpu.SemaphoreType.DMA((steps,))] * 6
-        + [pltpu.SemaphoreType.DMA((steps + 1,))] * 2
+        + [pltpu.SemaphoreType.DMA((steps + 1,))] * 4
         + [
             pltpu.SemaphoreType.DMA((2,)),
             pltpu.VMEM((kept, out_width // 2), BF16),

time: 552 us -> 550 us (level)
  no operation moved by 1% of the time
where the time goes in v7:
time: 550 us; the launch traced here: 541 us
  Pallas kernels  508 us (92%)
  between operations  15.3 us (3%)
  local copies, waits for them, and re-layouts  7.11 us (1%)
  starting transfers between devices  6.78 us (1%)
    pallas_call x1, Pallas kernels, nets(): pl.pallas_call(partial(nets_kernel, peers=peers, capacity=capacity, rb=rb...  187 us
    pallas_call x1, Pallas kernels, front(): pl.pallas_call(partial(front_kernel, peers=peers, experts=experts, half=h...  112 us
    pallas_call x1, Pallas kernels, tail(): pl.pallas_call(partial(tail_kernel, groups=groups, size=size, rb=rb, smal...  79.8 us
    pallas_call x2, Pallas kernels, attention_backward(): pl.pallas_call(partial(attention_backward_kernel, terms=terms, carried=bo...  70.4 us
    pallas_call x1, Pallas kernels, ffn_pull(): pl.pallas_call(partial(ffn_pull_kernel, parts=len(weights), experts=exper...  39.1 us
  transfers between devices with their start and end apart: 5, of which 0 were waited for; matrix products, arithmetic and copies ran while one was open for 0% of the time, Pallas kernels for 37%

profile of v7, /device:TPU:0, one launch (start us, length us, event | category | flops | bytes accessed | tf_op | source)
XLA Modules:
  0.0 540.5 jit_solution(14505474147061713119)
XLA Ops:
  7.2 0.0 reduce-scatter.3.cloned.1.call-start
  7.2 0.8 pad_maximum_fusion.1
  8.0 0.2 copy.37
  8.2 0.7 maximum_convert_fusion
  8.9 0.6 reshape.66.refs_7_.refs_11_
  10.2 0.5 compare_convert_fusion.sel_ref
  10.7 0.8 pad.8.refs_8_.rm_ref
  11.5 111.6 %layer_front.1 = (bf16[2048,1024]{1,0:T(8,128)(2,1)}, bf16[2048,1536]{1,0:T(8,128)(2,1)}, bf16[2048,512]{1,0:T(8,128)(2,1)}, bf16[2048,512]{1,0:T(8,128)(2,1)}, ...) custom-call(bf16[2048,1024]{1,0:T(8,128)(2,1)} %refs_0_.3, ...), custom_call_target="tpu_custom_call" | custom-call | flops 671088640 | bytes 983040 | tf_op jit(solution)/shard_map/layer_front/pallas_call | solution.py:747
  123.1 187.3 %feed_forward_nets.1 = (bf16[2048,1024]{1,0:T(8,128)(2,1)}, bf16[2048,1024]{1,0:T(8,128)(2,1)}, f32[2048,128]{1,0:T(8,128)}, bf16[1024,2048]{1,0:T(8,128)(2,1)},...) custom-call(bf16[2048,1024]{1,0:T(8,128)(2,1)} %get-tuple-element.85, ...), custom_call_target="tpu_custom_call" | custom-call | flops 1610612736 | bytes 1310720 | tf_op jit(solution)/shard_map/feed_forward_nets/pallas_call | solution.py:1278
  310.4 0.0 reduce-scatter.3.cloned.1.call-update
  310.4 0.0 reduce-scatter.5.cloned.1.call-start
  310.5 0.0 copy-start.6
  310.5 0.7 reduce-scatter.5.cloned.1.call-update
  311.2 4.5 all-to-all-start
  315.7 0.0 copy-done.6
  315.8 0.6 pad.9.refs_10_
  316.4 0.0 copy-start.2
  316.4 39.1 %ffn_norm_pull.1 = (bf16[2048,1024]{1,0:T(8,128)(2,1)}, bf16[2048,256]{1,0:T(8,128)(2,1)}, bf16[2048,256]{1,0:T(8,128)(2,1)}, bf16[2048,256]{1,0:T(8,128)(2,1)},...) custom-call(f32[2048,128]{1,0:T(8,128)} %get-tuple-element.84.refs_0_.info_ref, ...), custom_call_target="tpu_custom_call" | custom-call | flops 201326592 | bytes 524288 | tf_op jit(solution)/shard_map/ffn_norm_pull/pallas_call | solution.py:1490
  355.5 0.6 collective-permute-start
  356.1 0.0 copy-done.2
  356.2 35.1 %attention_backward.2 = (bf16[2048,256]{1,0:T(8,128)(2,1)S(1)}, bf16[2048,256]{1,0:T(8,128)(2,1)}, bf16[2048,256]{1,0:T(8,128)(2,1)}, f32[1024,2048]{1,0:T(8,128)}) custom-call(bf16[2048,1536]{1,0:T(8,128)(2,1)} %get-tuple-element.117.q_ref.k_ref.v_ref, bf16[2048,1536]{1,0:T(8,128)(2,1)} %get-tuple-element.117.q_ref.k_ref.v_ref, ...), custom_call_target="tpu_custom_call" | custom-call | flops 335544320 | bytes 131072 | tf_op jit(solution)/shard_map/attention_backward/pallas_call | solution.py:284
  391.3 0.0 copy-start
  391.3 1.0 copy-done
  392.3 0.0 collective-permute-done.refs_1_
  392.3 0.0 copy-start.4
  392.3 0.0 all-to-all-done
  392.3 0.0 copy-start.3
  392.3 1.3 copy-done.3
  393.6 0.0 copy-start.7
  393.6 10.2 %combine_nets.1 = (bf16[1024,1024]{1,0:T(8,128)(2,1)}, bf16[1024,1024]{1,0:T(8,128)(2,1)}) custom-call(s32[1]{0:T(128)} %bitcast.7.at_ref, f32[2048,128]{1,0:T(8,128)} %get-tuple-element.84.refs_0_.info_ref, bf16[2048,1024]{1,0:T(8,128)(2,1)} %get-tuple-element.113.y_ref, f32[2048,128]{1,0:T(8,128)} %get-tuple-element.90.refs_2_.chance_ref, ...), custom_call_target="tpu_custom_call" | custom-call | flops 134217728 | bytes 262144 | tf_op jit(solution)/shard_map/combine_nets/pallas_call | solution.py:1654
  403.9 1.6 collective-permute-start.1
  405.4 0.9 slice.7
  406.3 0.0 copy-done.7
  406.3 0.7 pad_maximum_fusion.refs_10_
  407.0 0.0 copy-done.4
  407.0 35.3 %attention_backward.3 = (bf16[2048,256]{1,0:T(8,128)(2,1)S(1)}, bf16[2048,256]{1,0:T(8,128)(2,1)}, bf16[2048,256]{1,0:T(8,128)(2,1)}, f32[1024,2048]{1,0:T(8,128)}) custom-call(bf16[2048,1536]{1,0:T(8,128)(2,1)} %get-tuple-element.117.q_ref.k_ref.v_ref, bf16[2048,1536]{1,0:T(8,128)(2,1)} %get-tuple-element.117.q_ref.k_ref.v_ref, ...), custom_call_target="tpu_custom_call" | custom-call | flops 335544320 | bytes 131072 | tf_op jit(solution)/shard_map/attention_backward/pallas_call | solution.py:284
  442.3 0.0 copy-start.1
  442.3 1.0 copy-done.1
  443.3 79.8 %backward_tail.1 = (f32[1024,1024]{1,0:T(8,128)}, bf16[1024,1024]{1,0:T(8,128)(2,1)}, f32[64,1536]{1,0:T(8,128)}, f32[64,512]{1,0:T(8,128)}, f32[40,1024]{1,0:T(8,128)}) custom-call(bf16[2048,1024]{1,0:T(8,128)(2,1)} %refs_0_.3, bf16[2048,1024]{1,0:T(8,128)(2,1)} %get-tuple-element.98.refs_1_, bf16[2048,1024]{1,0:T(8,128)(2,1)} %get-tuple-element.99.refs_2_, ...), custom_call_target="tpu_custom_call" | custom-call | flops 201326592 | bytes 524288 | tf_op jit(solution)/shard_map/backward_tail/pallas_call | solution.py:1989
  523.1 0.0 collective-permute-done.1.theirs_ref
  523.2 0.0 reduce-scatter.3.cloned.1.call-done.h_ref
  523.2 0.0 reduce-scatter.5.cloned.1.call-done.r_ref
  523.2 0.0 copy-start.5
  523.2 9.3 %results.1 = (f32[1024,1024]{1,0:T(8,128)}, bf16[1024,1024]{1,0:T(8,128)(2,1)}, f32[64,512]{1,0:T(8,128)}, f32[64,512]{1,0:T(8,128)}, f32[64,512]{1,0:T(8,128)},...) custom-call(s32[1]{0:T(128)} %bitcast.at_ref, ...), custom_call_target="tpu_custom_call" | custom-call | flops 16384 | bytes 360448 | tf_op jit(solution)/shard_map/results/pallas_call | solution.py:2094
  532.6 0.0 copy-done.5
  532.6 0.7 copy.41
  (2 shorter events, 0.0 us)
Async XLA Ops:
  7.2 516.0 %reduce-scatter.3.cloned.1.call-start = ((), (), s32[]{:S(2)}) async-start(), calls=%async_computation.3 | async-start | bytes 4456448 | tf_op jit(solution)/shard_map/reduce_scatter | solution.py:2181
  310.4 212.8 %reduce-scatter.5.cloned.1.call-start = ((), (), s32[]{:S(2)}) async-start(), calls=%async_computation.4 | async-start | bytes 4456448 | tf_op jit(solution)/shard_map/reduce_scatter | solution.py:2181
  310.5 5.2 copy-start.6
  311.2 81.1 %all-to-all-start = ((bf16[16,64,1024]{2,1,0:T(8,128)(2,1)}), bf16[16,64,1024]{2,1,0:T(8,128)(2,1)S(1)}, u32[]{:S(2)}, u32[]{:S(2)}) async-start(bf16[16,64,1024]{2,1,0:T(8,128)(2,1)} %get-tuple-element.114), calls=%async_computation | async-start | bytes 4194304 | tf_op jit(solution)/shard_map/all_to_all | solution.py:2168
  316.4 39.8 %copy-start.2 = (f32[4,2,2048]{2,1,0:T(2,128)S(1)}, f32[4,2,2048]{2,1,0:T(2,128)}, u32[]{:S(2)}) copy-start(f32[4,2,2048]{2,1,0:T(2,128)} %get-tuple-element.103.lse_ref) | copy-start | bytes 196612
  355.5 36.8 %collective-permute-start = (bf16[2048,256]{1,0:T(8,128)(2,1)}, bf16[2048,256]{1,0:T(8,128)(2,1)S(1)}, u32[]{:S(2)}, u32[]{:S(2)}) collective-permute-start(bf16[2048,256]{1,0:T(8,128)(2,1)} %get-tuple-element.111), channel_id=1, source_target_pairs={{0,1},{1,0},{2,3},{3,2},{4,5},{5,4},{6,7},{7,6},{8,9},{9,8},{10,11... | collective-permute-start | bytes 3145736 | tf_op jit(solution)/shard_map/ppermute | solution.py:2165
  391.3 1.0 copy-start
  392.3 14.7 %copy-start.4 = (bf16[2048,256]{1,0:T(8,128)(2,1)}, bf16[2048,256]{1,0:T(8,128)(2,1)S(1)}, u32[]{:S(2)}) copy-start(bf16[2048,256]{1,0:T(8,128)(2,1)S(1)} %collective-permute-done.refs_1_) | copy-start | bytes 3145732
  392.3 1.3 copy-start.3
  393.6 12.7 %copy-start.7 = (f32[8,1024]{1,0:T(8,128)S(1)}, f32[8,1024]{1,0:T(8,128)}, u32[]{:S(2)}) copy-start(f32[8,1024]{1,0:T(8,128)} %get-tuple-element.126) | copy-start | bytes 98308
  403.9 119.3 %collective-permute-start.1 = (bf16[1024,1024]{1,0:T(8,128)(2,1)}, bf16[1024,1024]{1,0:T(8,128)(2,1)}, u32[]{:S(2)}, u32[]{:S(2)}) collective-permute-start(bf16[1024,1024]{1,0:T(8,128)(2,1)} %get-tuple-element.131), channel_id=1, source_target_pairs={{0,1},{1,0},{2,3},{3,2},{4,5},{5,4},{6,7},{7,6},{8,9},{9,8},{10,11... | collective-permute-start | bytes 6291464 | tf_op jit(solution)/shard_map/ppermute | solution.py:2165
  442.3 1.0 copy-start.1
  523.2 9.4 %copy-start.5 = (f32[64,512]{1,0:T(8,128)S(1)}, f32[64,512]{1,0:T(8,128)}, u32[]{:S(2)}) copy-start(f32[64,512]{1,0:T(8,128)} %get-tuple-element.173) | copy-start | bytes 393220
Sparse Core Ops, SparseCore 0:
  310.6 86.3 reduce-scatter.2
  401.3 72.8 reduce-scatter.4
